TPU v7x, 32 devices: a whole 2x2x4 slice. The times are simulated.
32 devices in a mesh: dp: 8 (over y, x, core), seq: 4 (over z).
Axes of the slice: x: 2, y: 2, z: 4, core: 2. Of those that a mesh axis runs over, the one named last changes fastest.
Arguments:
- tokens: bfloat16 [24, 1024, 768], P('dp', 'seq'), may hold values from -6 to 6
- init_state: float32 [24, 384, 2], P('dp', 'seq'), may hold values from -6 to 6
- norm_mix: float32 [768], replicated, may hold values from 0.1 to 1.9
- w_in: bfloat16 [768, 768], replicated, may hold values from -0.21875 to 0.21875
- w_forget: bfloat16 [768, 384], replicated, may hold values from -0.21875 to 0.21875
- forget_bias: float32 [384], replicated, may hold values from 2 to 8
- phase: float32 [384], P('seq'), may hold values from -3.140625 to 3.140625
- w_ogate: bfloat16 [768, 768], replicated, may hold values from -0.21875 to 0.21875
- norm_group: float32 [768], replicated, may hold values from 0.1 to 1.9
- w_out: bfloat16 [768, 768], replicated, may hold values from -0.21875 to 0.21875
- norm_ffn: float32 [768], replicated, may hold values from 0.1 to 1.9
- w_gate: bfloat16 [768, 1536], replicated, may hold values from -0.21875 to 0.21875
- w_up: bfloat16 [768, 1536], replicated, may hold values from -0.21875 to 0.21875
- w_down: bfloat16 [1536, 768], replicated, may hold values from -0.15625 to 0.15625
- cotangent: bfloat16 [24, 1024, 768], P('dp', 'seq'), may hold values from -6 to 6
Outputs:
- mixed_out: bfloat16 [24, 1024, 768], P('dp', 'seq')
- grad_tokens: bfloat16 [24, 1024, 768], P('dp', 'seq')
- final_state: float32 [24, 384, 2], P('dp', 'seq')
- grad_norm_mix: float32 [768], P('dp')
- grad_w_in: float32 [768, 768], P('dp')
- grad_w_forget: float32 [768, 384], P('dp')
- grad_forget_bias: float32 [384], P('seq')
- grad_phase: float32 [384], P('seq')
- grad_w_ogate: float32 [768, 768], P('dp')
- grad_norm_group: float32 [768], P('dp')
- grad_w_out: float32 [768, 768], P('dp')
- grad_norm_ffn: float32 [768], P('dp')
- grad_w_gate: float32 [768, 1536], P('dp')
- grad_w_up: float32 [768, 1536], P('dp')
- grad_w_down: float32 [1536, 768], P('dp')
All inputs are finite; a program needn't handle non-finite values.
Results may differ from a plain program's by a relative error of at most 0.015.
Values may be sent and summed in bfloat16 or wider, within the bound.
No kernel may reach another device: no remote copies, remote signals or barrier semaphores. Data moves between devices by JAX's collectives and lax.ppermute only.
A program may use at most 192 MiB of HBM per device.

v0:
```python
import functools

import jax
import jax.numpy as jnp
from jax import lax
from jax.experimental import pallas as pl
from jax.experimental.pallas import tpu as pltpu
from jax.sharding import PartitionSpec as P

GROUPS = 8
CHUNKS = 8
LANES = 128
TILE = 16
epsilon = 1e-06
BF = jnp.bfloat16
F32 = jnp.float32
NT = ((1,), (1,))


def dot(a, b, dims=((1,), (0,))):
    return lax.dot_general(a, b, (dims, ((), ())), preferred_element_type=F32)


def silu_slope(values, logistic):
    return logistic * (1.0 + values * (1.0 - logistic))


def cmul(ar, ai, br, bi):
    return ar * br - ai * bi, ar * bi + ai * br


def row_mean(v):
    return jnp.mean(v, axis=-1, keepdims=True)


def split_dot(v, m, dims):
    high = v.astype(BF)
    low = (v - high.astype(F32)).astype(BF)
    return dot(high, m, dims) + dot(low, m, dims)


def group_mean(v, member):
    return split_dot(v, member, ((1,), (0,))) * (GROUPS / v.shape[1])


def group_spread(v, member):
    return split_dot(v, member, NT)


def put_halves(ref, t, col, lo, bit):
    half = ref.shape[0] // 2
    for b in range(t.shape[0] // lo):
        at = jnp.where(bit == b % 2, half, 0) + (b // 2) * lo
        ref[pl.ds(pl.multiple_of(at, TILE), lo), col : col + t.shape[1]] = t[b * lo : (b + 1) * lo, :]


def put(ref, value):
    for g in range(ref.shape[0]):
        ref[g] = value[:, g * LANES : (g + 1) * LANES]


def get(ref):
    return jnp.concatenate([ref[g] for g in range(ref.shape[0])], axis=1)


def lanes(value, parts):
    return [value[:, g * LANES : (g + 1) * LANES] for g in range(parts)]


def decays(pre, trig, lam_re, lam_im):
    ch = lam_re.shape[0] * LANES
    forget = jax.nn.sigmoid(pre[:, 2 * ch :])
    put(lam_re, forget * trig[0:1, :])
    put(lam_im, forget * trig[1:2, :])
    return forget


def drives(pre, trig, lam_re, lam_im, drv_re, drv_im):
    ch = lam_re.shape[0] * LANES
    forget = decays(pre, trig, lam_re, lam_im)
    put(drv_re, (1.0 - forget) * jax.nn.silu(pre[:, :ch]))
    put(drv_im, (1.0 - forget) * jax.nn.silu(pre[:, ch : 2 * ch]))


def project_kernel(bit_ref, x_ref, gain_ref, w_in_ref, w_forget_ref, bias_ref, perm_ref, normed_ref, turned_ref, pre_ref, *, lo):
    width = x_ref.shape[1]
    x = x_ref[...].astype(F32)
    normed = (x * lax.rsqrt(row_mean(x * x) + epsilon) * gain_ref[...][None]).astype(BF)
    normed_ref[...] = normed
    put_halves(turned_ref, normed.T, 0, lo, bit_ref[0])
    mixed = dot(normed, w_in_ref[...]).astype(BF)
    pre_ref[:, :width] = dot(mixed, perm_ref[...]).astype(BF)
    pre_ref[:, width:] = (dot(normed, w_forget_ref[...]) + bias_ref[...][None]).astype(BF)


def summary_kernel(*refs, ranks):
    pre_ref, infos = refs[0], refs[1 : 1 + ranks]
    trig_ref, chunk_ref, total_ref, lam_re, lam_im, drv_re, drv_im = refs[1 + ranks :]
    parts, span, _ = lam_re.shape
    step = span // CHUNKS
    trig = infos[0][...]
    for info in infos[1:]:
        trig = trig + info[...]
    trig_ref[...] = trig
    drives(pre_ref[...].astype(F32), trig, lam_re, lam_im, drv_re, drv_im)
    carried = [None] * parts
    for t in range(step):
        rows = pl.ds(t, CHUNKS, stride=step)
        for g in range(parts):
            lr, li = lam_re[g, rows, :], lam_im[g, rows, :]
            br, bi = drv_re[g, rows, :], drv_im[g, rows, :]
            if t == 0:
                carried[g] = (lr, li, br, bi)
            else:
                pr, pi, hr, hi = carried[g]
                pr, pi = cmul(lr, li, pr, pi)
                hr, hi = cmul(lr, li, hr, hi)
                carried[g] = (pr, pi, hr + br, hi + bi)
    pr, pi, hr, hi = (jnp.concatenate([carried[g][q] for g in range(parts)], axis=1) for q in range(4))
    chunk_ref[0], chunk_ref[1], chunk_ref[2], chunk_ref[3] = pr, pi, hr, hi
    tp_r, tp_i, th_r, th_i = pr[0:1], pi[0:1], hr[0:1], hi[0:1]
    for k in range(1, CHUNKS):
        lr, li = pr[k : k + 1], pi[k : k + 1]
        th_r, th_i = cmul(lr, li, th_r, th_i)
        th_r, th_i = th_r + hr[k : k + 1], th_i + hi[k : k + 1]
        tp_r, tp_i = cmul(lr, li, tp_r, tp_i)
    total_ref[...] = jnp.concatenate([tp_r, tp_i, th_r, th_i], axis=0)


def mixer_kernel(*refs, ranks, lo):
    scalars, refs = refs[0], refs[1:]
    totals, inits, refs = refs[:ranks], refs[ranks : 2 * ranks], refs[2 * ranks :]
    pre_ref, trig_ref, chunk_ref, perm_ref, x_ref, og_ref, gain_ref, member_ref, w_out_ref = refs[:9]
    y_ref, hr_ref, hi_ref, start_ref, final_ref, turned_ref, middle_ref = refs[9:16]
    lam_re, lam_im, drv_re, drv_im = refs[16:]
    parts, span, _ = lam_re.shape
    step = span // CHUNKS
    rank, bit = scalars[0], scalars[1]
    drives(pre_ref[...].astype(F32), trig_ref[...], lam_re, lam_im, drv_re, drv_im)
    init = inits[0][...]
    for info in inits[1:]:
        init = init + info[...]
    cr, ci = init[0:1], init[1:2]

    def after(k, cr, ci, take):
        total = totals[k][...]
        nr, ni = cmul(total[0:1], total[1:2], cr, ci)
        nr, ni = nr + total[2:3], ni + total[3:4]
        return jnp.where(take, nr, cr), jnp.where(take, ni, ci)

    for k in range(ranks - 1, 0, -1):
        cr, ci = after(k, cr, ci, k <= rank)
    start_ref[...] = jnp.concatenate([cr, ci], axis=0)
    er, ei = after(0, cr, ci, rank >= 0)
    for k in range(ranks - 1, 0, -1):
        er, ei = after(k, er, ei, k > rank)
    final_ref[...] = jnp.concatenate([er, ei], axis=0)
    rows_r, rows_i = [cr], [ci]
    for k in range(CHUNKS - 1):
        cr, ci = cmul(chunk_ref[0, k : k + 1, :], chunk_ref[1, k : k + 1, :], cr, ci)
        cr, ci = cr + chunk_ref[2, k : k + 1, :], ci + chunk_ref[3, k : k + 1, :]
        rows_r.append(cr)
        rows_i.append(ci)
    carried = list(
        zip(lanes(jnp.concatenate(rows_r, axis=0), parts), lanes(jnp.concatenate(rows_i, axis=0), parts), strict=True)
    )
    for t in range(step):
        rows = pl.ds(t, CHUNKS, stride=step)
        for g in range(parts):
            hr, hi = cmul(lam_re[g, rows, :], lam_im[g, rows, :], *carried[g])
            hr, hi = hr + drv_re[g, rows, :], hi + drv_im[g, rows, :]
            hr_ref[g, rows, :] = hr
            hi_ref[g, rows, :] = hi
            carried[g] = (hr, hi)
    split = jnp.concatenate([get(hr_ref).astype(BF), get(hi_ref).astype(BF)], axis=1)
    yf = dot(split, perm_ref[...], NT)
    y_ref[...] = yf.astype(BF)
    member = member_ref[...]
    inv = group_spread(lax.rsqrt(group_mean(yf * yf, member) + epsilon), member)
    gated = (yf * inv * gain_ref[...][None] * jax.nn.silu(og_ref[...])).astype(BF)
    put_halves(turned_ref, gated.T, 0, lo, bit)
    middle_ref[...] = x_ref[...].astype(F32) + dot(gated, w_out_ref[...])


def ffn_kernel(
    bit_ref, middle_ref, gain_ref, cot_ref, wg_ref, wu_ref, wd_ref,
    gsend_ref, gkeep_ref, dsend_ref, dkeep_ref, mixed_ref, dn_ref,
    n_ref, nt_ref, acc_ref, hid_ref, dgv_ref, duv_ref, ht_ref,
    *, lo, dlo, rt,
):
    j, last = pl.program_id(0), pl.num_programs(0) - 1
    bit = bit_ref[0]
    count, width = middle_ref.shape
    tile = wg_ref.shape[1]
    spans = [slice(r, r + rt) for r in range(0, count, rt)]

    @pl.when(j == 0)
    def _():
        for rows in spans:
            v = middle_ref[rows, :]
            normed = (v * lax.rsqrt(row_mean(v * v) + epsilon) * gain_ref[...][None]).astype(BF)
            n_ref[rows, :] = normed
            put_halves(nt_ref, normed.T, rows.start, lo, bit)

    for rows in spans:
        g, u = dot(n_ref[rows, :], wg_ref[...]), dot(n_ref[rows, :], wu_ref[...])
        dh = dot(cot_ref[rows, :], wd_ref[...], NT)
        sig = jax.nn.sigmoid(g)
        act = g * sig
        hid_ref[rows, :] = (act * u).astype(BF)
        dgv_ref[rows, :] = (dh * u * silu_slope(g, sig)).astype(BF)
        duv_ref[rows, :] = (dh * act).astype(BF)
    for rows in spans:
        put_halves(ht_ref, hid_ref[rows, :].T, rows.start, dlo, bit)
    for lhs, ref in ((nt_ref[: width // 2, :], gsend_ref), (nt_ref[width // 2 :, :], gkeep_ref)):
        ref[:, :tile] = dot(lhs, dgv_ref[...]).astype(BF)
        ref[:, tile:] = dot(lhs, duv_ref[...]).astype(BF)
    for lhs, ref in ((ht_ref[: tile // 2, :], dsend_ref), (ht_ref[tile // 2 :, :], dkeep_ref)):
        ref[...] = dot(lhs, cot_ref[...]).astype(BF)
    for rows in spans:
        out = dot(hid_ref[rows, :], wd_ref[...])
        dn = dot(dgv_ref[rows, :], wg_ref[...], NT) + dot(duv_ref[rows, :], wu_ref[...], NT)

        @pl.when(j == 0)
        def _():
            acc_ref[rows, :] = middle_ref[rows, :] + out
            dn_ref[rows, :] = dn

        @pl.when(j > 0)
        def _():
            acc_ref[rows, :] += out
            dn_ref[rows, :] += dn

        @pl.when(j == last)
        def _():
            mixed_ref[rows, :] = acc_ref[rows, :].astype(BF)


def turn_kernel(
    dn_ref, middle_ref, cot_ref, ffn_gain_ref, w_out_ref, y_ref, og_ref, gain_ref, member_ref, perm_ref,
    pre_ref, trig_ref, chunk_ref,
    dmiddle_ref, dbranch_ref, dog_ref, split_ref, chain_ref, total_ref, gains_ref,
    lam_re, lam_im, dy_re, dy_im,
):
    parts, span, _ = lam_re.shape
    ch = parts * LANES
    step = span // CHUNKS
    v, up = middle_ref[...], dn_ref[...]
    inv = lax.rsqrt(row_mean(v * v) + epsilon)
    unit = v * inv
    through = up * ffn_gain_ref[...][None]
    dmiddle = cot_ref[...].astype(F32) + inv * (through - unit * row_mean(through * unit))
    gain_ffn = jnp.sum(up * unit, axis=0, keepdims=True)
    dmiddle_ref[...] = dmiddle
    dbranch = dmiddle.astype(BF)
    dbranch_ref[...] = dbranch
    dgated = dot(dbranch, w_out_ref[...], NT)
    og, yf, member, gain = og_ref[...], y_ref[...].astype(F32), member_ref[...], gain_ref[...][None]
    ginv = group_spread(lax.rsqrt(group_mean(yf * yf, member) + epsilon), member)
    gunit = yf * ginv
    sig = jax.nn.sigmoid(og)
    dog_ref[...] = (dgated * gunit * gain * silu_slope(og, sig)).astype(BF)
    dgn = dgated * og * sig
    gains = jnp.concatenate([gain_ffn, jnp.sum(dgn * gunit, axis=0, keepdims=True)], axis=0)

    @pl.when(pl.program_id(0) == 0)
    def _():
        gains_ref[...] = gains

    @pl.when(pl.program_id(0) > 0)
    def _():
        gains_ref[...] += gains

    through = dgn * gain
    dy = (ginv * (through - gunit * group_spread(group_mean(through * gunit, member), member))).astype(BF)
    split = dot(dy, perm_ref[...])
    split_ref[...] = split.astype(BF)
    decays(pre_ref[...].astype(F32), trig_ref[...], lam_re, lam_im)
    put(dy_re, split[:, :ch])
    put(dy_im, split[:, ch:])
    carried = [None] * parts
    for t in range(step - 1, -1, -1):
        rows = pl.ds(t, CHUNKS, stride=step)
        for g in range(parts):
            gr, gi = dy_re[g, rows, :], dy_im[g, rows, :]
            if carried[g] is not None:
                gr, gi = gr + carried[g][0], gi + carried[g][1]
            carried[g] = cmul(lam_re[g, rows, :], -lam_im[g, rows, :], gr, gi)
    ar, ai = (jnp.concatenate([carried[g][q] for g in range(parts)], axis=1) for q in range(2))
    chain_ref[0], chain_ref[1] = ar, ai
    er, ei = ar[CHUNKS - 1 :], ai[CHUNKS - 1 :]
    for k in range(CHUNKS - 2, -1, -1):
        er, ei = cmul(chunk_ref[0, k : k + 1, :], -chunk_ref[1, k : k + 1, :], er, ei)
        er, ei = er + ar[k : k + 1], ei + ai[k : k + 1]
    total_ref[...] = jnp.concatenate([er, ei], axis=0)


def adjoint_kernel(*refs, ranks):
    scalars, refs = refs[0], refs[1:]
    totals, adjs, refs = refs[:ranks], refs[ranks : 2 * ranks], refs[2 * ranks :]
    pre_ref, trig_ref, dy_ref, hr_ref, hi_ref, start_ref, chunk_ref, chain_ref, perm_ref = refs[:9]
    dpre_ref, sums_ref, lam_re, lam_im, dy_re, dy_im = refs[9:]
    parts, span, _ = lam_re.shape
    ch = parts * LANES
    step = span // CHUNKS
    rank = scalars[0]
    pre = pre_ref[...].astype(F32)
    trig = trig_ref[...]
    forget = decays(pre, trig, lam_re, lam_im)
    put(dy_re, dy_ref[:, :ch].astype(F32))
    put(dy_im, dy_ref[:, ch:].astype(F32))
    cr = jnp.zeros((1, ch), F32)
    ci = jnp.zeros((1, ch), F32)
    for k in range(1, ranks):
        total, adj = totals[k][...], adjs[k][...]
        nr, ni = cmul(total[0:1], -total[1:2], cr, ci)
        nr, ni = nr + adj[0:1], ni + adj[1:2]
        cr, ci = jnp.where(k > rank, nr, cr), jnp.where(k > rank, ni, ci)
    rows_r, rows_i = [cr], [ci]
    for k in range(CHUNKS - 1, 0, -1):
        cr, ci = cmul(chunk_ref[0, k : k + 1, :], -chunk_ref[1, k : k + 1, :], cr, ci)
        cr, ci = cr + chain_ref[0, k : k + 1, :], ci + chain_ref[1, k : k + 1, :]
        rows_r.append(cr)
        rows_i.append(ci)
    carried = list(
        zip(
            lanes(jnp.concatenate(rows_r[::-1], axis=0), parts),
            lanes(jnp.concatenate(rows_i[::-1], axis=0), parts),
            strict=True,
        )
    )
    for t in range(step - 1, -1, -1):
        rows = pl.ds(t, CHUNKS, stride=step)
        for g in range(parts):
            gr, gi = dy_re[g, rows, :] + carried[g][0], dy_im[g, rows, :] + carried[g][1]
            dy_re[g, rows, :] = gr
            dy_im[g, rows, :] = gi
            carried[g] = cmul(lam_re[g, rows, :], -lam_im[g, rows, :], gr, gi)
    gr, gi = get(dy_re), get(dy_im)
    first = lax.broadcasted_iota(jnp.int32, (span, ch), 0) == 0
    qr = jnp.where(first, start_ref[0:1, :], pltpu.roll(get(hr_ref), 1, 0))
    qi = jnp.where(first, start_ref[1:2, :], pltpu.roll(get(hi_ref), 1, 0))
    pin_re, pin_im = pre[:, :ch], pre[:, ch : 2 * ch]
    sig_re, sig_im = jax.nn.sigmoid(pin_re), jax.nn.sigmoid(pin_im)
    lr = gr * qr + gi * qi
    li = gi * qr - gr * qi
    turned_re = lr * trig[0:1, :] + li * trig[1:2, :]
    turned_im = li * trig[0:1, :] - lr * trig[1:2, :]
    df = turned_re - (gr * pin_re * sig_re + gi * pin_im * sig_im)
    keep = 1.0 - forget
    dre = (keep * gr * silu_slope(pin_re, sig_re)).astype(BF)
    dim = (keep * gi * silu_slope(pin_im, sig_im)).astype(BF)
    dpz = (forget * keep * df).astype(BF)
    dpre_ref[:, : 2 * ch] = dot(jnp.concatenate([dre, dim], axis=1), perm_ref[...], NT).astype(BF)
    dpre_ref[:, 2 * ch :] = dpz
    sums = jnp.concatenate(
        [
            jnp.sum(dpz.astype(F32), axis=0, keepdims=True),
            jnp.sum(forget * turned_im, axis=0, keepdims=True),
        ],
        axis=0,
    )

    @pl.when(pl.program_id(0) == 0)
    def _():
        sums_ref[...] = sums

    @pl.when(pl.program_id(0) > 0)
    def _():
        sums_ref[...] += sums


def grads_kernel(*refs, pairs):
    ins, (send_ref, keep_ref) = refs[: 2 * pairs], refs[2 * pairs :]
    at = 0
    for p in range(pairs):
        lhs_ref, rhs_ref = ins[2 * p], ins[2 * p + 1]
        half, n = lhs_ref.shape[0] // 2, rhs_ref.shape[1]
        send_ref[:, at : at + n] = dot(lhs_ref[:half, :], rhs_ref[...]).astype(BF)
        keep_ref[:, at : at + n] = dot(lhs_ref[half:, :], rhs_ref[...]).astype(BF)
        at += n


def tokens_kernel(
    dpre_ref, dog_ref, w_in_ref, w_forget_ref, w_ogate_ref, x_ref, gain_ref, dmiddle_ref, out_ref, gains_ref
):
    width = x_ref.shape[1]
    up = (
        dot(dpre_ref[:, :width], w_in_ref[...], NT)
        + dot(dpre_ref[:, width:], w_forget_ref[...], NT)
        + dot(dog_ref[...], w_ogate_ref[...], NT)
    )
    x = x_ref[...].astype(F32)
    inv = lax.rsqrt(row_mean(x * x) + epsilon)
    unit = x * inv
    through = up * gain_ref[...][None]
    out_ref[...] = (dmiddle_ref[...] + inv * (through - unit * row_mean(through * unit))).astype(BF)
    gains = jnp.sum(up * unit, axis=0, keepdims=True)

    @pl.when(pl.program_id(0) == 0)
    def _():
        gains_ref[...] = gains

    @pl.when(pl.program_id(0) > 0)
    def _():
        gains_ref[...] += gains


def seg(*shape):
    zeros = (0,) * len(shape)
    return pl.BlockSpec((None,) + shape, lambda s, *_: (s,) + zeros)


def rows(*shape):
    return pl.BlockSpec(shape, lambda s, *_: (s, 0))


def cols(*shape):
    return pl.BlockSpec(shape, lambda s, *_: (0, s))


def whole(*shape):
    zeros = (0,) * len(shape)
    return pl.BlockSpec(shape, lambda s, *_: zeros)


def call(kernel, steps, ins, outs, scratch, scalars, name, after=()):
    first, extra = len(scalars) + len(ins), len(after)

    def body(*refs):
        kernel(*refs[:first], *refs[first + extra :])

    return pl.pallas_call(
        body,
        grid_spec=pltpu.PrefetchScalarGridSpec(
            num_scalar_prefetch=len(scalars),
            grid=(steps,),
            in_specs=[s for s, _ in ins] + [pl.BlockSpec(memory_space=pl.ANY)] * extra,
            out_specs=[s for s, _, _ in outs],
            scratch_shapes=scratch,
        ),
        out_shape=[jax.ShapeDtypeStruct(s, d) for _, s, d in outs],
        compiler_params=pltpu.CompilerParams(vmem_limit_bytes=56 * 1024 * 1024),
        cost_estimate=pl.CostEstimate(flops=1, bytes_accessed=1, transcendentals=0),
        name=name,
    )(*scalars, *[a for _, a in ins], *after)


def shift_all(payload, axis, n):
    return [payload] + [lax.ppermute(payload, axis, [(i, (i + k) % n) for i in range(n)]) for k in range(1, n)]


def own_bit(axis, bit):
    return (lax.axis_index(axis) // bit) % 2


def swap(v, axis, n, bit):
    return lax.ppermute(v, axis, [(i, i ^ bit) for i in range(n)])


def bits_of(n):
    return [1 << i for i in range((n - 1).bit_length())]


def combine_kernel(bits_ref, *refs, layout):
    n_in = sum(2 * addends for lane in layout for addends, _ in lane)
    ins, outs = list(refs[:n_in]), list(refs[n_in:])
    for lane in layout:
        for out in (outs.pop(0), outs.pop(0)):
            at = 0
            for addends, width in lane:
                acc = ins.pop(0)[...].astype(F32)
                for _ in range(addends - 1):
                    acc = acc + ins.pop(0)[...].astype(F32)
                out[:, at : at + width] = acc.astype(out.dtype)
                at += width


def combine(lanes_in, name, after=()):
    scalars = jnp.stack([bit for _, bit, _ in lanes_in]).astype(jnp.int32)
    ins, outs, layout, steps = [], [], [], None
    for n, (pos, _, sources) in enumerate(lanes_in):
        width = sum(src[4] for src in sources)
        addends, mult = sources[0][0], sources[0][1]
        per = addends[0].shape[1]
        count = addends[0].shape[0] // mult // 2
        assert steps in (None, count)
        steps = count
        for flip in (1, 0):
            for addends, mult, off, col, w in sources:
                def index(i, bits, n=n, pos=pos, flip=flip, mult=mult, off=off, col=col):
                    own = bits[n] if not flip else 1 - bits[n]
                    low = i % (1 << pos)
                    return (((i - low) * 2 + own * (1 << pos) + low) * mult + off, 0, col)

                ins += [(pl.BlockSpec((None, per, w), index), a) for a in addends]
        layout.append([(len(src[0]), src[4]) for src in sources])
        outs += [(pl.BlockSpec((None, per, width), lambda i, *_: (i, 0, 0)), (count, per, width), BF)] * 2
    got = call(
        functools.partial(combine_kernel, layout=layout), steps, ins, outs, [], [scalars], name, after
    )
    return [(got[2 * n], got[2 * n + 1]) for n in range(len(lanes_in))]


def add_kernel(*refs):
    n = len(refs) // 3
    for i in range(n):
        refs[2 * n + i][...] = (refs[2 * i][...].astype(F32) + refs[2 * i + 1][...].astype(F32)).astype(BF)


def add_pairs(pairs, name, after=()):
    ins = [(whole(*a.shape), a) for pair in pairs for a in pair]
    outs = [(whole(*p[0].shape), p[0].shape, BF) for p in pairs]
    return call(add_kernel, 1, ins, outs, [], [], name, after)


def finish_kernel(bits_ref, *refs, moves, lanes_n):
    halves, outs = refs[: 2 * lanes_n], refs[2 * lanes_n :]
    for lane, col, width, out, row, at in moves:
        own, other = halves[2 * lane], halves[2 * lane + 1]
        half = own.shape[0]
        for h in range(2):
            pick = bits_ref[lane] == h
            value = jnp.where(pick, own[:, col : col + width].astype(F32), other[:, col : col + width].astype(F32))
            outs[out][row + h * half : row + (h + 1) * half, at : at + width] = value


def finish(halves, bits, moves, shapes, name, after=()):
    ins = [(whole(*a.shape), a) for pair in halves for a in pair]
    outs = [(whole(*s), s, F32) for s in shapes]
    return call(
        functools.partial(finish_kernel, moves=moves, lanes_n=len(halves)), 1, ins, outs, [],
        [jnp.stack(bits).astype(jnp.int32)], name, after,
    )


def total(parts):
    out = parts[0].astype(F32)
    for p in parts[1:]:
        out = out + p.astype(F32)
    return out.astype(BF)


def halve(parts, dim, axis, n, bit):
    mine = own_bit(axis, bit)
    got = swap(total([lax.dynamic_index_in_dim(p, 1 - mine, dim, keepdims=False) for p in parts]), axis, n, bit)
    return [lax.dynamic_index_in_dim(p, mine, dim, keepdims=False) for p in parts] + [got]


def plain_reduce(parts, bits, ndp, nseq):
    left = sorted(bits, reverse=True)
    for b in bits:
        parts = halve(parts, left.index(b), "dp", ndp, b)
        left.remove(b)
    out = total(parts)
    for b in bits_of(nseq):
        out = total([out, swap(out, "seq", nseq, b)])
    return out.astype(F32)


def local(
    ndp, nseq,
    tokens, init_state, norm_mix, w_in, w_forget, forget_bias, phase, w_ogate,
    norm_group, w_out, norm_ffn, w_gate, w_up, w_down, cotangent,
):
    segs, span, width = tokens.shape
    ch = w_forget.shape[1]
    hidden = w_gate.shape[1]
    count = segs * span
    mine = ch // nseq
    per = width // ndp
    tall = hidden // width
    rank = lax.axis_index("seq").astype(jnp.int32)
    bits = bits_of(ndp)
    first = next(b for b in bits if (per * b) % TILE == 0)
    rest = [b for b in bits if b != first]
    bit = own_bit("dp", first).astype(jnp.int32)
    lo = per * first
    scan_scratch = [pltpu.VMEM((ch // LANES, span, LANES), F32)] * 4

    own = jnp.concatenate(
        [jnp.stack([jnp.cos(phase), jnp.sin(phase)])[None], init_state.transpose(0, 2, 1)], axis=0
    )
    place = (jnp.arange(ch) // mine) == rank
    infos = shift_all(jnp.where(place, jnp.concatenate([own] * nseq, axis=2), 0.0), "seq", nseq)

    col = jnp.arange(width)
    perm = (col[:, None] == 2 * (col % ch)[None, :] + (col // ch)[None, :]).astype(BF)
    member = ((col[:, None] // (width // GROUPS)) == jnp.arange(LANES)[None, :]).astype(BF)

    x = tokens.reshape(count, width)
    cot = cotangent.reshape(count, width)
    normed, normed_t, pre = call(
        functools.partial(project_kernel, lo=lo), segs,
        [
            (rows(span, width), x), (whole(width), norm_mix), (whole(width, width), w_in),
            (whole(width, ch), w_forget), (whole(ch), forget_bias), (whole(width, width), perm),
        ],
        [
            (rows(span, width), (count, width), BF),
            (cols(width, span), (width, count), BF),
            (seg(span, 3 * ch), (segs, span, 3 * ch), BF),
        ],
        [], [bit[None]], "project",
    )
    trig, chunk, totals = call(
        functools.partial(summary_kernel, ranks=nseq), segs,
        [(seg(span, 3 * ch), pre)] + [(pl.BlockSpec((None, 2, ch), lambda s, *_: (0, 0, 0)), i) for i in infos],
        [
            (whole(2, ch), (2, ch), F32),
            (seg(4, CHUNKS, ch), (segs, 4, CHUNKS, ch), F32),
            (seg(4, ch), (segs, 4, ch), F32),
        ],
        scan_scratch, [], "summary",
    )
    totals = shift_all(totals, "seq", nseq)
    og = dot(normed, w_ogate)
    y, h_re, h_im, start, final, gated_t, middle = call(
        functools.partial(mixer_kernel, ranks=nseq, lo=lo), segs,
        [(seg(4, ch), t) for t in totals]
        + [(pl.BlockSpec((None, 2, ch), lambda s, *_: (1 + s, 0, 0)), i) for i in infos]
        + [
            (seg(span, 3 * ch), pre), (whole(2, ch), trig), (seg(4, CHUNKS, ch), chunk), (whole(width, width), perm),
            (rows(span, width), x), (rows(span, width), og), (whole(width), norm_group),
            (whole(width, LANES), member), (whole(width, width), w_out),
        ],
        [
            (rows(span, width), (count, width), BF),
            (seg(ch // LANES, span, LANES), (segs, ch // LANES, span, LANES), F32),
            (seg(ch // LANES, span, LANES), (segs, ch // LANES, span, LANES), F32),
            (seg(2, ch), (segs, 2, ch), F32),
            (seg(2, ch), (segs, 2, ch), F32),
            (cols(width, span), (width, count), BF),
            (rows(span, width), (count, width), F32),
        ],
        scan_scratch, [jnp.stack([rank, bit])], "mixer",
    )
    final_state = lax.dynamic_slice_in_dim(final, rank * mine, mine, axis=2).transpose(0, 2, 1)

    tile = width
    gsend, gkeep, dsend, dkeep, mixed_out, dn = call(
        functools.partial(ffn_kernel, lo=lo, dlo=lo * tall, rt=span), hidden // tile,
        [
            (whole(count, width), middle), (whole(width), norm_ffn), (whole(count, width), cot),
            (cols(width, tile), w_gate), (cols(width, tile), w_up), (rows(tile, width), w_down),
        ],
        [
            (cols(width // 2, 2 * tile), (width // 2, 2 * hidden), BF),
            (cols(width // 2, 2 * tile), (width // 2, 2 * hidden), BF),
            (rows(tile // 2, width), (hidden // 2, width), BF),
            (rows(tile // 2, width), (hidden // 2, width), BF),
            (whole(count, width), (count, width), BF),
            (whole(count, width), (count, width), F32),
        ],
        [
            pltpu.VMEM((count, width), BF), pltpu.VMEM((width, count), BF), pltpu.VMEM((count, width), F32),
            pltpu.VMEM((count, tile), BF), pltpu.VMEM((count, tile), BF), pltpu.VMEM((count, tile), BF),
            pltpu.VMEM((tile, count), BF),
        ],
        [bit[None]], "ffn",
    )

    ggot, dgot = swap(gsend, "dp", ndp, first), swap(dsend, "dp", ndp, first)

    dmiddle, dbranch, dog, dy_split, chain, adj, gains = call(
        turn_kernel, segs,
        [
            (rows(span, width), dn), (rows(span, width), middle), (rows(span, width), cot), (whole(width), norm_ffn),
            (whole(width, width), w_out), (rows(span, width), y), (rows(span, width), og), (whole(width), norm_group),
            (whole(width, LANES), member), (whole(width, width), perm), (seg(span, 3 * ch), pre), (whole(2, ch), trig),
            (seg(4, CHUNKS, ch), chunk),
        ],
        [
            (rows(span, width), (count, width), F32),
            (rows(span, width), (count, width), BF),
            (rows(span, width), (count, width), BF),
            (rows(span, width), (count, width), BF),
            (seg(2, CHUNKS, ch), (segs, 2, CHUNKS, ch), F32),
            (seg(2, ch), (segs, 2, ch), F32),
            (whole(2, width), (2, width), F32),
        ],
        scan_scratch, [], "turn",
    )
    adjs = shift_all(adj, "seq", nseq)

    ntile = width // 3
    osend, okeep = call(
        functools.partial(grads_kernel, pairs=2), width // ntile,
        [
            (whole(width, count), normed_t), (cols(count, ntile), dog),
            (whole(width, count), gated_t), (cols(count, ntile), dbranch),
        ],
        [
            (cols(width // 2, 2 * ntile), (width // 2, 2 * width), BF),
            (cols(width // 2, 2 * ntile), (width // 2, 2 * width), BF),
        ],
        [], [], "mixer_grads",
    )
    ogot = swap(osend, "dp", ndp, first)
    nblk = ndp // 2
    fast = ndp == 8 and nseq == 4 and per % (2 * TILE) == 0
    x_bit, y_bit = (own_bit("dp", b) for b in rest[:2]) if fast else (None, None)
    z_bits = [own_bit("seq", b) for b in bits_of(nseq)]

    def blocks(a, cols_n, tall_n=1):
        return a.reshape(nblk * tall_n, per, cols_n)

    order = ()
    if fast:
        g = [blocks(a, 2 * hidden) for a in (gkeep, ggot)]
        d = [blocks(a, width, tall) for a in (dkeep, dgot)]
        fa = [(g, 1, 0, 0, 3 * width)]
        fb = [(g, 1, 0, 3, width)] + [(d, tall, i, 0, width) for i in range(tall)]
        (fa_send, fa_keep), (fb_send, fb_keep) = combine([(0, x_bit, fa), (1, y_bit, fb)], "ffn_sum1", (osend,))
        fa_got, fb_got = swap(fa_send, "dp", ndp, rest[0]), swap(fb_send, "dp", ndp, rest[1])
        order = (fa_keep,)

    dpre, sums = call(
        functools.partial(adjoint_kernel, ranks=nseq), segs,
        [(seg(4, ch), t) for t in totals] + [(seg(2, ch), a) for a in adjs]
        + [
            (seg(span, 3 * ch), pre), (whole(2, ch), trig), (rows(span, width), dy_split),
            (seg(ch // LANES, span, LANES), h_re), (seg(ch // LANES, span, LANES), h_im), (seg(2, ch), start),
            (seg(4, CHUNKS, ch), chunk), (seg(2, CHUNKS, ch), chain), (whole(width, width), perm),
        ],
        [(rows(span, 3 * ch), (count, 3 * ch), BF), (whole(2, ch), (2, ch), F32)],
        scan_scratch, [rank[None]], "adjoint", order,
    )
    isend, ikeep = call(
        functools.partial(grads_kernel, pairs=1), 3,
        [(whole(width, count), normed_t), (cols(count, ch), dpre)],
        [
            (cols(width // 2, ch), (width // 2, 3 * ch), BF),
            (cols(width // 2, ch), (width // 2, 3 * ch), BF),
        ],
        [], [], "input_grads",
    )
    igot = swap(isend, "dp", ndp, first)
    order = ()
    if fast:
        def one(keep, got):
            return [([keep, got], 1, 0, 0, keep.shape[2])]

        def rows_of(keep, got):
            return one(*(a.reshape(2, per // 2, a.shape[2]) for a in (keep, got)))

        (fa_send, fa_keep), (fb_send, fb_keep) = combine(
            [(0, y_bit, one(fa_keep, fa_got)), (0, x_bit, one(fb_keep, fb_got))], "ffn_sum2", (isend,)
        )
        fa_got, fb_got = swap(fa_send, "dp", ndp, rest[1]), swap(fb_send, "dp", ndp, rest[0])
        o = [blocks(a, 2 * width) for a in (okeep, ogot)]
        i = [blocks(a, 3 * ch) for a in (ikeep, igot)]
        (ra_send, ra_keep), (rb_send, rb_keep) = combine(
            [(0, x_bit, [(o, 1, 0, 0, 2 * width)]), (1, y_bit, [(i, 1, 0, 0, 3 * ch)])], "mixer_sum1", (fa_keep,)
        )
        ra_got, rb_got = swap(ra_send, "dp", ndp, rest[0]), swap(rb_send, "dp", ndp, rest[1])
        order = (ra_keep,)

    grad_tokens, gain_mix = call(
        tokens_kernel, segs,
        [
            (rows(span, 3 * ch), dpre), (rows(span, width), dog), (whole(width, width), w_in),
            (whole(width, ch), w_forget), (whole(width, width), w_ogate), (rows(span, width), x),
            (whole(width), norm_mix), (rows(span, width), dmiddle),
        ],
        [(rows(span, width), (count, width), BF), (whole(1, width), (1, width), F32)],
        [], [], "tokens", order,
    )

    vec = jnp.concatenate([gains.reshape(-1), gain_mix.reshape(-1), sums.reshape(-1)]).reshape(-1, LANES)
    for axis, n in (("dp", ndp), ("seq", nseq)):
        for b in bits_of(n):
            vec = vec + swap(vec, axis, n, b)
    vec = vec.reshape(-1)
    place = lax.axis_index("dp") * per

    def own_gain(i):
        return lax.dynamic_slice_in_dim(vec, i * width + place, per)

    def own_sum(i):
        return lax.dynamic_slice_in_dim(vec, 3 * width + i * ch + rank * mine, mine)

    shapes_f = [(per, hidden), (per, hidden), (tall * per, width)]
    shapes_r = [(per, width), (per, width), (per, width), (per, ch)]
    if fast:
        lead, other = bits_of(nseq)

        def over(send, axis_n, bit):
            return swap(send, "seq", axis_n, bit)

        (fa_send, fa_keep), (fb_send, fb_keep) = combine(
            [(0, z_bits[0], rows_of(fa_keep, fa_got)), (0, z_bits[1], rows_of(fb_keep, fb_got))],
            "ffn_sum3", (grad_tokens,),
        )
        fa_got, fb_got = over(fa_send, nseq, lead), over(fb_send, nseq, other)
        (ra_send, ra_keep), (rb_send, rb_keep) = combine(
            [(0, y_bit, one(ra_keep, ra_got)), (0, x_bit, one(rb_keep, rb_got))], "mixer_sum2", (fa_keep,)
        )
        ra_got, rb_got = swap(ra_send, "dp", ndp, rest[1]), swap(rb_send, "dp", ndp, rest[0])
        fa, fb = add_pairs([(fa_keep, fa_got), (fb_keep, fb_got)], "ffn_sum4", (ra_keep,))
        fa_got, fb_got = over(fa, nseq, other), over(fb, nseq, lead)
        (ra_send, ra_keep), (rb_send, rb_keep) = combine(
            [(0, z_bits[0], rows_of(ra_keep, ra_got)), (0, z_bits[1], rows_of(rb_keep, rb_got))], "mixer_sum3", (fa,)
        )
        ra_got, rb_got = over(ra_send, nseq, lead), over(rb_send, nseq, other)
        fa, fb = add_pairs([(fa, fa_got), (fb, fb_got)], "ffn_sum5", (ra_keep,))
        fa_got, fb_got = over(fa, nseq, lead), over(fb, nseq, other)
        ra, rb = add_pairs([(ra_keep, ra_got), (rb_keep, rb_got)], "mixer_sum4", (fa,))
        ra_got, rb_got = over(ra, nseq, other), over(rb, nseq, lead)

        def flat(*pairs):
            return [tuple(a.reshape(per // 2, a.shape[2]) for a in pair) for pair in pairs]

        guv = [(0, c * width) for c in range(3)] + [(1, 0)]
        moves = [
            (lane, col, width, n % 2, 0, (n // 2) * width) for n, (lane, col) in enumerate(guv)
        ] + [(1, (1 + t) * width, width, 2, t * per, 0) for t in range(tall)]
        part_gate, part_up, part_down = finish(
            flat((fa, fa_got), (fb, fb_got)), z_bits, moves, shapes_f, "ffn_out", (ra,)
        )
        ra, rb = add_pairs([(ra, ra_got), (rb, rb_got)], "mixer_sum5", (part_gate,))
        ra_got, rb_got = over(ra, nseq, lead), over(rb, nseq, other)
        moves = [(0, n * ntile, ntile, n % 2, 0, (n // 2) * ntile) for n in range(2 * width // ntile)]
        moves += [(1, 0, width, 2, 0, 0), (1, width, ch, 3, 0, 0)]
        part_ogate, part_out, part_in, part_forget = finish(
            flat((ra, ra_got), (rb, rb_got)), z_bits, moves, shapes_r, "mixer_out"
        )
    else:
        def plain(keep, got, cols_n, tall_n=1):
            shape = [2] * len(rest) + [tall_n * per, cols_n]
            return plain_reduce([keep.reshape(shape), got.reshape(shape)], rest, ndp, nseq)

        guv = plain(gkeep, ggot, 2 * hidden)
        guv = [guv[:, n * tile : (n + 1) * tile] for n in range(2 * hidden // tile)]
        part_gate, part_up = jnp.concatenate(guv[0::2], axis=1), jnp.concatenate(guv[1::2], axis=1)
        part_down = plain(dkeep, dgot, width, tall)
        mix = plain(okeep, ogot, 2 * width)
        mix = [mix[:, n * ntile : (n + 1) * ntile] for n in range(2 * width // ntile)]
        part_ogate, part_out = jnp.concatenate(mix[0::2], axis=1), jnp.concatenate(mix[1::2], axis=1)
        into = plain(ikeep, igot, 3 * ch)
        part_in, part_forget = into[:, :width], into[:, width:]
    return (
        mixed_out.reshape(segs, span, width),
        grad_tokens.reshape(segs, span, width),
        final_state,
        own_gain(2), part_in, part_forget, own_sum(0), own_sum(1), part_ogate, own_gain(1), part_out, own_gain(0),
        part_gate, part_up, part_down,
    )


def solution(mesh):
    ndp, nseq = mesh.shape["dp"], mesh.shape["seq"]
    tok, vec, col = P("dp", "seq", None), P("dp"), P("dp", None)
    return jax.shard_map(
        functools.partial(local, ndp, nseq),
        mesh=mesh,
        in_specs=(tok, tok, P(), P(), P(), P(), P("seq"), P(), P(), P(), P(), P(), P(), P(), tok),
        out_specs=(tok, tok, tok, vec, col, col, P("seq"), P("seq"), col, vec, col, vec, col, col, col),
        check_vma=False,
    )
```

profile of v0, /device:TPU:0, one launch (start us, length us, event | category | flops | bytes accessed | tf_op | source)
XLA Modules:
  0.0 243.5 jit_solution(14907683964915957059)
XLA Ops:
  2.3 5.1 %collective-permute-start.2 = (f32[4,2,384]{2,1,0:T(2,128)S(1)}, f32[4,2,384]{2,1,0:T(2,128)S(1)}, u32[]{:S(2)}, u32[]{:S(2)}) collective-permute-start(f32[4,2,384]{2,1,0:T(2,128)S(1)} %maximum_select_fusion.refs_1_.refs_5_), channel_id=1, source_target_pairs={{0,3},{1,0},{2,1},{3,2},{4,7},{5,4},{6,5},{7,6},{8,11},{9,8},{10,9... | collective-permute-start | bytes 36872 | tf_op jit(solution)/shard_map/ppermute | solution.py:450
  9.9 6.7 %project.1 = (bf16[768,768]{1,0:T(8,128)(2,1)}, bf16[768,768]{1,0:T(8,128)(2,1)}, bf16[3,256,1152]{2,1,0:T(8,128)(2,1)}) custom-call(s32[1]{0:T(128)} %bitcast.refs_0_, bf16[768,768]{1,0:T(8,128)(2,1)} %bitcast.69, f32[768]{0:T(1024)} %refs_6_.3, bf16[768,768]{1,0:T(8,128)(2,1)} %refs_2_.5, bf16[768,384]{1,0:T(8,128)(2,1)} %refs_3_.5, f32[384]{0:T(512)} %refs_5_.2, ...), custom_call_target="tpu_custom_call" | custom-call | flops 1 | bytes 1 | tf_op jit(solution)/shard_map/project/pallas_call | solution.py:433
  16.6 3.8 %fusion.18.refs_14_.refs_6_ = f32[768,768]{1,0:T(8,128)} fusion(bf16[768,768]{1,0:T(8,128)(2,1)} %get-tuple-element.92, bf16[768,768]{1,0:T(8,128)(2,1)S(1)} %copy-done.9), kind=kOutput, calls=%fused_computation.42 | convolution fusion | flops 905969664 | bytes 4718592 | tf_op jit(solution)/shard_map/dot_general | solution.py:21
  21.9 5.6 %summary.1 = (f32[2,384]{1,0:T(2,128)}, f32[3,4,8,384]{3,2,1,0:T(8,128)}, f32[3,4,384]{2,1,0:T(4,128)}) custom-call(bf16[3,256,1152]{2,1,0:T(8,128)(2,1)} %get-tuple-element.88.refs_0_.refs_9_.refs_10_, f32[4,2,384]{2,1,0:T(2,128)} %copy-done.24, f32[4,2,384]{2,1,0:T(2,128)} %copy-done.30, f32[4,2,384]{2,1,0:T(2,128)} %copy-done.29, f32[4,2,384]{2,1,0:T(2,128)} %copy-done.28), custom_call_target="tpu_custom_call" | custom-call | flops 1 | bytes 1 | tf_op jit(solution)/shard_map/summary/pallas_call | solution.py:433
  27.5 2.8 %collective-permute-start.5 = (f32[3,4,384]{2,1,0:T(4,128)}, f32[3,4,384]{2,1,0:T(4,128)S(1)}, u32[]{:S(2)}, u32[]{:S(2)}) collective-permute-start(f32[3,4,384]{2,1,0:T(4,128)} %get-tuple-element.89.refs_1_), channel_id=1, source_target_pairs={{0,3},{1,0},{2,1},{3,2},{4,7},{5,4},{6,5},{7,6},{8,11},{9,8},{10,9... | collective-permute-start | bytes 55304 | tf_op jit(solution)/shard_map/ppermute | solution.py:450
  32.1 3.1 %collective-permute-done.4.refs_3_ = f32[3,4,384]{2,1,0:T(4,128)S(1)} collective-permute-done((f32[3,4,384]{2,1,0:T(4,128)}, f32[3,4,384]{2,1,0:T(4,128)S(1)}, u32[]{:S(2)}, u32[]{:S(2)}) %collective-permute-start.4) | collective-permute-done | bytes 18464 | tf_op jit(solution)/shard_map/ppermute | solution.py:450
  35.2 2.0 collective-permute-done.3.refs_2_
  37.8 13.6 %mixer.1 = (bf16[768,768]{1,0:T(8,128)(2,1)}, f32[3,3,256,128]{3,2,1,0:T(8,128)}, f32[3,3,256,128]{3,2,1,0:T(8,128)}, f32[3,2,384]{2,1,0:T(2,128)}, f32[3,2,384]...) custom-call(s32[2]{0:T(128)} %pad_add_fusion.refs_0_, f32[3,4,384]{2,1,0:T(4,128)} %get-tuple-element.89.refs_1_, ...), custom_call_target="tpu_custom_call" | custom-call | flops 1 | bytes 1 | tf_op jit(solution)/shard_map/mixer/pallas_call | solution.py:433
  51.5 27.6 %ffn.1 = (bf16[384,3072]{1,0:T(8,128)(2,1)}, bf16[384,3072]{1,0:T(8,128)(2,1)}, bf16[768,768]{1,0:T(8,128)(2,1)}, bf16[768,768]{1,0:T(8,128)(2,1)}, bf16[768,768]{1,0:T(8,128)(2,1)}, /*index=5*/f32[768,768]{1,0:T(8,128)}) custom-call(s32[1]{0:T(128)} %bitcast.refs_0_, f32[768,768]{1,0:T(8,128)} %get-tuple-element.93.refs_1_, f32[768]{0:T(1024)} %refs_3_.4, ...), custom_call_target="tpu_custom_call" | custom-call | flops 1 | bytes 1 | tf_op jit(solution)/shard_map/ffn/pallas_call | solution.py:433
  79.7 15.2 %turn.1 = (f32[768,768]{1,0:T(8,128)}, bf16[768,768]{1,0:T(8,128)(2,1)}, bf16[768,768]{1,0:T(8,128)(2,1)}, bf16[768,768]{1,0:T(8,128)(2,1)}, f32[3,2,8,384]{3,2,...) custom-call(f32[768,768]{1,0:T(8,128)} %get-tuple-element.95.refs_0_, f32[768,768]{1,0:T(8,128)} %get-tuple-element.93.refs_1_, ...), custom_call_target="tpu_custom_call" | custom-call | flops 1 | bytes 1 | tf_op jit(solution)/shard_map/turn/pallas_call | solution.py:433
  94.9 5.8 %mixer_grads.1 = (bf16[384,1536]{1,0:T(8,128)(2,1)}, bf16[384,1536]{1,0:T(8,128)(2,1)}) custom-call(bf16[768,768]{1,0:T(8,128)(2,1)} %get-tuple-element.107.refs_0_, bf16[768,768]{1,0:T(8,128)(2,1)} %get-tuple-element.108.refs_1_, bf16[768,768]{1,0:T(8,128)(2,1)} %get-tuple-element.109.refs_2_, bf16[768,768]{1,0:T(8,128)(2,1)} %get-tuple-element.110.refs_3_), custom_call_target="tpu_custom_call" | custom-call | flops 1 | bytes 1 | tf_op jit(solution)/shard_map/mixer_grads/pallas_call | solution.py:433
  100.9 2.0 collective-permute-start.6
  104.9 5.6 %ffn_sum1.1 = (bf16[2,96,2304]{2,1,0:T(8,128)(2,1)}, bf16[2,96,2304]{2,1,0:T(8,128)(2,1)}, bf16[2,96,2304]{2,1,0:T(8,128)(2,1)}, bf16[2,96,2304]{2,1,0:T(8,128)(2,1)}) custom-call(s32[2]{0:T(128)} %pad_add_fusion.1.refs_0_, bf16[4,96,3072]{2,1,0:T(8,128)(2,1)} %bitcast.53, bf16[4,96,3072]{2,1,0:T(8,128)(2,1)} %bitcast.57, bf16[4,96,3072]{2,1,0:T(8,128)(2,1)} %bitcast.54, ...), custom_call_target="tpu_custom_call" | custom-call | flops 1 | bytes 1 | tf_op jit(solution)/shard_map/ffn_sum1/pallas_call | solution.py:433
  110.5 1.6 collective-permute-start.13
  112.1 1.5 collective-permute-start.14
  114.2 10.6 %adjoint.1 = (bf16[768,1152]{1,0:T(8,128)(2,1)}, f32[2,384]{1,0:T(2,128)}) custom-call(s32[1]{0:T(128)} %bitcast.1.refs_0_, f32[3,4,384]{2,1,0:T(4,128)} %get-tuple-element.89.refs_1_, f32[3,4,384]{2,1,0:T(4,128)} %copy-done.27, f32[3,4,384]{2,1,0:T(4,128)} %copy-done.26, f32[3,4,384]{2,1,0:T(4,128)} %copy-done.25, f32[3,2,384]{2,1,0:T(2,128)} %get-tuple-element.97.refs_5_, ...), custom_call_target="tpu_custom_call" | custom-call | flops 1 | bytes 1 | tf_op jit(solution)/shard_map/adjoint/pallas_call | solution.py:433
  124.9 4.9 %input_grads.1 = (bf16[384,1152]{1,0:T(8,128)(2,1)}, bf16[384,1152]{1,0:T(8,128)(2,1)}) custom-call(bf16[768,768]{1,0:T(8,128)(2,1)} %get-tuple-element.107.refs_0_, bf16[768,1152]{1,0:T(8,128)(2,1)} %get-tuple-element.113.refs_1_.refs_0_), custom_call_target="tpu_custom_call" | custom-call | flops 1 | bytes 1 | tf_op jit(solution)/shard_map/input_grads/pallas_call | solution.py:433
  130.4 1.8 collective-permute-done.13.refs_2_.refs_4_
  134.4 3.9 %ffn_sum2.1 = (bf16[1,96,2304]{2,1,0:T(8,128)(2,1)}, bf16[1,96,2304]{2,1,0:T(8,128)(2,1)}, bf16[1,96,2304]{2,1,0:T(8,128)(2,1)}, bf16[1,96,2304]{2,1,0:T(8,128)(2,1)}) custom-call(s32[2]{0:T(128)} %pad_add_fusion.2.refs_0_, bf16[2,96,2304]{2,1,0:T(8,128)(2,1)} %get-tuple-element.112.refs_18_.refs_1_.refs_3_, bf16[2,96,2304]{2,1,0:T(8,128)(2,1)} %copy-done.3, ...), custom_call_target="tpu_custom_call" | custom-call | flops 1 | bytes 1 | tf_op jit(solution)/shard_map/ffn_sum2/pallas_call | solution.py:433
  139.3 4.1 %mixer_sum1.1 = (bf16[2,96,1536]{2,1,0:T(8,128)(2,1)}, bf16[2,96,1536]{2,1,0:T(8,128)(2,1)}, bf16[2,96,1152]{2,1,0:T(8,128)(2,1)}, bf16[2,96,1152]{2,1,0:T(8,128)(2,1)}) custom-call(s32[2]{0:T(128)} %pad_add_fusion.1.refs_0_, bf16[4,96,1536]{2,1,0:T(8,128)(2,1)} %bitcast.72, bf16[4,96,1536]{2,1,0:T(8,128)(2,1)} %bitcast.16.refs_2_.refs_4_, ...), custom_call_target="tpu_custom_call" | custom-call | flops 1 | bytes 1 | tf_op jit(solution)/shard_map/mixer_sum1/pallas_call | solution.py:433
  144.0 1.5 collective-permute-start.22
  145.5 1.5 collective-permute-start.23
  148.1 7.5 %tokens.1 = (bf16[768,768]{1,0:T(8,128)(2,1)}, f32[1,768]{1,0:T(1,128)}) custom-call(bf16[768,1152]{1,0:T(8,128)(2,1)} %get-tuple-element.113.refs_1_.refs_0_, bf16[768,768]{1,0:T(8,128)(2,1)} %get-tuple-element.108.refs_1_, bf16[768,768]{1,0:T(8,128)(2,1)} %refs_2_.5, bf16[768,384]{1,0:T(8,128)(2,1)} %refs_3_.5, bf16[768,768]{1,0:T(8,128)(2,1)} %refs_4_.7, ...), custom_call_target="tpu_custom_call" | custom-call | flops 1 | bytes 1 | tf_op jit(solution)/shard_map/tokens/pallas_call | solution.py:433
  155.6 1.5 collective-permute-done.22
  157.1 9.9 %collective-permute-done.23 = bf16[1,96,2304]{2,1,0:T(8,128)(2,1)S(1)} collective-permute-done((bf16[1,96,2304]{2,1,0:T(8,128)(2,1)S(1)}, bf16[1,96,2304]{2,1,0:T(8,128)(2,1)S(1)}, u32[]{:S(2)}, u32[]{:S(2)}) %collective-permute-start.23) | collective-permute-done | bytes 442400 | tf_op jit(solution)/shard_map/ppermute | solution.py:458
  167.8 3.1 %ffn_sum3.1 = (bf16[1,48,2304]{2,1,0:T(8,128)(2,1)}, bf16[1,48,2304]{2,1,0:T(8,128)(2,1)}, bf16[1,48,2304]{2,1,0:T(8,128)(2,1)}, bf16[1,48,2304]{2,1,0:T(8,128)(2,1)}) custom-call(s32[2]{0:T(128)} %pad_add_fusion.3.refs_0_, bf16[2,48,2304]{2,1,0:T(8,128)(2,1)} %bitcast.76, bf16[2,48,2304]{2,1,0:T(8,128)(2,1)} %bitcast.86, bf16[2,48,2304]{2,1,0:T(8,128)(2,1)} %bitcast.77, ...), custom_call_target="tpu_custom_call" | custom-call | flops 1 | bytes 1 | tf_op jit(solution)/shard_map/ffn_sum3/pallas_call | solution.py:433
  172.0 3.3 %mixer_sum2.1 = (bf16[1,96,1536]{2,1,0:T(8,128)(2,1)}, bf16[1,96,1536]{2,1,0:T(8,128)(2,1)}, bf16[1,96,1152]{2,1,0:T(8,128)(2,1)}, bf16[1,96,1152]{2,1,0:T(8,128)(2,1)}) custom-call(s32[2]{0:T(128)} %pad_add_fusion.2.refs_0_, bf16[2,96,1536]{2,1,0:T(8,128)(2,1)} %get-tuple-element.122.refs_8_.refs_1_.refs_3_, bf16[2,96,1536]{2,1,0:T(8,128)(2,1)} %copy-done.5, ...), custom_call_target="tpu_custom_call" | custom-call | flops 1 | bytes 1 | tf_op jit(solution)/shard_map/mixer_sum2/pallas_call | solution.py:433
  175.3 1.5 collective-permute-start.24
  178.1 1.6 collective-permute-start.27
  180.8 5.2 %collective-permute-done.26.refs_1_ = bf16[1,48,2304]{2,1,0:T(8,128)(2,1)S(1)} collective-permute-done((bf16[1,48,2304]{2,1,0:T(8,128)(2,1)S(1)}, bf16[1,48,2304]{2,1,0:T(8,128)(2,1)S(1)}, u32[]{:S(2)}, u32[]{:S(2)}) %collective-permute-start.26) | collective-permute-done | bytes 221216 | tf_op jit(solution)/shard_map/ppermute | solution.py:458
  186.0 2.3 collective-permute-done.27.refs_3_
  189.0 2.1 ffn_sum4.1
  191.3 2.6 %collective-permute-start.30 = (bf16[1,48,2304]{2,1,0:T(8,128)(2,1)}, bf16[1,48,2304]{2,1,0:T(8,128)(2,1)S(1)}, u32[]{:S(2)}, u32[]{:S(2)}) collective-permute-start(bf16[1,48,2304]{2,1,0:T(8,128)(2,1)} %get-tuple-element.142.refs_9_.refs_0_), channel_id=1, source_target_pairs={{0,2},{1,3},{2,0},{3,1},{4,6},{5,7},{6,4},{7,5},{8,10},{9,11},{10,... | collective-permute-start | bytes 663560 | tf_op jit(solution)/shard_map/ppermute | solution.py:458
  194.6 2.8 %mixer_sum3.1 = (bf16[1,48,1536]{2,1,0:T(8,128)(2,1)}, bf16[1,48,1536]{2,1,0:T(8,128)(2,1)}, bf16[1,48,1152]{2,1,0:T(8,128)(2,1)}, bf16[1,48,1152]{2,1,0:T(8,128)(2,1)}) custom-call(s32[2]{0:T(128)} %pad_add_fusion.3.refs_0_, bf16[2,48,1536]{2,1,0:T(8,128)(2,1)} %bitcast.82, bf16[2,48,1536]{2,1,0:T(8,128)(2,1)} %bitcast.90, bf16[2,48,1536]{2,1,0:T(8,128)(2,1)} %bitcast.83, ...), custom_call_target="tpu_custom_call" | custom-call | flops 1 | bytes 1 | tf_op jit(solution)/shard_map/mixer_sum3/pallas_call | solution.py:433
  197.7 1.8 collective-permute-start.28
  200.9 2.2 collective-permute-done.31.refs_3_
  203.1 3.8 %collective-permute-done.30.refs_1_ = bf16[1,48,2304]{2,1,0:T(8,128)(2,1)S(1)} collective-permute-done((bf16[1,48,2304]{2,1,0:T(8,128)(2,1)}, bf16[1,48,2304]{2,1,0:T(8,128)(2,1)S(1)}, u32[]{:S(2)}, u32[]{:S(2)}) %collective-permute-start.30) | collective-permute-done | bytes 221216 | tf_op jit(solution)/shard_map/ppermute | solution.py:458
  207.6 2.1 ffn_sum5.1
  211.6 1.8 mixer_sum4.1
  213.4 1.7 collective-permute-start.32
  215.8 3.2 %collective-permute-done.17 = f32[24,128]{1,0:T(8,128)S(1)} collective-permute-done((f32[24,128]{1,0:T(8,128)S(1)}, f32[24,128]{1,0:T(8,128)S(1)}, u32[]{:S(2)}, u32[]{:S(2)}) %collective-permute-start.17) | collective-permute-done | bytes 12320 | tf_op jit(solution)/shard_map/ppermute | solution.py:458
  218.9 2.0 collective-permute-start.18
  220.9 1.7 collective-permute-done.18
  227.2 3.2 %ffn_out.1 = (f32[96,1536]{1,0:T(8,128)}, f32[96,1536]{1,0:T(8,128)}, f32[192,768]{1,0:T(8,128)}) custom-call(s32[2]{0:T(128)} %pad_add_fusion.3.refs_0_, bf16[48,2304]{1,0:T(8,128)(2,1)} %bitcast.97, bf16[48,2304]{1,0:T(8,128)(2,1)} %bitcast.100, bf16[48,2304]{1,0:T(8,128)(2,1)} %bitcast.98, bf16[48,2304]{1,0:T(8,128)(2,1)} %bitcast.99, ...), custom_call_target="tpu_custom_call" | custom-call | flops 1 | bytes 1 | tf_op jit(solution)/shard_map/ffn_out/pallas_call | solution.py:433
  231.7 1.9 mixer_sum5.1
  233.8 1.8 collective-permute-start.37
  236.2 3.6 %collective-permute-done.37 = bf16[1,48,1152]{2,1,0:T(8,128)(2,1)S(1)} collective-permute-done((bf16[1,48,1152]{2,1,0:T(8,128)(2,1)}, bf16[1,48,1152]{2,1,0:T(8,128)(2,1)S(1)}, u32[]{:S(2)}, u32[]{:S(2)}) %collective-permute-start.37) | collective-permute-done | bytes 110624 | tf_op jit(solution)/shard_map/ppermute | solution.py:458
  240.8 2.7 %mixer_out.1 = (f32[96,768]{1,0:T(8,128)}, f32[96,768]{1,0:T(8,128)}, f32[96,768]{1,0:T(8,128)}, f32[96,384]{1,0:T(8,128)}) custom-call(s32[2]{0:T(128)} %pad_add_fusion.3.refs_0_, bf16[48,1536]{1,0:T(8,128)(2,1)} %bitcast.101, bf16[48,1536]{1,0:T(8,128)(2,1)} %bitcast.102, bf16[48,1152]{1,0:T(8,128)(2,1)} %bitcast.103, bf16[48,1152]{1,0:T(8,128)(2,1)} %bitcast.104), custom_call_target="tpu_custom_call" | custom-call | flops 1 | bytes 1 | tf_op jit(solution)/shard_map/mixer_out/pallas_call | solution.py:433
  (157 shorter events, 34.9 us)
Async XLA Ops:
  2.3 14.3 %copy-start.24 = (f32[4,2,384]{2,1,0:T(2,128)}, f32[4,2,384]{2,1,0:T(2,128)S(1)}, u32[]{:S(2)}) copy-start(f32[4,2,384]{2,1,0:T(2,128)S(1)} %maximum_select_fusion.refs_1_.refs_5_) | copy-start | bytes 36868
  2.3 18.9 %collective-permute-start.2 = (f32[4,2,384]{2,1,0:T(2,128)S(1)}, f32[4,2,384]{2,1,0:T(2,128)S(1)}, u32[]{:S(2)}, u32[]{:S(2)}) collective-permute-start(f32[4,2,384]{2,1,0:T(2,128)S(1)} %maximum_select_fusion.refs_1_.refs_5_), channel_id=1, source_target_pairs={{0,3},{1,0},{2,1},{3,2},{4,7},{5,4},{6,5},{7,6},{8,11},{9,8},{10,9... | collective-permute-start | bytes 36872 | tf_op jit(solution)/shard_map/ppermute | solution.py:450
  7.4 13.8 %collective-permute-start.1 = (f32[4,2,384]{2,1,0:T(2,128)S(1)}, f32[4,2,384]{2,1,0:T(2,128)S(1)}, u32[]{:S(2)}, u32[]{:S(2)}) collective-permute-start(f32[4,2,384]{2,1,0:T(2,128)S(1)} %maximum_select_fusion.refs_1_.refs_5_), channel_id=1, source_target_pairs={{0,2},{1,3},{2,0},{3,1},{4,6},{5,7},{6,4},{7,5},{8,10},{9,11},{10,... | collective-permute-start | bytes 36872 | tf_op jit(solution)/shard_map/ppermute | solution.py:450
  7.4 13.8 %collective-permute-start = (f32[4,2,384]{2,1,0:T(2,128)S(1)}, f32[4,2,384]{2,1,0:T(2,128)S(1)}, u32[]{:S(2)}, u32[]{:S(2)}) collective-permute-start(f32[4,2,384]{2,1,0:T(2,128)S(1)} %maximum_select_fusion.refs_1_.refs_5_), channel_id=1, source_target_pairs={{0,1},{1,2},{2,3},{3,0},{4,5},{5,6},{6,7},{7,4},{8,9},{9,10},{10,1... | collective-permute-start | bytes 36872 | tf_op jit(solution)/shard_map/ppermute | solution.py:450
  9.9 6.7 %copy-start.9 = (bf16[768,768]{1,0:T(8,128)(2,1)S(1)}, bf16[768,768]{1,0:T(8,128)(2,1)}, u32[]{:S(2)}) copy-start(bf16[768,768]{1,0:T(8,128)(2,1)} %refs_4_.7) | copy-start | bytes 3538948
  27.5 4.5 %collective-permute-start.5 = (f32[3,4,384]{2,1,0:T(4,128)}, f32[3,4,384]{2,1,0:T(4,128)S(1)}, u32[]{:S(2)}, u32[]{:S(2)}) collective-permute-start(f32[3,4,384]{2,1,0:T(4,128)} %get-tuple-element.89.refs_1_), channel_id=1, source_target_pairs={{0,3},{1,0},{2,1},{3,2},{4,7},{5,4},{6,5},{7,6},{8,11},{9,8},{10,9... | collective-permute-start | bytes 55304 | tf_op jit(solution)/shard_map/ppermute | solution.py:450
  30.3 4.9 %collective-permute-start.4 = (f32[3,4,384]{2,1,0:T(4,128)}, f32[3,4,384]{2,1,0:T(4,128)S(1)}, u32[]{:S(2)}, u32[]{:S(2)}) collective-permute-start(f32[3,4,384]{2,1,0:T(4,128)} %get-tuple-element.89.refs_1_), channel_id=1, source_target_pairs={{0,2},{1,3},{2,0},{3,1},{4,6},{5,7},{6,4},{7,5},{8,10},{9,11},{10,... | collective-permute-start | bytes 55304 | tf_op jit(solution)/shard_map/ppermute | solution.py:450
  31.5 5.8 %collective-permute-start.3 = (f32[3,4,384]{2,1,0:T(4,128)}, f32[3,4,384]{2,1,0:T(4,128)S(1)}, u32[]{:S(2)}, u32[]{:S(2)}) collective-permute-start(f32[3,4,384]{2,1,0:T(4,128)} %get-tuple-element.89.refs_1_), channel_id=1, source_target_pairs={{0,1},{1,2},{2,3},{3,0},{4,5},{5,6},{6,7},{7,4},{8,9},{9,10},{10,1... | collective-permute-start | bytes 55304 | tf_op jit(solution)/shard_map/ppermute | solution.py:450
  32.1 5.2 %copy-start.25 = (f32[3,4,384]{2,1,0:T(4,128)}, f32[3,4,384]{2,1,0:T(4,128)S(1)}, u32[]{:S(2)}) copy-start(f32[3,4,384]{2,1,0:T(4,128)S(1)} %collective-permute-done.5.refs_4_) | copy-start | bytes 55300
  79.1 24.4 %collective-permute-start.9 = (bf16[384,3072]{1,0:T(8,128)(2,1)}, bf16[384,3072]{1,0:T(8,128)(2,1)S(1)}, u32[]{:S(2)}, u32[]{:S(2)}) collective-permute-start(bf16[384,3072]{1,0:T(8,128)(2,1)} %get-tuple-element.104), channel_id=1, source_target_pairs={{0,4},{4,0},{8,12},{12,8},{16,20},{20,16},{24,28},{28,24},{1,5},{5... | collective-permute-start | bytes 7077896 | tf_op jit(solution)/shard_map/ppermute | solution.py:458
  79.2 21.7 %collective-permute-start.10 = (bf16[768,768]{1,0:T(8,128)(2,1)}, bf16[768,768]{1,0:T(8,128)(2,1)S(1)}, u32[]{:S(2)}, u32[]{:S(2)}) collective-permute-start(bf16[768,768]{1,0:T(8,128)(2,1)} %get-tuple-element.106), channel_id=1, source_target_pairs={{0,4},{4,0},{8,12},{12,8},{16,20},{20,16},{24,28},{28,24},{1,5},{5... | collective-permute-start | bytes 3538952 | tf_op jit(solution)/shard_map/ppermute | solution.py:458
  94.9 5.9 %copy-start.31 = (f32[3,2,384]{2,1,0:T(2,128)S(1)}, f32[3,2,384]{2,1,0:T(2,128)}, u32[]{:S(2)}) copy-start(f32[3,2,384]{2,1,0:T(2,128)} %get-tuple-element.97.refs_5_) | copy-start | bytes 27652
  100.8 37.6 %collective-permute-start.11 = (bf16[384,1536]{1,0:T(8,128)(2,1)}, bf16[384,1536]{1,0:T(8,128)(2,1)}, u32[]{:S(2)}, u32[]{:S(2)}) collective-permute-start(bf16[384,1536]{1,0:T(8,128)(2,1)} %get-tuple-element.111.refs_17_), channel_id=1, source_target_pairs={{0,4},{4,0},{8,12},{12,8},{16,20},{20,16},{24,28},{28,24},{1,5},{5... | collective-permute-start | bytes 3538952 | tf_op jit(solution)/shard_map/ppermute | solution.py:458
  100.8 11.3 %collective-permute-start.8 = (f32[3,2,384]{2,1,0:T(2,128)S(1)}, f32[3,2,384]{2,1,0:T(2,128)S(1)}, u32[]{:S(2)}, u32[]{:S(2)}) collective-permute-start(f32[3,2,384]{2,1,0:T(2,128)S(1)} %copy-done.31), channel_id=1, source_target_pairs={{0,3},{1,0},{2,1},{3,2},{4,7},{5,4},{6,5},{7,6},{8,11},{9,8},{10,9... | collective-permute-start | bytes 27656 | tf_op jit(solution)/shard_map/ppermute | solution.py:450
  100.8 12.8 %collective-permute-start.7 = (f32[3,2,384]{2,1,0:T(2,128)S(1)}, f32[3,2,384]{2,1,0:T(2,128)S(1)}, u32[]{:S(2)}, u32[]{:S(2)}) collective-permute-start(f32[3,2,384]{2,1,0:T(2,128)S(1)} %copy-done.31), channel_id=1, source_target_pairs={{0,2},{1,3},{2,0},{3,1},{4,6},{5,7},{6,4},{7,5},{8,10},{9,11},{10,... | collective-permute-start | bytes 27656 | tf_op jit(solution)/shard_map/ppermute | solution.py:450
  100.9 12.7 %collective-permute-start.6 = (f32[3,2,384]{2,1,0:T(2,128)S(1)}, f32[3,2,384]{2,1,0:T(2,128)S(1)}, u32[]{:S(2)}, u32[]{:S(2)}) collective-permute-start(f32[3,2,384]{2,1,0:T(2,128)S(1)} %copy-done.31), channel_id=1, source_target_pairs={{0,1},{1,2},{2,3},{3,0},{4,5},{5,6},{6,7},{7,4},{8,9},{9,10},{10,1... | collective-permute-start | bytes 27656 | tf_op jit(solution)/shard_map/ppermute | solution.py:450
  110.5 21.7 %collective-permute-start.13 = (bf16[2,96,2304]{2,1,0:T(8,128)(2,1)}, bf16[2,96,2304]{2,1,0:T(8,128)(2,1)S(1)}, u32[]{:S(2)}, u32[]{:S(2)}) collective-permute-start(bf16[2,96,2304]{2,1,0:T(8,128)(2,1)} %get-tuple-element.118), channel_id=1, source_target_pairs={{0,8},{4,12},{8,0},{12,4},{16,24},{20,28},{24,16},{28,20},{1,9},{5... | collective-permute-start | bytes 2654216 | tf_op jit(solution)/shard_map/ppermute | solution.py:458
  112.1 21.4 %collective-permute-start.14 = (bf16[2,96,2304]{2,1,0:T(8,128)(2,1)}, bf16[2,96,2304]{2,1,0:T(8,128)(2,1)S(1)}, u32[]{:S(2)}, u32[]{:S(2)}) collective-permute-start(bf16[2,96,2304]{2,1,0:T(8,128)(2,1)} %get-tuple-element.120), channel_id=1, source_target_pairs={{0,16},{4,20},{8,24},{12,28},{16,0},{20,4},{24,8},{28,12},{1,17},{... | collective-permute-start | bytes 2654216 | tf_op jit(solution)/shard_map/ppermute | solution.py:458
  129.8 8.5 %collective-permute-start.12 = (bf16[384,1152]{1,0:T(8,128)(2,1)}, bf16[384,1152]{1,0:T(8,128)(2,1)S(1)}, u32[]{:S(2)}, u32[]{:S(2)}) collective-permute-start(bf16[384,1152]{1,0:T(8,128)(2,1)} %get-tuple-element.117.refs_9_), channel_id=1, source_target_pairs={{0,4},{4,0},{8,12},{12,8},{16,20},{20,16},{24,28},{28,24},{1,5},{5... | collective-permute-start | bytes 2654216 | tf_op jit(solution)/shard_map/ppermute | solution.py:458
  139.3 6.2 %copy-start.38 = (bf16[1,96,2304]{2,1,0:T(8,128)(2,1)S(1)}, bf16[1,96,2304]{2,1,0:T(8,128)(2,1)}, u32[]{:S(2)}) copy-start(bf16[1,96,2304]{2,1,0:T(8,128)(2,1)} %get-tuple-element.133) | copy-start | bytes 1327108
  143.4 27.6 %collective-permute-start.20 = (bf16[2,96,1536]{2,1,0:T(8,128)(2,1)}, bf16[2,96,1536]{2,1,0:T(8,128)(2,1)S(1)}, u32[]{:S(2)}, u32[]{:S(2)}) collective-permute-start(bf16[2,96,1536]{2,1,0:T(8,128)(2,1)} %get-tuple-element.128), channel_id=1, source_target_pairs={{0,8},{4,12},{8,0},{12,4},{16,24},{20,28},{24,16},{28,20},{1,9},{5... | collective-permute-start | bytes 1769480 | tf_op jit(solution)/shard_map/ppermute | solution.py:458
  144.0 13.1 %collective-permute-start.22 = (bf16[1,96,2304]{2,1,0:T(8,128)(2,1)S(1)}, bf16[1,96,2304]{2,1,0:T(8,128)(2,1)S(1)}, u32[]{:S(2)}, u32[]{:S(2)}) collective-permute-start(bf16[1,96,2304]{2,1,0:T(8,128)(2,1)S(1)} %copy-done.39), channel_id=1, source_target_pairs={{0,16},{4,20},{8,24},{12,28},{16,0},{20,4},{24,8},{28,12},{1,17},{... | collective-permute-start | bytes 1327112 | tf_op jit(solution)/shard_map/ppermute | solution.py:458
  145.5 21.5 %collective-permute-start.23 = (bf16[1,96,2304]{2,1,0:T(8,128)(2,1)S(1)}, bf16[1,96,2304]{2,1,0:T(8,128)(2,1)S(1)}, u32[]{:S(2)}, u32[]{:S(2)}) collective-permute-start(bf16[1,96,2304]{2,1,0:T(8,128)(2,1)S(1)} %copy-done.38), channel_id=1, source_target_pairs={{0,8},{4,12},{8,0},{12,4},{16,24},{20,28},{24,16},{28,20},{1,9},{5... | collective-permute-start | bytes 1327112 | tf_op jit(solution)/shard_map/ppermute | solution.py:458
  147.0 24.0 %collective-permute-start.21 = (bf16[2,96,1152]{2,1,0:T(8,128)(2,1)}, bf16[2,96,1152]{2,1,0:T(8,128)(2,1)S(1)}, u32[]{:S(2)}, u32[]{:S(2)}) collective-permute-start(bf16[2,96,1152]{2,1,0:T(8,128)(2,1)} %get-tuple-element.130), channel_id=1, source_target_pairs={{0,16},{4,20},{8,24},{12,28},{16,0},{20,4},{24,8},{28,12},{1,17},{... | collective-permute-start | bytes 1327112 | tf_op jit(solution)/shard_map/ppermute | solution.py:458
  157.1 9.9 %copy-start.7 = (bf16[1,96,2304]{2,1,0:T(8,128)(2,1)}, bf16[1,96,2304]{2,1,0:T(8,128)(2,1)S(1)}, u32[]{:S(2)}) copy-start(bf16[1,96,2304]{2,1,0:T(8,128)(2,1)S(1)} %collective-permute-done.22) | copy-start | bytes 1327108
  171.9 6.2 %copy-start.40 = (bf16[1,48,2304]{2,1,0:T(8,128)(2,1)S(1)}, bf16[1,48,2304]{2,1,0:T(8,128)(2,1)}, u32[]{:S(2)}) copy-start(bf16[1,48,2304]{2,1,0:T(8,128)(2,1)} %get-tuple-element.141) | copy-start | bytes 663556
  171.9 8.7 %copy-start.35 = (f32[2,768]{1,0:T(2,128)S(1)}, f32[2,768]{1,0:T(2,128)}, u32[]{:S(2)}) copy-start(f32[2,768]{1,0:T(2,128)} %get-tuple-element.125) | copy-start | bytes 18436
  171.9 8.7 %copy-start.36 = (f32[2,384]{1,0:T(2,128)S(1)}, f32[2,384]{1,0:T(2,128)}, u32[]{:S(2)}) copy-start(f32[2,384]{1,0:T(2,128)} %get-tuple-element.127) | copy-start | bytes 9220
  171.9 8.7 %copy-start.37 = (f32[1,768]{1,0:T(1,128)S(1)}, f32[1,768]{1,0:T(1,128)}, u32[]{:S(2)}) copy-start(f32[1,768]{1,0:T(1,128)} %get-tuple-element.126) | copy-start | bytes 9220
  175.3 18.6 %collective-permute-start.24 = (bf16[1,96,1536]{2,1,0:T(8,128)(2,1)}, bf16[1,96,1536]{2,1,0:T(8,128)(2,1)S(1)}, u32[]{:S(2)}, u32[]{:S(2)}) collective-permute-start(bf16[1,96,1536]{2,1,0:T(8,128)(2,1)} %get-tuple-element.136), channel_id=1, source_target_pairs={{0,16},{4,20},{8,24},{12,28},{16,0},{20,4},{24,8},{28,12},{1,17},{... | collective-permute-start | bytes 884744 | tf_op jit(solution)/shard_map/ppermute | solution.py:458
  176.8 9.2 %collective-permute-start.26 = (bf16[1,48,2304]{2,1,0:T(8,128)(2,1)S(1)}, bf16[1,48,2304]{2,1,0:T(8,128)(2,1)S(1)}, u32[]{:S(2)}, u32[]{:S(2)}) collective-permute-start(bf16[1,48,2304]{2,1,0:T(8,128)(2,1)S(1)} %copy-done.41), channel_id=1, source_target_pairs={{0,1},{1,0},{2,3},{3,2},{4,5},{5,4},{6,7},{7,6},{8,9},{9,8},{10,11... | collective-permute-start | bytes 663560 | tf_op jit(solution)/shard_map/ppermute | solution.py:458
  178.1 10.2 %collective-permute-start.27 = (bf16[1,48,2304]{2,1,0:T(8,128)(2,1)S(1)}, bf16[1,48,2304]{2,1,0:T(8,128)(2,1)S(1)}, u32[]{:S(2)}, u32[]{:S(2)}) collective-permute-start(bf16[1,48,2304]{2,1,0:T(8,128)(2,1)S(1)} %copy-done.40), channel_id=1, source_target_pairs={{0,2},{1,3},{2,0},{3,1},{4,6},{5,7},{6,4},{7,5},{8,10},{9,11},{10,... | collective-permute-start | bytes 663560 | tf_op jit(solution)/shard_map/ppermute | solution.py:458
  179.8 14.1 %collective-permute-start.25 = (bf16[1,96,1152]{2,1,0:T(8,128)(2,1)}, bf16[1,96,1152]{2,1,0:T(8,128)(2,1)S(1)}, u32[]{:S(2)}, u32[]{:S(2)}) collective-permute-start(bf16[1,96,1152]{2,1,0:T(8,128)(2,1)} %get-tuple-element.138), channel_id=1, source_target_pairs={{0,8},{4,12},{8,0},{12,4},{16,24},{20,28},{24,16},{28,20},{1,9},{5... | collective-permute-start | bytes 663560 | tf_op jit(solution)/shard_map/ppermute | solution.py:458
  180.7 18.9 %collective-permute-start.15 = (f32[24,128]{1,0:T(8,128)S(1)}, f32[24,128]{1,0:T(8,128)S(1)}, u32[]{:S(2)}, u32[]{:S(2)}) collective-permute-start(f32[24,128]{1,0:T(8,128)S(1)} %maximum_bitcast_fusion), channel_id=1, source_target_pairs={{0,4},{4,0},{8,12},{12,8},{16,20},{20,16},{24,28},{28,24},{1,5},{5... | collective-permute-start | bytes 36872 | tf_op jit(solution)/shard_map/ppermute | solution.py:458
  191.1 12.0 %collective-permute-start.31 = (bf16[1,48,2304]{2,1,0:T(8,128)(2,1)}, bf16[1,48,2304]{2,1,0:T(8,128)(2,1)S(1)}, u32[]{:S(2)}, u32[]{:S(2)}) collective-permute-start(bf16[1,48,2304]{2,1,0:T(8,128)(2,1)} %get-tuple-element.147.refs_2_), channel_id=1, source_target_pairs={{0,1},{1,0},{2,3},{3,2},{4,5},{5,4},{6,7},{7,6},{8,9},{9,8},{10,11... | collective-permute-start | bytes 663560 | tf_op jit(solution)/shard_map/ppermute | solution.py:458
  191.3 15.7 %collective-permute-start.30 = (bf16[1,48,2304]{2,1,0:T(8,128)(2,1)}, bf16[1,48,2304]{2,1,0:T(8,128)(2,1)S(1)}, u32[]{:S(2)}, u32[]{:S(2)}) collective-permute-start(bf16[1,48,2304]{2,1,0:T(8,128)(2,1)} %get-tuple-element.142.refs_9_.refs_0_), channel_id=1, source_target_pairs={{0,2},{1,3},{2,0},{3,1},{4,6},{5,7},{6,4},{7,5},{8,10},{9,11},{10,... | collective-permute-start | bytes 663560 | tf_op jit(solution)/shard_map/ppermute | solution.py:458
  197.4 13.5 %collective-permute-start.29 = (bf16[1,48,1152]{2,1,0:T(8,128)(2,1)}, bf16[1,48,1152]{2,1,0:T(8,128)(2,1)S(1)}, u32[]{:S(2)}, u32[]{:S(2)}) collective-permute-start(bf16[1,48,1152]{2,1,0:T(8,128)(2,1)} %get-tuple-element.146), channel_id=1, source_target_pairs={{0,2},{1,3},{2,0},{3,1},{4,6},{5,7},{6,4},{7,5},{8,10},{9,11},{10,... | collective-permute-start | bytes 331784 | tf_op jit(solution)/shard_map/ppermute | solution.py:458
  197.7 13.2 %collective-permute-start.28 = (bf16[1,48,1536]{2,1,0:T(8,128)(2,1)}, bf16[1,48,1536]{2,1,0:T(8,128)(2,1)S(1)}, u32[]{:S(2)}, u32[]{:S(2)}) collective-permute-start(bf16[1,48,1536]{2,1,0:T(8,128)(2,1)} %get-tuple-element.144), channel_id=1, source_target_pairs={{0,1},{1,0},{2,3},{3,2},{4,5},{5,4},{6,7},{7,6},{8,9},{9,8},{10,11... | collective-permute-start | bytes 442376 | tf_op jit(solution)/shard_map/ppermute | solution.py:458
  199.6 15.6 %collective-permute-start.16 = (f32[24,128]{1,0:T(8,128)S(1)}, f32[24,128]{1,0:T(8,128)S(1)}, u32[]{:S(2)}, u32[]{:S(2)}) collective-permute-start(f32[24,128]{1,0:T(8,128)S(1)} %fusion.21), channel_id=1, source_target_pairs={{0,8},{4,12},{8,0},{12,4},{16,24},{20,28},{24,16},{28,20},{1,9},{5... | collective-permute-start | bytes 36872 | tf_op jit(solution)/shard_map/ppermute | solution.py:458
  209.7 16.8 %collective-permute-start.35 = (bf16[1,48,2304]{2,1,0:T(8,128)(2,1)}, bf16[1,48,2304]{2,1,0:T(8,128)(2,1)S(1)}, u32[]{:S(2)}, u32[]{:S(2)}) collective-permute-start(bf16[1,48,2304]{2,1,0:T(8,128)(2,1)} %get-tuple-element.151), channel_id=1, source_target_pairs={{0,2},{1,3},{2,0},{3,1},{4,6},{5,7},{6,4},{7,5},{8,10},{9,11},{10,... | collective-permute-start | bytes 663560 | tf_op jit(solution)/shard_map/ppermute | solution.py:458
  209.7 16.8 %collective-permute-start.34 = (bf16[1,48,2304]{2,1,0:T(8,128)(2,1)}, bf16[1,48,2304]{2,1,0:T(8,128)(2,1)S(1)}, u32[]{:S(2)}, u32[]{:S(2)}) collective-permute-start(bf16[1,48,2304]{2,1,0:T(8,128)(2,1)} %get-tuple-element.148.refs_4_), channel_id=1, source_target_pairs={{0,1},{1,0},{2,3},{3,2},{4,5},{5,4},{6,7},{7,6},{8,9},{9,8},{10,11... | collective-permute-start | bytes 663560 | tf_op jit(solution)/shard_map/ppermute | solution.py:458
  213.4 17.6 %collective-permute-start.32 = (bf16[1,48,1536]{2,1,0:T(8,128)(2,1)}, bf16[1,48,1536]{2,1,0:T(8,128)(2,1)S(1)}, u32[]{:S(2)}, u32[]{:S(2)}) collective-permute-start(bf16[1,48,1536]{2,1,0:T(8,128)(2,1)} %get-tuple-element.149.refs_5_.refs_0_), channel_id=1, source_target_pairs={{0,2},{1,3},{2,0},{3,1},{4,6},{5,7},{6,4},{7,5},{8,10},{9,11},{10,... | collective-permute-start | bytes 442376 | tf_op jit(solution)/shard_map/ppermute | solution.py:458
  215.2 3.8 %collective-permute-start.17 = (f32[24,128]{1,0:T(8,128)S(1)}, f32[24,128]{1,0:T(8,128)S(1)}, u32[]{:S(2)}, u32[]{:S(2)}) collective-permute-start(f32[24,128]{1,0:T(8,128)S(1)} %fusion.22), channel_id=1, source_target_pairs={{0,16},{4,20},{8,24},{12,28},{16,0},{20,4},{24,8},{28,12},{1,17},{... | collective-permute-start | bytes 36872 | tf_op jit(solution)/shard_map/ppermute | solution.py:458
  218.9 3.7 %collective-permute-start.18 = (f32[24,128]{1,0:T(8,128)S(1)}, f32[24,128]{1,0:T(8,128)S(1)}, u32[]{:S(2)}, u32[]{:S(2)}) collective-permute-start(f32[24,128]{1,0:T(8,128)S(1)} %add.112), channel_id=1, source_target_pairs={{0,1},{1,0},{2,3},{3,2},{4,5},{5,4},{6,7},{7,6},{8,9},{9,8},{10,11... | collective-permute-start | bytes 36872 | tf_op jit(solution)/shard_map/ppermute | solution.py:458
  222.6 11.2 %collective-permute-start.19 = (f32[24,128]{1,0:T(8,128)S(1)}, f32[24,128]{1,0:T(8,128)S(1)}, u32[]{:S(2)}, u32[]{:S(2)}) collective-permute-start(f32[24,128]{1,0:T(8,128)S(1)} %add.113), channel_id=1, source_target_pairs={{0,2},{1,3},{2,0},{3,1},{4,6},{5,7},{6,4},{7,5},{8,10},{9,11},{10,... | collective-permute-start | bytes 36872 | tf_op jit(solution)/shard_map/ppermute | solution.py:458
  223.8 7.2 %collective-permute-start.33 = (bf16[1,48,1152]{2,1,0:T(8,128)(2,1)}, bf16[1,48,1152]{2,1,0:T(8,128)(2,1)S(1)}, u32[]{:S(2)}, u32[]{:S(2)}) collective-permute-start(bf16[1,48,1152]{2,1,0:T(8,128)(2,1)} %get-tuple-element.150.refs_2_), channel_id=1, source_target_pairs={{0,1},{1,0},{2,3},{3,2},{4,5},{5,4},{6,7},{7,6},{8,9},{9,8},{10,11... | collective-permute-start | bytes 331784 | tf_op jit(solution)/shard_map/ppermute | solution.py:458
  233.6 6.5 %collective-permute-start.36 = (bf16[1,48,1536]{2,1,0:T(8,128)(2,1)}, bf16[1,48,1536]{2,1,0:T(8,128)(2,1)S(1)}, u32[]{:S(2)}, u32[]{:S(2)}) collective-permute-start(bf16[1,48,1536]{2,1,0:T(8,128)(2,1)} %get-tuple-element.153), channel_id=1, source_target_pairs={{0,1},{1,0},{2,3},{3,2},{4,5},{5,4},{6,7},{7,6},{8,9},{9,8},{10,11... | collective-permute-start | bytes 442376 | tf_op jit(solution)/shard_map/ppermute | solution.py:458
  233.8 6.0 %collective-permute-start.37 = (bf16[1,48,1152]{2,1,0:T(8,128)(2,1)}, bf16[1,48,1152]{2,1,0:T(8,128)(2,1)S(1)}, u32[]{:S(2)}, u32[]{:S(2)}) collective-permute-start(bf16[1,48,1152]{2,1,0:T(8,128)(2,1)} %get-tuple-element.154), channel_id=1, source_target_pairs={{0,2},{1,3},{2,0},{3,1},{4,6},{5,7},{6,4},{7,5},{8,10},{9,11},{10,... | collective-permute-start | bytes 331784 | tf_op jit(solution)/shard_map/ppermute | solution.py:458
  (32 other events, 40.8 us)
where the time goes:
time: 244 us; the launch traced here: 243 us
  Pallas kernels  134 us (55%)
  waiting for transfers between devices  42.6 us (17%)
  starting transfers between devices  41.7 us (17%)
  local copies, waits for them, and re-layouts  14.4 us (6%)
  other arithmetic  5.71 us (2%)
  matrix products  3.79 us (2%)
    pallas_call x21, Pallas kernels, call(): pl.pallas_call(body, grid_spec=pltpu.PrefetchScalarGridSpec(num_scalar_pr...  134 us
    ppermute x29, waiting for transfers between devices, swap(): return lax.ppermute(v, axis, [(i, i ^ bit) for i in range(n)])  37.4 us
    ppermute x29, starting transfers between devices, swap(): return lax.ppermute(v, axis, [(i, i ^ bit) for i in range(n)])  29.6 us
    ppermute x9, starting transfers between devices, shift_all(): lax.ppermute(payload, axis, [(i, (i + k) % n) for i in range(n)])  12.1 us
    unnamed x84, local copies, waits for them, and re-layouts  11.7 us
    ppermute x9, waiting for transfers between devices, shift_all(): lax.ppermute(payload, axis, [(i, (i + k) % n) for i in range(n)])  5.19 us
  transfers between devices with their start and end apart: 38, of which 15 were waited for; matrix products, arithmetic and copies ran while one was open for 4% of the time, Pallas kernels for 32%

commit v1 on v0

--- a/solution.py
+++ b/solution.py
@@ -10,6 +10,12 @@
 GROUPS = 8
 CHUNKS = 8
 LANES = 128
+RANK, PLACE, FIRST, OTHERS = 0, 1, 2, 3
+MICROSECONDS = dict(
+    project=3.6, summary=4.8, mixer=10.9, ffn=22.0, turn=12.3, mixer_grads=3.4, adjoint=8.7, input_grads=2.4, tokens=4.5, out=3.5,
+    ffn_sum1=3.6, mixer_sum1=3.4,
+)
+COST = 1.15e9
 TILE = 16
 epsilon = 1e-06
 BF = jnp.bfloat16
@@ -82,12 +88,12 @@
     put(drv_im, (1.0 - forget) * jax.nn.silu(pre[:, ch : 2 * ch]))
 
 
-def project_kernel(bit_ref, x_ref, gain_ref, w_in_ref, w_forget_ref, bias_ref, perm_ref, normed_ref, turned_ref, pre_ref, *, lo):
+def project_kernel(here_ref, x_ref, gain_ref, w_in_ref, w_forget_ref, bias_ref, perm_ref, normed_ref, turned_ref, pre_ref, *, lo):
     width = x_ref.shape[1]
     x = x_ref[...].astype(F32)
     normed = (x * lax.rsqrt(row_mean(x * x) + epsilon) * gain_ref[...][None]).astype(BF)
     normed_ref[...] = normed
-    put_halves(turned_ref, normed.T, 0, lo, bit_ref[0])
+    put_halves(turned_ref, normed.T, 0, lo, here_ref[FIRST])
     mixed = dot(normed, w_in_ref[...]).astype(BF)
     pre_ref[:, :width] = dot(mixed, perm_ref[...]).astype(BF)
     pre_ref[:, width:] = (dot(normed, w_forget_ref[...]) + bias_ref[...][None]).astype(BF)
@@ -131,11 +137,12 @@
     scalars, refs = refs[0], refs[1:]
     totals, inits, refs = refs[:ranks], refs[ranks : 2 * ranks], refs[2 * ranks :]
     pre_ref, trig_ref, chunk_ref, perm_ref, x_ref, og_ref, gain_ref, member_ref, w_out_ref = refs[:9]
-    y_ref, hr_ref, hi_ref, start_ref, final_ref, turned_ref, middle_ref = refs[9:16]
-    lam_re, lam_im, drv_re, drv_im = refs[16:]
+    y_ref, split_ref, start_ref, final_ref, turned_ref, middle_ref = refs[9:15]
+    lam_re, lam_im, drv_re, drv_im = refs[15:]
     parts, span, _ = lam_re.shape
+    ch = parts * LANES
     step = span // CHUNKS
-    rank, bit = scalars[0], scalars[1]
+    rank, bit = scalars[RANK], scalars[FIRST]
     drives(pre_ref[...].astype(F32), trig_ref[...], lam_re, lam_im, drv_re, drv_im)
     init = inits[0][...]
     for info in inits[1:]:
@@ -154,7 +161,8 @@
     er, ei = after(0, cr, ci, rank >= 0)
     for k in range(ranks - 1, 0, -1):
         er, ei = after(k, er, ei, k > rank)
-    final_ref[...] = jnp.concatenate([er, ei], axis=0)
+    own = ch // ranks
+    final_ref[...] = pltpu.roll(jnp.concatenate([er, ei] * 4, axis=0), (ch - own * rank) % ch, 1)[:2, :own]
     rows_r, rows_i = [cr], [ci]
     for k in range(CHUNKS - 1):
         cr, ci = cmul(chunk_ref[0, k : k + 1, :], chunk_ref[1, k : k + 1, :], cr, ci)
@@ -169,27 +177,28 @@
         for g in range(parts):
             hr, hi = cmul(lam_re[g, rows, :], lam_im[g, rows, :], *carried[g])
             hr, hi = hr + drv_re[g, rows, :], hi + drv_im[g, rows, :]
-            hr_ref[g, rows, :] = hr
-            hi_ref[g, rows, :] = hi
+            drv_re[g, rows, :] = hr
+            drv_im[g, rows, :] = hi
             carried[g] = (hr, hi)
-    split = jnp.concatenate([get(hr_ref).astype(BF), get(hi_ref).astype(BF)], axis=1)
+    split = jnp.concatenate([get(drv_re).astype(BF), get(drv_im).astype(BF)], axis=1)
+    split_ref[...] = split
     yf = dot(split, perm_ref[...], NT)
     y_ref[...] = yf.astype(BF)
     member = member_ref[...]
     inv = group_spread(lax.rsqrt(group_mean(yf * yf, member) + epsilon), member)
-    gated = (yf * inv * gain_ref[...][None] * jax.nn.silu(og_ref[...])).astype(BF)
+    gated = (yf * inv * gain_ref[...][None] * jax.nn.silu(og_ref[...].astype(F32))).astype(BF)
     put_halves(turned_ref, gated.T, 0, lo, bit)
     middle_ref[...] = x_ref[...].astype(F32) + dot(gated, w_out_ref[...])
 
 
 def ffn_kernel(
-    bit_ref, middle_ref, gain_ref, cot_ref, wg_ref, wu_ref, wd_ref,
-    gsend_ref, gkeep_ref, dsend_ref, dkeep_ref, mixed_ref, dn_ref,
-    n_ref, nt_ref, acc_ref, hid_ref, dgv_ref, duv_ref, ht_ref,
+    here_ref, middle_ref, gain_ref, cot_ref, wg_ref, wu_ref, wd_ref,
+    gsend_ref, gkeep_ref, dsend_ref, dkeep_ref, hid_ref, dn_ref,
+    n_ref, nt_ref, dgv_ref, duv_ref, ht_ref,
     *, lo, dlo, rt,
 ):
-    j, last = pl.program_id(0), pl.num_programs(0) - 1
-    bit = bit_ref[0]
+    j = pl.program_id(0)
+    bit = here_ref[FIRST]
     count, width = middle_ref.shape
     tile = wg_ref.shape[1]
     spans = [slice(r, r + rt) for r in range(0, count, rt)]
@@ -218,22 +227,15 @@
     for lhs, ref in ((ht_ref[: tile // 2, :], dsend_ref), (ht_ref[tile // 2 :, :], dkeep_ref)):
         ref[...] = dot(lhs, cot_ref[...]).astype(BF)
     for rows in spans:
-        out = dot(hid_ref[rows, :], wd_ref[...])
         dn = dot(dgv_ref[rows, :], wg_ref[...], NT) + dot(duv_ref[rows, :], wu_ref[...], NT)
 
         @pl.when(j == 0)
         def _():
-            acc_ref[rows, :] = middle_ref[rows, :] + out
             dn_ref[rows, :] = dn
 
         @pl.when(j > 0)
         def _():
-            acc_ref[rows, :] += out
             dn_ref[rows, :] += dn
-
-        @pl.when(j == last)
-        def _():
-            mixed_ref[rows, :] = acc_ref[rows, :].astype(BF)
 
 
 def turn_kernel(
@@ -255,7 +257,7 @@
     dbranch = dmiddle.astype(BF)
     dbranch_ref[...] = dbranch
     dgated = dot(dbranch, w_out_ref[...], NT)
-    og, yf, member, gain = og_ref[...], y_ref[...].astype(F32), member_ref[...], gain_ref[...][None]
+    og, yf, member, gain = og_ref[...].astype(F32), y_ref[...].astype(F32), member_ref[...], gain_ref[...][None]
     ginv = group_spread(lax.rsqrt(group_mean(yf * yf, member) + epsilon), member)
     gunit = yf * ginv
     sig = jax.nn.sigmoid(og)
@@ -298,12 +300,12 @@
 def adjoint_kernel(*refs, ranks):
     scalars, refs = refs[0], refs[1:]
     totals, adjs, refs = refs[:ranks], refs[ranks : 2 * ranks], refs[2 * ranks :]
-    pre_ref, trig_ref, dy_ref, hr_ref, hi_ref, start_ref, chunk_ref, chain_ref, perm_ref = refs[:9]
-    dpre_ref, sums_ref, lam_re, lam_im, dy_re, dy_im = refs[9:]
+    pre_ref, trig_ref, dy_ref, split_ref, start_ref, chunk_ref, chain_ref, perm_ref = refs[:8]
+    dpre_ref, sums_ref, lam_re, lam_im, dy_re, dy_im = refs[8:]
     parts, span, _ = lam_re.shape
     ch = parts * LANES
     step = span // CHUNKS
-    rank = scalars[0]
+    rank = scalars[RANK]
     pre = pre_ref[...].astype(F32)
     trig = trig_ref[...]
     forget = decays(pre, trig, lam_re, lam_im)
@@ -338,8 +340,8 @@
             carried[g] = cmul(lam_re[g, rows, :], -lam_im[g, rows, :], gr, gi)
     gr, gi = get(dy_re), get(dy_im)
     first = lax.broadcasted_iota(jnp.int32, (span, ch), 0) == 0
-    qr = jnp.where(first, start_ref[0:1, :], pltpu.roll(get(hr_ref), 1, 0))
-    qi = jnp.where(first, start_ref[1:2, :], pltpu.roll(get(hi_ref), 1, 0))
+    qr = jnp.where(first, start_ref[0:1, :], pltpu.roll(split_ref[:, :ch].astype(F32), 1, 0))
+    qi = jnp.where(first, start_ref[1:2, :], pltpu.roll(split_ref[:, ch:].astype(F32), 1, 0))
     pin_re, pin_im = pre[:, :ch], pre[:, ch : 2 * ch]
     sig_re, sig_im = jax.nn.sigmoid(pin_re), jax.nn.sigmoid(pin_im)
     lr = gr * qr + gi * qi
@@ -381,8 +383,13 @@
         at += n
 
 
+def out_kernel(middle_ref, hid_ref, w_down_ref, out_ref):
+    out_ref[...] = (middle_ref[...] + dot(hid_ref[...], w_down_ref[...])).astype(BF)
+
+
 def tokens_kernel(
-    dpre_ref, dog_ref, w_in_ref, w_forget_ref, w_ogate_ref, x_ref, gain_ref, dmiddle_ref, out_ref, gains_ref
+    dpre_ref, dog_ref, w_in_ref, w_forget_ref, w_ogate_ref, x_ref, gain_ref, dmiddle_ref, others_ref, sums_ref,
+    out_ref, vectors_ref,
 ):
     width = x_ref.shape[1]
     up = (
@@ -399,49 +406,99 @@
 
     @pl.when(pl.program_id(0) == 0)
     def _():
-        gains_ref[...] = gains
+        vectors_ref[0:1, :] = gains
+        vectors_ref[1:3, :] = others_ref[...]
+        vectors_ref[3:4, :] = jnp.concatenate([sums_ref[0:1, :], sums_ref[1:2, :]], axis=1)
 
     @pl.when(pl.program_id(0) > 0)
     def _():
-        gains_ref[...] += gains
-
-
-def seg(*shape):
-    zeros = (0,) * len(shape)
-    return pl.BlockSpec((None,) + shape, lambda s, *_: (s,) + zeros)
+        vectors_ref[0:1, :] += gains
+
+
+def vectors_kernel(here_ref, vectors_ref, mix_ref, ffn_ref, group_ref, bias_ref, phase_ref):
+    width, ch = vectors_ref.shape[1], vectors_ref.shape[1] // 2
+    rows = jnp.concatenate([vectors_ref[...]] * 2, axis=0)
+    per, own = mix_ref.shape[1], bias_ref.shape[1]
+    gains = pltpu.roll(rows, (width - per * here_ref[PLACE]) % width, 1)
+    mix_ref[...], ffn_ref[...], group_ref[...] = gains[0:1, :per], gains[1:2, :per], gains[2:3, :per]
+    bias_ref[...] = pltpu.roll(rows[:, :ch], (ch - own * here_ref[RANK]) % ch, 1)[3:4, :own]
+    phase_ref[...] = pltpu.roll(rows[:, ch:], (ch - own * here_ref[RANK]) % ch, 1)[3:4, :own]
 
 
 def rows(*shape):
-    return pl.BlockSpec(shape, lambda s, *_: (s, 0))
+    return ("rows", shape)
 
 
 def cols(*shape):
-    return pl.BlockSpec(shape, lambda s, *_: (0, s))
+    return ("cols", shape)
+
+
+def seg(*shape, shift=0, fixed=False):
+    return ("seg", shape, shift, fixed)
 
 
 def whole(*shape):
-    zeros = (0,) * len(shape)
-    return pl.BlockSpec(shape, lambda s, *_: zeros)
-
-
-def call(kernel, steps, ins, outs, scratch, scalars, name, after=()):
-    first, extra = len(scalars) + len(ins), len(after)
+    return ("whole", shape)
+
+
+def moved(*shape, dim):
+    return ("moved", shape, dim)
+
+
+def spec_of(kind):
+    if kind[0] != "moved":
+        return pl.BlockSpec(memory_space=pltpu.VMEM)
+    _, shape, dim = kind
+    return pl.BlockSpec(shape, lambda s, *_: tuple(s if d == dim else 0 for d in range(len(shape))))
+
+
+def view_of(kind, ref):
+    step = pl.program_id(0)
+    if kind[0] == "rows":
+        n = kind[1][0]
+        return ref.at[pl.ds(pl.multiple_of(step * n, n), n)]
+    if kind[0] == "cols":
+        n = kind[1][1]
+        return ref.at[:, pl.ds(pl.multiple_of(step * n, n), n)]
+    if kind[0] == "seg":
+        return ref.at[kind[2] if kind[3] else step + kind[2]]
+    return ref
+
+
+def size_of(shape, dtype):
+    return functools.reduce(lambda p, q: p * q, shape) * jnp.dtype(dtype).itemsize
+
+
+def call(kernel, steps, ins, outs, scratch, scalars, name, after=(), room=6):
+    cost = int(COST * MICROSECONDS.get(name, 2.0))
+    lead, extra = len(scalars), len(after)
+    kinds_in, kinds_out = [k for k, _ in ins], [k for k, _, _ in outs]
 
     def body(*refs):
-        kernel(*refs[:first], *refs[first + extra :])
-
+        given, refs = refs[: lead + len(ins)], refs[lead + len(ins) + extra :]
+        kernel(
+            *given[:lead],
+            *[view_of(k, r) for k, r in zip(kinds_in, given[lead:], strict=True)],
+            *[view_of(k, r) for k, r in zip(kinds_out, refs[: len(outs)], strict=True)],
+            *refs[len(outs) :],
+        )
+
+    limit = room << 20
+    limit += sum(2 * size_of(k[1], a.dtype) for k, a in ins if k[0] == "moved")
+    limit += sum(2 * size_of(k[1], d) for k, _, d in outs if k[0] == "moved")
+    limit += sum(size_of(m.shape, m.dtype) for m in scratch)
     return pl.pallas_call(
         body,
         grid_spec=pltpu.PrefetchScalarGridSpec(
-            num_scalar_prefetch=len(scalars),
+            num_scalar_prefetch=lead,
             grid=(steps,),
-            in_specs=[s for s, _ in ins] + [pl.BlockSpec(memory_space=pl.ANY)] * extra,
-            out_specs=[s for s, _, _ in outs],
+            in_specs=[spec_of(k) for k in kinds_in] + [pl.BlockSpec(memory_space=pl.ANY)] * extra,
+            out_specs=[spec_of(k) for k in kinds_out],
             scratch_shapes=scratch,
         ),
         out_shape=[jax.ShapeDtypeStruct(s, d) for _, s, d in outs],
-        compiler_params=pltpu.CompilerParams(vmem_limit_bytes=56 * 1024 * 1024),
-        cost_estimate=pl.CostEstimate(flops=1, bytes_accessed=1, transcendentals=0),
+        compiler_params=pltpu.CompilerParams(vmem_limit_bytes=limit),
+        cost_estimate=pl.CostEstimate(flops=cost, bytes_accessed=1, transcendentals=0),
         name=name,
     )(*scalars, *[a for _, a in ins], *after)
 
@@ -451,7 +508,7 @@
 
 
 def own_bit(axis, bit):
-    return (lax.axis_index(axis) // bit) % 2
+    return lax.shift_right_logical(lax.axis_index(axis).astype(jnp.int32), jnp.int32(bit.bit_length() - 1)) & 1
 
 
 def swap(v, axis, n, bit):
@@ -462,42 +519,43 @@
     return [1 << i for i in range((n - 1).bit_length())]
 
 
-def combine_kernel(bits_ref, *refs, layout):
-    n_in = sum(2 * addends for lane in layout for addends, _ in lane)
-    ins, outs = list(refs[:n_in]), list(refs[n_in:])
-    for lane in layout:
-        for out in (outs.pop(0), outs.pop(0)):
-            at = 0
-            for addends, width in lane:
-                acc = ins.pop(0)[...].astype(F32)
-                for _ in range(addends - 1):
-                    acc = acc + ins.pop(0)[...].astype(F32)
-                out[:, at : at + width] = acc.astype(out.dtype)
-                at += width
-
-
-def combine(lanes_in, name, after=()):
-    scalars = jnp.stack([bit for _, bit, _ in lanes_in]).astype(jnp.int32)
-    ins, outs, layout, steps = [], [], [], None
-    for n, (pos, _, sources) in enumerate(lanes_in):
-        width = sum(src[4] for src in sources)
+def combine_kernel(here_ref, *refs, plan, n_in):
+    ins, outs = refs[:n_in], refs[n_in:]
+    for n, (pos, bit, count, sources) in enumerate(plan):
+        for flip in (1, 0):
+            own = 1 - here_ref[bit] if flip else here_ref[bit]
+            for i in range(count):
+                low = i % (1 << pos)
+                q = (i - low) * 2 + own * (1 << pos) + low
+                at = 0
+                for addends, mult, off, col, width in sources:
+                    cut = slice(col * width, (col + 1) * width)
+                    acc = ins[addends[0]][q * mult + off, :, cut].astype(F32)
+                    for k in addends[1:]:
+                        acc = acc + ins[k][q * mult + off, :, cut].astype(F32)
+                    outs[2 * n + 1 - flip][i, :, at : at + width] = acc.astype(BF)
+                    at += width
+
+
+def combine(here, lanes_in, name, after=()):
+    arrays, outs, plan = [], [], []
+
+    def operand(a):
+        for k, b in enumerate(arrays):
+            if a is b:
+                return k
+        arrays.append(a)
+        return len(arrays) - 1
+
+    for pos, bit, sources in lanes_in:
         addends, mult = sources[0][0], sources[0][1]
-        per = addends[0].shape[1]
-        count = addends[0].shape[0] // mult // 2
-        assert steps in (None, count)
-        steps = count
-        for flip in (1, 0):
-            for addends, mult, off, col, w in sources:
-                def index(i, bits, n=n, pos=pos, flip=flip, mult=mult, off=off, col=col):
-                    own = bits[n] if not flip else 1 - bits[n]
-                    low = i % (1 << pos)
-                    return (((i - low) * 2 + own * (1 << pos) + low) * mult + off, 0, col)
-
-                ins += [(pl.BlockSpec((None, per, w), index), a) for a in addends]
-        layout.append([(len(src[0]), src[4]) for src in sources])
-        outs += [(pl.BlockSpec((None, per, width), lambda i, *_: (i, 0, 0)), (count, per, width), BF)] * 2
+        per, count = addends[0].shape[1], addends[0].shape[0] // mult // 2
+        plan.append((pos, bit, count, [([operand(a) for a in src[0]], *src[1:]) for src in sources]))
+        shape = (count, per, sum(src[4] for src in sources))
+        outs += [(whole(*shape), shape, BF)] * 2
     got = call(
-        functools.partial(combine_kernel, layout=layout), steps, ins, outs, [], [scalars], name, after
+        functools.partial(combine_kernel, plan=plan, n_in=len(arrays)), 1, [(whole(), a) for a in arrays], outs, [],
+        [here], name, after, 4,
     )
     return [(got[2 * n], got[2 * n + 1]) for n in range(len(lanes_in))]
 
@@ -514,23 +572,23 @@
     return call(add_kernel, 1, ins, outs, [], [], name, after)
 
 
-def finish_kernel(bits_ref, *refs, moves, lanes_n):
+def finish_kernel(here_ref, *refs, moves, lanes_n, bits):
     halves, outs = refs[: 2 * lanes_n], refs[2 * lanes_n :]
     for lane, col, width, out, row, at in moves:
         own, other = halves[2 * lane], halves[2 * lane + 1]
         half = own.shape[0]
         for h in range(2):
-            pick = bits_ref[lane] == h
+            pick = here_ref[bits[lane]] == h
             value = jnp.where(pick, own[:, col : col + width].astype(F32), other[:, col : col + width].astype(F32))
             outs[out][row + h * half : row + (h + 1) * half, at : at + width] = value
 
 
-def finish(halves, bits, moves, shapes, name, after=()):
+def finish(here, halves, bits, moves, shapes, name, after=()):
     ins = [(whole(*a.shape), a) for pair in halves for a in pair]
     outs = [(whole(*s), s, F32) for s in shapes]
     return call(
-        functools.partial(finish_kernel, moves=moves, lanes_n=len(halves)), 1, ins, outs, [],
-        [jnp.stack(bits).astype(jnp.int32)], name, after,
+        functools.partial(finish_kernel, moves=moves, lanes_n=len(halves), bits=bits), 1, ins, outs, [], [here], name,
+        after,
     )
 
 
@@ -574,8 +632,10 @@
     bits = bits_of(ndp)
     first = next(b for b in bits if (per * b) % TILE == 0)
     rest = [b for b in bits if b != first]
-    bit = own_bit("dp", first).astype(jnp.int32)
     lo = per * first
+    here = [rank, lax.axis_index("dp"), own_bit("dp", first)]
+    here += [own_bit("dp", b) for b in rest] + [own_bit("seq", b) for b in bits_of(nseq)]
+    here = jnp.stack([h.astype(jnp.int32) for h in here])
     scan_scratch = [pltpu.VMEM((ch // LANES, span, LANES), F32)] * 4
 
     own = jnp.concatenate(
@@ -601,11 +661,11 @@
             (cols(width, span), (width, count), BF),
             (seg(span, 3 * ch), (segs, span, 3 * ch), BF),
         ],
-        [], [bit[None]], "project",
+        [], [here], "project",
     )
     trig, chunk, totals = call(
         functools.partial(summary_kernel, ranks=nseq), segs,
-        [(seg(span, 3 * ch), pre)] + [(pl.BlockSpec((None, 2, ch), lambda s, *_: (0, 0, 0)), i) for i in infos],
+        [(seg(span, 3 * ch), pre)] + [(seg(2, ch, fixed=True), i) for i in infos],
         [
             (whole(2, ch), (2, ch), F32),
             (seg(4, CHUNKS, ch), (segs, 4, CHUNKS, ch), F32),
@@ -614,11 +674,11 @@
         scan_scratch, [], "summary",
     )
     totals = shift_all(totals, "seq", nseq)
-    og = dot(normed, w_ogate)
-    y, h_re, h_im, start, final, gated_t, middle = call(
+    og = dot(normed, w_ogate).astype(BF)
+    y, y_split, start, final, gated_t, middle = call(
         functools.partial(mixer_kernel, ranks=nseq, lo=lo), segs,
         [(seg(4, ch), t) for t in totals]
-        + [(pl.BlockSpec((None, 2, ch), lambda s, *_: (1 + s, 0, 0)), i) for i in infos]
+        + [(seg(2, ch, shift=1), i) for i in infos]
         + [
             (seg(span, 3 * ch), pre), (whole(2, ch), trig), (seg(4, CHUNKS, ch), chunk), (whole(width, width), perm),
             (rows(span, width), x), (rows(span, width), og), (whole(width), norm_group),
@@ -626,19 +686,18 @@
         ],
         [
             (rows(span, width), (count, width), BF),
-            (seg(ch // LANES, span, LANES), (segs, ch // LANES, span, LANES), F32),
-            (seg(ch // LANES, span, LANES), (segs, ch // LANES, span, LANES), F32),
+            (rows(span, width), (count, width), BF),
             (seg(2, ch), (segs, 2, ch), F32),
-            (seg(2, ch), (segs, 2, ch), F32),
+            (seg(2, mine), (segs, 2, mine), F32),
             (cols(width, span), (width, count), BF),
             (rows(span, width), (count, width), F32),
         ],
-        scan_scratch, [jnp.stack([rank, bit])], "mixer",
-    )
-    final_state = lax.dynamic_slice_in_dim(final, rank * mine, mine, axis=2).transpose(0, 2, 1)
+        scan_scratch, [here], "mixer",
+    )
+    final_state = final.transpose(0, 2, 1)
 
     tile = width
-    gsend, gkeep, dsend, dkeep, mixed_out, dn = call(
+    gsend, gkeep, dsend, dkeep, hid, dn = call(
         functools.partial(ffn_kernel, lo=lo, dlo=lo * tall, rt=span), hidden // tile,
         [
             (whole(count, width), middle), (whole(width), norm_ffn), (whole(count, width), cot),
@@ -649,15 +708,15 @@
             (cols(width // 2, 2 * tile), (width // 2, 2 * hidden), BF),
             (rows(tile // 2, width), (hidden // 2, width), BF),
             (rows(tile // 2, width), (hidden // 2, width), BF),
-            (whole(count, width), (count, width), BF),
+            (cols(count, tile), (count, hidden), BF),
             (whole(count, width), (count, width), F32),
         ],
         [
-            pltpu.VMEM((count, width), BF), pltpu.VMEM((width, count), BF), pltpu.VMEM((count, width), F32),
-            pltpu.VMEM((count, tile), BF), pltpu.VMEM((count, tile), BF), pltpu.VMEM((count, tile), BF),
+            pltpu.VMEM((count, width), BF), pltpu.VMEM((width, count), BF),
+            pltpu.VMEM((count, tile), BF), pltpu.VMEM((count, tile), BF),
             pltpu.VMEM((tile, count), BF),
         ],
-        [bit[None]], "ffn",
+        [here], "ffn",
     )
 
     ggot, dgot = swap(gsend, "dp", ndp, first), swap(dsend, "dp", ndp, first)
@@ -699,8 +758,8 @@
     ogot = swap(osend, "dp", ndp, first)
     nblk = ndp // 2
     fast = ndp == 8 and nseq == 4 and per % (2 * TILE) == 0
-    x_bit, y_bit = (own_bit("dp", b) for b in rest[:2]) if fast else (None, None)
-    z_bits = [own_bit("seq", b) for b in bits_of(nseq)]
+    x_bit, y_bit = OTHERS, OTHERS + 1
+    z_bits = [OTHERS + len(rest) + i for i in range(len(bits_of(nseq)))]
 
     def blocks(a, cols_n, tall_n=1):
         return a.reshape(nblk * tall_n, per, cols_n)
@@ -711,7 +770,7 @@
         d = [blocks(a, width, tall) for a in (dkeep, dgot)]
         fa = [(g, 1, 0, 0, 3 * width)]
         fb = [(g, 1, 0, 3, width)] + [(d, tall, i, 0, width) for i in range(tall)]
-        (fa_send, fa_keep), (fb_send, fb_keep) = combine([(0, x_bit, fa), (1, y_bit, fb)], "ffn_sum1", (osend,))
+        (fa_send, fa_keep), (fb_send, fb_keep) = combine(here, [(0, x_bit, fa), (1, y_bit, fb)], "ffn_sum1", (osend,))
         fa_got, fb_got = swap(fa_send, "dp", ndp, rest[0]), swap(fb_send, "dp", ndp, rest[1])
         order = (fa_keep,)
 
@@ -720,11 +779,11 @@
         [(seg(4, ch), t) for t in totals] + [(seg(2, ch), a) for a in adjs]
         + [
             (seg(span, 3 * ch), pre), (whole(2, ch), trig), (rows(span, width), dy_split),
-            (seg(ch // LANES, span, LANES), h_re), (seg(ch // LANES, span, LANES), h_im), (seg(2, ch), start),
+            (rows(span, width), y_split), (seg(2, ch), start),
             (seg(4, CHUNKS, ch), chunk), (seg(2, CHUNKS, ch), chain), (whole(width, width), perm),
         ],
         [(rows(span, 3 * ch), (count, 3 * ch), BF), (whole(2, ch), (2, ch), F32)],
-        scan_scratch, [rank[None]], "adjoint", order,
+        scan_scratch, [here], "adjoint", order,
     )
     isend, ikeep = call(
         functools.partial(grads_kernel, pairs=1), 3,
@@ -745,40 +804,40 @@
             return one(*(a.reshape(2, per // 2, a.shape[2]) for a in (keep, got)))
 
         (fa_send, fa_keep), (fb_send, fb_keep) = combine(
-            [(0, y_bit, one(fa_keep, fa_got)), (0, x_bit, one(fb_keep, fb_got))], "ffn_sum2", (isend,)
+            here, [(0, y_bit, one(fa_keep, fa_got)), (0, x_bit, one(fb_keep, fb_got))], "ffn_sum2", (isend,)
         )
         fa_got, fb_got = swap(fa_send, "dp", ndp, rest[1]), swap(fb_send, "dp", ndp, rest[0])
         o = [blocks(a, 2 * width) for a in (okeep, ogot)]
         i = [blocks(a, 3 * ch) for a in (ikeep, igot)]
         (ra_send, ra_keep), (rb_send, rb_keep) = combine(
-            [(0, x_bit, [(o, 1, 0, 0, 2 * width)]), (1, y_bit, [(i, 1, 0, 0, 3 * ch)])], "mixer_sum1", (fa_keep,)
+            here, [(0, x_bit, [(o, 1, 0, 0, 2 * width)]), (1, y_bit, [(i, 1, 0, 0, 3 * ch)])], "mixer_sum1", (fa_keep,)
         )
         ra_got, rb_got = swap(ra_send, "dp", ndp, rest[0]), swap(rb_send, "dp", ndp, rest[1])
         order = (ra_keep,)
 
-    grad_tokens, gain_mix = call(
+    grad_tokens, vectors = call(
         tokens_kernel, segs,
         [
             (rows(span, 3 * ch), dpre), (rows(span, width), dog), (whole(width, width), w_in),
             (whole(width, ch), w_forget), (whole(width, width), w_ogate), (rows(span, width), x),
-            (whole(width), norm_mix), (rows(span, width), dmiddle),
-        ],
-        [(rows(span, width), (count, width), BF), (whole(1, width), (1, width), F32)],
+            (whole(width), norm_mix), (rows(span, width), dmiddle), (whole(2, width), gains), (whole(2, ch), sums),
+        ],
+        [(moved(span, width, dim=0), (count, width), BF), (whole(4, width), (4, width), F32)],
         [], [], "tokens", order,
     )
 
-    vec = jnp.concatenate([gains.reshape(-1), gain_mix.reshape(-1), sums.reshape(-1)]).reshape(-1, LANES)
+    (mixed_out,) = call(
+        out_kernel, segs, [(rows(span, width), middle), (rows(span, hidden), hid), (whole(hidden, width), w_down)],
+        [(moved(span, width, dim=0), (count, width), BF)], [], [], "out", (grad_tokens,),
+    )
+
     for axis, n in (("dp", ndp), ("seq", nseq)):
         for b in bits_of(n):
-            vec = vec + swap(vec, axis, n, b)
-    vec = vec.reshape(-1)
-    place = lax.axis_index("dp") * per
-
-    def own_gain(i):
-        return lax.dynamic_slice_in_dim(vec, i * width + place, per)
-
-    def own_sum(i):
-        return lax.dynamic_slice_in_dim(vec, 3 * width + i * ch + rank * mine, mine)
+            vectors = vectors + swap(vectors, axis, n, b)
+    part_mix, part_ffn, part_group, part_bias, part_phase = call(
+        vectors_kernel, 1, [(whole(4, width), vectors)],
+        [(whole(1, per), (1, per), F32)] * 3 + [(whole(1, mine), (1, mine), F32)] * 2, [], [here], "vectors",
+    )
 
     shapes_f = [(per, hidden), (per, hidden), (tall * per, width)]
     shapes_r = [(per, width), (per, width), (per, width), (per, ch)]
@@ -789,18 +848,18 @@
             return swap(send, "seq", axis_n, bit)
 
         (fa_send, fa_keep), (fb_send, fb_keep) = combine(
-            [(0, z_bits[0], rows_of(fa_keep, fa_got)), (0, z_bits[1], rows_of(fb_keep, fb_got))],
-            "ffn_sum3", (grad_tokens,),
+            here, [(0, z_bits[0], rows_of(fa_keep, fa_got)), (0, z_bits[1], rows_of(fb_keep, fb_got))],
+            "ffn_sum3", (mixed_out,),
         )
         fa_got, fb_got = over(fa_send, nseq, lead), over(fb_send, nseq, other)
         (ra_send, ra_keep), (rb_send, rb_keep) = combine(
-            [(0, y_bit, one(ra_keep, ra_got)), (0, x_bit, one(rb_keep, rb_got))], "mixer_sum2", (fa_keep,)
+            here, [(0, y_bit, one(ra_keep, ra_got)), (0, x_bit, one(rb_keep, rb_got))], "mixer_sum2", (fa_keep,)
         )
         ra_got, rb_got = swap(ra_send, "dp", ndp, rest[1]), swap(rb_send, "dp", ndp, rest[0])
         fa, fb = add_pairs([(fa_keep, fa_got), (fb_keep, fb_got)], "ffn_sum4", (ra_keep,))
         fa_got, fb_got = over(fa, nseq, other), over(fb, nseq, lead)
         (ra_send, ra_keep), (rb_send, rb_keep) = combine(
-            [(0, z_bits[0], rows_of(ra_keep, ra_got)), (0, z_bits[1], rows_of(rb_keep, rb_got))], "mixer_sum3", (fa,)
+            here, [(0, z_bits[0], rows_of(ra_keep, ra_got)), (0, z_bits[1], rows_of(rb_keep, rb_got))], "mixer_sum3", (fa,)
         )
         ra_got, rb_got = over(ra_send, nseq, lead), over(rb_send, nseq, other)
         fa, fb = add_pairs([(fa, fa_got), (fb, fb_got)], "ffn_sum5", (ra_keep,))
@@ -816,14 +875,14 @@
             (lane, col, width, n % 2, 0, (n // 2) * width) for n, (lane, col) in enumerate(guv)
         ] + [(1, (1 + t) * width, width, 2, t * per, 0) for t in range(tall)]
         part_gate, part_up, part_down = finish(
-            flat((fa, fa_got), (fb, fb_got)), z_bits, moves, shapes_f, "ffn_out", (ra,)
+            here, flat((fa, fa_got), (fb, fb_got)), z_bits, moves, shapes_f, "ffn_out", (ra,)
         )
         ra, rb = add_pairs([(ra, ra_got), (rb, rb_got)], "mixer_sum5", (part_gate,))
         ra_got, rb_got = over(ra, nseq, lead), over(rb, nseq, other)
         moves = [(0, n * ntile, ntile, n % 2, 0, (n // 2) * ntile) for n in range(2 * width // ntile)]
         moves += [(1, 0, width, 2, 0, 0), (1, width, ch, 3, 0, 0)]
         part_ogate, part_out, part_in, part_forget = finish(
-            flat((ra, ra_got), (rb, rb_got)), z_bits, moves, shapes_r, "mixer_out"
+            here, flat((ra, ra_got), (rb, rb_got)), z_bits, moves, shapes_r, "mixer_out"
         )
     else:
         def plain(keep, got, cols_n, tall_n=1):
@@ -843,7 +902,7 @@
         mixed_out.reshape(segs, span, width),
         grad_tokens.reshape(segs, span, width),
         final_state,
-        own_gain(2), part_in, part_forget, own_sum(0), own_sum(1), part_ogate, own_gain(1), part_out, own_gain(0),
+        part_mix[0], part_in, part_forget, part_bias[0], part_phase[0], part_ogate, part_group[0], part_out, part_ffn[0],
         part_gate, part_up, part_down,
     )
 

time: 244 us -> 183 us (0.75)
  Pallas kernels: 134 us -> 79.9 us
  local copies, waits for them, and re-layouts: 14.4 us -> 6.88 us
  other arithmetic: 5.71 us -> 1.57 us
  waiting for transfers between devices: 42.6 us -> 46.5 us
  starting transfers between devices: 41.7 us -> 45.3 us
  matrix products: 3.79 us -> 1.09 us
    pallas_call x21 -> x23, Pallas kernels: 134 us -> 79.9 us  [call(): pl.pallas_call(body, grid_spec=pltpu.PrefetchScalarGridSpec(num_scalar_pr...]
    unnamed x84 -> x36, local copies, waits for them, and re-layouts: 11.7 us -> 6 us
    ppermute x29, waiting for transfers between devices: 37.4 us -> 41.1 us  [swap(): return lax.ppermute(v, axis, [(i, i ^ bit) for i in range(n)])]
    ppermute x29, starting transfers between devices: 29.6 us -> 33.1 us  [swap(): return lax.ppermute(v, axis, [(i, i ^ bit) for i in range(n)])]
    dot_general x1, matrix products: 3.79 us -> 1.09 us  [dot(): return lax.dot_general(a, b, (dims, ((), ())), preferred_element_type=F32)]
  transfers between devices with their start and end apart: 38 -> 38, of which waited for: 15 -> 17; matrix products, arithmetic and copies ran while one was open for 4% -> 1% of each run, Pallas kernels for 32% -> 24%
where the time goes in v1:
time: 183 us; the launch traced here: 182 us
  Pallas kernels  79.9 us (44%)
  waiting for transfers between devices  46.5 us (25%)
  starting transfers between devices  45.3 us (25%)
  local copies, waits for them, and re-layouts  6.88 us (4%)
    pallas_call x23, Pallas kernels, call(): pl.pallas_call(body, grid_spec=pltpu.PrefetchScalarGridSpec(num_scalar_pr...  79.9 us
    ppermute x29, waiting for transfers between devices, swap(): return lax.ppermute(v, axis, [(i, i ^ bit) for i in range(n)])  41.1 us
    ppermute x29, starting transfers between devices, swap(): return lax.ppermute(v, axis, [(i, i ^ bit) for i in range(n)])  33.1 us
    ppermute x9, starting transfers between devices, shift_all(): lax.ppermute(payload, axis, [(i, (i + k) % n) for i in range(n)])  12.2 us
    unnamed x36, local copies, waits for them, and re-layouts  6 us
    ppermute x9, waiting for transfers between devices, shift_all(): lax.ppermute(payload, axis, [(i, (i + k) % n) for i in range(n)])  5.4 us
  transfers between devices with their start and end apart: 38, of which 17 were waited for; matrix products, arithmetic and copies ran while one was open for 1% of the time, Pallas kernels for 24%

profile of v1, /device:TPU:0, one launch (start us, length us, event | category | flops | bytes accessed | tf_op | source)
XLA Modules:
  0.0 182.3 jit_solution(13725819319855558024)
XLA Ops:
  2.4 5.1 %collective-permute-start.2 = (f32[4,2,384]{2,1,0:T(2,128)S(1)}, f32[4,2,384]{2,1,0:T(2,128)S(1)}, u32[]{:S(2)}, u32[]{:S(2)}) collective-permute-start(f32[4,2,384]{2,1,0:T(2,128)S(1)} %maximum_select_fusion.refs_1_.refs_5_), channel_id=1, source_target_pairs={{0,3},{1,0},{2,1},{3,2},{4,7},{5,4},{6,5},{7,6},{8,11},{9,8},{10,9... | collective-permute-start | bytes 36872 | tf_op jit(solution)/shard_map/ppermute | solution.py:507
  9.1 1.3 copy-done.6
  11.4 4.2 %project.1 = (bf16[768,768]{1,0:T(8,128)(2,1)S(1)}, bf16[768,768]{1,0:T(8,128)(2,1)S(1)}, bf16[3,256,1152]{2,1,0:T(8,128)(2,1)S(1)}) custom-call(s32[7]{0:T(128)S(1)} %stack.40.refs_0_, bf16[768,768]{1,0:T(8,128)(2,1)S(1)} %bitcast.53, f32[768]{0:T(1024)S(1)} %copy-done.13, bf16[768,768]{1,0:T(8,128)(2,1)S(1)} %copy-done.6, bf16[768,384]{1,0:T(8,128)(2,1)S(1)} %copy-done.9, ...), custom_call_target="tpu_custom_call" | custom-call | flops 4140000000 | bytes 1 | tf_op jit(solution)/shard_map/project/pallas_call | solution.py:490
  16.8 4.0 %summary.1 = (f32[2,384]{1,0:T(2,128)S(1)}, f32[3,4,8,384]{3,2,1,0:T(8,128)S(1)}, f32[3,4,384]{2,1,0:T(4,128)S(1)}) custom-call(bf16[3,256,1152]{2,1,0:T(8,128)(2,1)S(1)} %get-tuple-element.92.refs_0_.refs_9_.refs_10_, f32[4,2,384]{2,1,0:T(2,128)S(1)} %maximum_select_fusion.refs_1_.refs_5_, f32[4,2,384]{2,1,0:T(2,128)S(1)} %collective-permute-done.refs_2_.refs_6_, ...), custom_call_target="tpu_custom_call" | custom-call | flops 5520000000 | bytes 1 | tf_op jit(solution)/shard_map/summary/pallas_call | solution.py:490
  20.8 2.9 %collective-permute-start.5 = (f32[3,4,384]{2,1,0:T(4,128)S(1)}, f32[3,4,384]{2,1,0:T(4,128)S(1)}, u32[]{:S(2)}, u32[]{:S(2)}) collective-permute-start(f32[3,4,384]{2,1,0:T(4,128)S(1)} %get-tuple-element.93.refs_1_), channel_id=1, source_target_pairs={{0,3},{1,0},{2,1},{3,2},{4,7},{5,4},{6,5},{7,6},{8,11},{9,8},{10,9... | collective-permute-start | bytes 55304 | tf_op jit(solution)/shard_map/ppermute | solution.py:507
  23.7 1.1 collective-permute-start.4
  25.2 3.2 %collective-permute-done.4.refs_3_ = f32[3,4,384]{2,1,0:T(4,128)S(1)} collective-permute-done((f32[3,4,384]{2,1,0:T(4,128)S(1)}, f32[3,4,384]{2,1,0:T(4,128)S(1)}, u32[]{:S(2)}, u32[]{:S(2)}) %collective-permute-start.4) | collective-permute-done | bytes 18464 | tf_op jit(solution)/shard_map/ppermute | solution.py:507
  28.4 2.0 %collective-permute-done.3.refs_2_ = f32[3,4,384]{2,1,0:T(4,128)S(1)} collective-permute-done((f32[3,4,384]{2,1,0:T(4,128)S(1)}, f32[3,4,384]{2,1,0:T(4,128)S(1)}, u32[]{:S(2)}, u32[]{:S(2)}) %collective-permute-start.3) | collective-permute-done | bytes 18464 | tf_op jit(solution)/shard_map/ppermute | solution.py:507
  30.4 10.2 %mixer.1 = (bf16[768,768]{1,0:T(8,128)(2,1)S(1)}, bf16[768,768]{1,0:T(8,128)(2,1)S(1)}, f32[3,2,384]{2,1,0:T(2,128)S(1)}, f32[3,2,96]{2,1,0:T(2,128)}, bf16[768,...) custom-call(s32[7]{0:T(128)S(1)} %stack.40.refs_0_, f32[3,4,384]{2,1,0:T(4,128)S(1)} %get-tuple-element.93.refs_1_, ...), custom_call_target="tpu_custom_call" | custom-call | flops 12535000064 | bytes 1 | tf_op jit(solution)/shard_map/mixer/pallas_call | solution.py:490
  40.7 19.5 %ffn.1 = (bf16[384,3072]{1,0:T(8,128)(2,1)S(1)}, bf16[384,3072]{1,0:T(8,128)(2,1)S(1)}, bf16[768,768]{1,0:T(8,128)(2,1)S(1)}, bf16[768,768]{1,0:T(8,128)(2,1)S(1...) custom-call(s32[7]{0:T(128)S(1)} %stack.40.refs_0_, f32[768,768]{1,0:T(8,128)S(1)} %get-tuple-element.97.refs_1_.refs_0_, ...), custom_call_target="tpu_custom_call" | custom-call | flops 25300000768 | bytes 1 | tf_op jit(solution)/shard_map/ffn/pallas_call | solution.py:490
  60.8 10.8 %turn.1 = (f32[768,768]{1,0:T(8,128)S(1)}, bf16[768,768]{1,0:T(8,128)(2,1)S(1)}, bf16[768,768]{1,0:T(8,128)(2,1)S(1)}, bf16[768,768]{1,0:T(8,128)(2,1)S(1)}, f32...) custom-call(f32[768,768]{1,0:T(8,128)S(1)} %get-tuple-element.99.refs_0_, ...), custom_call_target="tpu_custom_call" | custom-call | flops 14145000448 | bytes 1 | tf_op jit(solution)/shard_map/turn/pallas_call | solution.py:490
  71.8 1.9 %collective-permute-start.6 = (f32[3,2,384]{2,1,0:T(2,128)S(1)}, f32[3,2,384]{2,1,0:T(2,128)S(1)}, u32[]{:S(2)}, u32[]{:S(2)}) collective-permute-start(f32[3,2,384]{2,1,0:T(2,128)S(1)} %get-tuple-element.101.refs_5_), channel_id=1, source_target_pairs={{0,1},{1,2},{2,3},{3,0},{4,5},{5,6},{6,7},{7,4},{8,9},{9,10},{10,1... | collective-permute-start | bytes 27656 | tf_op jit(solution)/shard_map/ppermute | solution.py:507
  73.7 2.4 %mixer_grads.1 = (bf16[384,1536]{1,0:T(8,128)(2,1)S(1)}, bf16[384,1536]{1,0:T(8,128)(2,1)S(1)}) custom-call(bf16[768,768]{1,0:T(8,128)(2,1)S(1)} %get-tuple-element.110.refs_0_, bf16[768,768]{1,0:T(8,128)(2,1)S(1)} %get-tuple-element.111.refs_1_, bf16[768,768]{1,0:T(8,128)(2,1)S(1)} %get-tuple-element.112.refs_2_, ...), custom_call_target="tpu_custom_call" | custom-call | flops 3910000128 | bytes 1 | tf_op jit(solution)/shard_map/mixer_grads/pallas_call | solution.py:490
  76.2 1.4 ffn_sum1.1
  77.5 1.6 collective-permute-start.13
  79.1 1.5 collective-permute-start.14
  80.6 8.3 %adjoint.1 = (bf16[768,1152]{1,0:T(8,128)(2,1)S(1)}, f32[2,384]{1,0:T(2,128)S(1)}) custom-call(s32[7]{0:T(128)S(1)} %stack.40.refs_0_, f32[3,4,384]{2,1,0:T(4,128)S(1)} %get-tuple-element.93.refs_1_, f32[3,4,384]{2,1,0:T(4,128)S(1)} %collective-permute-done.3.refs_2_, f32[3,4,384]{2,1,0:T(4,128)S(1)} %collective-permute-done.4.refs_3_, ...), custom_call_target="tpu_custom_call" | custom-call | flops 10005000192 | bytes 1 | tf_op jit(solution)/shard_map/adjoint/pallas_call | solution.py:490
  89.0 2.4 %input_grads.1 = (bf16[384,1152]{1,0:T(8,128)(2,1)S(1)}, bf16[384,1152]{1,0:T(8,128)(2,1)S(1)}) custom-call(bf16[768,768]{1,0:T(8,128)(2,1)S(1)} %get-tuple-element.110.refs_0_, bf16[768,1152]{1,0:T(8,128)(2,1)S(1)} %get-tuple-element.116.refs_1_.refs_0_), custom_call_target="tpu_custom_call" | custom-call | flops 2760000000 | bytes 1 | tf_op jit(solution)/shard_map/input_grads/pallas_call | solution.py:490
  91.4 8.2 %collective-permute-done.13.refs_2_ = bf16[2,96,2304]{2,1,0:T(8,128)(2,1)S(1)} collective-permute-done((bf16[2,96,2304]{2,1,0:T(8,128)(2,1)S(1)}, bf16[2,96,2304]{2,1,0:T(8,128)(2,1)S(1)}, u32[]{:S(2)}, u32[]{:S(2)}) %collective-permute-start.13) | collective-permute-done | bytes 884768 | tf_op jit(solution)/shard_map/ppermute | solution.py:515
  99.6 1.2 collective-permute-done.14.refs_4_
  101.8 1.6 collective-permute-start.22
  105.5 1.5 collective-permute-start.20
  107.0 4.6 %tokens.1 = (bf16[768,768]{1,0:T(8,128)(2,1)}, f32[4,768]{1,0:T(4,128)S(1)}) custom-call(bf16[768,1152]{1,0:T(8,128)(2,1)S(1)} %get-tuple-element.116.refs_1_.refs_0_, bf16[768,768]{1,0:T(8,128)(2,1)S(1)} %get-tuple-element.111.refs_1_, bf16[768,768]{1,0:T(8,128)(2,1)S(1)} %copy-done.7, bf16[768,384]{1,0:T(8,128)(2,1)S(1)} %copy-done.10, ...), custom_call_target="tpu_custom_call" | custom-call | flops 5175000064 | bytes 1 | tf_op jit(solution)/shard_map/tokens/pallas_call | solution.py:490
  111.6 1.3 copy-done.15
  112.8 3.1 %out.1.refs_5_ = bf16[768,768]{1,0:T(8,128)(2,1)} custom-call(f32[768,768]{1,0:T(8,128)S(1)} %get-tuple-element.97.refs_1_.refs_0_, bf16[768,1536]{1,0:T(8,128)(2,1)S(1)} %get-tuple-element.98.refs_1_, bf16[1536,768]{1,0:T(8,128)(2,1)S(1)} %copy-done.2, bf16[768,768]{1,0:T(8,128)(2,1)S(1)} %copy-done.15), custom_call_target="tpu_custom_call" | custom-call | flops 4024999936 | bytes 1 | tf_op jit(solution)/shard_map/out/pallas_call | solution.py:490
  116.5 1.3 copy-done.16
  118.5 1.6 collective-permute-start.26
  120.1 1.5 collective-permute-start.27
  121.6 1.2 collective-permute-done.21.refs_4_
  122.8 4.4 %collective-permute-done.20.refs_2_ = bf16[2,96,1536]{2,1,0:T(8,128)(2,1)S(1)} collective-permute-done((bf16[2,96,1536]{2,1,0:T(8,128)(2,1)S(1)}, bf16[2,96,1536]{2,1,0:T(8,128)(2,1)S(1)}, u32[]{:S(2)}, u32[]{:S(2)}) %collective-permute-start.20) | collective-permute-done | bytes 589856 | tf_op jit(solution)/shard_map/ppermute | solution.py:515
  128.5 1.2 collective-permute-done.15
  130.3 3.1 %collective-permute-done.16 = f32[4,768]{1,0:T(4,128)S(1)} collective-permute-done((f32[4,768]{1,0:T(4,128)S(1)}, f32[4,768]{1,0:T(4,128)S(1)}, u32[]{:S(2)}, u32[]{:S(2)}) %collective-permute-start.16) | collective-permute-done | bytes 12320 | tf_op jit(solution)/shard_map/ppermute | solution.py:515
  133.4 1.5 collective-permute-start.17
  135.6 1.6 collective-permute-done.17
  137.1 1.5 collective-permute-start.18
  139.3 2.9 %collective-permute-start.30 = (bf16[1,48,2304]{2,1,0:T(8,128)(2,1)S(1)}, bf16[1,48,2304]{2,1,0:T(8,128)(2,1)S(1)}, u32[]{:S(2)}, u32[]{:S(2)}) collective-permute-start(bf16[1,48,2304]{2,1,0:T(8,128)(2,1)S(1)} %get-tuple-element.146.refs_5_.refs_0_), channel_id=1, source_target_pairs={{0,2},{1,3},{2,0},{3,1},{4,6},{5,7},{6,4},{7,5},{8,10},{9,11},{10,... | collective-permute-start | bytes 663560 | tf_op jit(solution)/shard_map/ppermute | solution.py:515
  144.6 2.2 %collective-permute-start.29 = (bf16[1,48,1152]{2,1,0:T(8,128)(2,1)S(1)}, bf16[1,48,1152]{2,1,0:T(8,128)(2,1)S(1)}, u32[]{:S(2)}, u32[]{:S(2)}) collective-permute-start(bf16[1,48,1152]{2,1,0:T(8,128)(2,1)S(1)} %get-tuple-element.150), channel_id=1, source_target_pairs={{0,2},{1,3},{2,0},{3,1},{4,6},{5,7},{6,4},{7,5},{8,10},{9,11},{10,... | collective-permute-start | bytes 331784 | tf_op jit(solution)/shard_map/ppermute | solution.py:515
  146.9 3.9 %collective-permute-done.31.refs_3_ = bf16[1,48,2304]{2,1,0:T(8,128)(2,1)S(1)} collective-permute-done((bf16[1,48,2304]{2,1,0:T(8,128)(2,1)S(1)}, bf16[1,48,2304]{2,1,0:T(8,128)(2,1)S(1)}, u32[]{:S(2)}, u32[]{:S(2)}) %collective-permute-start.31) | collective-permute-done | bytes 221216 | tf_op jit(solution)/shard_map/ppermute | solution.py:515
  150.7 6.2 %collective-permute-done.30.refs_1_ = bf16[1,48,2304]{2,1,0:T(8,128)(2,1)S(1)} collective-permute-done((bf16[1,48,2304]{2,1,0:T(8,128)(2,1)S(1)}, bf16[1,48,2304]{2,1,0:T(8,128)(2,1)S(1)}, u32[]{:S(2)}, u32[]{:S(2)}) %collective-permute-start.30) | collective-permute-done | bytes 221216 | tf_op jit(solution)/shard_map/ppermute | solution.py:515
  157.1 3.2 %collective-permute-start.34 = (bf16[1,48,2304]{2,1,0:T(8,128)(2,1)S(1)}, bf16[1,48,2304]{2,1,0:T(8,128)(2,1)S(1)}, u32[]{:S(2)}, u32[]{:S(2)}) collective-permute-start(bf16[1,48,2304]{2,1,0:T(8,128)(2,1)S(1)} %get-tuple-element.152.refs_4_), channel_id=1, source_target_pairs={{0,1},{1,0},{2,3},{3,2},{4,5},{5,4},{6,7},{7,6},{8,9},{9,8},{10,11... | collective-permute-start | bytes 663560 | tf_op jit(solution)/shard_map/ppermute | solution.py:515
  160.5 2.5 %collective-permute-start.32 = (bf16[1,48,1536]{2,1,0:T(8,128)(2,1)S(1)}, bf16[1,48,1536]{2,1,0:T(8,128)(2,1)S(1)}, u32[]{:S(2)}, u32[]{:S(2)}) collective-permute-start(bf16[1,48,1536]{2,1,0:T(8,128)(2,1)S(1)} %get-tuple-element.153.refs_5_.refs_0_), channel_id=1, source_target_pairs={{0,2},{1,3},{2,0},{3,1},{4,6},{5,7},{6,4},{7,5},{8,10},{9,11},{10,... | collective-permute-start | bytes 442376 | tf_op jit(solution)/shard_map/ppermute | solution.py:515
  163.0 5.1 %collective-permute-done.35 = bf16[1,48,2304]{2,1,0:T(8,128)(2,1)S(1)} collective-permute-done((bf16[1,48,2304]{2,1,0:T(8,128)(2,1)S(1)}, bf16[1,48,2304]{2,1,0:T(8,128)(2,1)S(1)}, u32[]{:S(2)}, u32[]{:S(2)}) %collective-permute-start.35) | collective-permute-done | bytes 221216 | tf_op jit(solution)/shard_map/ppermute | solution.py:515
  168.2 1.8 ffn_out.1
  170.0 1.6 collective-permute-done.32.refs_1_
  172.8 4.8 %collective-permute-start.36 = (bf16[1,48,1536]{2,1,0:T(8,128)(2,1)S(1)}, bf16[1,48,1536]{2,1,0:T(8,128)(2,1)S(1)}, u32[]{:S(2)}, u32[]{:S(2)}) collective-permute-start(bf16[1,48,1536]{2,1,0:T(8,128)(2,1)S(1)} %get-tuple-element.157), channel_id=1, source_target_pairs={{0,1},{1,0},{2,3},{3,2},{4,5},{5,4},{6,7},{7,6},{8,9},{9,8},{10,11... | collective-permute-start | bytes 442376 | tf_op jit(solution)/shard_map/ppermute | solution.py:515
  177.7 1.2 vectors.1
  178.8 2.0 %collective-permute-done.36 = bf16[1,48,1536]{2,1,0:T(8,128)(2,1)S(1)} collective-permute-done((bf16[1,48,1536]{2,1,0:T(8,128)(2,1)S(1)}, bf16[1,48,1536]{2,1,0:T(8,128)(2,1)S(1)}, u32[]{:S(2)}, u32[]{:S(2)}) %collective-permute-start.36) | collective-permute-done | bytes 147488 | tf_op jit(solution)/shard_map/ppermute | solution.py:515
  180.8 1.5 mixer_out.1
  (102 shorter events, 18.1 us)
Async XLA Ops:
  0.6 8.4 %copy-start.13 = (f32[768]{0:T(1024)S(1)}, f32[768]{0:T(1024)}, u32[]{:S(2)}) copy-start(f32[768]{0:T(1024)} %refs_6_.3) | copy-start | bytes 9220
  0.7 8.4 %copy-start.14 = (f32[384]{0:T(512)S(1)}, f32[384]{0:T(512)}, u32[]{:S(2)}) copy-start(f32[384]{0:T(512)} %refs_5_.2) | copy-start | bytes 4612
  0.7 8.4 %copy-start.5 = (bf16[3,256,768]{2,1,0:T(8,128)(2,1)S(1)}, bf16[3,256,768]{2,1,0:T(8,128)(2,1)}, u32[]{:S(2)}) copy-start(bf16[3,256,768]{2,1,0:T(8,128)(2,1)} %param.15) | copy-start | bytes 3538948
  2.4 14.3 %collective-permute-start.2 = (f32[4,2,384]{2,1,0:T(2,128)S(1)}, f32[4,2,384]{2,1,0:T(2,128)S(1)}, u32[]{:S(2)}, u32[]{:S(2)}) collective-permute-start(f32[4,2,384]{2,1,0:T(2,128)S(1)} %maximum_select_fusion.refs_1_.refs_5_), channel_id=1, source_target_pairs={{0,3},{1,0},{2,1},{3,2},{4,7},{5,4},{6,5},{7,6},{8,11},{9,8},{10,9... | collective-permute-start | bytes 36872 | tf_op jit(solution)/shard_map/ppermute | solution.py:507
  7.5 9.3 %collective-permute-start.1 = (f32[4,2,384]{2,1,0:T(2,128)S(1)}, f32[4,2,384]{2,1,0:T(2,128)S(1)}, u32[]{:S(2)}, u32[]{:S(2)}) collective-permute-start(f32[4,2,384]{2,1,0:T(2,128)S(1)} %maximum_select_fusion.refs_1_.refs_5_), channel_id=1, source_target_pairs={{0,2},{1,3},{2,0},{3,1},{4,6},{5,7},{6,4},{7,5},{8,10},{9,11},{10,... | collective-permute-start | bytes 36872 | tf_op jit(solution)/shard_map/ppermute | solution.py:507
  7.5 9.3 %collective-permute-start = (f32[4,2,384]{2,1,0:T(2,128)S(1)}, f32[4,2,384]{2,1,0:T(2,128)S(1)}, u32[]{:S(2)}, u32[]{:S(2)}) collective-permute-start(f32[4,2,384]{2,1,0:T(2,128)S(1)} %maximum_select_fusion.refs_1_.refs_5_), channel_id=1, source_target_pairs={{0,1},{1,2},{2,3},{3,0},{4,5},{5,6},{6,7},{7,4},{8,9},{9,10},{10,1... | collective-permute-start | bytes 36872 | tf_op jit(solution)/shard_map/ppermute | solution.py:507
  16.8 13.6 %copy-start.3 = (bf16[768,768]{1,0:T(8,128)(2,1)S(1)}, bf16[768,768]{1,0:T(8,128)(2,1)}, u32[]{:S(2)}) copy-start(bf16[768,768]{1,0:T(8,128)(2,1)} %refs_4_.6) | copy-start | bytes 3538948
  16.8 13.6 %copy-start.11 = (f32[768]{0:T(1024)S(1)}, f32[768]{0:T(1024)}, u32[]{:S(2)}) copy-start(f32[768]{0:T(1024)} %refs_7_.1) | copy-start | bytes 9220
  20.8 4.3 %collective-permute-start.5 = (f32[3,4,384]{2,1,0:T(4,128)S(1)}, f32[3,4,384]{2,1,0:T(4,128)S(1)}, u32[]{:S(2)}, u32[]{:S(2)}) collective-permute-start(f32[3,4,384]{2,1,0:T(4,128)S(1)} %get-tuple-element.93.refs_1_), channel_id=1, source_target_pairs={{0,3},{1,0},{2,1},{3,2},{4,7},{5,4},{6,5},{7,6},{8,11},{9,8},{10,9... | collective-permute-start | bytes 55304 | tf_op jit(solution)/shard_map/ppermute | solution.py:507
  23.7 4.7 %collective-permute-start.4 = (f32[3,4,384]{2,1,0:T(4,128)S(1)}, f32[3,4,384]{2,1,0:T(4,128)S(1)}, u32[]{:S(2)}, u32[]{:S(2)}) collective-permute-start(f32[3,4,384]{2,1,0:T(4,128)S(1)} %get-tuple-element.93.refs_1_), channel_id=1, source_target_pairs={{0,2},{1,3},{2,0},{3,1},{4,6},{5,7},{6,4},{7,5},{8,10},{9,11},{10,... | collective-permute-start | bytes 55304 | tf_op jit(solution)/shard_map/ppermute | solution.py:507
  24.8 5.6 %collective-permute-start.3 = (f32[3,4,384]{2,1,0:T(4,128)S(1)}, f32[3,4,384]{2,1,0:T(4,128)S(1)}, u32[]{:S(2)}, u32[]{:S(2)}) collective-permute-start(f32[3,4,384]{2,1,0:T(4,128)S(1)} %get-tuple-element.93.refs_1_), channel_id=1, source_target_pairs={{0,1},{1,2},{2,3},{3,0},{4,5},{5,6},{6,7},{7,4},{8,9},{9,10},{10,1... | collective-permute-start | bytes 55304 | tf_op jit(solution)/shard_map/ppermute | solution.py:507
  30.4 10.3 %copy-start = (bf16[768,1536]{1,0:T(8,128)(2,1)S(1)}, bf16[768,1536]{1,0:T(8,128)(2,1)}, u32[]{:S(2)}) copy-start(bf16[768,1536]{1,0:T(8,128)(2,1)} %refs_4_.5) | copy-start | bytes 7077892
  30.4 10.3 %copy-start.1 = (bf16[768,1536]{1,0:T(8,128)(2,1)S(1)}, bf16[768,1536]{1,0:T(8,128)(2,1)}, u32[]{:S(2)}) copy-start(bf16[768,1536]{1,0:T(8,128)(2,1)} %refs_5_.3) | copy-start | bytes 7077892
  30.4 10.3 %copy-start.2 = (bf16[1536,768]{1,0:T(8,128)(2,1)S(1)}, bf16[1536,768]{1,0:T(8,128)(2,1)}, u32[]{:S(2)}) copy-start(bf16[1536,768]{1,0:T(8,128)(2,1)} %refs_2_.7) | copy-start | bytes 7077892
  30.4 10.3 %copy-start.4 = (bf16[3,256,768]{2,1,0:T(8,128)(2,1)S(1)}, bf16[3,256,768]{2,1,0:T(8,128)(2,1)}, u32[]{:S(2)}) copy-start(bf16[3,256,768]{2,1,0:T(8,128)(2,1)} %param.29) | copy-start | bytes 3538948
  30.4 10.3 %copy-start.12 = (f32[768]{0:T(1024)S(1)}, f32[768]{0:T(1024)}, u32[]{:S(2)}) copy-start(f32[768]{0:T(1024)} %refs_3_.4) | copy-start | bytes 9220
  60.2 15.9 %collective-permute-start.9 = (bf16[384,3072]{1,0:T(8,128)(2,1)S(1)}, bf16[384,3072]{1,0:T(8,128)(2,1)S(1)}, u32[]{:S(2)}, u32[]{:S(2)}) collective-permute-start(bf16[384,3072]{1,0:T(8,128)(2,1)S(1)} %get-tuple-element.107), channel_id=1, source_target_pairs={{0,4},{4,0},{8,12},{12,8},{16,20},{20,16},{24,28},{28,24},{1,5},{5... | collective-permute-start | bytes 7077896 | tf_op jit(solution)/shard_map/ppermute | solution.py:515
  60.3 15.8 %collective-permute-start.10 = (bf16[768,768]{1,0:T(8,128)(2,1)S(1)}, bf16[768,768]{1,0:T(8,128)(2,1)S(1)}, u32[]{:S(2)}, u32[]{:S(2)}) collective-permute-start(bf16[768,768]{1,0:T(8,128)(2,1)S(1)} %get-tuple-element.109), channel_id=1, source_target_pairs={{0,4},{4,0},{8,12},{12,8},{16,20},{20,16},{24,28},{28,24},{1,5},{5... | collective-permute-start | bytes 3538952 | tf_op jit(solution)/shard_map/ppermute | solution.py:515
  71.6 7.5 %collective-permute-start.8 = (f32[3,2,384]{2,1,0:T(2,128)S(1)}, f32[3,2,384]{2,1,0:T(2,128)S(1)}, u32[]{:S(2)}, u32[]{:S(2)}) collective-permute-start(f32[3,2,384]{2,1,0:T(2,128)S(1)} %get-tuple-element.101.refs_5_), channel_id=1, source_target_pairs={{0,3},{1,0},{2,1},{3,2},{4,7},{5,4},{6,5},{7,6},{8,11},{9,8},{10,9... | collective-permute-start | bytes 27656 | tf_op jit(solution)/shard_map/ppermute | solution.py:507
  71.7 8.9 %collective-permute-start.7 = (f32[3,2,384]{2,1,0:T(2,128)S(1)}, f32[3,2,384]{2,1,0:T(2,128)S(1)}, u32[]{:S(2)}, u32[]{:S(2)}) collective-permute-start(f32[3,2,384]{2,1,0:T(2,128)S(1)} %get-tuple-element.101.refs_5_), channel_id=1, source_target_pairs={{0,2},{1,3},{2,0},{3,1},{4,6},{5,7},{6,4},{7,5},{8,10},{9,11},{10,... | collective-permute-start | bytes 27656 | tf_op jit(solution)/shard_map/ppermute | solution.py:507
  71.8 8.9 %collective-permute-start.6 = (f32[3,2,384]{2,1,0:T(2,128)S(1)}, f32[3,2,384]{2,1,0:T(2,128)S(1)}, u32[]{:S(2)}, u32[]{:S(2)}) collective-permute-start(f32[3,2,384]{2,1,0:T(2,128)S(1)} %get-tuple-element.101.refs_5_), channel_id=1, source_target_pairs={{0,1},{1,2},{2,3},{3,0},{4,5},{5,6},{6,7},{7,4},{8,9},{9,10},{10,1... | collective-permute-start | bytes 27656 | tf_op jit(solution)/shard_map/ppermute | solution.py:507
  76.1 27.8 %collective-permute-start.11 = (bf16[384,1536]{1,0:T(8,128)(2,1)S(1)}, bf16[384,1536]{1,0:T(8,128)(2,1)S(1)}, u32[]{:S(2)}, u32[]{:S(2)}) collective-permute-start(bf16[384,1536]{1,0:T(8,128)(2,1)S(1)} %get-tuple-element.114.refs_5_), channel_id=1, source_target_pairs={{0,4},{4,0},{8,12},{12,8},{16,20},{20,16},{24,28},{28,24},{1,5},{5... | collective-permute-start | bytes 3538952 | tf_op jit(solution)/shard_map/ppermute | solution.py:515
  77.5 22.1 %collective-permute-start.13 = (bf16[2,96,2304]{2,1,0:T(8,128)(2,1)S(1)}, bf16[2,96,2304]{2,1,0:T(8,128)(2,1)S(1)}, u32[]{:S(2)}, u32[]{:S(2)}) collective-permute-start(bf16[2,96,2304]{2,1,0:T(8,128)(2,1)S(1)} %get-tuple-element.123), channel_id=1, source_target_pairs={{0,8},{4,12},{8,0},{12,4},{16,24},{20,28},{24,16},{28,20},{1,9},{5... | collective-permute-start | bytes 2654216 | tf_op jit(solution)/shard_map/ppermute | solution.py:515
  79.1 21.8 %collective-permute-start.14 = (bf16[2,96,2304]{2,1,0:T(8,128)(2,1)S(1)}, bf16[2,96,2304]{2,1,0:T(8,128)(2,1)S(1)}, u32[]{:S(2)}, u32[]{:S(2)}) collective-permute-start(bf16[2,96,2304]{2,1,0:T(8,128)(2,1)S(1)} %get-tuple-element.125), channel_id=1, source_target_pairs={{0,16},{4,20},{8,24},{12,28},{16,0},{20,4},{24,8},{28,12},{1,17},{... | collective-permute-start | bytes 2654216 | tf_op jit(solution)/shard_map/ppermute | solution.py:515
  91.3 12.6 %collective-permute-start.12 = (bf16[384,1152]{1,0:T(8,128)(2,1)S(1)}, bf16[384,1152]{1,0:T(8,128)(2,1)S(1)}, u32[]{:S(2)}, u32[]{:S(2)}) collective-permute-start(bf16[384,1152]{1,0:T(8,128)(2,1)S(1)} %get-tuple-element.122.refs_5_), channel_id=1, source_target_pairs={{0,4},{4,0},{8,12},{12,8},{16,20},{20,16},{24,28},{28,24},{1,5},{5... | collective-permute-start | bytes 2654216 | tf_op jit(solution)/shard_map/ppermute | solution.py:515
  101.8 14.2 %collective-permute-start.22 = (bf16[1,96,2304]{2,1,0:T(8,128)(2,1)S(1)}, bf16[1,96,2304]{2,1,0:T(8,128)(2,1)S(1)}, u32[]{:S(2)}, u32[]{:S(2)}) collective-permute-start(bf16[1,96,2304]{2,1,0:T(8,128)(2,1)S(1)} %get-tuple-element.135), channel_id=1, source_target_pairs={{0,16},{4,20},{8,24},{12,28},{16,0},{20,4},{24,8},{28,12},{1,17},{... | collective-permute-start | bytes 1327112 | tf_op jit(solution)/shard_map/ppermute | solution.py:515
  103.4 13.1 %collective-permute-start.23 = (bf16[1,96,2304]{2,1,0:T(8,128)(2,1)S(1)}, bf16[1,96,2304]{2,1,0:T(8,128)(2,1)S(1)}, u32[]{:S(2)}, u32[]{:S(2)}) collective-permute-start(bf16[1,96,2304]{2,1,0:T(8,128)(2,1)S(1)} %get-tuple-element.137), channel_id=1, source_target_pairs={{0,8},{4,12},{8,0},{12,4},{16,24},{20,28},{24,16},{28,20},{1,9},{5... | collective-permute-start | bytes 1327112 | tf_op jit(solution)/shard_map/ppermute | solution.py:515
  105.0 17.8 %collective-permute-start.21 = (bf16[2,96,1152]{2,1,0:T(8,128)(2,1)S(1)}, bf16[2,96,1152]{2,1,0:T(8,128)(2,1)S(1)}, u32[]{:S(2)}, u32[]{:S(2)}) collective-permute-start(bf16[2,96,1152]{2,1,0:T(8,128)(2,1)S(1)} %get-tuple-element.134), channel_id=1, source_target_pairs={{0,16},{4,20},{8,24},{12,28},{16,0},{20,4},{24,8},{28,12},{1,17},{... | collective-permute-start | bytes 1327112 | tf_op jit(solution)/shard_map/ppermute | solution.py:515
  105.5 21.7 %collective-permute-start.20 = (bf16[2,96,1536]{2,1,0:T(8,128)(2,1)S(1)}, bf16[2,96,1536]{2,1,0:T(8,128)(2,1)S(1)}, u32[]{:S(2)}, u32[]{:S(2)}) collective-permute-start(bf16[2,96,1536]{2,1,0:T(8,128)(2,1)S(1)} %get-tuple-element.132), channel_id=1, source_target_pairs={{0,8},{4,12},{8,0},{12,4},{16,24},{20,28},{24,16},{28,20},{1,9},{5... | collective-permute-start | bytes 1769480 | tf_op jit(solution)/shard_map/ppermute | solution.py:515
  118.5 20.2 %collective-permute-start.26 = (bf16[1,48,2304]{2,1,0:T(8,128)(2,1)S(1)}, bf16[1,48,2304]{2,1,0:T(8,128)(2,1)S(1)}, u32[]{:S(2)}, u32[]{:S(2)}) collective-permute-start(bf16[1,48,2304]{2,1,0:T(8,128)(2,1)S(1)} %get-tuple-element.143), channel_id=1, source_target_pairs={{0,1},{1,0},{2,3},{3,2},{4,5},{5,4},{6,7},{7,6},{8,9},{9,8},{10,11... | collective-permute-start | bytes 663560 | tf_op jit(solution)/shard_map/ppermute | solution.py:515
  120.1 18.6 %collective-permute-start.27 = (bf16[1,48,2304]{2,1,0:T(8,128)(2,1)S(1)}, bf16[1,48,2304]{2,1,0:T(8,128)(2,1)S(1)}, u32[]{:S(2)}, u32[]{:S(2)}) collective-permute-start(bf16[1,48,2304]{2,1,0:T(8,128)(2,1)S(1)} %get-tuple-element.145), channel_id=1, source_target_pairs={{0,2},{1,3},{2,0},{3,1},{4,6},{5,7},{6,4},{7,5},{8,10},{9,11},{10,... | collective-permute-start | bytes 663560 | tf_op jit(solution)/shard_map/ppermute | solution.py:515
  128.0 16.0 %collective-permute-start.24 = (bf16[1,96,1536]{2,1,0:T(8,128)(2,1)S(1)}, bf16[1,96,1536]{2,1,0:T(8,128)(2,1)S(1)}, u32[]{:S(2)}, u32[]{:S(2)}) collective-permute-start(bf16[1,96,1536]{2,1,0:T(8,128)(2,1)S(1)} %get-tuple-element.140), channel_id=1, source_target_pairs={{0,16},{4,20},{8,24},{12,28},{16,0},{20,4},{24,8},{28,12},{1,17},{... | collective-permute-start | bytes 884744 | tf_op jit(solution)/shard_map/ppermute | solution.py:515
  128.5 1.2 collective-permute-start.15
  129.7 3.7 %collective-permute-start.16 = (f32[4,768]{1,0:T(4,128)S(1)}, f32[4,768]{1,0:T(4,128)S(1)}, u32[]{:S(2)}, u32[]{:S(2)}) collective-permute-start(f32[4,768]{1,0:T(4,128)S(1)} %add.59), channel_id=1, source_target_pairs={{0,8},{4,12},{8,0},{12,4},{16,24},{20,28},{24,16},{28,20},{1,9},{5... | collective-permute-start | bytes 36872 | tf_op jit(solution)/shard_map/ppermute | solution.py:515
  133.4 3.7 %collective-permute-start.17 = (f32[4,768]{1,0:T(4,128)S(1)}, f32[4,768]{1,0:T(4,128)S(1)}, u32[]{:S(2)}, u32[]{:S(2)}) collective-permute-start(f32[4,768]{1,0:T(4,128)S(1)} %add.60), channel_id=1, source_target_pairs={{0,16},{4,20},{8,24},{12,28},{16,0},{20,4},{24,8},{28,12},{1,17},{... | collective-permute-start | bytes 36872 | tf_op jit(solution)/shard_map/ppermute | solution.py:515
  135.0 9.0 %collective-permute-start.25 = (bf16[1,96,1152]{2,1,0:T(8,128)(2,1)S(1)}, bf16[1,96,1152]{2,1,0:T(8,128)(2,1)S(1)}, u32[]{:S(2)}, u32[]{:S(2)}) collective-permute-start(bf16[1,96,1152]{2,1,0:T(8,128)(2,1)S(1)} %get-tuple-element.142), channel_id=1, source_target_pairs={{0,8},{4,12},{8,0},{12,4},{16,24},{20,28},{24,16},{28,20},{1,9},{5... | collective-permute-start | bytes 663560 | tf_op jit(solution)/shard_map/ppermute | solution.py:515
  137.1 6.0 %collective-permute-start.18 = (f32[4,768]{1,0:T(4,128)S(1)}, f32[4,768]{1,0:T(4,128)S(1)}, u32[]{:S(2)}, u32[]{:S(2)}) collective-permute-start(f32[4,768]{1,0:T(4,128)S(1)} %add.61), channel_id=1, source_target_pairs={{0,1},{1,0},{2,3},{3,2},{4,5},{5,4},{6,7},{7,6},{8,9},{9,8},{10,11... | collective-permute-start | bytes 36872 | tf_op jit(solution)/shard_map/ppermute | solution.py:515
  138.8 11.9 %collective-permute-start.31 = (bf16[1,48,2304]{2,1,0:T(8,128)(2,1)S(1)}, bf16[1,48,2304]{2,1,0:T(8,128)(2,1)S(1)}, u32[]{:S(2)}, u32[]{:S(2)}) collective-permute-start(bf16[1,48,2304]{2,1,0:T(8,128)(2,1)S(1)} %get-tuple-element.151.refs_2_), channel_id=1, source_target_pairs={{0,1},{1,0},{2,3},{3,2},{4,5},{5,4},{6,7},{7,6},{8,9},{9,8},{10,11... | collective-permute-start | bytes 663560 | tf_op jit(solution)/shard_map/ppermute | solution.py:515
  139.3 17.6 %collective-permute-start.30 = (bf16[1,48,2304]{2,1,0:T(8,128)(2,1)S(1)}, bf16[1,48,2304]{2,1,0:T(8,128)(2,1)S(1)}, u32[]{:S(2)}, u32[]{:S(2)}) collective-permute-start(bf16[1,48,2304]{2,1,0:T(8,128)(2,1)S(1)} %get-tuple-element.146.refs_5_.refs_0_), channel_id=1, source_target_pairs={{0,2},{1,3},{2,0},{3,1},{4,6},{5,7},{6,4},{7,5},{8,10},{9,11},{10,... | collective-permute-start | bytes 663560 | tf_op jit(solution)/shard_map/ppermute | solution.py:515
  143.2 17.2 %collective-permute-start.19 = (f32[4,768]{1,0:T(4,128)S(1)}, f32[4,768]{1,0:T(4,128)S(1)}, u32[]{:S(2)}, u32[]{:S(2)}) collective-permute-start(f32[4,768]{1,0:T(4,128)S(1)} %add.62), channel_id=1, source_target_pairs={{0,2},{1,3},{2,0},{3,1},{4,6},{5,7},{6,4},{7,5},{8,10},{9,11},{10,... | collective-permute-start | bytes 36872 | tf_op jit(solution)/shard_map/ppermute | solution.py:515
  144.6 15.7 %collective-permute-start.29 = (bf16[1,48,1152]{2,1,0:T(8,128)(2,1)S(1)}, bf16[1,48,1152]{2,1,0:T(8,128)(2,1)S(1)}, u32[]{:S(2)}, u32[]{:S(2)}) collective-permute-start(bf16[1,48,1152]{2,1,0:T(8,128)(2,1)S(1)} %get-tuple-element.150), channel_id=1, source_target_pairs={{0,2},{1,3},{2,0},{3,1},{4,6},{5,7},{6,4},{7,5},{8,10},{9,11},{10,... | collective-permute-start | bytes 331784 | tf_op jit(solution)/shard_map/ppermute | solution.py:515
  146.9 13.5 %collective-permute-start.28 = (bf16[1,48,1536]{2,1,0:T(8,128)(2,1)S(1)}, bf16[1,48,1536]{2,1,0:T(8,128)(2,1)S(1)}, u32[]{:S(2)}, u32[]{:S(2)}) collective-permute-start(bf16[1,48,1536]{2,1,0:T(8,128)(2,1)S(1)} %get-tuple-element.148), channel_id=1, source_target_pairs={{0,1},{1,0},{2,3},{3,2},{4,5},{5,4},{6,7},{7,6},{8,9},{9,8},{10,11... | collective-permute-start | bytes 442376 | tf_op jit(solution)/shard_map/ppermute | solution.py:515
  157.1 11.1 %collective-permute-start.35 = (bf16[1,48,2304]{2,1,0:T(8,128)(2,1)S(1)}, bf16[1,48,2304]{2,1,0:T(8,128)(2,1)S(1)}, u32[]{:S(2)}, u32[]{:S(2)}) collective-permute-start(bf16[1,48,2304]{2,1,0:T(8,128)(2,1)S(1)} %get-tuple-element.155), channel_id=1, source_target_pairs={{0,2},{1,3},{2,0},{3,1},{4,6},{5,7},{6,4},{7,5},{8,10},{9,11},{10,... | collective-permute-start | bytes 663560 | tf_op jit(solution)/shard_map/ppermute | solution.py:515
  157.1 11.0 %collective-permute-start.34 = (bf16[1,48,2304]{2,1,0:T(8,128)(2,1)S(1)}, bf16[1,48,2304]{2,1,0:T(8,128)(2,1)S(1)}, u32[]{:S(2)}, u32[]{:S(2)}) collective-permute-start(bf16[1,48,2304]{2,1,0:T(8,128)(2,1)S(1)} %get-tuple-element.152.refs_4_), channel_id=1, source_target_pairs={{0,1},{1,0},{2,3},{3,2},{4,5},{5,4},{6,7},{7,6},{8,9},{9,8},{10,11... | collective-permute-start | bytes 663560 | tf_op jit(solution)/shard_map/ppermute | solution.py:515
  160.4 9.5 %collective-permute-start.33 = (bf16[1,48,1152]{2,1,0:T(8,128)(2,1)S(1)}, bf16[1,48,1152]{2,1,0:T(8,128)(2,1)S(1)}, u32[]{:S(2)}, u32[]{:S(2)}) collective-permute-start(bf16[1,48,1152]{2,1,0:T(8,128)(2,1)S(1)} %get-tuple-element.154.refs_2_), channel_id=1, source_target_pairs={{0,1},{1,0},{2,3},{3,2},{4,5},{5,4},{6,7},{7,6},{8,9},{9,8},{10,11... | collective-permute-start | bytes 331784 | tf_op jit(solution)/shard_map/ppermute | solution.py:515
  160.5 11.1 %collective-permute-start.32 = (bf16[1,48,1536]{2,1,0:T(8,128)(2,1)S(1)}, bf16[1,48,1536]{2,1,0:T(8,128)(2,1)S(1)}, u32[]{:S(2)}, u32[]{:S(2)}) collective-permute-start(bf16[1,48,1536]{2,1,0:T(8,128)(2,1)S(1)} %get-tuple-element.153.refs_5_.refs_0_), channel_id=1, source_target_pairs={{0,2},{1,3},{2,0},{3,1},{4,6},{5,7},{6,4},{7,5},{8,10},{9,11},{10,... | collective-permute-start | bytes 442376 | tf_op jit(solution)/shard_map/ppermute | solution.py:515
  172.8 6.1 %collective-permute-start.37 = (bf16[1,48,1152]{2,1,0:T(8,128)(2,1)S(1)}, bf16[1,48,1152]{2,1,0:T(8,128)(2,1)S(1)}, u32[]{:S(2)}, u32[]{:S(2)}) collective-permute-start(bf16[1,48,1152]{2,1,0:T(8,128)(2,1)S(1)} %get-tuple-element.158), channel_id=1, source_target_pairs={{0,2},{1,3},{2,0},{3,1},{4,6},{5,7},{6,4},{7,5},{8,10},{9,11},{10,... | collective-permute-start | bytes 331784 | tf_op jit(solution)/shard_map/ppermute | solution.py:515
  172.8 7.9 %collective-permute-start.36 = (bf16[1,48,1536]{2,1,0:T(8,128)(2,1)S(1)}, bf16[1,48,1536]{2,1,0:T(8,128)(2,1)S(1)}, u32[]{:S(2)}, u32[]{:S(2)}) collective-permute-start(bf16[1,48,1536]{2,1,0:T(8,128)(2,1)S(1)} %get-tuple-element.157), channel_id=1, source_target_pairs={{0,1},{1,0},{2,3},{3,2},{4,5},{5,4},{6,7},{7,6},{8,9},{9,8},{10,11... | collective-permute-start | bytes 442376 | tf_op jit(solution)/shard_map/ppermute | solution.py:515
  (8 other events, 16.4 us)

commit v2 on v1

--- a/solution.py
+++ b/solution.py
@@ -10,10 +10,10 @@
 GROUPS = 8
 CHUNKS = 8
 LANES = 128
-RANK, PLACE, FIRST, OTHERS = 0, 1, 2, 3
+RANK, PLACE = 0, 1
 MICROSECONDS = dict(
-    project=3.6, summary=4.8, mixer=10.9, ffn=22.0, turn=12.3, mixer_grads=3.4, adjoint=8.7, input_grads=2.4, tokens=4.5, out=3.5,
-    ffn_sum1=3.6, mixer_sum1=3.4,
+    project=4, summary=4, hidden_grad=2.5, mixer=8, ffn=18, turn=7, chains=3.5, mixer_grads=1, adjoint=1, input_grads=1, tokens=4.5, out=3.5,
+    ffn_sum1=1.3, mixer_sum1=1.0, ffn_sum2=5,
 )
 COST = 1.15e9
 TILE = 16
@@ -53,6 +53,10 @@
     return split_dot(v, member, NT)
 
 
+def bit_of(here_ref, which, bit):
+    return lax.shift_right_logical(here_ref[which], bit.bit_length() - 1) & 1
+
+
 def put_halves(ref, t, col, lo, bit):
     half = ref.shape[0] // 2
     for b in range(t.shape[0] // lo):
@@ -73,27 +77,14 @@
     return [value[:, g * LANES : (g + 1) * LANES] for g in range(parts)]
 
 
-def decays(pre, trig, lam_re, lam_im):
-    ch = lam_re.shape[0] * LANES
-    forget = jax.nn.sigmoid(pre[:, 2 * ch :])
-    put(lam_re, forget * trig[0:1, :])
-    put(lam_im, forget * trig[1:2, :])
-    return forget
-
-
-def drives(pre, trig, lam_re, lam_im, drv_re, drv_im):
-    ch = lam_re.shape[0] * LANES
-    forget = decays(pre, trig, lam_re, lam_im)
-    put(drv_re, (1.0 - forget) * jax.nn.silu(pre[:, :ch]))
-    put(drv_im, (1.0 - forget) * jax.nn.silu(pre[:, ch : 2 * ch]))
-
-
-def project_kernel(here_ref, x_ref, gain_ref, w_in_ref, w_forget_ref, bias_ref, perm_ref, normed_ref, turned_ref, pre_ref, *, lo):
+def project_kernel(
+    here_ref, x_ref, gain_ref, w_in_ref, w_forget_ref, bias_ref, perm_ref, normed_ref, turned_ref, pre_ref, *, lo, first
+):
     width = x_ref.shape[1]
     x = x_ref[...].astype(F32)
     normed = (x * lax.rsqrt(row_mean(x * x) + epsilon) * gain_ref[...][None]).astype(BF)
     normed_ref[...] = normed
-    put_halves(turned_ref, normed.T, 0, lo, here_ref[FIRST])
+    put_halves(turned_ref, normed.T, 0, lo, bit_of(here_ref, PLACE, first))
     mixed = dot(normed, w_in_ref[...]).astype(BF)
     pre_ref[:, :width] = dot(mixed, perm_ref[...]).astype(BF)
     pre_ref[:, width:] = (dot(normed, w_forget_ref[...]) + bias_ref[...][None]).astype(BF)
@@ -108,7 +99,13 @@
     for info in infos[1:]:
         trig = trig + info[...]
     trig_ref[...] = trig
-    drives(pre_ref[...].astype(F32), trig, lam_re, lam_im, drv_re, drv_im)
+    ch = parts * LANES
+    pre = pre_ref[...].astype(F32)
+    forget = jax.nn.sigmoid(pre[:, 2 * ch :])
+    put(lam_re, forget * trig[0:1, :])
+    put(lam_im, forget * trig[1:2, :])
+    put(drv_re, (1.0 - forget) * jax.nn.silu(pre[:, :ch]))
+    put(drv_im, (1.0 - forget) * jax.nn.silu(pre[:, ch : 2 * ch]))
     carried = [None] * parts
     for t in range(step):
         rows = pl.ds(t, CHUNKS, stride=step)
@@ -133,17 +130,15 @@
     total_ref[...] = jnp.concatenate([tp_r, tp_i, th_r, th_i], axis=0)
 
 
-def mixer_kernel(*refs, ranks, lo):
+def mixer_kernel(*refs, ranks, lo, first):
     scalars, refs = refs[0], refs[1:]
     totals, inits, refs = refs[:ranks], refs[ranks : 2 * ranks], refs[2 * ranks :]
-    pre_ref, trig_ref, chunk_ref, perm_ref, x_ref, og_ref, gain_ref, member_ref, w_out_ref = refs[:9]
-    y_ref, split_ref, start_ref, final_ref, turned_ref, middle_ref = refs[9:15]
-    lam_re, lam_im, drv_re, drv_im = refs[15:]
+    lam_re, lam_im, drv_re, drv_im, chunk_ref, perm_ref, x_ref, og_ref, gain_ref, member_ref, w_out_ref = refs[:11]
+    y_ref, split_ref, start_ref, final_ref, turned_ref, middle_ref, st_re, st_im = refs[11:]
     parts, span, _ = lam_re.shape
     ch = parts * LANES
     step = span // CHUNKS
-    rank, bit = scalars[RANK], scalars[FIRST]
-    drives(pre_ref[...].astype(F32), trig_ref[...], lam_re, lam_im, drv_re, drv_im)
+    rank, bit = scalars[RANK], bit_of(scalars, PLACE, first)
     init = inits[0][...]
     for info in inits[1:]:
         init = init + info[...]
@@ -177,10 +172,10 @@
         for g in range(parts):
             hr, hi = cmul(lam_re[g, rows, :], lam_im[g, rows, :], *carried[g])
             hr, hi = hr + drv_re[g, rows, :], hi + drv_im[g, rows, :]
-            drv_re[g, rows, :] = hr
-            drv_im[g, rows, :] = hi
+            st_re[g, rows, :] = hr
+            st_im[g, rows, :] = hi
             carried[g] = (hr, hi)
-    split = jnp.concatenate([get(drv_re).astype(BF), get(drv_im).astype(BF)], axis=1)
+    split = jnp.concatenate([get(st_re).astype(BF), get(st_im).astype(BF)], axis=1)
     split_ref[...] = split
     yf = dot(split, perm_ref[...], NT)
     y_ref[...] = yf.astype(BF)
@@ -192,13 +187,13 @@
 
 
 def ffn_kernel(
-    here_ref, middle_ref, gain_ref, cot_ref, wg_ref, wu_ref, wd_ref,
+    here_ref, middle_ref, gain_ref, cot_ref, wg_ref, wu_ref, dh_ref,
     gsend_ref, gkeep_ref, dsend_ref, dkeep_ref, hid_ref, dn_ref,
     n_ref, nt_ref, dgv_ref, duv_ref, ht_ref,
-    *, lo, dlo, rt,
+    *, lo, dlo, rt, first,
 ):
     j = pl.program_id(0)
-    bit = here_ref[FIRST]
+    bit = bit_of(here_ref, PLACE, first)
     count, width = middle_ref.shape
     tile = wg_ref.shape[1]
     spans = [slice(r, r + rt) for r in range(0, count, rt)]
@@ -213,7 +208,7 @@
 
     for rows in spans:
         g, u = dot(n_ref[rows, :], wg_ref[...]), dot(n_ref[rows, :], wu_ref[...])
-        dh = dot(cot_ref[rows, :], wd_ref[...], NT)
+        dh = dh_ref[rows, :].astype(F32)
         sig = jax.nn.sigmoid(g)
         act = g * sig
         hid_ref[rows, :] = (act * u).astype(BF)
@@ -238,21 +233,23 @@
             dn_ref[rows, :] += dn
 
 
+def gate_kernel(normed_ref, w_ref, og_ref):
+    og_ref[...] = dot(normed_ref[...], w_ref[...]).astype(BF)
+
+
+def hidden_grad_kernel(cot_ref, wd_ref, dh_ref):
+    dh_ref[...] = dot(cot_ref[...], wd_ref[...], NT).astype(BF)
+
+
 def turn_kernel(
     dn_ref, middle_ref, cot_ref, ffn_gain_ref, w_out_ref, y_ref, og_ref, gain_ref, member_ref, perm_ref,
-    pre_ref, trig_ref, chunk_ref,
-    dmiddle_ref, dbranch_ref, dog_ref, split_ref, chain_ref, total_ref, gains_ref,
-    lam_re, lam_im, dy_re, dy_im,
+    dmiddle_ref, dbranch_ref, dog_ref, split_ref,
 ):
-    parts, span, _ = lam_re.shape
-    ch = parts * LANES
-    step = span // CHUNKS
     v, up = middle_ref[...], dn_ref[...]
     inv = lax.rsqrt(row_mean(v * v) + epsilon)
     unit = v * inv
     through = up * ffn_gain_ref[...][None]
     dmiddle = cot_ref[...].astype(F32) + inv * (through - unit * row_mean(through * unit))
-    gain_ffn = jnp.sum(up * unit, axis=0, keepdims=True)
     dmiddle_ref[...] = dmiddle
     dbranch = dmiddle.astype(BF)
     dbranch_ref[...] = dbranch
@@ -262,24 +259,17 @@
     gunit = yf * ginv
     sig = jax.nn.sigmoid(og)
     dog_ref[...] = (dgated * gunit * gain * silu_slope(og, sig)).astype(BF)
-    dgn = dgated * og * sig
-    gains = jnp.concatenate([gain_ffn, jnp.sum(dgn * gunit, axis=0, keepdims=True)], axis=0)
-
-    @pl.when(pl.program_id(0) == 0)
-    def _():
-        gains_ref[...] = gains
-
-    @pl.when(pl.program_id(0) > 0)
-    def _():
-        gains_ref[...] += gains
-
-    through = dgn * gain
+    through = dgated * og * sig * gain
     dy = (ginv * (through - gunit * group_spread(group_mean(through * gunit, member), member))).astype(BF)
-    split = dot(dy, perm_ref[...])
-    split_ref[...] = split.astype(BF)
-    decays(pre_ref[...].astype(F32), trig_ref[...], lam_re, lam_im)
-    put(dy_re, split[:, :ch])
-    put(dy_im, split[:, ch:])
+    split_ref[...] = dot(dy, perm_ref[...]).astype(BF)
+
+
+def chains_kernel(split_ref, lam_re, lam_im, chunk_ref, chain_ref, total_ref, dy_re, dy_im):
+    parts, span, _ = lam_re.shape
+    ch = parts * LANES
+    step = span // CHUNKS
+    put(dy_re, split_ref[:, :ch].astype(F32))
+    put(dy_im, split_ref[:, ch:].astype(F32))
     carried = [None] * parts
     for t in range(step - 1, -1, -1):
         rows = pl.ds(t, CHUNKS, stride=step)
@@ -300,15 +290,15 @@
 def adjoint_kernel(*refs, ranks):
     scalars, refs = refs[0], refs[1:]
     totals, adjs, refs = refs[:ranks], refs[ranks : 2 * ranks], refs[2 * ranks :]
-    pre_ref, trig_ref, dy_ref, split_ref, start_ref, chunk_ref, chain_ref, perm_ref = refs[:8]
-    dpre_ref, sums_ref, lam_re, lam_im, dy_re, dy_im = refs[8:]
+    pre_ref, trig_ref, lam_re, lam_im, dy_ref, split_ref, start_ref, chunk_ref, chain_ref, perm_ref = refs[:10]
+    dpre_ref, sums_ref, dy_re, dy_im = refs[10:]
     parts, span, _ = lam_re.shape
     ch = parts * LANES
     step = span // CHUNKS
     rank = scalars[RANK]
     pre = pre_ref[...].astype(F32)
     trig = trig_ref[...]
-    forget = decays(pre, trig, lam_re, lam_im)
+    forget = jax.nn.sigmoid(pre[:, 2 * ch :])
     put(dy_re, dy_ref[:, :ch].astype(F32))
     put(dy_im, dy_ref[:, ch:].astype(F32))
     cr = jnp.zeros((1, ch), F32)
@@ -387,10 +377,22 @@
     out_ref[...] = (middle_ref[...] + dot(hid_ref[...], w_down_ref[...])).astype(BF)
 
 
-def tokens_kernel(
-    dpre_ref, dog_ref, w_in_ref, w_forget_ref, w_ogate_ref, x_ref, gain_ref, dmiddle_ref, others_ref, sums_ref,
-    out_ref, vectors_ref,
-):
+def input_grads_kernel(lhs_ref, dpre_ref, sums_ref, send_ref, keep_ref, *, per):
+    half, n = lhs_ref.shape[0] // 2, dpre_ref.shape[1]
+    send_ref[:, :n] = dot(lhs_ref[:half, :], dpre_ref[...]).astype(BF)
+    keep_ref[:, :n] = dot(lhs_ref[half:, :], dpre_ref[...]).astype(BF)
+    parts = n // 3 // LANES
+    flat = [sums_ref[k : k + 1, g * LANES : (g + 1) * LANES] for k in range(2) for g in range(parts)]
+    flat.append(jnp.zeros((-2 * parts % 8, LANES), F32))
+    flat = jnp.concatenate(flat, axis=0).astype(BF)
+    shape = (half, flat.shape[0])
+    row, k = lax.broadcasted_iota(jnp.int32, shape, 0), lax.broadcasted_iota(jnp.int32, shape, 1)
+    beside = dot((row % per == k).astype(F32).astype(BF), flat).astype(BF)
+    send_ref[:, n:] = beside
+    keep_ref[:, n:] = beside
+
+
+def tokens_kernel(dpre_ref, dog_ref, w_in_ref, w_forget_ref, w_ogate_ref, x_ref, gain_ref, dmiddle_ref, out_ref):
     width = x_ref.shape[1]
     up = (
         dot(dpre_ref[:, :width], w_in_ref[...], NT)
@@ -402,27 +404,6 @@
     unit = x * inv
     through = up * gain_ref[...][None]
     out_ref[...] = (dmiddle_ref[...] + inv * (through - unit * row_mean(through * unit))).astype(BF)
-    gains = jnp.sum(up * unit, axis=0, keepdims=True)
-
-    @pl.when(pl.program_id(0) == 0)
-    def _():
-        vectors_ref[0:1, :] = gains
-        vectors_ref[1:3, :] = others_ref[...]
-        vectors_ref[3:4, :] = jnp.concatenate([sums_ref[0:1, :], sums_ref[1:2, :]], axis=1)
-
-    @pl.when(pl.program_id(0) > 0)
-    def _():
-        vectors_ref[0:1, :] += gains
-
-
-def vectors_kernel(here_ref, vectors_ref, mix_ref, ffn_ref, group_ref, bias_ref, phase_ref):
-    width, ch = vectors_ref.shape[1], vectors_ref.shape[1] // 2
-    rows = jnp.concatenate([vectors_ref[...]] * 2, axis=0)
-    per, own = mix_ref.shape[1], bias_ref.shape[1]
-    gains = pltpu.roll(rows, (width - per * here_ref[PLACE]) % width, 1)
-    mix_ref[...], ffn_ref[...], group_ref[...] = gains[0:1, :per], gains[1:2, :per], gains[2:3, :per]
-    bias_ref[...] = pltpu.roll(rows[:, :ch], (ch - own * here_ref[RANK]) % ch, 1)[3:4, :own]
-    phase_ref[...] = pltpu.roll(rows[:, ch:], (ch - own * here_ref[RANK]) % ch, 1)[3:4, :own]
 
 
 def rows(*shape):
@@ -445,8 +426,20 @@
     return ("moved", shape, dim)
 
 
+def ours(*shape):
+    return ("own", shape)
+
+
+def full(*shape):
+    return ("full", shape)
+
+
 def spec_of(kind):
-    if kind[0] != "moved":
+    if kind[0] == "full":
+        return pl.BlockSpec(kind[1], lambda s, *_: (0,) * len(kind[1]))
+    if kind[0] == "own":
+        return pl.BlockSpec(kind[1], lambda s, here: (here[PLACE], 0))
+    if kind[0] not in ("moved",):
         return pl.BlockSpec(memory_space=pltpu.VMEM)
     _, shape, dim = kind
     return pl.BlockSpec(shape, lambda s, *_: tuple(s if d == dim else 0 for d in range(len(shape))))
@@ -469,8 +462,8 @@
     return functools.reduce(lambda p, q: p * q, shape) * jnp.dtype(dtype).itemsize
 
 
-def call(kernel, steps, ins, outs, scratch, scalars, name, after=(), room=6):
-    cost = int(COST * MICROSECONDS.get(name, 2.0))
+def call(kernel, steps, ins, outs, scratch, scalars, name, after=(), room=5):
+    cost = int(COST * MICROSECONDS.get(name, 0.8))
     lead, extra = len(scalars), len(after)
     kinds_in, kinds_out = [k for k, _ in ins], [k for k, _, _ in outs]
 
@@ -484,8 +477,8 @@
         )
 
     limit = room << 20
-    limit += sum(2 * size_of(k[1], a.dtype) for k, a in ins if k[0] == "moved")
-    limit += sum(2 * size_of(k[1], d) for k, _, d in outs if k[0] == "moved")
+    limit += sum(2 * size_of(k[1], a.dtype) for k, a in ins if k[0] in ("moved", "own"))
+    limit += sum(2 * size_of(k[1], d) for k, _, d in outs if k[0] in ("moved", "full"))
     limit += sum(size_of(m.shape, m.dtype) for m in scratch)
     return pl.pallas_call(
         body,
@@ -523,7 +516,7 @@
     ins, outs = refs[:n_in], refs[n_in:]
     for n, (pos, bit, count, sources) in enumerate(plan):
         for flip in (1, 0):
-            own = 1 - here_ref[bit] if flip else here_ref[bit]
+            own = 1 - bit_of(here_ref, *bit) if flip else bit_of(here_ref, *bit)
             for i in range(count):
                 low = i % (1 << pos)
                 q = (i - low) * 2 + own * (1 << pos) + low
@@ -572,23 +565,50 @@
     return call(add_kernel, 1, ins, outs, [], [], name, after)
 
 
-def finish_kernel(here_ref, *refs, moves, lanes_n, bits):
-    halves, outs = refs[: 2 * lanes_n], refs[2 * lanes_n :]
-    for lane, col, width, out, row, at in moves:
-        own, other = halves[2 * lane], halves[2 * lane + 1]
-        half = own.shape[0]
+def own_part(row, at, n):
+    width = row.shape[1]
+    return pltpu.roll(jnp.concatenate([row] * 8, axis=0), (width - at) % width, 1)[0:1, :n]
+
+
+def finish_kernel(here_ref, *refs, moves, bits, gains, n_out, vectors, ranks):
+    lanes_n = len(bits)
+    halves, refs = refs[: 2 * lanes_n], refs[2 * lanes_n :]
+    ins, outs = refs[: len(refs) - n_out], refs[len(refs) - n_out :]
+    half = halves[0].shape[0]
+
+    def at(lane, h, cut):
+        pick = bit_of(here_ref, *bits[lane]) == h
+        return jnp.where(pick, halves[2 * lane][:, cut].astype(F32), halves[2 * lane + 1][:, cut].astype(F32))
+
+    for lane, col, width, out, row, to in moves:
         for h in range(2):
-            pick = here_ref[bits[lane]] == h
-            value = jnp.where(pick, own[:, col : col + width].astype(F32), other[:, col : col + width].astype(F32))
-            outs[out][row + h * half : row + (h + 1) * half, at : at + width] = value
-
-
-def finish(here, halves, bits, moves, shapes, name, after=()):
-    ins = [(whole(*a.shape), a) for pair in halves for a in pair]
-    outs = [(whole(*s), s, F32) for s in shapes]
+            outs[out][row + h * half : row + (h + 1) * half, to : to + width] = at(lane, h, slice(col, col + width))
+    for out, norm, terms in gains:
+        acc = 0.0
+        for weight, grad in terms:
+            product = ins[weight][...].astype(F32) * outs[grad][...]
+            ones = jnp.ones((8, product.shape[1]), BF)
+            high = product.astype(BF)
+            acc = acc + dot(ones, high, NT) + dot(ones, (product - high.astype(F32)).astype(BF), NT)
+        per = acc.shape[1]
+        outs[out][...] = (acc[0:1] / own_part(ins[norm][...][None], per * here_ref[PLACE], per))[0]
+    if vectors:
+        lane, col, first_out = vectors
+        block = at(lane, 0, slice(col, col + LANES))
+        n = outs[first_out].shape[0]
+        parts = n * ranks // LANES
+        for k in range(2):
+            row = jnp.concatenate([block[k * parts + g : k * parts + g + 1] for g in range(parts)], axis=1)
+            outs[first_out + k][...] = own_part(row, n * here_ref[RANK], n)[0]
+
+
+def finish(here, halves, bits, moves, extra, outs, gains, vectors, ranks, name, after=()):
+    ins = [(whole(*a.shape), a) for pair in halves for a in pair] + extra
     return call(
-        functools.partial(finish_kernel, moves=moves, lanes_n=len(halves), bits=bits), 1, ins, outs, [], [here], name,
-        after,
+        functools.partial(
+            finish_kernel, moves=moves, bits=bits, gains=gains, n_out=len(outs), vectors=vectors, ranks=ranks
+        ),
+        1, ins, [(k(*shape), shape, F32) for k, shape in outs], [], [here], name, after,
     )
 
 
@@ -633,10 +653,10 @@
     first = next(b for b in bits if (per * b) % TILE == 0)
     rest = [b for b in bits if b != first]
     lo = per * first
-    here = [rank, lax.axis_index("dp"), own_bit("dp", first)]
-    here += [own_bit("dp", b) for b in rest] + [own_bit("seq", b) for b in bits_of(nseq)]
-    here = jnp.stack([h.astype(jnp.int32) for h in here])
-    scan_scratch = [pltpu.VMEM((ch // LANES, span, LANES), F32)] * 4
+    here = jnp.stack([rank, lax.axis_index("dp").astype(jnp.int32)])
+    scan = seg(ch // LANES, span, LANES)
+    scanned = (scan, (segs, ch // LANES, span, LANES), F32)
+    scan_scratch = [pltpu.VMEM((ch // LANES, span, LANES), F32)] * 2
 
     own = jnp.concatenate(
         [jnp.stack([jnp.cos(phase), jnp.sin(phase)])[None], init_state.transpose(0, 2, 1)], axis=0
@@ -651,7 +671,7 @@
     x = tokens.reshape(count, width)
     cot = cotangent.reshape(count, width)
     normed, normed_t, pre = call(
-        functools.partial(project_kernel, lo=lo), segs,
+        functools.partial(project_kernel, lo=lo, first=first), segs,
         [
             (rows(span, width), x), (whole(width), norm_mix), (whole(width, width), w_in),
             (whole(width, ch), w_forget), (whole(ch), forget_bias), (whole(width, width), perm),
@@ -663,25 +683,33 @@
         ],
         [], [here], "project",
     )
-    trig, chunk, totals = call(
+    trig, chunk, totals, lam_re, lam_im, drv_re, drv_im = call(
         functools.partial(summary_kernel, ranks=nseq), segs,
         [(seg(span, 3 * ch), pre)] + [(seg(2, ch, fixed=True), i) for i in infos],
         [
             (whole(2, ch), (2, ch), F32),
             (seg(4, CHUNKS, ch), (segs, 4, CHUNKS, ch), F32),
             (seg(4, ch), (segs, 4, ch), F32),
-        ],
-        scan_scratch, [], "summary",
+            scanned, scanned, scanned, scanned,
+        ],
+        [], [], "summary",
     )
     totals = shift_all(totals, "seq", nseq)
-    og = dot(normed, w_ogate).astype(BF)
+    (og,) = call(
+        gate_kernel, 1, [(whole(count, width), normed), (whole(width, width), w_ogate)],
+        [(whole(count, width), (count, width), BF)], [], [], "gate", (lam_re,),
+    )
+    (dh,) = call(
+        hidden_grad_kernel, tall, [(whole(count, width), cot), (rows(width, width), w_down)],
+        [(cols(count, width), (count, hidden), BF)], [], [], "hidden_grad", (lam_re,),
+    )
     y, y_split, start, final, gated_t, middle = call(
-        functools.partial(mixer_kernel, ranks=nseq, lo=lo), segs,
+        functools.partial(mixer_kernel, ranks=nseq, lo=lo, first=first), segs,
         [(seg(4, ch), t) for t in totals]
         + [(seg(2, ch, shift=1), i) for i in infos]
         + [
-            (seg(span, 3 * ch), pre), (whole(2, ch), trig), (seg(4, CHUNKS, ch), chunk), (whole(width, width), perm),
-            (rows(span, width), x), (rows(span, width), og), (whole(width), norm_group),
+            (scan, lam_re), (scan, lam_im), (scan, drv_re), (scan, drv_im), (seg(4, CHUNKS, ch), chunk),
+            (whole(width, width), perm), (rows(span, width), x), (rows(span, width), og), (whole(width), norm_group),
             (whole(width, LANES), member), (whole(width, width), w_out),
         ],
         [
@@ -698,10 +726,10 @@
 
     tile = width
     gsend, gkeep, dsend, dkeep, hid, dn = call(
-        functools.partial(ffn_kernel, lo=lo, dlo=lo * tall, rt=span), hidden // tile,
+        functools.partial(ffn_kernel, lo=lo, dlo=lo * tall, rt=span, first=first), hidden // tile,
         [
             (whole(count, width), middle), (whole(width), norm_ffn), (whole(count, width), cot),
-            (cols(width, tile), w_gate), (cols(width, tile), w_up), (rows(tile, width), w_down),
+            (cols(width, tile), w_gate), (cols(width, tile), w_up), (cols(count, tile), dh),
         ],
         [
             (cols(width // 2, 2 * tile), (width // 2, 2 * hidden), BF),
@@ -716,50 +744,30 @@
             pltpu.VMEM((count, tile), BF), pltpu.VMEM((count, tile), BF),
             pltpu.VMEM((tile, count), BF),
         ],
-        [here], "ffn",
+        [here], "ffn", (), 7,
     )
 
     ggot, dgot = swap(gsend, "dp", ndp, first), swap(dsend, "dp", ndp, first)
 
-    dmiddle, dbranch, dog, dy_split, chain, adj, gains = call(
+    dmiddle, dbranch, dog, dy_split = call(
         turn_kernel, segs,
         [
             (rows(span, width), dn), (rows(span, width), middle), (rows(span, width), cot), (whole(width), norm_ffn),
             (whole(width, width), w_out), (rows(span, width), y), (rows(span, width), og), (whole(width), norm_group),
-            (whole(width, LANES), member), (whole(width, width), perm), (seg(span, 3 * ch), pre), (whole(2, ch), trig),
-            (seg(4, CHUNKS, ch), chunk),
+            (whole(width, LANES), member), (whole(width, width), perm),
         ],
         [
             (rows(span, width), (count, width), F32),
             (rows(span, width), (count, width), BF),
             (rows(span, width), (count, width), BF),
             (rows(span, width), (count, width), BF),
-            (seg(2, CHUNKS, ch), (segs, 2, CHUNKS, ch), F32),
-            (seg(2, ch), (segs, 2, ch), F32),
-            (whole(2, width), (2, width), F32),
-        ],
-        scan_scratch, [], "turn",
-    )
-    adjs = shift_all(adj, "seq", nseq)
-
-    ntile = width // 3
-    osend, okeep = call(
-        functools.partial(grads_kernel, pairs=2), width // ntile,
-        [
-            (whole(width, count), normed_t), (cols(count, ntile), dog),
-            (whole(width, count), gated_t), (cols(count, ntile), dbranch),
-        ],
-        [
-            (cols(width // 2, 2 * ntile), (width // 2, 2 * width), BF),
-            (cols(width // 2, 2 * ntile), (width // 2, 2 * width), BF),
-        ],
-        [], [], "mixer_grads",
-    )
-    ogot = swap(osend, "dp", ndp, first)
+        ],
+        [], [], "turn",
+    )
     nblk = ndp // 2
     fast = ndp == 8 and nseq == 4 and per % (2 * TILE) == 0
-    x_bit, y_bit = OTHERS, OTHERS + 1
-    z_bits = [OTHERS + len(rest) + i for i in range(len(bits_of(nseq)))]
+    x_bit, y_bit = (PLACE, rest[0]), (PLACE, rest[1])
+    z_bits = [(RANK, b) for b in bits_of(nseq)]
 
     def blocks(a, cols_n, tall_n=1):
         return a.reshape(nblk * tall_n, per, cols_n)
@@ -770,29 +778,50 @@
         d = [blocks(a, width, tall) for a in (dkeep, dgot)]
         fa = [(g, 1, 0, 0, 3 * width)]
         fb = [(g, 1, 0, 3, width)] + [(d, tall, i, 0, width) for i in range(tall)]
-        (fa_send, fa_keep), (fb_send, fb_keep) = combine(here, [(0, x_bit, fa), (1, y_bit, fb)], "ffn_sum1", (osend,))
+        (fa_send, fa_keep), (fb_send, fb_keep) = combine(here, [(0, x_bit, fa), (1, y_bit, fb)], "ffn_sum1", (dog,))
         fa_got, fb_got = swap(fa_send, "dp", ndp, rest[0]), swap(fb_send, "dp", ndp, rest[1])
         order = (fa_keep,)
 
+    chain, adj = call(
+        chains_kernel, segs,
+        [(rows(span, width), dy_split), (scan, lam_re), (scan, lam_im), (seg(4, CHUNKS, ch), chunk)],
+        [(seg(2, CHUNKS, ch), (segs, 2, CHUNKS, ch), F32), (seg(2, ch), (segs, 2, ch), F32)],
+        scan_scratch, [], "chains", order,
+    )
+    adjs = shift_all(adj, "seq", nseq)
+
+    ntile = width // 3
+    osend, okeep = call(
+        functools.partial(grads_kernel, pairs=2), width // ntile,
+        [
+            (whole(width, count), normed_t), (cols(count, ntile), dog),
+            (whole(width, count), gated_t), (cols(count, ntile), dbranch),
+        ],
+        [
+            (cols(width // 2, 2 * ntile), (width // 2, 2 * width), BF),
+            (cols(width // 2, 2 * ntile), (width // 2, 2 * width), BF),
+        ],
+        [], [], "mixer_grads", (chain,),
+    )
+    late, *adjs = lax.optimization_barrier((osend, *adjs))
+    ogot = swap(late, "dp", ndp, first)
     dpre, sums = call(
         functools.partial(adjoint_kernel, ranks=nseq), segs,
         [(seg(4, ch), t) for t in totals] + [(seg(2, ch), a) for a in adjs]
         + [
-            (seg(span, 3 * ch), pre), (whole(2, ch), trig), (rows(span, width), dy_split),
+            (seg(span, 3 * ch), pre), (whole(2, ch), trig), (scan, lam_re), (scan, lam_im),
+            (rows(span, width), dy_split),
             (rows(span, width), y_split), (seg(2, ch), start),
             (seg(4, CHUNKS, ch), chunk), (seg(2, CHUNKS, ch), chain), (whole(width, width), perm),
         ],
         [(rows(span, 3 * ch), (count, 3 * ch), BF), (whole(2, ch), (2, ch), F32)],
-        scan_scratch, [here], "adjoint", order,
-    )
+        scan_scratch, [here], "adjoint", (osend,),
+    )
+    into = 3 * ch + LANES
     isend, ikeep = call(
-        functools.partial(grads_kernel, pairs=1), 3,
-        [(whole(width, count), normed_t), (cols(count, ch), dpre)],
-        [
-            (cols(width // 2, ch), (width // 2, 3 * ch), BF),
-            (cols(width // 2, ch), (width // 2, 3 * ch), BF),
-        ],
-        [], [], "input_grads",
+        functools.partial(input_grads_kernel, per=per), 1,
+        [(whole(width, count), normed_t), (whole(count, 3 * ch), dpre), (whole(2, ch), sums)],
+        [(whole(width // 2, into), (width // 2, into), BF)] * 2, [], [], "input_grads",
     )
     igot = swap(isend, "dp", ndp, first)
     order = ()
@@ -807,57 +836,50 @@
             here, [(0, y_bit, one(fa_keep, fa_got)), (0, x_bit, one(fb_keep, fb_got))], "ffn_sum2", (isend,)
         )
         fa_got, fb_got = swap(fa_send, "dp", ndp, rest[1]), swap(fb_send, "dp", ndp, rest[0])
+        order = (fa_keep,)
+
+    (grad_tokens,) = call(
+        tokens_kernel, segs,
+        [
+            (rows(span, 3 * ch), dpre), (rows(span, width), dog), (whole(width, width), w_in),
+            (whole(width, ch), w_forget), (whole(width, width), w_ogate), (rows(span, width), x),
+            (whole(width), norm_mix), (rows(span, width), dmiddle),
+        ],
+        [(moved(span, width, dim=0), (count, width), BF)],
+        [], [], "tokens", order,
+    )
+
+    def output(*after):
+        return call(
+            out_kernel, segs, [(rows(span, width), middle), (rows(span, hidden), hid), (whole(hidden, width), w_down)],
+            [(moved(span, width, dim=0), (count, width), BF)], [], [], "out", after,
+        )[0]
+
+    if fast:
+        lead, other = bits_of(nseq)
+
         o = [blocks(a, 2 * width) for a in (okeep, ogot)]
-        i = [blocks(a, 3 * ch) for a in (ikeep, igot)]
+        i = [blocks(a, into) for a in (ikeep, igot)]
         (ra_send, ra_keep), (rb_send, rb_keep) = combine(
-            here, [(0, x_bit, [(o, 1, 0, 0, 2 * width)]), (1, y_bit, [(i, 1, 0, 0, 3 * ch)])], "mixer_sum1", (fa_keep,)
+            here, [(0, x_bit, [(o, 1, 0, 0, 2 * width)]), (1, y_bit, [(i, 1, 0, 0, into)])], "mixer_sum1", (grad_tokens,)
         )
         ra_got, rb_got = swap(ra_send, "dp", ndp, rest[0]), swap(rb_send, "dp", ndp, rest[1])
-        order = (ra_keep,)
-
-    grad_tokens, vectors = call(
-        tokens_kernel, segs,
-        [
-            (rows(span, 3 * ch), dpre), (rows(span, width), dog), (whole(width, width), w_in),
-            (whole(width, ch), w_forget), (whole(width, width), w_ogate), (rows(span, width), x),
-            (whole(width), norm_mix), (rows(span, width), dmiddle), (whole(2, width), gains), (whole(2, ch), sums),
-        ],
-        [(moved(span, width, dim=0), (count, width), BF), (whole(4, width), (4, width), F32)],
-        [], [], "tokens", order,
-    )
-
-    (mixed_out,) = call(
-        out_kernel, segs, [(rows(span, width), middle), (rows(span, hidden), hid), (whole(hidden, width), w_down)],
-        [(moved(span, width, dim=0), (count, width), BF)], [], [], "out", (grad_tokens,),
-    )
-
-    for axis, n in (("dp", ndp), ("seq", nseq)):
-        for b in bits_of(n):
-            vectors = vectors + swap(vectors, axis, n, b)
-    part_mix, part_ffn, part_group, part_bias, part_phase = call(
-        vectors_kernel, 1, [(whole(4, width), vectors)],
-        [(whole(1, per), (1, per), F32)] * 3 + [(whole(1, mine), (1, mine), F32)] * 2, [], [here], "vectors",
-    )
-
-    shapes_f = [(per, hidden), (per, hidden), (tall * per, width)]
-    shapes_r = [(per, width), (per, width), (per, width), (per, ch)]
-    if fast:
-        lead, other = bits_of(nseq)
 
         def over(send, axis_n, bit):
             return swap(send, "seq", axis_n, bit)
 
         (fa_send, fa_keep), (fb_send, fb_keep) = combine(
             here, [(0, z_bits[0], rows_of(fa_keep, fa_got)), (0, z_bits[1], rows_of(fb_keep, fb_got))],
-            "ffn_sum3", (mixed_out,),
+            "ffn_sum3", (ra_keep,),
         )
         fa_got, fb_got = over(fa_send, nseq, lead), over(fb_send, nseq, other)
+        mixed_out = output(fa_keep)
+        fa, fb = add_pairs([(fa_keep, fa_got), (fb_keep, fb_got)], "ffn_sum4", (mixed_out,))
+        fa_got, fb_got = over(fa, nseq, other), over(fb, nseq, lead)
         (ra_send, ra_keep), (rb_send, rb_keep) = combine(
-            here, [(0, y_bit, one(ra_keep, ra_got)), (0, x_bit, one(rb_keep, rb_got))], "mixer_sum2", (fa_keep,)
+            here, [(0, y_bit, one(ra_keep, ra_got)), (0, x_bit, one(rb_keep, rb_got))], "mixer_sum2", (fa,)
         )
         ra_got, rb_got = swap(ra_send, "dp", ndp, rest[1]), swap(rb_send, "dp", ndp, rest[0])
-        fa, fb = add_pairs([(fa_keep, fa_got), (fb_keep, fb_got)], "ffn_sum4", (ra_keep,))
-        fa_got, fb_got = over(fa, nseq, other), over(fb, nseq, lead)
         (ra_send, ra_keep), (rb_send, rb_keep) = combine(
             here, [(0, z_bits[0], rows_of(ra_keep, ra_got)), (0, z_bits[1], rows_of(rb_keep, rb_got))], "mixer_sum3", (fa,)
         )
@@ -874,17 +896,28 @@
         moves = [
             (lane, col, width, n % 2, 0, (n // 2) * width) for n, (lane, col) in enumerate(guv)
         ] + [(1, (1 + t) * width, width, 2, t * per, 0) for t in range(tall)]
-        part_gate, part_up, part_down = finish(
-            here, flat((fa, fa_got), (fb, fb_got)), z_bits, moves, shapes_f, "ffn_out", (ra,)
+        part_gate, part_up, part_down, part_ffn = finish(
+            here, flat((fa, fa_got), (fb, fb_got)), z_bits, moves,
+            [(ours(per, hidden), w_gate), (ours(per, hidden), w_up), (whole(width), norm_ffn)],
+            [(full, (per, hidden)), (full, (per, hidden)), (full, (tall * per, width)), (full, (per,))],
+            [(3, 2, [(0, 0), (1, 1)])], None, nseq, "ffn_out", (ra,),
         )
         ra, rb = add_pairs([(ra, ra_got), (rb, rb_got)], "mixer_sum5", (part_gate,))
         ra_got, rb_got = over(ra, nseq, lead), over(rb, nseq, other)
         moves = [(0, n * ntile, ntile, n % 2, 0, (n // 2) * ntile) for n in range(2 * width // ntile)]
         moves += [(1, 0, width, 2, 0, 0), (1, width, ch, 3, 0, 0)]
-        part_ogate, part_out, part_in, part_forget = finish(
-            here, flat((ra, ra_got), (rb, rb_got)), z_bits, moves, shapes_r, "mixer_out"
+        part_ogate, part_out, part_in, part_forget, part_mix, part_group, part_bias, part_phase = finish(
+            here, flat((ra, ra_got), (rb, rb_got)), z_bits, moves,
+            [
+                (ours(per, width), w_ogate), (ours(per, width), w_out), (ours(per, width), w_in), (ours(per, ch), w_forget),
+                (whole(width), norm_mix), (whole(width), norm_group),
+            ],
+            [(full, (per, n)) for n in (width, width, width, ch)] + [(full, (n,)) for n in (per, per, mine, mine)],
+            [(4, 4, [(0, 0), (2, 2), (3, 3)]), (5, 5, [(1, 1)])], (1, 3 * ch, 6), nseq, "mixer_out",
         )
     else:
+        mixed_out = output()
+
         def plain(keep, got, cols_n, tall_n=1):
             shape = [2] * len(rest) + [tall_n * per, cols_n]
             return plain_reduce([keep.reshape(shape), got.reshape(shape)], rest, ndp, nseq)
@@ -896,13 +929,25 @@
         mix = plain(okeep, ogot, 2 * width)
         mix = [mix[:, n * ntile : (n + 1) * ntile] for n in range(2 * width // ntile)]
         part_ogate, part_out = jnp.concatenate(mix[0::2], axis=1), jnp.concatenate(mix[1::2], axis=1)
-        into = plain(ikeep, igot, 3 * ch)
-        part_in, part_forget = into[:, :width], into[:, width:]
+        both = plain(ikeep, igot, into)
+        part_in, part_forget = both[:, :width], both[:, width : 3 * ch]
+        shared = both[: 2 * ch // LANES, 3 * ch :].reshape(2, ch)
+        part_bias, part_phase = lax.dynamic_slice_in_dim(shared, rank * mine, mine, axis=1)
+
+        def own_rows(a):
+            return lax.dynamic_slice_in_dim(a, lax.axis_index("dp") * per, per, axis=0).astype(F32)
+
+        def gain_of(norm, *pairs):
+            return sum(jnp.sum(own_rows(w) * gw, axis=1) for w, gw in pairs) / own_rows(norm)
+
+        part_ffn = gain_of(norm_ffn, (w_gate, part_gate), (w_up, part_up))
+        part_mix = gain_of(norm_mix, (w_in, part_in), (w_forget, part_forget), (w_ogate, part_ogate))
+        part_group = gain_of(norm_group, (w_out, part_out))
     return (
         mixed_out.reshape(segs, span, width),
         grad_tokens.reshape(segs, span, width),
         final_state,
-        part_mix[0], part_in, part_forget, part_bias[0], part_phase[0], part_ogate, part_group[0], part_out, part_ffn[0],
+        part_mix, part_in, part_forget, part_bias, part_phase, part_ogate, part_group, part_out, part_ffn,
         part_gate, part_up, part_down,
     )
 

time: 183 us -> 162 us (0.89)
  waiting for transfers between devices: 46.5 us -> 34.2 us
  starting transfers between devices: 45.3 us -> 39.3 us
    ppermute x29 -> x24, waiting for transfers between devices: 41.1 us -> 29.6 us  [swap(): return lax.ppermute(v, axis, [(i, i ^ bit) for i in range(n)])]
    ppermute x29 -> x24, starting transfers between devices: 33.1 us -> 26.4 us  [swap(): return lax.ppermute(v, axis, [(i, i ^ bit) for i in range(n)])]
    pallas_call x23 -> x25, Pallas kernels: 79.9 us -> 79.1 us  [call(): pl.pallas_call(body, grid_spec=pltpu.PrefetchScalarGridSpec(num_scalar_pr...]
  transfers between devices with their start and end apart: 38 -> 33, of which waited for: 17 -> 14; matrix products, arithmetic and copies ran while one was open for 1% -> 0% of each run, Pallas kernels for 24% -> 27%
where the time goes in v2:
time: 162 us
  Pallas kernels  79.1 us (49%)
  starting transfers between devices  39.3 us (24%)
  waiting for transfers between devices  34.2 us (21%)
  local copies, waits for them, and re-layouts  6.79 us (4%)
  other arithmetic  1.62 us (1%)
    pallas_call x25, Pallas kernels, call(): pl.pallas_call(body, grid_spec=pltpu.PrefetchScalarGridSpec(num_scalar_pr...  79.1 us
    ppermute x24, waiting for transfers between devices, swap(): return lax.ppermute(v, axis, [(i, i ^ bit) for i in range(n)])  29.6 us
    ppermute x24, starting transfers between devices, swap(): return lax.ppermute(v, axis, [(i, i ^ bit) for i in range(n)])  26.4 us
    ppermute x9, starting transfers between devices, shift_all(): lax.ppermute(payload, axis, [(i, (i + k) % n) for i in range(n)])  12.9 us
    unnamed x36, local copies, waits for them, and re-layouts  6 us
    ppermute x9, waiting for transfers between devices, shift_all(): lax.ppermute(payload, axis, [(i, (i + k) % n) for i in range(n)])  4.56 us
  transfers between devices with their start and end apart: 33, of which 14 were waited for; matrix products, arithmetic and copies ran while one was open for 0% of the time, Pallas kernels for 27%

profile of v2, /device:TPU:0, one launch (start us, length us, event | category | flops | bytes accessed | tf_op | source)
XLA Modules:
  0.0 162.1 jit_solution(6823551847828129208)
XLA Ops:
  2.4 5.1 %collective-permute-start.2 = (f32[4,2,384]{2,1,0:T(2,128)S(1)}, f32[4,2,384]{2,1,0:T(2,128)S(1)}, u32[]{:S(2)}, u32[]{:S(2)}) collective-permute-start(f32[4,2,384]{2,1,0:T(2,128)S(1)} %maximum_select_fusion.refs_1_.refs_5_), channel_id=1, source_target_pairs={{0,3},{1,0},{2,1},{3,2},{4,7},{5,4},{6,5},{7,6},{8,11},{9,8},{10,9... | collective-permute-start | bytes 36872 | tf_op jit(solution)/shard_map/ppermute | solution.py:500
  7.5 1.0 collective-permute-start
  9.1 1.1 copy-done.6
  10.1 1.3 copy-done.13
  11.4 4.2 %project.1 = (bf16[768,768]{1,0:T(8,128)(2,1)S(1)}, bf16[768,768]{1,0:T(8,128)(2,1)S(1)}, bf16[3,256,1152]{2,1,0:T(8,128)(2,1)S(1)}) custom-call(s32[2]{0:T(128)S(1)} %pad_add_fusion.refs_0_, bf16[768,768]{1,0:T(8,128)(2,1)S(1)} %bitcast.58, f32[768]{0:T(1024)S(1)} %copy-done.9, bf16[768,768]{1,0:T(8,128)(2,1)S(1)} %copy-done.3, ...), custom_call_target="tpu_custom_call" | custom-call | flops 4600000000 | bytes 1 | tf_op jit(solution)/shard_map/project/pallas_call | solution.py:483
  15.8 4.0 %summary.1 = (f32[2,384]{1,0:T(2,128)S(1)}, f32[3,4,8,384]{3,2,1,0:T(8,128)S(1)}, f32[3,4,384]{2,1,0:T(4,128)S(1)}, f32[3,3,256,128]{3,2,1,0:T(8,128)S(1)}, f32[...) custom-call(bf16[3,256,1152]{2,1,0:T(8,128)(2,1)S(1)} %get-tuple-element.98.refs_0_.refs_9, ...), custom_call_target="tpu_custom_call" | custom-call | flops 4600000000 | bytes 1 | tf_op jit(solution)/shard_map/summary/pallas_call | solution.py:483
  19.8 2.9 %collective-permute-start.5 = (f32[3,4,384]{2,1,0:T(4,128)S(1)}, f32[3,4,384]{2,1,0:T(4,128)S(1)}, u32[]{:S(2)}, u32[]{:S(2)}) collective-permute-start(f32[3,4,384]{2,1,0:T(4,128)S(1)} %get-tuple-element.99.refs_1_), channel_id=1, source_target_pairs={{0,3},{1,0},{2,1},{3,2},{4,7},{5,4},{6,5},{7,6},{8,11},{9,8},{10,9... | collective-permute-start | bytes 55304 | tf_op jit(solution)/shard_map/ppermute | solution.py:500
  22.7 1.1 collective-permute-start.4
  23.8 2.3 %hidden_grad.1.refs_6_ = bf16[768,1536]{1,0:T(8,128)(2,1)S(1)} custom-call(bf16[768,768]{1,0:T(8,128)(2,1)S(1)} %bitcast.55, bf16[1536,768]{1,0:T(8,128)(2,1)S(1)} %copy-done.11, f32[3,3,256,128]{3,2,1,0:T(8,128)S(1)} %get-tuple-element.100.refs_2_.refs_9_.refs_1_.refs_11_), custom_call_target="tpu_custom_call" | custom-call | flops 2875000064 | bytes 1 | tf_op jit(solution)/shard_map/hidden_grad/pallas_call | solution.py:483
  26.2 1.1 gate.1.refs_16_.refs_6_
  27.3 2.0 %collective-permute-done.3.refs_2_ = f32[3,4,384]{2,1,0:T(4,128)S(1)} collective-permute-done((f32[3,4,384]{2,1,0:T(4,128)S(1)}, f32[3,4,384]{2,1,0:T(4,128)S(1)}, u32[]{:S(2)}, u32[]{:S(2)}) %collective-permute-start.3) | collective-permute-done | bytes 18464 | tf_op jit(solution)/shard_map/ppermute | solution.py:500
  29.4 9.6 %mixer.1 = (bf16[768,768]{1,0:T(8,128)(2,1)S(1)}, bf16[768,768]{1,0:T(8,128)(2,1)S(1)}, f32[3,2,384]{2,1,0:T(2,128)S(1)}, f32[3,2,96]{2,1,0:T(2,128)}, bf16[768,...) custom-call(s32[2]{0:T(128)S(1)} %pad_add_fusion.refs_0_, f32[3,4,384]{2,1,0:T(4,128)S(1)} %get-tuple-element.99.refs_1_, ...), custom_call_target="tpu_custom_call" | custom-call | flops 9200000000 | bytes 1 | tf_op jit(solution)/shard_map/mixer/pallas_call | solution.py:483
  39.0 17.3 %ffn.1 = (bf16[384,3072]{1,0:T(8,128)(2,1)S(1)}, bf16[384,3072]{1,0:T(8,128)(2,1)S(1)}, bf16[768,768]{1,0:T(8,128)(2,1)S(1)}, bf16[768,768]{1,0:T(8,128)(2,1)S(1...) custom-call(s32[2]{0:T(128)S(1)} %pad_add_fusion.refs_0_, f32[768,768]{1,0:T(8,128)S(1)} %get-tuple-element.106.refs_1_.refs_0_, ...), custom_call_target="tpu_custom_call" | custom-call | flops 20700000256 | bytes 1 | tf_op jit(solution)/shard_map/ffn/pallas_call | solution.py:483
  57.0 8.0 %turn.1 = (f32[768,768]{1,0:T(8,128)S(1)}, bf16[768,768]{1,0:T(8,128)(2,1)S(1)}, bf16[768,768]{1,0:T(8,128)(2,1)S(1)}, bf16[768,768]{1,0:T(8,128)(2,1)S(1)}) custom-call(f32[768,768]{1,0:T(8,128)S(1)} %get-tuple-element.112.refs_0_, f32[768,768]{1,0:T(8,128)S(1)} %get-tuple-element.106.refs_1_.refs_0_, bf16[768,768]{1,0:T(8,128)(2,1)S(1)} %bitcast.57, ...), custom_call_target="tpu_custom_call" | custom-call | flops 8049999872 | bytes 1 | tf_op jit(solution)/shard_map/turn/pallas_call | solution.py:483
  65.0 1.3 ffn_sum1.1
  66.4 1.6 collective-permute-start.8
  67.9 1.5 collective-permute-start.9
  69.5 3.0 %chains.1 = (f32[3,2,8,384]{3,2,1,0:T(8,128)S(1)}, f32[3,2,384]{2,1,0:T(2,128)S(1)}) custom-call(bf16[768,768]{1,0:T(8,128)(2,1)S(1)} %get-tuple-element.122.refs_0_.refs_13_, f32[3,3,256,128]{3,2,1,0:T(8,128)S(1)} %get-tuple-element.100.refs_2_.refs_9_.refs_1_.refs_11_, f32[3,3,256,128]{3,2,1,0:T(8,128)S(1)} %get-tuple-element.101.refs_10_.refs_2_.refs_12_, ...), custom_call_target="tpu_custom_call" | custom-call | flops 4024999936 | bytes 1 | tf_op jit(solution)/shard_map/chains/pallas_call | solution.py:483
  72.5 2.2 %collective-permute-start.12 = (f32[3,2,384]{2,1,0:T(2,128)S(1)}, f32[3,2,384]{2,1,0:T(2,128)S(1)}, u32[]{:S(2)}, u32[]{:S(2)}) collective-permute-start(f32[3,2,384]{2,1,0:T(2,128)S(1)} %get-tuple-element.126.refs_5_), channel_id=1, source_target_pairs={{0,3},{1,0},{2,1},{3,2},{4,7},{5,4},{6,5},{7,6},{8,11},{9,8},{10,9... | collective-permute-start | bytes 27656 | tf_op jit(solution)/shard_map/ppermute | solution.py:500
  75.3 2.4 %mixer_grads.1 = (bf16[384,1536]{1,0:T(8,128)(2,1)S(1)}, bf16[384,1536]{1,0:T(8,128)(2,1)S(1)}) custom-call(bf16[768,768]{1,0:T(8,128)(2,1)S(1)} %get-tuple-element.119.refs_0_, bf16[768,768]{1,0:T(8,128)(2,1)S(1)} %get-tuple-element.114.refs_5_.refs_1_, bf16[768,768]{1,0:T(8,128)(2,1)S(1)} %get-tuple-element.120.refs_2_, ...), custom_call_target="tpu_custom_call" | custom-call | flops 1150000000 | bytes 1 | tf_op jit(solution)/shard_map/mixer_grads/pallas_call | solution.py:483
  77.7 1.5 collective-permute-done.11.refs_7_
  80.1 8.2 %adjoint.1 = (bf16[768,1152]{1,0:T(8,128)(2,1)S(1)}, f32[2,384]{1,0:T(2,128)S(1)}) custom-call(s32[2]{0:T(128)S(1)} %pad_add_fusion.refs_0_, f32[3,4,384]{2,1,0:T(4,128)S(1)} %get-tuple-element.99.refs_1_, f32[3,4,384]{2,1,0:T(4,128)S(1)} %collective-permute-done.3.refs_2_, f32[3,4,384]{2,1,0:T(4,128)S(1)} %collective-permute-done.4.refs_3_, ...), custom_call_target="tpu_custom_call" | custom-call | flops 1150000000 | bytes 1 | tf_op jit(solution)/shard_map/adjoint/pallas_call | solution.py:483
  88.3 1.7 %input_grads.1 = (bf16[384,1280]{1,0:T(8,128)(2,1)S(1)}, bf16[384,1280]{1,0:T(8,128)(2,1)S(1)}) custom-call(bf16[768,768]{1,0:T(8,128)(2,1)S(1)} %get-tuple-element.119.refs_0_, bf16[768,1152]{1,0:T(8,128)(2,1)S(1)} %get-tuple-element.133.refs_1_.refs_0_, f32[2,384]{1,0:T(2,128)S(1)} %get-tuple-element.134.refs_2_), custom_call_target="tpu_custom_call" | custom-call | flops 1150000000 | bytes 1 | tf_op jit(solution)/shard_map/input_grads/pallas_call | solution.py:483
  92.7 4.5 %tokens.1.refs_5_ = bf16[768,768]{1,0:T(8,128)(2,1)} custom-call(bf16[768,1152]{1,0:T(8,128)(2,1)S(1)} %get-tuple-element.133.refs_1_.refs_0_, bf16[768,768]{1,0:T(8,128)(2,1)S(1)} %get-tuple-element.114.refs_5_.refs_1_, bf16[768,768]{1,0:T(8,128)(2,1)S(1)} %copy-done.3, bf16[768,384]{1,0:T(8,128)(2,1)S(1)} %copy-done.7, bf16[768,768]{1,0:T(8,128)(2,1)S(1)} %copy-done, ...), custom_call_target="tpu_custom_call" | custom-call | flops 5175000064 | bytes 1 | tf_op jit(solution)/shard_map/tokens/pallas_call | solution.py:483
  97.3 1.3 copy-done.5
  98.5 1.0 mixer_sum1.1
  99.6 1.6 collective-permute-start.17
  101.1 1.5 collective-permute-start.18
  102.6 1.9 %collective-permute-done.13 = bf16[1,96,2304]{2,1,0:T(8,128)(2,1)S(1)} collective-permute-done((bf16[1,96,2304]{2,1,0:T(8,128)(2,1)S(1)}, bf16[1,96,2304]{2,1,0:T(8,128)(2,1)S(1)}, u32[]{:S(2)}, u32[]{:S(2)}) %collective-permute-start.13) | collective-permute-done | bytes 442400 | tf_op jit(solution)/shard_map/ppermute | solution.py:508
  106.5 1.9 %collective-permute-start.20 = (bf16[1,48,2304]{2,1,0:T(8,128)(2,1)S(1)}, bf16[1,48,2304]{2,1,0:T(8,128)(2,1)S(1)}, u32[]{:S(2)}, u32[]{:S(2)}) collective-permute-start(bf16[1,48,2304]{2,1,0:T(8,128)(2,1)S(1)} %get-tuple-element.152), channel_id=1, source_target_pairs={{0,2},{1,3},{2,0},{3,1},{4,6},{5,7},{6,4},{7,5},{8,10},{9,11},{10,... | collective-permute-start | bytes 663560 | tf_op jit(solution)/shard_map/ppermute | solution.py:508
  108.5 3.1 %out.1.refs_4_ = bf16[768,768]{1,0:T(8,128)(2,1)} custom-call(f32[768,768]{1,0:T(8,128)S(1)} %get-tuple-element.106.refs_1_.refs_0_, bf16[768,1536]{1,0:T(8,128)(2,1)S(1)} %get-tuple-element.107.refs_1_, bf16[1536,768]{1,0:T(8,128)(2,1)S(1)} %copy-done.11, bf16[1,48,2304]{2,1,0:T(8,128)(2,1)S(1)} %get-tuple-element.145.refs_3_.refs_0_), custom_call_target="tpu_custom_call" | custom-call | flops 4024999936 | bytes 1 | tf_op jit(solution)/shard_map/out/pallas_call | solution.py:483
  111.6 3.8 %collective-permute-done.19.refs_1_ = bf16[1,48,2304]{2,1,0:T(8,128)(2,1)S(1)} collective-permute-done((bf16[1,48,2304]{2,1,0:T(8,128)(2,1)S(1)}, bf16[1,48,2304]{2,1,0:T(8,128)(2,1)S(1)}, u32[]{:S(2)}, u32[]{:S(2)}) %collective-permute-start.19) | collective-permute-done | bytes 221216 | tf_op jit(solution)/shard_map/ppermute | solution.py:508
  115.4 1.6 collective-permute-done.20.refs_3_
  117.0 1.3 copy-done.17
  119.2 1.5 collective-permute-start.21
  121.4 2.5 %collective-permute-start.25 = (bf16[1,48,2304]{2,1,0:T(8,128)(2,1)S(1)}, bf16[1,48,2304]{2,1,0:T(8,128)(2,1)S(1)}, u32[]{:S(2)}, u32[]{:S(2)}) collective-permute-start(bf16[1,48,2304]{2,1,0:T(8,128)(2,1)S(1)} %get-tuple-element.153.refs_5_.refs_0_), channel_id=1, source_target_pairs={{0,2},{1,3},{2,0},{3,1},{4,6},{5,7},{6,4},{7,5},{8,10},{9,11},{10,... | collective-permute-start | bytes 663560 | tf_op jit(solution)/shard_map/ppermute | solution.py:508
  123.9 3.1 %collective-permute-done.22 = bf16[1,96,1280]{2,1,0:T(8,128)(2,1)S(1)} collective-permute-done((bf16[1,96,1280]{2,1,0:T(8,128)(2,1)S(1)}, bf16[1,96,1280]{2,1,0:T(8,128)(2,1)S(1)}, u32[]{:S(2)}, u32[]{:S(2)}) %collective-permute-start.22) | collective-permute-done | bytes 245792 | tf_op jit(solution)/shard_map/ppermute | solution.py:508
  128.0 2.2 %collective-permute-start.23 = (bf16[1,48,1536]{2,1,0:T(8,128)(2,1)S(1)}, bf16[1,48,1536]{2,1,0:T(8,128)(2,1)S(1)}, u32[]{:S(2)}, u32[]{:S(2)}) collective-permute-start(bf16[1,48,1536]{2,1,0:T(8,128)(2,1)S(1)} %get-tuple-element.159), channel_id=1, source_target_pairs={{0,1},{1,0},{2,3},{3,2},{4,5},{5,4},{6,7},{7,6},{8,9},{9,8},{10,11... | collective-permute-start | bytes 442376 | tf_op jit(solution)/shard_map/ppermute | solution.py:508
  130.3 1.3 collective-permute-done.26.refs_3_
  131.6 6.4 %collective-permute-done.25.refs_1_ = bf16[1,48,2304]{2,1,0:T(8,128)(2,1)S(1)} collective-permute-done((bf16[1,48,2304]{2,1,0:T(8,128)(2,1)S(1)}, bf16[1,48,2304]{2,1,0:T(8,128)(2,1)S(1)}, u32[]{:S(2)}, u32[]{:S(2)}) %collective-permute-start.25) | collective-permute-done | bytes 221216 | tf_op jit(solution)/shard_map/ppermute | solution.py:508
  138.2 2.9 %collective-permute-start.29 = (bf16[1,48,2304]{2,1,0:T(8,128)(2,1)S(1)}, bf16[1,48,2304]{2,1,0:T(8,128)(2,1)S(1)}, u32[]{:S(2)}, u32[]{:S(2)}) collective-permute-start(bf16[1,48,2304]{2,1,0:T(8,128)(2,1)S(1)} %get-tuple-element.163.refs_4_), channel_id=1, source_target_pairs={{0,1},{1,0},{2,3},{3,2},{4,5},{5,4},{6,7},{7,6},{8,9},{9,8},{10,11... | collective-permute-start | bytes 663560 | tf_op jit(solution)/shard_map/ppermute | solution.py:508
  141.3 2.4 %collective-permute-start.28 = (bf16[1,48,1280]{2,1,0:T(8,128)(2,1)S(1)}, bf16[1,48,1280]{2,1,0:T(8,128)(2,1)S(1)}, u32[]{:S(2)}, u32[]{:S(2)}) collective-permute-start(bf16[1,48,1280]{2,1,0:T(8,128)(2,1)S(1)} %get-tuple-element.165.refs_2_), channel_id=1, source_target_pairs={{0,1},{1,0},{2,3},{3,2},{4,5},{5,4},{6,7},{7,6},{8,9},{9,8},{10,11... | collective-permute-start | bytes 368648 | tf_op jit(solution)/shard_map/ppermute | solution.py:508
  143.7 7.0 %collective-permute-done.30 = bf16[1,48,2304]{2,1,0:T(8,128)(2,1)S(1)} collective-permute-done((bf16[1,48,2304]{2,1,0:T(8,128)(2,1)S(1)}, bf16[1,48,2304]{2,1,0:T(8,128)(2,1)S(1)}, u32[]{:S(2)}, u32[]{:S(2)}) %collective-permute-start.30) | collective-permute-done | bytes 221216 | tf_op jit(solution)/shard_map/ppermute | solution.py:508
  150.7 2.0 %ffn_out.1 = (f32[96,1536]{1,0:T(8,128)}, f32[96,1536]{1,0:T(8,128)}, f32[192,768]{1,0:T(8,128)}, f32[96]{0:T(128)}) custom-call(s32[2]{0:T(128)S(1)} %pad_add_fusion.refs_0_, bf16[48,2304]{1,0:T(8,128)(2,1)S(1)} %bitcast.47, bf16[48,2304]{1,0:T(8,128)(2,1)S(1)} %bitcast.50, bf16[48,2304]{1,0:T(8,128)(2,1)S(1)} %bitcast.48, bf16[48,2304]{1,0:T(8,128)(2,1)S(1)} %bitcast.49, ...), custom_call_target="tpu_custom_call" | custom-call | flops 920000000 | bytes 1 | tf_op jit(solution)/shard_map/ffn_out/pallas_call | solution.py:483
  152.7 1.1 copy-done.15
  153.9 2.7 %collective-permute-start.32 = (bf16[1,48,1280]{2,1,0:T(8,128)(2,1)S(1)}, bf16[1,48,1280]{2,1,0:T(8,128)(2,1)S(1)}, u32[]{:S(2)}, u32[]{:S(2)}) collective-permute-start(bf16[1,48,1280]{2,1,0:T(8,128)(2,1)S(1)} %get-tuple-element.169), channel_id=1, source_target_pairs={{0,2},{1,3},{2,0},{3,1},{4,6},{5,7},{6,4},{7,5},{8,10},{9,11},{10,... | collective-permute-start | bytes 368648 | tf_op jit(solution)/shard_map/ppermute | solution.py:508
  156.6 3.3 %collective-permute-done.32 = bf16[1,48,1280]{2,1,0:T(8,128)(2,1)S(1)} collective-permute-done((bf16[1,48,1280]{2,1,0:T(8,128)(2,1)S(1)}, bf16[1,48,1280]{2,1,0:T(8,128)(2,1)S(1)}, u32[]{:S(2)}, u32[]{:S(2)}) %collective-permute-start.32) | collective-permute-done | bytes 122912 | tf_op jit(solution)/shard_map/ppermute | solution.py:508
  160.4 1.8 %mixer_out.1 = (f32[96,768]{1,0:T(8,128)}, f32[96,768]{1,0:T(8,128)}, f32[96,768]{1,0:T(8,128)}, f32[96,384]{1,0:T(8,128)}, f32[96]{0:T(128)}, /*index=5*/f32[96]{0:T(128)}, f32[96]{0:T(128)}, f32[96]{0:T(128)}) custom-call(s32[2]{0:T(128)S(1)} %pad_add_fusion.refs_0_, bf16[48,1536]{1,0:T(8,128)(2,1)S(1)} %bitcast.51, bf16[48,1536]{1,0:T(8,128)(2,1)S(1)} %bitcast.52, ...), custom_call_target="tpu_custom_call" | custom-call | flops 920000000 | bytes 1 | tf_op jit(solution)/shard_map/mixer_out/pallas_call | solution.py:483
  (88 shorter events, 13.0 us)
Async XLA Ops:
  0.6 8.4 %copy-start.3 = (bf16[768,768]{1,0:T(8,128)(2,1)S(1)}, bf16[768,768]{1,0:T(8,128)(2,1)}, u32[]{:S(2)}) copy-start(bf16[768,768]{1,0:T(8,128)(2,1)} %refs_7_.5) | copy-start | bytes 3538948
  0.7 8.4 %copy-start.9 = (f32[768]{0:T(1024)S(1)}, f32[768]{0:T(1024)}, u32[]{:S(2)}) copy-start(f32[768]{0:T(1024)} %refs_9_.1) | copy-start | bytes 9220
  0.7 8.4 %copy-start.16 = (f32[384]{0:T(512)S(1)}, f32[384]{0:T(512)}, u32[]{:S(2)}) copy-start(f32[384]{0:T(512)} %refs_5_.4) | copy-start | bytes 4612
  2.4 13.3 %collective-permute-start.2 = (f32[4,2,384]{2,1,0:T(2,128)S(1)}, f32[4,2,384]{2,1,0:T(2,128)S(1)}, u32[]{:S(2)}, u32[]{:S(2)}) collective-permute-start(f32[4,2,384]{2,1,0:T(2,128)S(1)} %maximum_select_fusion.refs_1_.refs_5_), channel_id=1, source_target_pairs={{0,3},{1,0},{2,1},{3,2},{4,7},{5,4},{6,5},{7,6},{8,11},{9,8},{10,9... | collective-permute-start | bytes 36872 | tf_op jit(solution)/shard_map/ppermute | solution.py:500
  7.5 8.2 %collective-permute-start.1 = (f32[4,2,384]{2,1,0:T(2,128)S(1)}, f32[4,2,384]{2,1,0:T(2,128)S(1)}, u32[]{:S(2)}, u32[]{:S(2)}) collective-permute-start(f32[4,2,384]{2,1,0:T(2,128)S(1)} %maximum_select_fusion.refs_1_.refs_5_), channel_id=1, source_target_pairs={{0,2},{1,3},{2,0},{3,1},{4,6},{5,7},{6,4},{7,5},{8,10},{9,11},{10,... | collective-permute-start | bytes 36872 | tf_op jit(solution)/shard_map/ppermute | solution.py:500
  7.5 8.2 %collective-permute-start = (f32[4,2,384]{2,1,0:T(2,128)S(1)}, f32[4,2,384]{2,1,0:T(2,128)S(1)}, u32[]{:S(2)}, u32[]{:S(2)}) collective-permute-start(f32[4,2,384]{2,1,0:T(2,128)S(1)} %maximum_select_fusion.refs_1_.refs_5_), channel_id=1, source_target_pairs={{0,1},{1,2},{2,3},{3,0},{4,5},{5,6},{6,7},{7,4},{8,9},{9,10},{10,1... | collective-permute-start | bytes 36872 | tf_op jit(solution)/shard_map/ppermute | solution.py:500
  15.8 8.0 %copy-start.11 = (bf16[1536,768]{1,0:T(8,128)(2,1)S(1)}, bf16[1536,768]{1,0:T(8,128)(2,1)}, u32[]{:S(2)}) copy-start(bf16[1536,768]{1,0:T(8,128)(2,1)} %refs_2_.7) | copy-start | bytes 7077892
  15.8 8.0 %copy-start.12 = (bf16[3,256,768]{2,1,0:T(8,128)(2,1)S(1)}, bf16[3,256,768]{2,1,0:T(8,128)(2,1)}, u32[]{:S(2)}) copy-start(bf16[3,256,768]{2,1,0:T(8,128)(2,1)} %param.29) | copy-start | bytes 3538948
  19.8 7.4 %collective-permute-start.5 = (f32[3,4,384]{2,1,0:T(4,128)S(1)}, f32[3,4,384]{2,1,0:T(4,128)S(1)}, u32[]{:S(2)}, u32[]{:S(2)}) collective-permute-start(f32[3,4,384]{2,1,0:T(4,128)S(1)} %get-tuple-element.99.refs_1_), channel_id=1, source_target_pairs={{0,3},{1,0},{2,1},{3,2},{4,7},{5,4},{6,5},{7,6},{8,11},{9,8},{10,9... | collective-permute-start | bytes 55304 | tf_op jit(solution)/shard_map/ppermute | solution.py:500
  22.7 4.7 %collective-permute-start.4 = (f32[3,4,384]{2,1,0:T(4,128)S(1)}, f32[3,4,384]{2,1,0:T(4,128)S(1)}, u32[]{:S(2)}, u32[]{:S(2)}) collective-permute-start(f32[3,4,384]{2,1,0:T(4,128)S(1)} %get-tuple-element.99.refs_1_), channel_id=1, source_target_pairs={{0,2},{1,3},{2,0},{3,1},{4,6},{5,7},{6,4},{7,5},{8,10},{9,11},{10,... | collective-permute-start | bytes 55304 | tf_op jit(solution)/shard_map/ppermute | solution.py:500
  23.8 5.6 %collective-permute-start.3 = (f32[3,4,384]{2,1,0:T(4,128)S(1)}, f32[3,4,384]{2,1,0:T(4,128)S(1)}, u32[]{:S(2)}, u32[]{:S(2)}) collective-permute-start(f32[3,4,384]{2,1,0:T(4,128)S(1)} %get-tuple-element.99.refs_1_), channel_id=1, source_target_pairs={{0,1},{1,2},{2,3},{3,0},{4,5},{5,6},{6,7},{7,4},{8,9},{9,10},{10,1... | collective-permute-start | bytes 55304 | tf_op jit(solution)/shard_map/ppermute | solution.py:500
  23.8 2.3 %copy-start = (bf16[768,768]{1,0:T(8,128)(2,1)S(1)}, bf16[768,768]{1,0:T(8,128)(2,1)}, u32[]{:S(2)}) copy-start(bf16[768,768]{1,0:T(8,128)(2,1)} %refs_5_.7) | copy-start | bytes 3538948
  26.1 3.2 %copy-start.4 = (bf16[768,768]{1,0:T(8,128)(2,1)S(1)}, bf16[768,768]{1,0:T(8,128)(2,1)}, u32[]{:S(2)}) copy-start(bf16[768,768]{1,0:T(8,128)(2,1)} %refs_6_.5) | copy-start | bytes 3538948
  26.1 3.2 %copy-start.10 = (f32[768]{0:T(1024)S(1)}, f32[768]{0:T(1024)}, u32[]{:S(2)}) copy-start(f32[768]{0:T(1024)} %refs_10_.1) | copy-start | bytes 9220
  26.1 3.2 %copy-start.14 = (bf16[3,256,768]{2,1,0:T(8,128)(2,1)S(1)}, bf16[3,256,768]{2,1,0:T(8,128)(2,1)}, u32[]{:S(2)}) copy-start(bf16[3,256,768]{2,1,0:T(8,128)(2,1)} %param.15) | copy-start | bytes 3538948
  29.4 9.6 %copy-start.1 = (bf16[768,1536]{1,0:T(8,128)(2,1)S(1)}, bf16[768,1536]{1,0:T(8,128)(2,1)}, u32[]{:S(2)}) copy-start(bf16[768,1536]{1,0:T(8,128)(2,1)} %refs_5_.6) | copy-start | bytes 7077892
  29.4 9.6 %copy-start.2 = (bf16[768,1536]{1,0:T(8,128)(2,1)S(1)}, bf16[768,1536]{1,0:T(8,128)(2,1)}, u32[]{:S(2)}) copy-start(bf16[768,1536]{1,0:T(8,128)(2,1)} %refs_6_.4) | copy-start | bytes 7077892
  29.4 9.6 %copy-start.8 = (f32[768]{0:T(1024)S(1)}, f32[768]{0:T(1024)}, u32[]{:S(2)}) copy-start(f32[768]{0:T(1024)} %refs_7_.4) | copy-start | bytes 9220
  56.4 8.6 %collective-permute-start.6 = (bf16[384,3072]{1,0:T(8,128)(2,1)S(1)}, bf16[384,3072]{1,0:T(8,128)(2,1)S(1)}, u32[]{:S(2)}, u32[]{:S(2)}) collective-permute-start(bf16[384,3072]{1,0:T(8,128)(2,1)S(1)} %get-tuple-element.109), channel_id=1, source_target_pairs={{0,4},{4,0},{8,12},{12,8},{16,20},{20,16},{24,28},{28,24},{1,5},{5... | collective-permute-start | bytes 7077896 | tf_op jit(solution)/shard_map/ppermute | solution.py:508
  56.5 8.5 %collective-permute-start.7 = (bf16[768,768]{1,0:T(8,128)(2,1)S(1)}, bf16[768,768]{1,0:T(8,128)(2,1)S(1)}, u32[]{:S(2)}, u32[]{:S(2)}) collective-permute-start(bf16[768,768]{1,0:T(8,128)(2,1)S(1)} %get-tuple-element.111), channel_id=1, source_target_pairs={{0,4},{4,0},{8,12},{12,8},{16,20},{20,16},{24,28},{28,24},{1,5},{5... | collective-permute-start | bytes 3538952 | tf_op jit(solution)/shard_map/ppermute | solution.py:508
  66.4 24.2 %collective-permute-start.8 = (bf16[2,96,2304]{2,1,0:T(8,128)(2,1)S(1)}, bf16[2,96,2304]{2,1,0:T(8,128)(2,1)S(1)}, u32[]{:S(2)}, u32[]{:S(2)}) collective-permute-start(bf16[2,96,2304]{2,1,0:T(8,128)(2,1)S(1)} %get-tuple-element.116), channel_id=1, source_target_pairs={{0,8},{4,12},{8,0},{12,4},{16,24},{20,28},{24,16},{28,20},{1,9},{5... | collective-permute-start | bytes 2654216 | tf_op jit(solution)/shard_map/ppermute | solution.py:508
  67.9 22.7 %collective-permute-start.9 = (bf16[2,96,2304]{2,1,0:T(8,128)(2,1)S(1)}, bf16[2,96,2304]{2,1,0:T(8,128)(2,1)S(1)}, u32[]{:S(2)}, u32[]{:S(2)}) collective-permute-start(bf16[2,96,2304]{2,1,0:T(8,128)(2,1)S(1)} %get-tuple-element.118), channel_id=1, source_target_pairs={{0,16},{4,20},{8,24},{12,28},{16,0},{20,4},{24,8},{28,12},{1,17},{... | collective-permute-start | bytes 2654216 | tf_op jit(solution)/shard_map/ppermute | solution.py:508
  72.5 5.2 %collective-permute-start.12 = (f32[3,2,384]{2,1,0:T(2,128)S(1)}, f32[3,2,384]{2,1,0:T(2,128)S(1)}, u32[]{:S(2)}, u32[]{:S(2)}) collective-permute-start(f32[3,2,384]{2,1,0:T(2,128)S(1)} %get-tuple-element.126.refs_5_), channel_id=1, source_target_pairs={{0,3},{1,0},{2,1},{3,2},{4,7},{5,4},{6,5},{7,6},{8,11},{9,8},{10,9... | collective-permute-start | bytes 27656 | tf_op jit(solution)/shard_map/ppermute | solution.py:500
  74.7 4.6 %collective-permute-start.11 = (f32[3,2,384]{2,1,0:T(2,128)S(1)}, f32[3,2,384]{2,1,0:T(2,128)S(1)}, u32[]{:S(2)}, u32[]{:S(2)}) collective-permute-start(f32[3,2,384]{2,1,0:T(2,128)S(1)} %get-tuple-element.126.refs_5_), channel_id=1, source_target_pairs={{0,2},{1,3},{2,0},{3,1},{4,6},{5,7},{6,4},{7,5},{8,10},{9,11},{10,... | collective-permute-start | bytes 27656 | tf_op jit(solution)/shard_map/ppermute | solution.py:500
  74.7 5.5 %collective-permute-start.10 = (f32[3,2,384]{2,1,0:T(2,128)S(1)}, f32[3,2,384]{2,1,0:T(2,128)S(1)}, u32[]{:S(2)}, u32[]{:S(2)}) collective-permute-start(f32[3,2,384]{2,1,0:T(2,128)S(1)} %get-tuple-element.126.refs_5_), channel_id=1, source_target_pairs={{0,1},{1,2},{2,3},{3,0},{4,5},{5,6},{6,7},{7,4},{8,9},{9,10},{10,1... | collective-permute-start | bytes 27656 | tf_op jit(solution)/shard_map/ppermute | solution.py:500
  80.1 17.1 %collective-permute-start.15 = (bf16[384,1536]{1,0:T(8,128)(2,1)S(1)}, bf16[384,1536]{1,0:T(8,128)(2,1)S(1)}, u32[]{:S(2)}, u32[]{:S(2)}) collective-permute-start(bf16[384,1536]{1,0:T(8,128)(2,1)S(1)} %get-tuple-element.141.refs_19_), channel_id=1, source_target_pairs={{0,4},{4,0},{8,12},{12,8},{16,20},{20,16},{24,28},{28,24},{1,5},{5... | collective-permute-start | bytes 3538952 | tf_op jit(solution)/shard_map/ppermute | solution.py:508
  90.0 7.2 %collective-permute-start.16 = (bf16[384,1280]{1,0:T(8,128)(2,1)S(1)}, bf16[384,1280]{1,0:T(8,128)(2,1)S(1)}, u32[]{:S(2)}, u32[]{:S(2)}) collective-permute-start(bf16[384,1280]{1,0:T(8,128)(2,1)S(1)} %get-tuple-element.135.refs_5_), channel_id=1, source_target_pairs={{0,4},{4,0},{8,12},{12,8},{16,20},{20,16},{24,28},{28,24},{1,5},{5... | collective-permute-start | bytes 2949128 | tf_op jit(solution)/shard_map/ppermute | solution.py:508
  90.6 2.1 %copy-start.7 = (bf16[768,384]{1,0:T(8,128)(2,1)S(1)}, bf16[768,384]{1,0:T(8,128)(2,1)}, u32[]{:S(2)}) copy-start(bf16[768,384]{1,0:T(8,128)(2,1)} %refs_8_.1) | copy-start | bytes 1769476
  91.6 13.0 %collective-permute-start.13 = (bf16[1,96,2304]{2,1,0:T(8,128)(2,1)S(1)}, bf16[1,96,2304]{2,1,0:T(8,128)(2,1)S(1)}, u32[]{:S(2)}, u32[]{:S(2)}) collective-permute-start(bf16[1,96,2304]{2,1,0:T(8,128)(2,1)S(1)} %get-tuple-element.137), channel_id=1, source_target_pairs={{0,16},{4,20},{8,24},{12,28},{16,0},{20,4},{24,8},{28,12},{1,17},{... | collective-permute-start | bytes 1327112 | tf_op jit(solution)/shard_map/ppermute | solution.py:508
  92.2 13.1 %collective-permute-start.14 = (bf16[1,96,2304]{2,1,0:T(8,128)(2,1)S(1)}, bf16[1,96,2304]{2,1,0:T(8,128)(2,1)S(1)}, u32[]{:S(2)}, u32[]{:S(2)}) collective-permute-start(bf16[1,96,2304]{2,1,0:T(8,128)(2,1)S(1)} %get-tuple-element.139), channel_id=1, source_target_pairs={{0,8},{4,12},{8,0},{12,4},{16,24},{20,28},{24,16},{28,20},{1,9},{5... | collective-permute-start | bytes 1327112 | tf_op jit(solution)/shard_map/ppermute | solution.py:508
  97.3 1.3 copy-start.5
  99.6 18.8 %collective-permute-start.17 = (bf16[2,96,1536]{2,1,0:T(8,128)(2,1)S(1)}, bf16[2,96,1536]{2,1,0:T(8,128)(2,1)S(1)}, u32[]{:S(2)}, u32[]{:S(2)}) collective-permute-start(bf16[2,96,1536]{2,1,0:T(8,128)(2,1)S(1)} %get-tuple-element.147), channel_id=1, source_target_pairs={{0,8},{4,12},{8,0},{12,4},{16,24},{20,28},{24,16},{28,20},{1,9},{5... | collective-permute-start | bytes 1769480 | tf_op jit(solution)/shard_map/ppermute | solution.py:508
  101.1 17.3 %collective-permute-start.18 = (bf16[2,96,1280]{2,1,0:T(8,128)(2,1)S(1)}, bf16[2,96,1280]{2,1,0:T(8,128)(2,1)S(1)}, u32[]{:S(2)}, u32[]{:S(2)}) collective-permute-start(bf16[2,96,1280]{2,1,0:T(8,128)(2,1)S(1)} %get-tuple-element.149), channel_id=1, source_target_pairs={{0,16},{4,20},{8,24},{12,28},{16,0},{20,4},{24,8},{28,12},{1,17},{... | collective-permute-start | bytes 1474568 | tf_op jit(solution)/shard_map/ppermute | solution.py:508
  106.0 9.4 %collective-permute-start.19 = (bf16[1,48,2304]{2,1,0:T(8,128)(2,1)S(1)}, bf16[1,48,2304]{2,1,0:T(8,128)(2,1)S(1)}, u32[]{:S(2)}, u32[]{:S(2)}) collective-permute-start(bf16[1,48,2304]{2,1,0:T(8,128)(2,1)S(1)} %get-tuple-element.150), channel_id=1, source_target_pairs={{0,1},{1,0},{2,3},{3,2},{4,5},{5,4},{6,7},{7,6},{8,9},{9,8},{10,11... | collective-permute-start | bytes 663560 | tf_op jit(solution)/shard_map/ppermute | solution.py:508
  106.5 10.5 %collective-permute-start.20 = (bf16[1,48,2304]{2,1,0:T(8,128)(2,1)S(1)}, bf16[1,48,2304]{2,1,0:T(8,128)(2,1)S(1)}, u32[]{:S(2)}, u32[]{:S(2)}) collective-permute-start(bf16[1,48,2304]{2,1,0:T(8,128)(2,1)S(1)} %get-tuple-element.152), channel_id=1, source_target_pairs={{0,2},{1,3},{2,0},{3,1},{4,6},{5,7},{6,4},{7,5},{8,10},{9,11},{10,... | collective-permute-start | bytes 663560 | tf_op jit(solution)/shard_map/ppermute | solution.py:508
  117.0 1.3 copy-start.17
  119.2 7.7 %collective-permute-start.21 = (bf16[1,96,1536]{2,1,0:T(8,128)(2,1)S(1)}, bf16[1,96,1536]{2,1,0:T(8,128)(2,1)S(1)}, u32[]{:S(2)}, u32[]{:S(2)}) collective-permute-start(bf16[1,96,1536]{2,1,0:T(8,128)(2,1)S(1)} %get-tuple-element.155), channel_id=1, source_target_pairs={{0,16},{4,20},{8,24},{12,28},{16,0},{20,4},{24,8},{28,12},{1,17},{... | collective-permute-start | bytes 884744 | tf_op jit(solution)/shard_map/ppermute | solution.py:508
  120.8 6.2 %collective-permute-start.22 = (bf16[1,96,1280]{2,1,0:T(8,128)(2,1)S(1)}, bf16[1,96,1280]{2,1,0:T(8,128)(2,1)S(1)}, u32[]{:S(2)}, u32[]{:S(2)}) collective-permute-start(bf16[1,96,1280]{2,1,0:T(8,128)(2,1)S(1)} %get-tuple-element.157), channel_id=1, source_target_pairs={{0,8},{4,12},{8,0},{12,4},{16,24},{20,28},{24,16},{28,20},{1,9},{5... | collective-permute-start | bytes 737288 | tf_op jit(solution)/shard_map/ppermute | solution.py:508
  121.3 10.3 %collective-permute-start.26 = (bf16[1,48,2304]{2,1,0:T(8,128)(2,1)S(1)}, bf16[1,48,2304]{2,1,0:T(8,128)(2,1)S(1)}, u32[]{:S(2)}, u32[]{:S(2)}) collective-permute-start(bf16[1,48,2304]{2,1,0:T(8,128)(2,1)S(1)} %get-tuple-element.162.refs_2_), channel_id=1, source_target_pairs={{0,1},{1,0},{2,3},{3,2},{4,5},{5,4},{6,7},{7,6},{8,9},{9,8},{10,11... | collective-permute-start | bytes 663560 | tf_op jit(solution)/shard_map/ppermute | solution.py:508
  121.4 16.6 %collective-permute-start.25 = (bf16[1,48,2304]{2,1,0:T(8,128)(2,1)S(1)}, bf16[1,48,2304]{2,1,0:T(8,128)(2,1)S(1)}, u32[]{:S(2)}, u32[]{:S(2)}) collective-permute-start(bf16[1,48,2304]{2,1,0:T(8,128)(2,1)S(1)} %get-tuple-element.153.refs_5_.refs_0_), channel_id=1, source_target_pairs={{0,2},{1,3},{2,0},{3,1},{4,6},{5,7},{6,4},{7,5},{8,10},{9,11},{10,... | collective-permute-start | bytes 663560 | tf_op jit(solution)/shard_map/ppermute | solution.py:508
  127.6 13.5 %collective-permute-start.24 = (bf16[1,48,1280]{2,1,0:T(8,128)(2,1)S(1)}, bf16[1,48,1280]{2,1,0:T(8,128)(2,1)S(1)}, u32[]{:S(2)}, u32[]{:S(2)}) collective-permute-start(bf16[1,48,1280]{2,1,0:T(8,128)(2,1)S(1)} %get-tuple-element.161), channel_id=1, source_target_pairs={{0,2},{1,3},{2,0},{3,1},{4,6},{5,7},{6,4},{7,5},{8,10},{9,11},{10,... | collective-permute-start | bytes 368648 | tf_op jit(solution)/shard_map/ppermute | solution.py:508
  128.0 13.1 %collective-permute-start.23 = (bf16[1,48,1536]{2,1,0:T(8,128)(2,1)S(1)}, bf16[1,48,1536]{2,1,0:T(8,128)(2,1)S(1)}, u32[]{:S(2)}, u32[]{:S(2)}) collective-permute-start(bf16[1,48,1536]{2,1,0:T(8,128)(2,1)S(1)} %get-tuple-element.159), channel_id=1, source_target_pairs={{0,1},{1,0},{2,3},{3,2},{4,5},{5,4},{6,7},{7,6},{8,9},{9,8},{10,11... | collective-permute-start | bytes 442376 | tf_op jit(solution)/shard_map/ppermute | solution.py:508
  138.1 12.5 %collective-permute-start.30 = (bf16[1,48,2304]{2,1,0:T(8,128)(2,1)S(1)}, bf16[1,48,2304]{2,1,0:T(8,128)(2,1)S(1)}, u32[]{:S(2)}, u32[]{:S(2)}) collective-permute-start(bf16[1,48,2304]{2,1,0:T(8,128)(2,1)S(1)} %get-tuple-element.166), channel_id=1, source_target_pairs={{0,2},{1,3},{2,0},{3,1},{4,6},{5,7},{6,4},{7,5},{8,10},{9,11},{10,... | collective-permute-start | bytes 663560 | tf_op jit(solution)/shard_map/ppermute | solution.py:508
  138.2 12.5 %collective-permute-start.29 = (bf16[1,48,2304]{2,1,0:T(8,128)(2,1)S(1)}, bf16[1,48,2304]{2,1,0:T(8,128)(2,1)S(1)}, u32[]{:S(2)}, u32[]{:S(2)}) collective-permute-start(bf16[1,48,2304]{2,1,0:T(8,128)(2,1)S(1)} %get-tuple-element.163.refs_4_), channel_id=1, source_target_pairs={{0,1},{1,0},{2,3},{3,2},{4,5},{5,4},{6,7},{7,6},{8,9},{9,8},{10,11... | collective-permute-start | bytes 663560 | tf_op jit(solution)/shard_map/ppermute | solution.py:508
  141.2 11.5 %collective-permute-start.27 = (bf16[1,48,1536]{2,1,0:T(8,128)(2,1)S(1)}, bf16[1,48,1536]{2,1,0:T(8,128)(2,1)S(1)}, u32[]{:S(2)}, u32[]{:S(2)}) collective-permute-start(bf16[1,48,1536]{2,1,0:T(8,128)(2,1)S(1)} %get-tuple-element.164.refs_8_.refs_0_), channel_id=1, source_target_pairs={{0,2},{1,3},{2,0},{3,1},{4,6},{5,7},{6,4},{7,5},{8,10},{9,11},{10,... | collective-permute-start | bytes 442376 | tf_op jit(solution)/shard_map/ppermute | solution.py:508
  141.3 11.4 %collective-permute-start.28 = (bf16[1,48,1280]{2,1,0:T(8,128)(2,1)S(1)}, bf16[1,48,1280]{2,1,0:T(8,128)(2,1)S(1)}, u32[]{:S(2)}, u32[]{:S(2)}) collective-permute-start(bf16[1,48,1280]{2,1,0:T(8,128)(2,1)S(1)} %get-tuple-element.165.refs_2_), channel_id=1, source_target_pairs={{0,1},{1,0},{2,3},{3,2},{4,5},{5,4},{6,7},{7,6},{8,9},{9,8},{10,11... | collective-permute-start | bytes 368648 | tf_op jit(solution)/shard_map/ppermute | solution.py:508
  153.8 6.5 %collective-permute-start.31 = (bf16[1,48,1536]{2,1,0:T(8,128)(2,1)S(1)}, bf16[1,48,1536]{2,1,0:T(8,128)(2,1)S(1)}, u32[]{:S(2)}, u32[]{:S(2)}) collective-permute-start(bf16[1,48,1536]{2,1,0:T(8,128)(2,1)S(1)} %get-tuple-element.168), channel_id=1, source_target_pairs={{0,1},{1,0},{2,3},{3,2},{4,5},{5,4},{6,7},{7,6},{8,9},{9,8},{10,11... | collective-permute-start | bytes 442376 | tf_op jit(solution)/shard_map/ppermute | solution.py:508
  153.9 6.0 %collective-permute-start.32 = (bf16[1,48,1280]{2,1,0:T(8,128)(2,1)S(1)}, bf16[1,48,1280]{2,1,0:T(8,128)(2,1)S(1)}, u32[]{:S(2)}, u32[]{:S(2)}) collective-permute-start(bf16[1,48,1280]{2,1,0:T(8,128)(2,1)S(1)} %get-tuple-element.169), channel_id=1, source_target_pairs={{0,2},{1,3},{2,0},{3,1},{4,6},{5,7},{6,4},{7,5},{8,10},{9,11},{10,... | collective-permute-start | bytes 368648 | tf_op jit(solution)/shard_map/ppermute | solution.py:508
  (3 other events, 3.4 us)

commit v3 on v2

--- a/solution.py
+++ b/solution.py
@@ -12,8 +12,8 @@
 LANES = 128
 RANK, PLACE = 0, 1
 MICROSECONDS = dict(
-    project=4, summary=4, hidden_grad=2.5, mixer=8, ffn=18, turn=7, chains=3.5, mixer_grads=1, adjoint=1, input_grads=1, tokens=4.5, out=3.5,
-    ffn_sum1=1.3, mixer_sum1=1.0, ffn_sum2=5,
+    project=4, summary=4, hidden_grad=2.5, mixer=8, ffn_first=6, ffn_rest=12, turn=7, chains=0.3, mixer_grads=0.3, adjoint=0.3, input_grads=0.3, tokens=0.3, ffn_sum4=8, out=3.5,
+    ffn_sum1=1.3, mixer_sum1=1.0, ffn_sum2=3, ffn_sum3=20,
 )
 COST = 1.15e9
 TILE = 16
@@ -64,24 +64,37 @@
         ref[pl.ds(pl.multiple_of(at, TILE), lo), col : col + t.shape[1]] = t[b * lo : (b + 1) * lo, :]
 
 
-def put(ref, value):
-    for g in range(ref.shape[0]):
-        ref[g] = value[:, g * LANES : (g + 1) * LANES]
-
-
-def get(ref):
-    return jnp.concatenate([ref[g] for g in range(ref.shape[0])], axis=1)
-
-
-def lanes(value, parts):
-    return [value[:, g * LANES : (g + 1) * LANES] for g in range(parts)]
+def at_step(t):
+    return slice(CHUNKS * t, CHUNKS * (t + 1))
+
+
+def reorder(order_ref, v, back=False):
+    return dot(order_ref[...], v, ((0,), (0,)) if back else ((1,), (0,))).astype(BF)
+
+
+def own_kernel(phase_ref, init_ref, infos_ref, here_ref, line_ref):
+    own = phase_ref.shape[0]
+    rank, place = lax.axis_index("seq"), lax.axis_index("dp")
+    here_ref[RANK], here_ref[PLACE] = rank, place
+    theta = phase_ref[...][None]
+    line_ref[...] = jnp.zeros_like(line_ref)
+    line_ref[0:1, :own] = jnp.cos(theta)
+    line_ref[1:2, :own] = jnp.sin(theta)
+    for n in range(init_ref.shape[0]):
+        line_ref[2 + 2 * n : 4 + 2 * n, :own] = init_ref[n]
+    placed = pltpu.roll(line_ref[...], own * rank, 1)
+    for n in range(infos_ref.shape[0]):
+        infos_ref[n] = placed[2 * n : 2 * n + 2, :]
 
 
 def project_kernel(
-    here_ref, x_ref, gain_ref, w_in_ref, w_forget_ref, bias_ref, perm_ref, normed_ref, turned_ref, pre_ref, *, lo, first
+    here_ref, x_ref, gain_ref, w_in_ref, w_forget_ref, bias_ref, perm_ref, order_ref, xs_ref, normed_ref, turned_ref,
+    pre_ref, *, lo, first
 ):
     width = x_ref.shape[1]
-    x = x_ref[...].astype(F32)
+    xs = reorder(order_ref, x_ref[...])
+    xs_ref[...] = xs
+    x = xs.astype(F32)
     normed = (x * lax.rsqrt(row_mean(x * x) + epsilon) * gain_ref[...][None]).astype(BF)
     normed_ref[...] = normed
     put_halves(turned_ref, normed.T, 0, lo, bit_of(here_ref, PLACE, first))
@@ -93,33 +106,24 @@
 def summary_kernel(*refs, ranks):
     pre_ref, infos = refs[0], refs[1 : 1 + ranks]
     trig_ref, chunk_ref, total_ref, lam_re, lam_im, drv_re, drv_im = refs[1 + ranks :]
-    parts, span, _ = lam_re.shape
-    step = span // CHUNKS
+    span, ch = lam_re.shape
     trig = infos[0][...]
     for info in infos[1:]:
         trig = trig + info[...]
     trig_ref[...] = trig
-    ch = parts * LANES
     pre = pre_ref[...].astype(F32)
     forget = jax.nn.sigmoid(pre[:, 2 * ch :])
-    put(lam_re, forget * trig[0:1, :])
-    put(lam_im, forget * trig[1:2, :])
-    put(drv_re, (1.0 - forget) * jax.nn.silu(pre[:, :ch]))
-    put(drv_im, (1.0 - forget) * jax.nn.silu(pre[:, ch : 2 * ch]))
-    carried = [None] * parts
-    for t in range(step):
-        rows = pl.ds(t, CHUNKS, stride=step)
-        for g in range(parts):
-            lr, li = lam_re[g, rows, :], lam_im[g, rows, :]
-            br, bi = drv_re[g, rows, :], drv_im[g, rows, :]
-            if t == 0:
-                carried[g] = (lr, li, br, bi)
-            else:
-                pr, pi, hr, hi = carried[g]
-                pr, pi = cmul(lr, li, pr, pi)
-                hr, hi = cmul(lr, li, hr, hi)
-                carried[g] = (pr, pi, hr + br, hi + bi)
-    pr, pi, hr, hi = (jnp.concatenate([carried[g][q] for g in range(parts)], axis=1) for q in range(4))
+    lam_re[...] = forget * trig[0:1, :]
+    lam_im[...] = forget * trig[1:2, :]
+    drv_re[...] = (1.0 - forget) * jax.nn.silu(pre[:, :ch])
+    drv_im[...] = (1.0 - forget) * jax.nn.silu(pre[:, ch : 2 * ch])
+    first = at_step(0)
+    pr, pi, hr, hi = lam_re[first, :], lam_im[first, :], drv_re[first, :], drv_im[first, :]
+    for t in range(1, span // CHUNKS):
+        lr, li = lam_re[at_step(t), :], lam_im[at_step(t), :]
+        pr, pi = cmul(lr, li, pr, pi)
+        hr, hi = cmul(lr, li, hr, hi)
+        hr, hi = hr + drv_re[at_step(t), :], hi + drv_im[at_step(t), :]
     chunk_ref[0], chunk_ref[1], chunk_ref[2], chunk_ref[3] = pr, pi, hr, hi
     tp_r, tp_i, th_r, th_i = pr[0:1], pi[0:1], hr[0:1], hi[0:1]
     for k in range(1, CHUNKS):
@@ -135,9 +139,7 @@
     totals, inits, refs = refs[:ranks], refs[ranks : 2 * ranks], refs[2 * ranks :]
     lam_re, lam_im, drv_re, drv_im, chunk_ref, perm_ref, x_ref, og_ref, gain_ref, member_ref, w_out_ref = refs[:11]
     y_ref, split_ref, start_ref, final_ref, turned_ref, middle_ref, st_re, st_im = refs[11:]
-    parts, span, _ = lam_re.shape
-    ch = parts * LANES
-    step = span // CHUNKS
+    span, ch = lam_re.shape
     rank, bit = scalars[RANK], bit_of(scalars, PLACE, first)
     init = inits[0][...]
     for info in inits[1:]:
@@ -164,18 +166,13 @@
         cr, ci = cr + chunk_ref[2, k : k + 1, :], ci + chunk_ref[3, k : k + 1, :]
         rows_r.append(cr)
         rows_i.append(ci)
-    carried = list(
-        zip(lanes(jnp.concatenate(rows_r, axis=0), parts), lanes(jnp.concatenate(rows_i, axis=0), parts), strict=True)
-    )
-    for t in range(step):
-        rows = pl.ds(t, CHUNKS, stride=step)
-        for g in range(parts):
-            hr, hi = cmul(lam_re[g, rows, :], lam_im[g, rows, :], *carried[g])
-            hr, hi = hr + drv_re[g, rows, :], hi + drv_im[g, rows, :]
-            st_re[g, rows, :] = hr
-            st_im[g, rows, :] = hi
-            carried[g] = (hr, hi)
-    split = jnp.concatenate([get(st_re).astype(BF), get(st_im).astype(BF)], axis=1)
+    hr, hi = jnp.concatenate(rows_r, axis=0), jnp.concatenate(rows_i, axis=0)
+    for t in range(span // CHUNKS):
+        hr, hi = cmul(lam_re[at_step(t), :], lam_im[at_step(t), :], hr, hi)
+        hr, hi = hr + drv_re[at_step(t), :], hi + drv_im[at_step(t), :]
+        st_re[at_step(t), :] = hr
+        st_im[at_step(t), :] = hi
+    split = jnp.concatenate([st_re[...].astype(BF), st_im[...].astype(BF)], axis=1)
     split_ref[...] = split
     yf = dot(split, perm_ref[...], NT)
     y_ref[...] = yf.astype(BF)
@@ -186,59 +183,80 @@
     middle_ref[...] = x_ref[...].astype(F32) + dot(gated, w_out_ref[...])
 
 
-def ffn_kernel(
-    here_ref, middle_ref, gain_ref, cot_ref, wg_ref, wu_ref, dh_ref,
-    gsend_ref, gkeep_ref, dsend_ref, dkeep_ref, hid_ref, dn_ref,
-    n_ref, nt_ref, dgv_ref, duv_ref, ht_ref,
-    *, lo, dlo, rt, first,
+def hidden_tile(n_ref, rows, cut, wg_ref, wu_ref, dh_ref, hid_ref, dgv_ref, duv_ref, to):
+    g, u = dot(n_ref[rows, :], wg_ref[:, cut]), dot(n_ref[rows, :], wu_ref[:, cut])
+    dh = dh_ref[rows, cut].astype(F32)
+    sig = jax.nn.sigmoid(g)
+    act = g * sig
+    hid_ref[rows, to] = (act * u).astype(BF)
+    dgv_ref[rows, to] = (dh * u * silu_slope(g, sig)).astype(BF)
+    duv_ref[rows, to] = (dh * act).astype(BF)
+
+
+def two_halves(lhs_ref, rhs, send_ref, keep_ref, to):
+    half = lhs_ref.shape[0] // 2
+    send_ref[:, to] = dot(lhs_ref[:half, :], rhs).astype(BF)
+    keep_ref[:, to] = dot(lhs_ref[half:, :], rhs).astype(BF)
+
+
+def ffn_first_kernel(
+    here_ref, middle_ref, gain_ref, wg_ref, wu_ref, dh_ref,
+    gsend_ref, gkeep_ref, n_ref, nt_ref, hid_ref, dgv_ref, duv_ref,
+    *, lo, rt, first,
 ):
-    j = pl.program_id(0)
     bit = bit_of(here_ref, PLACE, first)
     count, width = middle_ref.shape
-    tile = wg_ref.shape[1]
+    cut = slice(0, width)
+    for r in range(0, count, rt):
+        rows = slice(r, r + rt)
+        v = middle_ref[rows, :]
+        normed = (v * lax.rsqrt(row_mean(v * v) + epsilon) * gain_ref[...][None]).astype(BF)
+        n_ref[rows, :] = normed
+        put_halves(nt_ref, normed.T, r, lo, bit)
+        hidden_tile(n_ref, rows, cut, wg_ref, wu_ref, dh_ref, hid_ref, dgv_ref, duv_ref, cut)
+    two_halves(nt_ref, dgv_ref[...], gsend_ref, gkeep_ref, cut)
+    two_halves(nt_ref, duv_ref[...], gsend_ref, gkeep_ref, slice(width, 2 * width))
+
+
+def ffn_rest_kernel(
+    here_ref, n_ref, nt_ref, cot_ref, wg_ref, wu_ref, dh_ref, hid0_ref, dgv0_ref, duv0_ref,
+    gsend_ref, gkeep_ref, dsend_ref, dkeep_ref, hid_ref, dn_ref,
+    dgv_ref, duv_ref, ht_ref,
+    *, lo, rt, first,
+):
+    bit = bit_of(here_ref, PLACE, first)
+    count, width = n_ref.shape
     spans = [slice(r, r + rt) for r in range(0, count, rt)]
-
-    @pl.when(j == 0)
-    def _():
+    cut, own = slice(width, 2 * width), slice(0, width)
+    for rows in spans:
+        hidden_tile(n_ref, rows, cut, wg_ref, wu_ref, dh_ref, hid_ref, dgv_ref, duv_ref, own)
+    two_halves(nt_ref, dgv_ref[...], gsend_ref, gkeep_ref, own)
+    two_halves(nt_ref, duv_ref[...], gsend_ref, gkeep_ref, cut)
+    half = width // 2
+    for j, ref in enumerate((hid0_ref, hid_ref)):
         for rows in spans:
-            v = middle_ref[rows, :]
-            normed = (v * lax.rsqrt(row_mean(v * v) + epsilon) * gain_ref[...][None]).astype(BF)
-            n_ref[rows, :] = normed
-            put_halves(nt_ref, normed.T, rows.start, lo, bit)
-
+            put_halves(ht_ref.at[j], ref[rows, :].T, rows.start, lo, bit)
+    for j in range(2):
+        out = slice(j * half, (j + 1) * half)
+        dsend_ref[out, :] = dot(ht_ref[j, :half, :], cot_ref[...]).astype(BF)
+        dkeep_ref[out, :] = dot(ht_ref[j, half:, :], cot_ref[...]).astype(BF)
     for rows in spans:
-        g, u = dot(n_ref[rows, :], wg_ref[...]), dot(n_ref[rows, :], wu_ref[...])
-        dh = dh_ref[rows, :].astype(F32)
-        sig = jax.nn.sigmoid(g)
-        act = g * sig
-        hid_ref[rows, :] = (act * u).astype(BF)
-        dgv_ref[rows, :] = (dh * u * silu_slope(g, sig)).astype(BF)
-        duv_ref[rows, :] = (dh * act).astype(BF)
-    for rows in spans:
-        put_halves(ht_ref, hid_ref[rows, :].T, rows.start, dlo, bit)
-    for lhs, ref in ((nt_ref[: width // 2, :], gsend_ref), (nt_ref[width // 2 :, :], gkeep_ref)):
-        ref[:, :tile] = dot(lhs, dgv_ref[...]).astype(BF)
-        ref[:, tile:] = dot(lhs, duv_ref[...]).astype(BF)
-    for lhs, ref in ((ht_ref[: tile // 2, :], dsend_ref), (ht_ref[tile // 2 :, :], dkeep_ref)):
-        ref[...] = dot(lhs, cot_ref[...]).astype(BF)
-    for rows in spans:
-        dn = dot(dgv_ref[rows, :], wg_ref[...], NT) + dot(duv_ref[rows, :], wu_ref[...], NT)
-
-        @pl.when(j == 0)
-        def _():
-            dn_ref[rows, :] = dn
-
-        @pl.when(j > 0)
-        def _():
-            dn_ref[rows, :] += dn
+        dn_ref[rows, :] = (
+            dot(dgv0_ref[rows, :], wg_ref[:, own], NT)
+            + dot(duv0_ref[rows, :], wu_ref[:, own], NT)
+            + dot(dgv_ref[rows, :], wg_ref[:, cut], NT)
+            + dot(duv_ref[rows, :], wu_ref[:, cut], NT)
+        )
 
 
 def gate_kernel(normed_ref, w_ref, og_ref):
     og_ref[...] = dot(normed_ref[...], w_ref[...]).astype(BF)
 
 
-def hidden_grad_kernel(cot_ref, wd_ref, dh_ref):
-    dh_ref[...] = dot(cot_ref[...], wd_ref[...], NT).astype(BF)
+def hidden_grad_kernel(cot_ref, wd_ref, order_ref, cots_ref, dh_ref):
+    cots = reorder(order_ref, cot_ref[...])
+    cots_ref[...] = cots
+    dh_ref[...] = dot(cots, wd_ref[...], NT).astype(BF)
 
 
 def turn_kernel(
@@ -265,20 +283,15 @@
 
 
 def chains_kernel(split_ref, lam_re, lam_im, chunk_ref, chain_ref, total_ref, dy_re, dy_im):
-    parts, span, _ = lam_re.shape
-    ch = parts * LANES
-    step = span // CHUNKS
-    put(dy_re, split_ref[:, :ch].astype(F32))
-    put(dy_im, split_ref[:, ch:].astype(F32))
-    carried = [None] * parts
-    for t in range(step - 1, -1, -1):
-        rows = pl.ds(t, CHUNKS, stride=step)
-        for g in range(parts):
-            gr, gi = dy_re[g, rows, :], dy_im[g, rows, :]
-            if carried[g] is not None:
-                gr, gi = gr + carried[g][0], gi + carried[g][1]
-            carried[g] = cmul(lam_re[g, rows, :], -lam_im[g, rows, :], gr, gi)
-    ar, ai = (jnp.concatenate([carried[g][q] for g in range(parts)], axis=1) for q in range(2))
+    span, ch = lam_re.shape
+    dy_re[...] = split_ref[:, :ch].astype(F32)
+    dy_im[...] = split_ref[:, ch:].astype(F32)
+    last = span // CHUNKS - 1
+    gr, gi = dy_re[at_step(last), :], dy_im[at_step(last), :]
+    ar, ai = cmul(lam_re[at_step(last), :], -lam_im[at_step(last), :], gr, gi)
+    for t in range(last - 1, -1, -1):
+        gr, gi = dy_re[at_step(t), :] + ar, dy_im[at_step(t), :] + ai
+        ar, ai = cmul(lam_re[at_step(t), :], -lam_im[at_step(t), :], gr, gi)
     chain_ref[0], chain_ref[1] = ar, ai
     er, ei = ar[CHUNKS - 1 :], ai[CHUNKS - 1 :]
     for k in range(CHUNKS - 2, -1, -1):
@@ -292,15 +305,13 @@
     totals, adjs, refs = refs[:ranks], refs[ranks : 2 * ranks], refs[2 * ranks :]
     pre_ref, trig_ref, lam_re, lam_im, dy_ref, split_ref, start_ref, chunk_ref, chain_ref, perm_ref = refs[:10]
     dpre_ref, sums_ref, dy_re, dy_im = refs[10:]
-    parts, span, _ = lam_re.shape
-    ch = parts * LANES
-    step = span // CHUNKS
+    span, ch = lam_re.shape
     rank = scalars[RANK]
     pre = pre_ref[...].astype(F32)
     trig = trig_ref[...]
     forget = jax.nn.sigmoid(pre[:, 2 * ch :])
-    put(dy_re, dy_ref[:, :ch].astype(F32))
-    put(dy_im, dy_ref[:, ch:].astype(F32))
+    dy_re[...] = dy_ref[:, :ch].astype(F32)
+    dy_im[...] = dy_ref[:, ch:].astype(F32)
     cr = jnp.zeros((1, ch), F32)
     ci = jnp.zeros((1, ch), F32)
     for k in range(1, ranks):
@@ -314,24 +325,21 @@
         cr, ci = cr + chain_ref[0, k : k + 1, :], ci + chain_ref[1, k : k + 1, :]
         rows_r.append(cr)
         rows_i.append(ci)
-    carried = list(
-        zip(
-            lanes(jnp.concatenate(rows_r[::-1], axis=0), parts),
-            lanes(jnp.concatenate(rows_i[::-1], axis=0), parts),
-            strict=True,
-        )
-    )
-    for t in range(step - 1, -1, -1):
-        rows = pl.ds(t, CHUNKS, stride=step)
-        for g in range(parts):
-            gr, gi = dy_re[g, rows, :] + carried[g][0], dy_im[g, rows, :] + carried[g][1]
-            dy_re[g, rows, :] = gr
-            dy_im[g, rows, :] = gi
-            carried[g] = cmul(lam_re[g, rows, :], -lam_im[g, rows, :], gr, gi)
-    gr, gi = get(dy_re), get(dy_im)
-    first = lax.broadcasted_iota(jnp.int32, (span, ch), 0) == 0
-    qr = jnp.where(first, start_ref[0:1, :], pltpu.roll(split_ref[:, :ch].astype(F32), 1, 0))
-    qi = jnp.where(first, start_ref[1:2, :], pltpu.roll(split_ref[:, ch:].astype(F32), 1, 0))
+    ar, ai = jnp.concatenate(rows_r[::-1], axis=0), jnp.concatenate(rows_i[::-1], axis=0)
+    for t in range(span // CHUNKS - 1, -1, -1):
+        gr, gi = dy_re[at_step(t), :] + ar, dy_im[at_step(t), :] + ai
+        dy_re[at_step(t), :] = gr
+        dy_im[at_step(t), :] = gi
+        ar, ai = cmul(lam_re[at_step(t), :], -lam_im[at_step(t), :], gr, gi)
+    gr, gi = dy_re[...], dy_im[...]
+
+    def before(states, start):
+        ends = pltpu.roll(states[span - CHUNKS :, :], 1, 0)
+        ends = jnp.where(lax.broadcasted_iota(jnp.int32, ends.shape, 0) == 0, start, ends)
+        return jnp.concatenate([ends, states[: span - CHUNKS, :]], axis=0)
+
+    qr = before(split_ref[:, :ch].astype(F32), start_ref[0:1, :])
+    qi = before(split_ref[:, ch:].astype(F32), start_ref[1:2, :])
     pin_re, pin_im = pre[:, :ch], pre[:, ch : 2 * ch]
     sig_re, sig_im = jax.nn.sigmoid(pin_re), jax.nn.sigmoid(pin_im)
     lr = gr * qr + gi * qi
@@ -373,8 +381,12 @@
         at += n
 
 
-def out_kernel(middle_ref, hid_ref, w_down_ref, out_ref):
-    out_ref[...] = (middle_ref[...] + dot(hid_ref[...], w_down_ref[...])).astype(BF)
+def out_kernel(middle_ref, hid0_ref, hid_ref, w_down_ref, order_ref, out_ref, done_ref):
+    width = middle_ref.shape[1]
+    branch = dot(hid0_ref[...], w_down_ref[:width, :]) + dot(hid_ref[...], w_down_ref[width:, :])
+    out = (middle_ref[...] + branch).astype(BF)
+    out_ref[...] = reorder(order_ref, out, True)
+    done_ref[...] = jnp.zeros_like(done_ref)
 
 
 def input_grads_kernel(lhs_ref, dpre_ref, sums_ref, send_ref, keep_ref, *, per):
@@ -392,7 +404,9 @@
     keep_ref[:, n:] = beside
 
 
-def tokens_kernel(dpre_ref, dog_ref, w_in_ref, w_forget_ref, w_ogate_ref, x_ref, gain_ref, dmiddle_ref, out_ref):
+def tokens_kernel(
+    dpre_ref, dog_ref, w_in_ref, w_forget_ref, w_ogate_ref, x_ref, gain_ref, dmiddle_ref, order_ref, out_ref, done_ref
+):
     width = x_ref.shape[1]
     up = (
         dot(dpre_ref[:, :width], w_in_ref[...], NT)
@@ -403,7 +417,9 @@
     inv = lax.rsqrt(row_mean(x * x) + epsilon)
     unit = x * inv
     through = up * gain_ref[...][None]
-    out_ref[...] = (dmiddle_ref[...] + inv * (through - unit * row_mean(through * unit))).astype(BF)
+    out = (dmiddle_ref[...] + inv * (through - unit * row_mean(through * unit))).astype(BF)
+    out_ref[...] = reorder(order_ref, out, True)
+    done_ref[...] = jnp.zeros_like(done_ref)
 
 
 def rows(*shape):
@@ -435,6 +451,8 @@
 
 
 def spec_of(kind):
+    if kind[0] == "smem":
+        return pl.BlockSpec(memory_space=pltpu.SMEM)
     if kind[0] == "full":
         return pl.BlockSpec(kind[1], lambda s, *_: (0,) * len(kind[1]))
     if kind[0] == "own":
@@ -512,8 +530,10 @@
     return [1 << i for i in range((n - 1).bit_length())]
 
 
-def combine_kernel(here_ref, *refs, plan, n_in):
+def combine_kernel(here_ref, *refs, plan, n_in, sums):
     ins, outs = refs[:n_in], refs[n_in:]
+    for n, (a, b) in enumerate(sums):
+        outs[2 * len(plan) + n][...] = (ins[a][...].astype(F32) + ins[b][...].astype(F32)).astype(BF)
     for n, (pos, bit, count, sources) in enumerate(plan):
         for flip in (1, 0):
             own = 1 - bit_of(here_ref, *bit) if flip else bit_of(here_ref, *bit)
@@ -530,7 +550,7 @@
                     at += width
 
 
-def combine(here, lanes_in, name, after=()):
+def combine(here, lanes_in, name, after=(), sums=()):
     arrays, outs, plan = [], [], []
 
     def operand(a):
@@ -546,11 +566,13 @@
         plan.append((pos, bit, count, [([operand(a) for a in src[0]], *src[1:]) for src in sources]))
         shape = (count, per, sum(src[4] for src in sources))
         outs += [(whole(*shape), shape, BF)] * 2
+    pairs = [tuple(operand(a) for a in pair) for pair in sums]
+    outs += [(whole(*pair[0].shape), pair[0].shape, BF) for pair in sums]
     got = call(
-        functools.partial(combine_kernel, plan=plan, n_in=len(arrays)), 1, [(whole(), a) for a in arrays], outs, [],
+        functools.partial(combine_kernel, plan=plan, n_in=len(arrays), sums=pairs), 1, [(whole(), a) for a in arrays], outs, [],
         [here], name, after, 4,
     )
-    return [(got[2 * n], got[2 * n + 1]) for n in range(len(lanes_in))]
+    return [(got[2 * n], got[2 * n + 1]) for n in range(len(lanes_in))] + list(got[2 * len(lanes_in) :])
 
 
 def add_kernel(*refs):
@@ -572,7 +594,8 @@
 
 def finish_kernel(here_ref, *refs, moves, bits, gains, n_out, vectors, ranks):
     lanes_n = len(bits)
-    halves, refs = refs[: 2 * lanes_n], refs[2 * lanes_n :]
+    halves, done_ref, refs = refs[: 2 * lanes_n], refs[-1], refs[2 * lanes_n : -1]
+    done_ref[...] = jnp.zeros_like(done_ref)
     ins, outs = refs[: len(refs) - n_out], refs[len(refs) - n_out :]
     half = halves[0].shape[0]
 
@@ -608,7 +631,7 @@
         functools.partial(
             finish_kernel, moves=moves, bits=bits, gains=gains, n_out=len(outs), vectors=vectors, ranks=ranks
         ),
-        1, ins, [(k(*shape), shape, F32) for k, shape in outs], [], [here], name, after,
+        1, ins, [(k(*shape), shape, F32) for k, shape in outs] + [(whole(), (8, LANES), F32)], [], [here], name, after,
     )
 
 
@@ -653,30 +676,33 @@
     first = next(b for b in bits if (per * b) % TILE == 0)
     rest = [b for b in bits if b != first]
     lo = per * first
-    here = jnp.stack([rank, lax.axis_index("dp").astype(jnp.int32)])
-    scan = seg(ch // LANES, span, LANES)
-    scanned = (scan, (segs, ch // LANES, span, LANES), F32)
-    scan_scratch = [pltpu.VMEM((ch // LANES, span, LANES), F32)] * 2
-
-    own = jnp.concatenate(
-        [jnp.stack([jnp.cos(phase), jnp.sin(phase)])[None], init_state.transpose(0, 2, 1)], axis=0
-    )
-    place = (jnp.arange(ch) // mine) == rank
-    infos = shift_all(jnp.where(place, jnp.concatenate([own] * nseq, axis=2), 0.0), "seq", nseq)
+    scan = rows(span, ch)
+    scanned = (scan, (count, ch), F32)
+    scan_scratch = [pltpu.VMEM((span, ch), F32)] * 2
+
+    infos, here = call(
+        own_kernel, 1, [(whole(), phase), (whole(), init_state.transpose(0, 2, 1))],
+        [(whole(), (1 + segs, 2, ch), F32), (("smem",), (2,), jnp.int32)],
+        [pltpu.VMEM((-(-(2 + 2 * segs) // 8) * 8, ch), F32)], [], "own",
+    )
+    infos = shift_all(infos, "seq", nseq)
 
     col = jnp.arange(width)
     perm = (col[:, None] == 2 * (col % ch)[None, :] + (col // ch)[None, :]).astype(BF)
     member = ((col[:, None] // (width // GROUPS)) == jnp.arange(LANES)[None, :]).astype(BF)
 
-    x = tokens.reshape(count, width)
-    cot = cotangent.reshape(count, width)
-    normed, normed_t, pre = call(
+    place_of = jnp.arange(span)
+    step_order = ((place_of % CHUNKS) * (span // CHUNKS) + place_of // CHUNKS)[:, None] == place_of[None, :]
+    step_order = (whole(span, span), step_order.astype(BF))
+
+    x, normed, normed_t, pre = call(
         functools.partial(project_kernel, lo=lo, first=first), segs,
         [
-            (rows(span, width), x), (whole(width), norm_mix), (whole(width, width), w_in),
-            (whole(width, ch), w_forget), (whole(ch), forget_bias), (whole(width, width), perm),
+            (rows(span, width), tokens.reshape(count, width)), (whole(width), norm_mix), (whole(width, width), w_in),
+            (whole(width, ch), w_forget), (whole(ch), forget_bias), (whole(width, width), perm), step_order,
         ],
         [
+            (rows(span, width), (count, width), BF),
             (rows(span, width), (count, width), BF),
             (cols(width, span), (width, count), BF),
             (seg(span, 3 * ch), (segs, span, 3 * ch), BF),
@@ -699,9 +725,11 @@
         gate_kernel, 1, [(whole(count, width), normed), (whole(width, width), w_ogate)],
         [(whole(count, width), (count, width), BF)], [], [], "gate", (lam_re,),
     )
-    (dh,) = call(
-        hidden_grad_kernel, tall, [(whole(count, width), cot), (rows(width, width), w_down)],
-        [(cols(count, width), (count, hidden), BF)], [], [], "hidden_grad", (lam_re,),
+    cot, dh = call(
+        hidden_grad_kernel, segs,
+        [(rows(span, width), cotangent.reshape(count, width)), (whole(hidden, width), w_down), step_order],
+        [(rows(span, width), (count, width), BF), (rows(span, hidden), (count, hidden), BF)], [], [], "hidden_grad",
+        (lam_re,),
     )
     y, y_split, start, final, gated_t, middle = call(
         functools.partial(mixer_kernel, ranks=nseq, lo=lo, first=first), segs,
@@ -724,30 +752,50 @@
     )
     final_state = final.transpose(0, 2, 1)
 
-    tile = width
+    wide = (count, width)
+    done = (whole(), (8, LANES), F32)
+    psend, pkeep, normed_ffn, normed_ffn_t, hid0, dgv0, duv0 = call(
+        functools.partial(ffn_first_kernel, lo=lo, rt=span, first=first), 1,
+        [(whole(), a) for a in (middle, norm_ffn, w_gate, w_up, dh)],
+        [(whole(), (width // 2, 2 * width), BF)] * 2
+        + [(whole(), wide, BF), (whole(), (width, count), BF)]
+        + [(whole(), wide, BF)] * 3,
+        [], [here], "ffn_first", (), 7,
+    )
+    pgot = swap(psend, "dp", ndp, first)
     gsend, gkeep, dsend, dkeep, hid, dn = call(
-        functools.partial(ffn_kernel, lo=lo, dlo=lo * tall, rt=span, first=first), hidden // tile,
-        [
-            (whole(count, width), middle), (whole(width), norm_ffn), (whole(count, width), cot),
-            (cols(width, tile), w_gate), (cols(width, tile), w_up), (cols(count, tile), dh),
-        ],
-        [
-            (cols(width // 2, 2 * tile), (width // 2, 2 * hidden), BF),
-            (cols(width // 2, 2 * tile), (width // 2, 2 * hidden), BF),
-            (rows(tile // 2, width), (hidden // 2, width), BF),
-            (rows(tile // 2, width), (hidden // 2, width), BF),
-            (cols(count, tile), (count, hidden), BF),
-            (whole(count, width), (count, width), F32),
-        ],
-        [
-            pltpu.VMEM((count, width), BF), pltpu.VMEM((width, count), BF),
-            pltpu.VMEM((count, tile), BF), pltpu.VMEM((count, tile), BF),
-            pltpu.VMEM((tile, count), BF),
-        ],
-        [here], "ffn", (), 7,
-    )
-
+        functools.partial(ffn_rest_kernel, lo=lo * tall, rt=span, first=first), 1,
+        [(whole(), a) for a in (normed_ffn, normed_ffn_t, cot, w_gate, w_up, dh, hid0, dgv0, duv0)],
+        [(whole(), (width // 2, 2 * width), BF)] * 2
+        + [(whole(), (hidden // 2, width), BF)] * 2
+        + [(whole(), wide, BF), (whole(), wide, F32)],
+        [pltpu.VMEM(wide, BF), pltpu.VMEM(wide, BF), pltpu.VMEM((tall, width, count), BF)], [here], "ffn_rest", (psend,), 7,
+    )
     ggot, dgot = swap(gsend, "dp", ndp, first), swap(dsend, "dp", ndp, first)
+
+    nblk = ndp // 2
+    fast = ndp == 8 and nseq == 4 and per % (2 * TILE) == 0
+    x_bit, y_bit = (PLACE, rest[0]), (PLACE, rest[1])
+    z_bits = [(RANK, b) for b in bits_of(nseq)]
+
+    def blocks(a, cols_n, tall_n=1):
+        return a.reshape(nblk * tall_n, per, cols_n)
+
+    order = ()
+    if fast:
+        p = [blocks(a, 2 * width) for a in (pkeep, pgot)]
+        (pa_send, pa_keep), (pb_send, pb_keep) = combine(
+            here, [(0, x_bit, [(p, 1, 0, 0, width)]), (1, y_bit, [(p, 1, 0, 1, width)])], "first_sum1", (gkeep,)
+        )
+        pa_got, pb_got = swap(pa_send, "dp", ndp, rest[0]), swap(pb_send, "dp", ndp, rest[1])
+        g = [blocks(a, 2 * width) for a in (gkeep, ggot)]
+        d = [blocks(a, width, tall) for a in (dkeep, dgot)]
+        (fa_send, fa_keep), (fb_send, fb_keep) = combine(
+            here, [(0, x_bit, [(g, 1, 0, 0, 2 * width)]), (1, y_bit, [(d, tall, i, 0, width) for i in range(tall)])],
+            "ffn_sum1", (pa_keep,),
+        )
+        fa_got, fb_got = swap(fa_send, "dp", ndp, rest[0]), swap(fb_send, "dp", ndp, rest[1])
+        order = (fa_keep,)
 
     dmiddle, dbranch, dog, dy_split = call(
         turn_kernel, segs,
@@ -762,25 +810,12 @@
             (rows(span, width), (count, width), BF),
             (rows(span, width), (count, width), BF),
         ],
-        [], [], "turn",
-    )
-    nblk = ndp // 2
-    fast = ndp == 8 and nseq == 4 and per % (2 * TILE) == 0
-    x_bit, y_bit = (PLACE, rest[0]), (PLACE, rest[1])
-    z_bits = [(RANK, b) for b in bits_of(nseq)]
-
-    def blocks(a, cols_n, tall_n=1):
-        return a.reshape(nblk * tall_n, per, cols_n)
-
+        [], [], "turn", order,
+    )
     order = ()
     if fast:
-        g = [blocks(a, 2 * hidden) for a in (gkeep, ggot)]
-        d = [blocks(a, width, tall) for a in (dkeep, dgot)]
-        fa = [(g, 1, 0, 0, 3 * width)]
-        fb = [(g, 1, 0, 3, width)] + [(d, tall, i, 0, width) for i in range(tall)]
-        (fa_send, fa_keep), (fb_send, fb_keep) = combine(here, [(0, x_bit, fa), (1, y_bit, fb)], "ffn_sum1", (dog,))
-        fa_got, fb_got = swap(fa_send, "dp", ndp, rest[0]), swap(fb_send, "dp", ndp, rest[1])
-        order = (fa_keep,)
+        pa, pb = add_pairs([(pa_keep, pa_got), (pb_keep, pb_got)], "first_sum2", (dog,))
+        order = (pa,)
 
     chain, adj = call(
         chains_kernel, segs,
@@ -789,7 +824,6 @@
         scan_scratch, [], "chains", order,
     )
     adjs = shift_all(adj, "seq", nseq)
-
     ntile = width // 3
     osend, okeep = call(
         functools.partial(grads_kernel, pairs=2), width // ntile,
@@ -805,6 +839,25 @@
     )
     late, *adjs = lax.optimization_barrier((osend, *adjs))
     ogot = swap(late, "dp", ndp, first)
+    order = ()
+    if fast:
+        def one(keep, got):
+            return [([keep, got], 1, 0, 0, keep.shape[2])]
+
+        def rows_of(keep, got):
+            return one(*(a.reshape(2, per // 2, a.shape[2]) for a in (keep, got)))
+
+        (fa_send, fa_keep), (fb_send, fb_keep) = combine(
+            here,
+            [
+                (0, y_bit, [([pa], 1, 0, 0, width)] + one(fa_keep, fa_got)),
+                (0, x_bit, [([pb], 1, 0, 0, width)] + one(fb_keep, fb_got)),
+            ],
+            "ffn_sum2", (osend, *adjs),
+        )
+        fa_got, fb_got = swap(fa_send, "dp", ndp, rest[1]), swap(fb_send, "dp", ndp, rest[0])
+        order = (fa_keep,)
+
     dpre, sums = call(
         functools.partial(adjoint_kernel, ranks=nseq), segs,
         [(seg(4, ch), t) for t in totals] + [(seg(2, ch), a) for a in adjs]
@@ -815,7 +868,7 @@
             (seg(4, CHUNKS, ch), chunk), (seg(2, CHUNKS, ch), chain), (whole(width, width), perm),
         ],
         [(rows(span, 3 * ch), (count, 3 * ch), BF), (whole(2, ch), (2, ch), F32)],
-        scan_scratch, [here], "adjoint", (osend,),
+        scan_scratch, [here], "adjoint", order,
     )
     into = 3 * ch + LANES
     isend, ikeep = call(
@@ -826,62 +879,52 @@
     igot = swap(isend, "dp", ndp, first)
     order = ()
     if fast:
-        def one(keep, got):
-            return [([keep, got], 1, 0, 0, keep.shape[2])]
-
-        def rows_of(keep, got):
-            return one(*(a.reshape(2, per // 2, a.shape[2]) for a in (keep, got)))
+        lead, other = bits_of(nseq)
+
+        def over(send, axis_n, bit):
+            return swap(send, "seq", axis_n, bit)
 
         (fa_send, fa_keep), (fb_send, fb_keep) = combine(
-            here, [(0, y_bit, one(fa_keep, fa_got)), (0, x_bit, one(fb_keep, fb_got))], "ffn_sum2", (isend,)
-        )
-        fa_got, fb_got = swap(fa_send, "dp", ndp, rest[1]), swap(fb_send, "dp", ndp, rest[0])
-        order = (fa_keep,)
-
-    (grad_tokens,) = call(
+            here, [(0, z_bits[0], rows_of(fa_keep, fa_got)), (0, z_bits[1], rows_of(fb_keep, fb_got))],
+            "ffn_sum3", (isend,),
+        )
+        fa_got, fb_got = over(fa_send, nseq, lead), over(fb_send, nseq, other)
+        o = [blocks(a, 2 * width) for a in (okeep, ogot)]
+        i = [blocks(a, into) for a in (ikeep, igot)]
+        (ra_send, ra_keep), (rb_send, rb_keep) = combine(
+            here, [(0, x_bit, [(o, 1, 0, 0, 2 * width)]), (1, y_bit, [(i, 1, 0, 0, into)])], "mixer_sum1", (fa_keep,)
+        )
+        ra_got, rb_got = swap(ra_send, "dp", ndp, rest[0]), swap(rb_send, "dp", ndp, rest[1])
+        order = (ra_keep,)
+
+    grad_tokens, tokens_done = call(
         tokens_kernel, segs,
         [
             (rows(span, 3 * ch), dpre), (rows(span, width), dog), (whole(width, width), w_in),
             (whole(width, ch), w_forget), (whole(width, width), w_ogate), (rows(span, width), x),
-            (whole(width), norm_mix), (rows(span, width), dmiddle),
-        ],
-        [(moved(span, width, dim=0), (count, width), BF)],
+            (whole(width), norm_mix), (rows(span, width), dmiddle), step_order,
+        ],
+        [(moved(span, width, dim=0), (count, width), BF), done],
         [], [], "tokens", order,
     )
 
     def output(*after):
         return call(
-            out_kernel, segs, [(rows(span, width), middle), (rows(span, hidden), hid), (whole(hidden, width), w_down)],
-            [(moved(span, width, dim=0), (count, width), BF)], [], [], "out", after,
-        )[0]
+            out_kernel, segs,
+            [(rows(span, width), a) for a in (middle, hid0, hid)] + [(whole(hidden, width), w_down), step_order],
+            [(moved(span, width, dim=0), (count, width), BF), done], [], [], "out", after,
+        )
 
     if fast:
-        lead, other = bits_of(nseq)
-
-        o = [blocks(a, 2 * width) for a in (okeep, ogot)]
-        i = [blocks(a, into) for a in (ikeep, igot)]
-        (ra_send, ra_keep), (rb_send, rb_keep) = combine(
-            here, [(0, x_bit, [(o, 1, 0, 0, 2 * width)]), (1, y_bit, [(i, 1, 0, 0, into)])], "mixer_sum1", (grad_tokens,)
-        )
-        ra_got, rb_got = swap(ra_send, "dp", ndp, rest[0]), swap(rb_send, "dp", ndp, rest[1])
-
-        def over(send, axis_n, bit):
-            return swap(send, "seq", axis_n, bit)
-
-        (fa_send, fa_keep), (fb_send, fb_keep) = combine(
-            here, [(0, z_bits[0], rows_of(fa_keep, fa_got)), (0, z_bits[1], rows_of(fb_keep, fb_got))],
-            "ffn_sum3", (ra_keep,),
-        )
-        fa_got, fb_got = over(fa_send, nseq, lead), over(fb_send, nseq, other)
-        mixed_out = output(fa_keep)
-        fa, fb = add_pairs([(fa_keep, fa_got), (fb_keep, fb_got)], "ffn_sum4", (mixed_out,))
+        fa, fb = add_pairs([(fa_keep, fa_got), (fb_keep, fb_got)], "ffn_sum4", (tokens_done,))
         fa_got, fb_got = over(fa, nseq, other), over(fb, nseq, lead)
         (ra_send, ra_keep), (rb_send, rb_keep) = combine(
             here, [(0, y_bit, one(ra_keep, ra_got)), (0, x_bit, one(rb_keep, rb_got))], "mixer_sum2", (fa,)
         )
         ra_got, rb_got = swap(ra_send, "dp", ndp, rest[1]), swap(rb_send, "dp", ndp, rest[0])
+        mixed_out, out_done = output(ra_keep)
         (ra_send, ra_keep), (rb_send, rb_keep) = combine(
-            here, [(0, z_bits[0], rows_of(ra_keep, ra_got)), (0, z_bits[1], rows_of(rb_keep, rb_got))], "mixer_sum3", (fa,)
+            here, [(0, z_bits[0], rows_of(ra_keep, ra_got)), (0, z_bits[1], rows_of(rb_keep, rb_got))], "mixer_sum3", (out_done,)
         )
         ra_got, rb_got = over(ra_send, nseq, lead), over(rb_send, nseq, other)
         fa, fb = add_pairs([(fa, fa_got), (fb, fb_got)], "ffn_sum5", (ra_keep,))
@@ -892,21 +935,19 @@
         def flat(*pairs):
             return [tuple(a.reshape(per // 2, a.shape[2]) for a in pair) for pair in pairs]
 
-        guv = [(0, c * width) for c in range(3)] + [(1, 0)]
-        moves = [
-            (lane, col, width, n % 2, 0, (n // 2) * width) for n, (lane, col) in enumerate(guv)
-        ] + [(1, (1 + t) * width, width, 2, t * per, 0) for t in range(tall)]
-        part_gate, part_up, part_down, part_ffn = finish(
+        moves = [(0, 0, width, 0, 0, 0), (0, width, width, 0, 0, width), (0, 2 * width, width, 1, 0, width)]
+        moves += [(1, 0, width, 1, 0, 0)] + [(1, (1 + t) * width, width, 2, t * per, 0) for t in range(tall)]
+        part_gate, part_up, part_down, part_ffn, ffn_done = finish(
             here, flat((fa, fa_got), (fb, fb_got)), z_bits, moves,
             [(ours(per, hidden), w_gate), (ours(per, hidden), w_up), (whole(width), norm_ffn)],
             [(full, (per, hidden)), (full, (per, hidden)), (full, (tall * per, width)), (full, (per,))],
             [(3, 2, [(0, 0), (1, 1)])], None, nseq, "ffn_out", (ra,),
         )
-        ra, rb = add_pairs([(ra, ra_got), (rb, rb_got)], "mixer_sum5", (part_gate,))
+        ra, rb = add_pairs([(ra, ra_got), (rb, rb_got)], "mixer_sum5", (ffn_done,))
         ra_got, rb_got = over(ra, nseq, lead), over(rb, nseq, other)
         moves = [(0, n * ntile, ntile, n % 2, 0, (n // 2) * ntile) for n in range(2 * width // ntile)]
         moves += [(1, 0, width, 2, 0, 0), (1, width, ch, 3, 0, 0)]
-        part_ogate, part_out, part_in, part_forget, part_mix, part_group, part_bias, part_phase = finish(
+        part_ogate, part_out, part_in, part_forget, part_mix, part_group, part_bias, part_phase, _ = finish(
             here, flat((ra, ra_got), (rb, rb_got)), z_bits, moves,
             [
                 (ours(per, width), w_ogate), (ours(per, width), w_out), (ours(per, width), w_in), (ours(per, ch), w_forget),
@@ -916,15 +957,15 @@
             [(4, 4, [(0, 0), (2, 2), (3, 3)]), (5, 5, [(1, 1)])], (1, 3 * ch, 6), nseq, "mixer_out",
         )
     else:
-        mixed_out = output()
+        mixed_out, _ = output()
 
         def plain(keep, got, cols_n, tall_n=1):
             shape = [2] * len(rest) + [tall_n * per, cols_n]
             return plain_reduce([keep.reshape(shape), got.reshape(shape)], rest, ndp, nseq)
 
-        guv = plain(gkeep, ggot, 2 * hidden)
-        guv = [guv[:, n * tile : (n + 1) * tile] for n in range(2 * hidden // tile)]
-        part_gate, part_up = jnp.concatenate(guv[0::2], axis=1), jnp.concatenate(guv[1::2], axis=1)
+        guv = [plain(pkeep, pgot, 2 * width), plain(gkeep, ggot, 2 * width)]
+        part_gate = jnp.concatenate([a[:, :width] for a in guv], axis=1)
+        part_up = jnp.concatenate([a[:, width:] for a in guv], axis=1)
         part_down = plain(dkeep, dgot, width, tall)
         mix = plain(okeep, ogot, 2 * width)
         mix = [mix[:, n * ntile : (n + 1) * ntile] for n in range(2 * width // ntile)]

time: 162 us -> 143 us (0.88)
  Pallas kernels: 79.1 us -> 70.8 us
  waiting for transfers between devices: 34.2 us -> 28 us
  local copies, waits for them, and re-layouts: 6.79 us -> 1.4 us
    pallas_call x25 -> x29, Pallas kernels: 79.1 us -> 70.8 us  [call(): pl.pallas_call(body, grid_spec=pltpu.PrefetchScalarGridSpec(num_scalar_pr...]
    ppermute x24 -> x27, waiting for transfers between devices: 29.6 us -> 24 us  [swap(): return lax.ppermute(v, axis, [(i, i ^ bit) for i in range(n)])]
    unnamed x36 -> x30, local copies, waits for them, and re-layouts: 6 us -> 1.4 us
    ppermute x24 -> x27, starting transfers between devices: 26.4 us -> 27.2 us  [swap(): return lax.ppermute(v, axis, [(i, i ^ bit) for i in range(n)])]
  transfers between devices with their start and end apart: 33 -> 36, of which waited for: 14 -> 15; matrix products, arithmetic and copies ran while one was open for 0% -> 0% of each run, Pallas kernels for 27% -> 38%
where the time goes in v3:
time: 143 us; the launch traced here: 142 us
  Pallas kernels  70.8 us (50%)
  starting transfers between devices  40.3 us (28%)
  waiting for transfers between devices  28 us (20%)
    pallas_call x29, Pallas kernels, call(): pl.pallas_call(body, grid_spec=pltpu.PrefetchScalarGridSpec(num_scalar_pr...  70.8 us
    ppermute x27, starting transfers between devices, swap(): return lax.ppermute(v, axis, [(i, i ^ bit) for i in range(n)])  27.2 us
    ppermute x27, waiting for transfers between devices, swap(): return lax.ppermute(v, axis, [(i, i ^ bit) for i in range(n)])  24 us
    ppermute x9, starting transfers between devices, shift_all(): lax.ppermute(payload, axis, [(i, (i + k) % n) for i in range(n)])  13.1 us
    ppermute x9, waiting for transfers between devices, shift_all(): lax.ppermute(payload, axis, [(i, (i + k) % n) for i in range(n)])  4.07 us
  transfers between devices with their start and end apart: 36, of which 15 were waited for; matrix products, arithmetic and copies ran while one was open for 0% of the time, Pallas kernels for 38%

profile of v3, /device:TPU:0, one launch (start us, length us, event | category | flops | bytes accessed | tf_op | source)
XLA Modules:
  0.0 142.4 jit_solution(13114810806159064075)
XLA Ops:
  2.6 5.1 %collective-permute-start.2 = (f32[4,2,384]{2,1,0:T(2,128)S(1)}, f32[4,2,384]{2,1,0:T(2,128)S(1)}, u32[]{:S(2)}, u32[]{:S(2)}) collective-permute-start(f32[4,2,384]{2,1,0:T(2,128)S(1)} %get-tuple-element.123.refs_1_.refs_5_), channel_id=1, source_target_pairs={{0,3},{1,0},{2,1},{3,2},{4,7},{5,4},{6,5},{7,6},{8,11},{9,8},{10,9... | collective-permute-start | bytes 36872 | tf_op jit(solution)/shard_map/ppermute | solution.py:518
  7.7 1.0 collective-permute-start
  9.4 5.1 %project.1 = (bf16[768,768]{1,0:T(8,128)(2,1)S(1)}, bf16[768,768]{1,0:T(8,128)(2,1)S(1)}, bf16[768,768]{1,0:T(8,128)(2,1)S(1)}, bf16[3,256,1152]{2,1,0:T(8,128)(2,1)S(1)}) custom-call(s32[2]{0:T(128)S(1)} %get-tuple-element.121.refs_0_, bf16[768,768]{1,0:T(8,128)(2,1)S(1)} %bitcast.48, f32[768]{0:T(1024)S(1)} %copy-done.6, bf16[768,768]{1,0:T(8,128)(2,1)S(1)} %copy-done.1, ...), custom_call_target="tpu_custom_call" | custom-call | flops 4600000000 | bytes 1 | tf_op jit(solution)/shard_map/project/pallas_call | solution.py:501
  14.7 1.7 %summary.1 = (f32[2,384]{1,0:T(2,128)S(1)}, f32[3,4,8,384]{3,2,1,0:T(8,128)S(1)}, f32[3,4,384]{2,1,0:T(4,128)S(1)}, f32[768,384]{1,0:T(8,128)S(1)}, f32[768,384]...) custom-call(bf16[3,256,1152]{2,1,0:T(8,128)(2,1)S(1)} %get-tuple-element.122.refs_0_.refs_9_, ...), custom_call_target="tpu_custom_call" | custom-call | flops 4600000000 | bytes 1 | tf_op jit(solution)/shard_map/summary/pallas_call | solution.py:501
  16.4 2.9 %collective-permute-start.5 = (f32[3,4,384]{2,1,0:T(4,128)S(1)}, f32[3,4,384]{2,1,0:T(4,128)S(1)}, u32[]{:S(2)}, u32[]{:S(2)}) collective-permute-start(f32[3,4,384]{2,1,0:T(4,128)S(1)} %get-tuple-element.124.refs_1_), channel_id=1, source_target_pairs={{0,3},{1,0},{2,1},{3,2},{4,7},{5,4},{6,5},{7,6},{8,11},{9,8},{10,9... | collective-permute-start | bytes 55304 | tf_op jit(solution)/shard_map/ppermute | solution.py:518
  19.2 1.1 collective-permute-start.4
  20.4 2.8 %hidden_grad.1 = (bf16[768,768]{1,0:T(8,128)(2,1)S(1)}, bf16[768,1536]{1,0:T(8,128)(2,1)S(1)}) custom-call(bf16[768,768]{1,0:T(8,128)(2,1)S(1)} %bitcast.49, bf16[1536,768]{1,0:T(8,128)(2,1)S(1)} %copy-done.9, bf16[256,256]{1,0:T(8,128)(2,1)S(1)} %fusion.2.refs_7_.refs_2_.refs_8_.refs_4_, ...), custom_call_target="tpu_custom_call" | custom-call | flops 2875000064 | bytes 1 | tf_op jit(solution)/shard_map/hidden_grad/pallas_call | solution.py:501
  23.2 1.1 gate.1.refs_16_.refs_6_
  24.3 1.6 %collective-permute-done.3.refs_2_ = f32[3,4,384]{2,1,0:T(4,128)S(1)} collective-permute-done((f32[3,4,384]{2,1,0:T(4,128)S(1)}, f32[3,4,384]{2,1,0:T(4,128)S(1)}, u32[]{:S(2)}, u32[]{:S(2)}) %collective-permute-start.3) | collective-permute-done | bytes 18464 | tf_op jit(solution)/shard_map/ppermute | solution.py:518
  26.0 6.0 %mixer.1 = (bf16[768,768]{1,0:T(8,128)(2,1)S(1)}, bf16[768,768]{1,0:T(8,128)(2,1)S(1)}, f32[3,2,384]{2,1,0:T(2,128)S(1)}, f32[3,2,96]{2,1,0:T(2,128)}, bf16[768,...) custom-call(s32[2]{0:T(128)S(1)} %get-tuple-element.121.refs_0_, f32[3,4,384]{2,1,0:T(4,128)S(1)} %get-tuple-element.124.refs_1_, ...), custom_call_target="tpu_custom_call" | custom-call | flops 9200000000 | bytes 1 | tf_op jit(solution)/shard_map/mixer/pallas_call | solution.py:501
  32.0 5.5 %ffn_first.1 = (bf16[384,1536]{1,0:T(8,128)(2,1)S(1)}, bf16[384,1536]{1,0:T(8,128)(2,1)S(1)}, bf16[768,768]{1,0:T(8,128)(2,1)S(1)}, bf16[768,768]{1,0:T(8,128)(2...) custom-call(s32[2]{0:T(128)S(1)} %get-tuple-element.121.refs_0_, ...), custom_call_target="tpu_custom_call" | custom-call | flops 6899999744 | bytes 1 | tf_op jit(solution)/shard_map/ffn_first/pallas_call | solution.py:501
  37.6 11.1 %ffn_rest.1 = (bf16[384,1536]{1,0:T(8,128)(2,1)S(1)}, bf16[384,1536]{1,0:T(8,128)(2,1)S(1)}, bf16[768,768]{1,0:T(8,128)(2,1)S(1)}, bf16[768,768]{1,0:T(8,128)(2,...) custom-call(s32[2]{0:T(128)S(1)} %get-tuple-element.121.refs_0_, ...), custom_call_target="tpu_custom_call" | custom-call | flops 13799999488 | bytes 1 | tf_op jit(solution)/shard_map/ffn_rest/pallas_call | solution.py:501
  50.2 1.6 %collective-permute-start.9 = (bf16[2,96,768]{2,1,0:T(8,128)(2,1)S(1)}, bf16[2,96,768]{2,1,0:T(8,128)(2,1)S(1)}, u32[]{:S(2)}, u32[]{:S(2)}) collective-permute-start(bf16[2,96,768]{2,1,0:T(8,128)(2,1)S(1)} %get-tuple-element.156), channel_id=1, source_target_pairs={{0,8},{4,12},{8,0},{12,4},{16,24},{20,28},{24,16},{28,20},{1,9},{5... | collective-permute-start | bytes 884744 | tf_op jit(solution)/shard_map/ppermute | solution.py:526
  51.7 1.5 %collective-permute-start.10 = (bf16[2,96,768]{2,1,0:T(8,128)(2,1)S(1)}, bf16[2,96,768]{2,1,0:T(8,128)(2,1)S(1)}, u32[]{:S(2)}, u32[]{:S(2)}) collective-permute-start(bf16[2,96,768]{2,1,0:T(8,128)(2,1)S(1)} %get-tuple-element.158), channel_id=1, source_target_pairs={{0,16},{4,20},{8,24},{12,28},{16,0},{20,4},{24,8},{28,12},{1,17},{... | collective-permute-start | bytes 884744 | tf_op jit(solution)/shard_map/ppermute | solution.py:526
  53.4 1.1 ffn_sum1.1
  54.5 1.6 %collective-permute-start.15 = (bf16[2,96,1536]{2,1,0:T(8,128)(2,1)S(1)}, bf16[2,96,1536]{2,1,0:T(8,128)(2,1)S(1)}, u32[]{:S(2)}, u32[]{:S(2)}) collective-permute-start(bf16[2,96,1536]{2,1,0:T(8,128)(2,1)S(1)} %get-tuple-element.172), channel_id=1, source_target_pairs={{0,8},{4,12},{8,0},{12,4},{16,24},{20,28},{24,16},{28,20},{1,9},{5... | collective-permute-start | bytes 1769480 | tf_op jit(solution)/shard_map/ppermute | solution.py:526
  56.1 1.5 %collective-permute-start.16 = (bf16[2,96,1536]{2,1,0:T(8,128)(2,1)S(1)}, bf16[2,96,1536]{2,1,0:T(8,128)(2,1)S(1)}, u32[]{:S(2)}, u32[]{:S(2)}) collective-permute-start(bf16[2,96,1536]{2,1,0:T(8,128)(2,1)S(1)} %get-tuple-element.175), channel_id=1, source_target_pairs={{0,16},{4,20},{8,24},{12,28},{16,0},{20,4},{24,8},{28,12},{1,17},{... | collective-permute-start | bytes 1769480 | tf_op jit(solution)/shard_map/ppermute | solution.py:526
  57.6 7.9 %turn.1 = (f32[768,768]{1,0:T(8,128)S(1)}, bf16[768,768]{1,0:T(8,128)(2,1)S(1)}, bf16[768,768]{1,0:T(8,128)(2,1)S(1)}, bf16[768,768]{1,0:T(8,128)(2,1)S(1)}) custom-call(f32[768,768]{1,0:T(8,128)S(1)} %get-tuple-element.143.refs_0_, f32[768,768]{1,0:T(8,128)S(1)} %get-tuple-element.132.refs_1_.refs_0_, ...), custom_call_target="tpu_custom_call" | custom-call | flops 8049999872 | bytes 1 | tf_op jit(solution)/shard_map/turn/pallas_call | solution.py:501
  66.4 2.4 %collective-permute-start.13 = (f32[3,2,384]{2,1,0:T(2,128)S(1)}, f32[3,2,384]{2,1,0:T(2,128)S(1)}, u32[]{:S(2)}, u32[]{:S(2)}) collective-permute-start(f32[3,2,384]{2,1,0:T(2,128)S(1)} %get-tuple-element.165.refs_8_.refs_5_), channel_id=1, source_target_pairs={{0,3},{1,0},{2,1},{3,2},{4,7},{5,4},{6,5},{7,6},{8,11},{9,8},{10,9... | collective-permute-start | bytes 27656 | tf_op jit(solution)/shard_map/ppermute | solution.py:518
  69.4 2.4 %mixer_grads.1 = (bf16[384,1536]{1,0:T(8,128)(2,1)S(1)}, bf16[384,1536]{1,0:T(8,128)(2,1)S(1)}) custom-call(bf16[768,768]{1,0:T(8,128)(2,1)S(1)} %get-tuple-element.142.refs_0_, bf16[768,768]{1,0:T(8,128)(2,1)S(1)} %get-tuple-element.152.refs_4_.refs_1_, bf16[768,768]{1,0:T(8,128)(2,1)S(1)} %get-tuple-element.153.refs_2_, ...), custom_call_target="tpu_custom_call" | custom-call | flops 345000000 | bytes 1 | tf_op jit(solution)/shard_map/mixer_grads/pallas_call | solution.py:501
  71.8 1.5 %collective-permute-done.12.refs_10_.refs_7_ = f32[3,2,384]{2,1,0:T(2,128)S(1)} collective-permute-done((f32[3,2,384]{2,1,0:T(2,128)S(1)}, f32[3,2,384]{2,1,0:T(2,128)S(1)}, u32[]{:S(2)}, u32[]{:S(2)}) %collective-permute-start.12) | collective-permute-done | bytes 9248 | tf_op jit(solution)/shard_map/ppermute | solution.py:518
  76.4 4.4 %adjoint.1 = (bf16[768,1152]{1,0:T(8,128)(2,1)S(1)}, f32[2,384]{1,0:T(2,128)S(1)}) custom-call(s32[2]{0:T(128)S(1)} %get-tuple-element.121.refs_0_, f32[3,4,384]{2,1,0:T(4,128)S(1)} %get-tuple-element.124.refs_1_, f32[3,4,384]{2,1,0:T(4,128)S(1)} %collective-permute-done.3.refs_2_, f32[3,4,384]{2,1,0:T(4,128)S(1)} %collective-permute-done.4.refs_3_, ...), custom_call_target="tpu_custom_call" | custom-call | flops 345000000 | bytes 1 | tf_op jit(solution)/shard_map/adjoint/pallas_call | solution.py:501
  80.8 1.7 %input_grads.1 = (bf16[384,1280]{1,0:T(8,128)(2,1)S(1)}, bf16[384,1280]{1,0:T(8,128)(2,1)S(1)}) custom-call(bf16[768,768]{1,0:T(8,128)(2,1)S(1)} %get-tuple-element.142.refs_0_, bf16[768,1152]{1,0:T(8,128)(2,1)S(1)} %get-tuple-element.177.refs_1_.refs_0_, f32[2,384]{1,0:T(2,128)S(1)} %get-tuple-element.178.refs_2_), custom_call_target="tpu_custom_call" | custom-call | flops 345000000 | bytes 1 | tf_op jit(solution)/shard_map/input_grads/pallas_call | solution.py:501
  83.1 2.6 %collective-permute-done.18 = bf16[1,96,2304]{2,1,0:T(8,128)(2,1)S(1)} collective-permute-done((bf16[1,96,2304]{2,1,0:T(8,128)(2,1)S(1)}, bf16[1,96,2304]{2,1,0:T(8,128)(2,1)S(1)}, u32[]{:S(2)}, u32[]{:S(2)}) %collective-permute-start.18) | collective-permute-done | bytes 442400 | tf_op jit(solution)/shard_map/ppermute | solution.py:526
  85.8 1.2 collective-permute-done.19
  87.8 0.9 collective-permute-start.22
  88.7 2.0 %collective-permute-start.23 = (bf16[1,48,2304]{2,1,0:T(8,128)(2,1)S(1)}, bf16[1,48,2304]{2,1,0:T(8,128)(2,1)S(1)}, u32[]{:S(2)}, u32[]{:S(2)}) collective-permute-start(bf16[1,48,2304]{2,1,0:T(8,128)(2,1)S(1)} %get-tuple-element.191), channel_id=1, source_target_pairs={{0,2},{1,3},{2,0},{3,1},{4,6},{5,7},{6,4},{7,5},{8,10},{9,11},{10,... | collective-permute-start | bytes 663560 | tf_op jit(solution)/shard_map/ppermute | solution.py:526
  90.7 1.0 mixer_sum1.1
  92.9 5.5 %tokens.1 = (bf16[768,768]{1,0:T(8,128)(2,1)}, f32[8,128]{1,0:T(8,128)S(1)}) custom-call(bf16[768,1152]{1,0:T(8,128)(2,1)S(1)} %get-tuple-element.177.refs_1_.refs_0_, bf16[768,768]{1,0:T(8,128)(2,1)S(1)} %get-tuple-element.152.refs_4_.refs_1_, bf16[768,768]{1,0:T(8,128)(2,1)S(1)} %copy-done.1, bf16[768,384]{1,0:T(8,128)(2,1)S(1)} %copy-done.2, ...), custom_call_target="tpu_custom_call" | custom-call | flops 345000000 | bytes 1 | tf_op jit(solution)/shard_map/tokens/pallas_call | solution.py:501
  98.5 1.2 collective-permute-done.23.refs_3_
  99.8 2.3 %collective-permute-start.28 = (bf16[1,48,2304]{2,1,0:T(8,128)(2,1)S(1)}, bf16[1,48,2304]{2,1,0:T(8,128)(2,1)S(1)}, u32[]{:S(2)}, u32[]{:S(2)}) collective-permute-start(bf16[1,48,2304]{2,1,0:T(8,128)(2,1)S(1)} %get-tuple-element.194.refs_5_.refs_0_), channel_id=1, source_target_pairs={{0,2},{1,3},{2,0},{3,1},{4,6},{5,7},{6,4},{7,5},{8,10},{9,11},{10,... | collective-permute-start | bytes 663560 | tf_op jit(solution)/shard_map/ppermute | solution.py:526
  102.5 2.4 %collective-permute-done.20.refs_2_ = bf16[2,96,1536]{2,1,0:T(8,128)(2,1)S(1)} collective-permute-done((bf16[2,96,1536]{2,1,0:T(8,128)(2,1)S(1)}, bf16[2,96,1536]{2,1,0:T(8,128)(2,1)S(1)}, u32[]{:S(2)}, u32[]{:S(2)}) %collective-permute-start.20) | collective-permute-done | bytes 589856 | tf_op jit(solution)/shard_map/ppermute | solution.py:526
  106.4 1.5 %collective-permute-start.24 = (bf16[1,96,1536]{2,1,0:T(8,128)(2,1)S(1)}, bf16[1,96,1536]{2,1,0:T(8,128)(2,1)S(1)}, u32[]{:S(2)}, u32[]{:S(2)}) collective-permute-start(bf16[1,96,1536]{2,1,0:T(8,128)(2,1)S(1)} %get-tuple-element.199), channel_id=1, source_target_pairs={{0,16},{4,20},{8,24},{12,28},{16,0},{20,4},{24,8},{28,12},{1,17},{... | collective-permute-start | bytes 884744 | tf_op jit(solution)/shard_map/ppermute | solution.py:526
  107.9 4.0 %out.1 = (bf16[768,768]{1,0:T(8,128)(2,1)}, f32[8,128]{1,0:T(8,128)S(1)}) custom-call(f32[768,768]{1,0:T(8,128)S(1)} %get-tuple-element.132.refs_1_.refs_0_, bf16[768,768]{1,0:T(8,128)(2,1)S(1)} %get-tuple-element.134.refs_7_.refs_1_, bf16[768,768]{1,0:T(8,128)(2,1)S(1)} %get-tuple-element.141.refs_2_, bf16[1536,768]{1,0:T(8,128)(2,1)S(1)} %copy-done.9, ...), custom_call_target="tpu_custom_call" | custom-call | flops 4024999936 | bytes 1 | tf_op jit(solution)/shard_map/out/pallas_call | solution.py:501
  112.0 1.2 collective-permute-done.24
  113.9 1.0 collective-permute-start.27
  114.8 1.2 collective-permute-start.26
  116.1 1.3 collective-permute-start.33
  117.4 1.7 %collective-permute-start.32 = (bf16[1,48,2304]{2,1,0:T(8,128)(2,1)S(1)}, bf16[1,48,2304]{2,1,0:T(8,128)(2,1)S(1)}, u32[]{:S(2)}, u32[]{:S(2)}) collective-permute-start(bf16[1,48,2304]{2,1,0:T(8,128)(2,1)S(1)} %get-tuple-element.208.refs_4_), channel_id=1, source_target_pairs={{0,1},{1,0},{2,3},{3,2},{4,5},{5,4},{6,7},{7,6},{8,9},{9,8},{10,11... | collective-permute-start | bytes 663560 | tf_op jit(solution)/shard_map/ppermute | solution.py:526
  119.1 3.4 %collective-permute-done.27.refs_3_ = bf16[1,48,1280]{2,1,0:T(8,128)(2,1)S(1)} collective-permute-done((bf16[1,48,1280]{2,1,0:T(8,128)(2,1)S(1)}, bf16[1,48,1280]{2,1,0:T(8,128)(2,1)S(1)}, u32[]{:S(2)}, u32[]{:S(2)}) %collective-permute-start.27) | collective-permute-done | bytes 122912 | tf_op jit(solution)/shard_map/ppermute | solution.py:526
  122.4 2.7 %collective-permute-done.26.refs_1_ = bf16[1,48,1536]{2,1,0:T(8,128)(2,1)S(1)} collective-permute-done((bf16[1,48,1536]{2,1,0:T(8,128)(2,1)S(1)}, bf16[1,48,1536]{2,1,0:T(8,128)(2,1)S(1)}, u32[]{:S(2)}, u32[]{:S(2)}) %collective-permute-start.26) | collective-permute-done | bytes 147488 | tf_op jit(solution)/shard_map/ppermute | solution.py:526
  125.3 2.5 %collective-permute-start.31 = (bf16[1,48,1280]{2,1,0:T(8,128)(2,1)S(1)}, bf16[1,48,1280]{2,1,0:T(8,128)(2,1)S(1)}, u32[]{:S(2)}, u32[]{:S(2)}) collective-permute-start(bf16[1,48,1280]{2,1,0:T(8,128)(2,1)S(1)} %get-tuple-element.210.refs_2_), channel_id=1, source_target_pairs={{0,1},{1,0},{2,3},{3,2},{4,5},{5,4},{6,7},{7,6},{8,9},{9,8},{10,11... | collective-permute-start | bytes 368648 | tf_op jit(solution)/shard_map/ppermute | solution.py:526
  127.8 3.0 %collective-permute-done.33 = bf16[1,48,2304]{2,1,0:T(8,128)(2,1)S(1)} collective-permute-done((bf16[1,48,2304]{2,1,0:T(8,128)(2,1)S(1)}, bf16[1,48,2304]{2,1,0:T(8,128)(2,1)S(1)}, u32[]{:S(2)}, u32[]{:S(2)}) %collective-permute-start.33) | collective-permute-done | bytes 221216 | tf_op jit(solution)/shard_map/ppermute | solution.py:526
  130.8 2.0 %ffn_out.1 = (f32[96,1536]{1,0:T(8,128)}, f32[96,1536]{1,0:T(8,128)}, f32[192,768]{1,0:T(8,128)}, f32[96]{0:T(128)}, f32[8,128]{1,0:T(8,128)S(1)}) custom-call(s32[2]{0:T(128)S(1)} %get-tuple-element.121.refs_0_, bf16[48,2304]{1,0:T(8,128)(2,1)S(1)} %bitcast.40, bf16[48,2304]{1,0:T(8,128)(2,1)S(1)} %bitcast.43, bf16[48,2304]{1,0:T(8,128)(2,1)S(1)} %bitcast.41, ...), custom_call_target="tpu_custom_call" | custom-call | flops 920000000 | bytes 1 | tf_op jit(solution)/shard_map/ffn_out/pallas_call | solution.py:501
  132.9 1.1 collective-permute-done.30.refs_1_
  134.7 1.6 %collective-permute-start.35 = (bf16[1,48,1280]{2,1,0:T(8,128)(2,1)S(1)}, bf16[1,48,1280]{2,1,0:T(8,128)(2,1)S(1)}, u32[]{:S(2)}, u32[]{:S(2)}) collective-permute-start(bf16[1,48,1280]{2,1,0:T(8,128)(2,1)S(1)} %get-tuple-element.214), channel_id=1, source_target_pairs={{0,2},{1,3},{2,0},{3,1},{4,6},{5,7},{6,4},{7,5},{8,10},{9,11},{10,... | collective-permute-start | bytes 368648 | tf_op jit(solution)/shard_map/ppermute | solution.py:526
  136.2 4.3 %collective-permute-done.35 = bf16[1,48,1280]{2,1,0:T(8,128)(2,1)S(1)} collective-permute-done((bf16[1,48,1280]{2,1,0:T(8,128)(2,1)S(1)}, bf16[1,48,1280]{2,1,0:T(8,128)(2,1)S(1)}, u32[]{:S(2)}, u32[]{:S(2)}) %collective-permute-start.35) | collective-permute-done | bytes 122912 | tf_op jit(solution)/shard_map/ppermute | solution.py:526
  140.6 1.8 %mixer_out.1 = (f32[96,768]{1,0:T(8,128)}, f32[96,768]{1,0:T(8,128)}, f32[96,768]{1,0:T(8,128)}, f32[96,384]{1,0:T(8,128)}, f32[96]{0:T(128)}, /*index=5*/f32[96...) custom-call(s32[2]{0:T(128)S(1)} %get-tuple-element.121.refs_0_, bf16[48,1536]{1,0:T(8,128)(2,1)S(1)} %bitcast.44, ...), custom_call_target="tpu_custom_call" | custom-call | flops 920000000 | bytes 1 | tf_op jit(solution)/shard_map/mixer_out/pallas_call | solution.py:501
  (89 shorter events, 15.3 us)
Async XLA Ops:
  2.0 7.3 %copy-start.2 = (bf16[768,384]{1,0:T(8,128)(2,1)S(1)}, bf16[768,384]{1,0:T(8,128)(2,1)}, u32[]{:S(2)}) copy-start(bf16[768,384]{1,0:T(8,128)(2,1)} %refs_8_.1) | copy-start | bytes 1769476
  2.0 7.3 %copy-start.10 = (bf16[3,256,768]{2,1,0:T(8,128)(2,1)S(1)}, bf16[3,256,768]{2,1,0:T(8,128)(2,1)}, u32[]{:S(2)}) copy-start(bf16[3,256,768]{2,1,0:T(8,128)(2,1)} %param.15) | copy-start | bytes 3538948
  2.6 6.7 %copy-start.1 = (bf16[768,768]{1,0:T(8,128)(2,1)S(1)}, bf16[768,768]{1,0:T(8,128)(2,1)}, u32[]{:S(2)}) copy-start(bf16[768,768]{1,0:T(8,128)(2,1)} %refs_7_.5) | copy-start | bytes 3538948
  2.6 6.7 %copy-start.6 = (f32[768]{0:T(1024)S(1)}, f32[768]{0:T(1024)}, u32[]{:S(2)}) copy-start(f32[768]{0:T(1024)} %refs_9_.1) | copy-start | bytes 9220
  2.6 6.7 %copy-start.13 = (f32[384]{0:T(512)S(1)}, f32[384]{0:T(512)}, u32[]{:S(2)}) copy-start(f32[384]{0:T(512)} %refs_5_.4) | copy-start | bytes 4612
  2.6 12.0 %collective-permute-start.2 = (f32[4,2,384]{2,1,0:T(2,128)S(1)}, f32[4,2,384]{2,1,0:T(2,128)S(1)}, u32[]{:S(2)}, u32[]{:S(2)}) collective-permute-start(f32[4,2,384]{2,1,0:T(2,128)S(1)} %get-tuple-element.123.refs_1_.refs_5_), channel_id=1, source_target_pairs={{0,3},{1,0},{2,1},{3,2},{4,7},{5,4},{6,5},{7,6},{8,11},{9,8},{10,9... | collective-permute-start | bytes 36872 | tf_op jit(solution)/shard_map/ppermute | solution.py:518
  7.7 6.9 %collective-permute-start.1 = (f32[4,2,384]{2,1,0:T(2,128)S(1)}, f32[4,2,384]{2,1,0:T(2,128)S(1)}, u32[]{:S(2)}, u32[]{:S(2)}) collective-permute-start(f32[4,2,384]{2,1,0:T(2,128)S(1)} %get-tuple-element.123.refs_1_.refs_5_), channel_id=1, source_target_pairs={{0,2},{1,3},{2,0},{3,1},{4,6},{5,7},{6,4},{7,5},{8,10},{9,11},{10,... | collective-permute-start | bytes 36872 | tf_op jit(solution)/shard_map/ppermute | solution.py:518
  7.7 6.9 %collective-permute-start = (f32[4,2,384]{2,1,0:T(2,128)S(1)}, f32[4,2,384]{2,1,0:T(2,128)S(1)}, u32[]{:S(2)}, u32[]{:S(2)}) collective-permute-start(f32[4,2,384]{2,1,0:T(2,128)S(1)} %get-tuple-element.123.refs_1_.refs_5_), channel_id=1, source_target_pairs={{0,1},{1,2},{2,3},{3,0},{4,5},{5,6},{6,7},{7,4},{8,9},{9,10},{10,1... | collective-permute-start | bytes 36872 | tf_op jit(solution)/shard_map/ppermute | solution.py:518
  14.7 5.7 %copy-start.9 = (bf16[1536,768]{1,0:T(8,128)(2,1)S(1)}, bf16[1536,768]{1,0:T(8,128)(2,1)}, u32[]{:S(2)}) copy-start(bf16[1536,768]{1,0:T(8,128)(2,1)} %refs_3_.9) | copy-start | bytes 7077892
  14.7 5.7 %copy-start.11 = (bf16[3,256,768]{2,1,0:T(8,128)(2,1)S(1)}, bf16[3,256,768]{2,1,0:T(8,128)(2,1)}, u32[]{:S(2)}) copy-start(bf16[3,256,768]{2,1,0:T(8,128)(2,1)} %param.29) | copy-start | bytes 3538948
  16.4 7.9 %collective-permute-start.5 = (f32[3,4,384]{2,1,0:T(4,128)S(1)}, f32[3,4,384]{2,1,0:T(4,128)S(1)}, u32[]{:S(2)}, u32[]{:S(2)}) collective-permute-start(f32[3,4,384]{2,1,0:T(4,128)S(1)} %get-tuple-element.124.refs_1_), channel_id=1, source_target_pairs={{0,3},{1,0},{2,1},{3,2},{4,7},{5,4},{6,5},{7,6},{8,11},{9,8},{10,9... | collective-permute-start | bytes 55304 | tf_op jit(solution)/shard_map/ppermute | solution.py:518
  19.2 5.1 %collective-permute-start.4 = (f32[3,4,384]{2,1,0:T(4,128)S(1)}, f32[3,4,384]{2,1,0:T(4,128)S(1)}, u32[]{:S(2)}, u32[]{:S(2)}) collective-permute-start(f32[3,4,384]{2,1,0:T(4,128)S(1)} %get-tuple-element.124.refs_1_), channel_id=1, source_target_pairs={{0,2},{1,3},{2,0},{3,1},{4,6},{5,7},{6,4},{7,5},{8,10},{9,11},{10,... | collective-permute-start | bytes 55304 | tf_op jit(solution)/shard_map/ppermute | solution.py:518
  20.4 5.6 %collective-permute-start.3 = (f32[3,4,384]{2,1,0:T(4,128)S(1)}, f32[3,4,384]{2,1,0:T(4,128)S(1)}, u32[]{:S(2)}, u32[]{:S(2)}) collective-permute-start(f32[3,4,384]{2,1,0:T(4,128)S(1)} %get-tuple-element.124.refs_1_), channel_id=1, source_target_pairs={{0,1},{1,2},{2,3},{3,0},{4,5},{5,6},{6,7},{7,4},{8,9},{9,10},{10,1... | collective-permute-start | bytes 55304 | tf_op jit(solution)/shard_map/ppermute | solution.py:518
  20.4 2.8 %copy-start = (bf16[768,768]{1,0:T(8,128)(2,1)S(1)}, bf16[768,768]{1,0:T(8,128)(2,1)}, u32[]{:S(2)}) copy-start(bf16[768,768]{1,0:T(8,128)(2,1)} %refs_5_.7) | copy-start | bytes 3538948
  23.2 2.7 %copy-start.5 = (bf16[768,768]{1,0:T(8,128)(2,1)S(1)}, bf16[768,768]{1,0:T(8,128)(2,1)}, u32[]{:S(2)}) copy-start(bf16[768,768]{1,0:T(8,128)(2,1)} %refs_6_.5) | copy-start | bytes 3538948
  25.9 6.0 %copy-start.3 = (bf16[768,1536]{1,0:T(8,128)(2,1)S(1)}, bf16[768,1536]{1,0:T(8,128)(2,1)}, u32[]{:S(2)}) copy-start(bf16[768,1536]{1,0:T(8,128)(2,1)} %refs_5_.6) | copy-start | bytes 7077892
  25.9 6.0 %copy-start.4 = (bf16[768,1536]{1,0:T(8,128)(2,1)S(1)}, bf16[768,1536]{1,0:T(8,128)(2,1)}, u32[]{:S(2)}) copy-start(bf16[768,1536]{1,0:T(8,128)(2,1)} %refs_6_.4) | copy-start | bytes 7077892
  25.9 6.0 %copy-start.7 = (f32[768]{0:T(1024)S(1)}, f32[768]{0:T(1024)}, u32[]{:S(2)}) copy-start(f32[768]{0:T(1024)} %refs_7_.4) | copy-start | bytes 9220
  37.5 11.8 %collective-permute-start.8 = (bf16[384,1536]{1,0:T(8,128)(2,1)S(1)}, bf16[384,1536]{1,0:T(8,128)(2,1)S(1)}, u32[]{:S(2)}, u32[]{:S(2)}) collective-permute-start(bf16[384,1536]{1,0:T(8,128)(2,1)S(1)} %get-tuple-element.140.refs_10_), channel_id=1, source_target_pairs={{0,4},{4,0},{8,12},{12,8},{16,20},{20,16},{24,28},{28,24},{1,5},{5... | collective-permute-start | bytes 3538952 | tf_op jit(solution)/shard_map/ppermute | solution.py:526
  48.7 4.5 %collective-permute-start.6 = (bf16[384,1536]{1,0:T(8,128)(2,1)S(1)}, bf16[384,1536]{1,0:T(8,128)(2,1)S(1)}, u32[]{:S(2)}, u32[]{:S(2)}) collective-permute-start(bf16[384,1536]{1,0:T(8,128)(2,1)S(1)} %get-tuple-element.146), channel_id=1, source_target_pairs={{0,4},{4,0},{8,12},{12,8},{16,20},{20,16},{24,28},{28,24},{1,5},{5... | collective-permute-start | bytes 3538952 | tf_op jit(solution)/shard_map/ppermute | solution.py:526
  49.3 4.2 %collective-permute-start.7 = (bf16[768,768]{1,0:T(8,128)(2,1)S(1)}, bf16[768,768]{1,0:T(8,128)(2,1)S(1)}, u32[]{:S(2)}, u32[]{:S(2)}) collective-permute-start(bf16[768,768]{1,0:T(8,128)(2,1)S(1)} %get-tuple-element.148), channel_id=1, source_target_pairs={{0,4},{4,0},{8,12},{12,8},{16,20},{20,16},{24,28},{28,24},{1,5},{5... | collective-permute-start | bytes 3538952 | tf_op jit(solution)/shard_map/ppermute | solution.py:526
  50.2 15.3 %collective-permute-start.9 = (bf16[2,96,768]{2,1,0:T(8,128)(2,1)S(1)}, bf16[2,96,768]{2,1,0:T(8,128)(2,1)S(1)}, u32[]{:S(2)}, u32[]{:S(2)}) collective-permute-start(bf16[2,96,768]{2,1,0:T(8,128)(2,1)S(1)} %get-tuple-element.156), channel_id=1, source_target_pairs={{0,8},{4,12},{8,0},{12,4},{16,24},{20,28},{24,16},{28,20},{1,9},{5... | collective-permute-start | bytes 884744 | tf_op jit(solution)/shard_map/ppermute | solution.py:526
  51.7 13.8 %collective-permute-start.10 = (bf16[2,96,768]{2,1,0:T(8,128)(2,1)S(1)}, bf16[2,96,768]{2,1,0:T(8,128)(2,1)S(1)}, u32[]{:S(2)}, u32[]{:S(2)}) collective-permute-start(bf16[2,96,768]{2,1,0:T(8,128)(2,1)S(1)} %get-tuple-element.158), channel_id=1, source_target_pairs={{0,16},{4,20},{8,24},{12,28},{16,0},{20,4},{24,8},{28,12},{1,17},{... | collective-permute-start | bytes 884744 | tf_op jit(solution)/shard_map/ppermute | solution.py:526
  54.5 19.7 %collective-permute-start.15 = (bf16[2,96,1536]{2,1,0:T(8,128)(2,1)S(1)}, bf16[2,96,1536]{2,1,0:T(8,128)(2,1)S(1)}, u32[]{:S(2)}, u32[]{:S(2)}) collective-permute-start(bf16[2,96,1536]{2,1,0:T(8,128)(2,1)S(1)} %get-tuple-element.172), channel_id=1, source_target_pairs={{0,8},{4,12},{8,0},{12,4},{16,24},{20,28},{24,16},{28,20},{1,9},{5... | collective-permute-start | bytes 1769480 | tf_op jit(solution)/shard_map/ppermute | solution.py:526
  56.1 18.1 %collective-permute-start.16 = (bf16[2,96,1536]{2,1,0:T(8,128)(2,1)S(1)}, bf16[2,96,1536]{2,1,0:T(8,128)(2,1)S(1)}, u32[]{:S(2)}, u32[]{:S(2)}) collective-permute-start(bf16[2,96,1536]{2,1,0:T(8,128)(2,1)S(1)} %get-tuple-element.175), channel_id=1, source_target_pairs={{0,16},{4,20},{8,24},{12,28},{16,0},{20,4},{24,8},{28,12},{1,17},{... | collective-permute-start | bytes 1769480 | tf_op jit(solution)/shard_map/ppermute | solution.py:526
  66.4 5.4 %collective-permute-start.13 = (f32[3,2,384]{2,1,0:T(2,128)S(1)}, f32[3,2,384]{2,1,0:T(2,128)S(1)}, u32[]{:S(2)}, u32[]{:S(2)}) collective-permute-start(f32[3,2,384]{2,1,0:T(2,128)S(1)} %get-tuple-element.165.refs_8_.refs_5_), channel_id=1, source_target_pairs={{0,3},{1,0},{2,1},{3,2},{4,7},{5,4},{6,5},{7,6},{8,11},{9,8},{10,9... | collective-permute-start | bytes 27656 | tf_op jit(solution)/shard_map/ppermute | solution.py:518
  68.8 4.6 %collective-permute-start.12 = (f32[3,2,384]{2,1,0:T(2,128)S(1)}, f32[3,2,384]{2,1,0:T(2,128)S(1)}, u32[]{:S(2)}, u32[]{:S(2)}) collective-permute-start(f32[3,2,384]{2,1,0:T(2,128)S(1)} %get-tuple-element.165.refs_8_.refs_5_), channel_id=1, source_target_pairs={{0,2},{1,3},{2,0},{3,1},{4,6},{5,7},{6,4},{7,5},{8,10},{9,11},{10,... | collective-permute-start | bytes 27656 | tf_op jit(solution)/shard_map/ppermute | solution.py:518
  68.8 5.5 %collective-permute-start.11 = (f32[3,2,384]{2,1,0:T(2,128)S(1)}, f32[3,2,384]{2,1,0:T(2,128)S(1)}, u32[]{:S(2)}, u32[]{:S(2)}) collective-permute-start(f32[3,2,384]{2,1,0:T(2,128)S(1)} %get-tuple-element.165.refs_8_.refs_5_), channel_id=1, source_target_pairs={{0,1},{1,2},{2,3},{3,0},{4,5},{5,6},{6,7},{7,4},{8,9},{9,10},{10,1... | collective-permute-start | bytes 27656 | tf_op jit(solution)/shard_map/ppermute | solution.py:518
  75.1 10.7 %collective-permute-start.18 = (bf16[1,96,2304]{2,1,0:T(8,128)(2,1)S(1)}, bf16[1,96,2304]{2,1,0:T(8,128)(2,1)S(1)}, u32[]{:S(2)}, u32[]{:S(2)}) collective-permute-start(bf16[1,96,2304]{2,1,0:T(8,128)(2,1)S(1)} %get-tuple-element.181), channel_id=1, source_target_pairs={{0,16},{4,20},{8,24},{12,28},{16,0},{20,4},{24,8},{28,12},{1,17},{... | collective-permute-start | bytes 1327112 | tf_op jit(solution)/shard_map/ppermute | solution.py:526
  75.9 11.1 %collective-permute-start.19 = (bf16[1,96,2304]{2,1,0:T(8,128)(2,1)S(1)}, bf16[1,96,2304]{2,1,0:T(8,128)(2,1)S(1)}, u32[]{:S(2)}, u32[]{:S(2)}) collective-permute-start(bf16[1,96,2304]{2,1,0:T(8,128)(2,1)S(1)} %get-tuple-element.183), channel_id=1, source_target_pairs={{0,8},{4,12},{8,0},{12,4},{16,24},{20,28},{24,16},{28,20},{1,9},{5... | collective-permute-start | bytes 1327112 | tf_op jit(solution)/shard_map/ppermute | solution.py:526
  76.4 14.3 %collective-permute-start.14 = (bf16[384,1536]{1,0:T(8,128)(2,1)S(1)}, bf16[384,1536]{1,0:T(8,128)(2,1)S(1)}, u32[]{:S(2)}, u32[]{:S(2)}) collective-permute-start(bf16[384,1536]{1,0:T(8,128)(2,1)S(1)} %get-tuple-element.164.refs_7_), channel_id=1, source_target_pairs={{0,4},{4,0},{8,12},{12,8},{16,20},{20,16},{24,28},{28,24},{1,5},{5... | collective-permute-start | bytes 3538952 | tf_op jit(solution)/shard_map/ppermute | solution.py:526
  82.6 8.1 %collective-permute-start.17 = (bf16[384,1280]{1,0:T(8,128)(2,1)S(1)}, bf16[384,1280]{1,0:T(8,128)(2,1)S(1)}, u32[]{:S(2)}, u32[]{:S(2)}) collective-permute-start(bf16[384,1280]{1,0:T(8,128)(2,1)S(1)} %get-tuple-element.180.refs_5_), channel_id=1, source_target_pairs={{0,4},{4,0},{8,12},{12,8},{16,20},{20,16},{24,28},{28,24},{1,5},{5... | collective-permute-start | bytes 2949128 | tf_op jit(solution)/shard_map/ppermute | solution.py:526
  87.8 10.7 %collective-permute-start.22 = (bf16[1,48,2304]{2,1,0:T(8,128)(2,1)S(1)}, bf16[1,48,2304]{2,1,0:T(8,128)(2,1)S(1)}, u32[]{:S(2)}, u32[]{:S(2)}) collective-permute-start(bf16[1,48,2304]{2,1,0:T(8,128)(2,1)S(1)} %get-tuple-element.189), channel_id=1, source_target_pairs={{0,1},{1,0},{2,3},{3,2},{4,5},{5,4},{6,7},{7,6},{8,9},{9,8},{10,11... | collective-permute-start | bytes 663560 | tf_op jit(solution)/shard_map/ppermute | solution.py:526
  88.7 11.0 %collective-permute-start.23 = (bf16[1,48,2304]{2,1,0:T(8,128)(2,1)S(1)}, bf16[1,48,2304]{2,1,0:T(8,128)(2,1)S(1)}, u32[]{:S(2)}, u32[]{:S(2)}) collective-permute-start(bf16[1,48,2304]{2,1,0:T(8,128)(2,1)S(1)} %get-tuple-element.191), channel_id=1, source_target_pairs={{0,2},{1,3},{2,0},{3,1},{4,6},{5,7},{6,4},{7,5},{8,10},{9,11},{10,... | collective-permute-start | bytes 663560 | tf_op jit(solution)/shard_map/ppermute | solution.py:526
  91.7 10.8 %collective-permute-start.21 = (bf16[2,96,1280]{2,1,0:T(8,128)(2,1)S(1)}, bf16[2,96,1280]{2,1,0:T(8,128)(2,1)S(1)}, u32[]{:S(2)}, u32[]{:S(2)}) collective-permute-start(bf16[2,96,1280]{2,1,0:T(8,128)(2,1)S(1)} %get-tuple-element.188), channel_id=1, source_target_pairs={{0,16},{4,20},{8,24},{12,28},{16,0},{20,4},{24,8},{28,12},{1,17},{... | collective-permute-start | bytes 1474568 | tf_op jit(solution)/shard_map/ppermute | solution.py:526
  92.3 12.6 %collective-permute-start.20 = (bf16[2,96,1536]{2,1,0:T(8,128)(2,1)S(1)}, bf16[2,96,1536]{2,1,0:T(8,128)(2,1)S(1)}, u32[]{:S(2)}, u32[]{:S(2)}) collective-permute-start(bf16[2,96,1536]{2,1,0:T(8,128)(2,1)S(1)} %get-tuple-element.186), channel_id=1, source_target_pairs={{0,8},{4,12},{8,0},{12,4},{16,24},{20,28},{24,16},{28,20},{1,9},{5... | collective-permute-start | bytes 1769480 | tf_op jit(solution)/shard_map/ppermute | solution.py:526
  99.8 16.2 %collective-permute-start.29 = (bf16[1,48,2304]{2,1,0:T(8,128)(2,1)S(1)}, bf16[1,48,2304]{2,1,0:T(8,128)(2,1)S(1)}, u32[]{:S(2)}, u32[]{:S(2)}) collective-permute-start(bf16[1,48,2304]{2,1,0:T(8,128)(2,1)S(1)} %get-tuple-element.207.refs_2_), channel_id=1, source_target_pairs={{0,1},{1,0},{2,3},{3,2},{4,5},{5,4},{6,7},{7,6},{8,9},{9,8},{10,11... | collective-permute-start | bytes 663560 | tf_op jit(solution)/shard_map/ppermute | solution.py:526
  99.8 16.2 %collective-permute-start.28 = (bf16[1,48,2304]{2,1,0:T(8,128)(2,1)S(1)}, bf16[1,48,2304]{2,1,0:T(8,128)(2,1)S(1)}, u32[]{:S(2)}, u32[]{:S(2)}) collective-permute-start(bf16[1,48,2304]{2,1,0:T(8,128)(2,1)S(1)} %get-tuple-element.194.refs_5_.refs_0_), channel_id=1, source_target_pairs={{0,2},{1,3},{2,0},{3,1},{4,6},{5,7},{6,4},{7,5},{8,10},{9,11},{10,... | collective-permute-start | bytes 663560 | tf_op jit(solution)/shard_map/ppermute | solution.py:526
  105.7 6.3 %collective-permute-start.25 = (bf16[1,96,1280]{2,1,0:T(8,128)(2,1)S(1)}, bf16[1,96,1280]{2,1,0:T(8,128)(2,1)S(1)}, u32[]{:S(2)}, u32[]{:S(2)}) collective-permute-start(bf16[1,96,1280]{2,1,0:T(8,128)(2,1)S(1)} %get-tuple-element.201), channel_id=1, source_target_pairs={{0,8},{4,12},{8,0},{12,4},{16,24},{20,28},{24,16},{28,20},{1,9},{5... | collective-permute-start | bytes 737288 | tf_op jit(solution)/shard_map/ppermute | solution.py:526
  106.4 6.7 %collective-permute-start.24 = (bf16[1,96,1536]{2,1,0:T(8,128)(2,1)S(1)}, bf16[1,96,1536]{2,1,0:T(8,128)(2,1)S(1)}, u32[]{:S(2)}, u32[]{:S(2)}) collective-permute-start(bf16[1,96,1536]{2,1,0:T(8,128)(2,1)S(1)} %get-tuple-element.199), channel_id=1, source_target_pairs={{0,16},{4,20},{8,24},{12,28},{16,0},{20,4},{24,8},{28,12},{1,17},{... | collective-permute-start | bytes 884744 | tf_op jit(solution)/shard_map/ppermute | solution.py:526
  113.9 8.6 %collective-permute-start.27 = (bf16[1,48,1280]{2,1,0:T(8,128)(2,1)S(1)}, bf16[1,48,1280]{2,1,0:T(8,128)(2,1)S(1)}, u32[]{:S(2)}, u32[]{:S(2)}) collective-permute-start(bf16[1,48,1280]{2,1,0:T(8,128)(2,1)S(1)} %get-tuple-element.206), channel_id=1, source_target_pairs={{0,2},{1,3},{2,0},{3,1},{4,6},{5,7},{6,4},{7,5},{8,10},{9,11},{10,... | collective-permute-start | bytes 368648 | tf_op jit(solution)/shard_map/ppermute | solution.py:526
  114.8 10.3 %collective-permute-start.26 = (bf16[1,48,1536]{2,1,0:T(8,128)(2,1)S(1)}, bf16[1,48,1536]{2,1,0:T(8,128)(2,1)S(1)}, u32[]{:S(2)}, u32[]{:S(2)}) collective-permute-start(bf16[1,48,1536]{2,1,0:T(8,128)(2,1)S(1)} %get-tuple-element.204), channel_id=1, source_target_pairs={{0,1},{1,0},{2,3},{3,2},{4,5},{5,4},{6,7},{7,6},{8,9},{9,8},{10,11... | collective-permute-start | bytes 442376 | tf_op jit(solution)/shard_map/ppermute | solution.py:526
  116.1 14.7 %collective-permute-start.33 = (bf16[1,48,2304]{2,1,0:T(8,128)(2,1)S(1)}, bf16[1,48,2304]{2,1,0:T(8,128)(2,1)S(1)}, u32[]{:S(2)}, u32[]{:S(2)}) collective-permute-start(bf16[1,48,2304]{2,1,0:T(8,128)(2,1)S(1)} %get-tuple-element.211), channel_id=1, source_target_pairs={{0,2},{1,3},{2,0},{3,1},{4,6},{5,7},{6,4},{7,5},{8,10},{9,11},{10,... | collective-permute-start | bytes 663560 | tf_op jit(solution)/shard_map/ppermute | solution.py:526
  117.4 13.4 %collective-permute-start.32 = (bf16[1,48,2304]{2,1,0:T(8,128)(2,1)S(1)}, bf16[1,48,2304]{2,1,0:T(8,128)(2,1)S(1)}, u32[]{:S(2)}, u32[]{:S(2)}) collective-permute-start(bf16[1,48,2304]{2,1,0:T(8,128)(2,1)S(1)} %get-tuple-element.208.refs_4_), channel_id=1, source_target_pairs={{0,1},{1,0},{2,3},{3,2},{4,5},{5,4},{6,7},{7,6},{8,9},{9,8},{10,11... | collective-permute-start | bytes 663560 | tf_op jit(solution)/shard_map/ppermute | solution.py:526
  125.2 8.8 %collective-permute-start.30 = (bf16[1,48,1536]{2,1,0:T(8,128)(2,1)S(1)}, bf16[1,48,1536]{2,1,0:T(8,128)(2,1)S(1)}, u32[]{:S(2)}, u32[]{:S(2)}) collective-permute-start(bf16[1,48,1536]{2,1,0:T(8,128)(2,1)S(1)} %get-tuple-element.209.refs_8_.refs_0_), channel_id=1, source_target_pairs={{0,2},{1,3},{2,0},{3,1},{4,6},{5,7},{6,4},{7,5},{8,10},{9,11},{10,... | collective-permute-start | bytes 442376 | tf_op jit(solution)/shard_map/ppermute | solution.py:526
  125.3 7.5 %collective-permute-start.31 = (bf16[1,48,1280]{2,1,0:T(8,128)(2,1)S(1)}, bf16[1,48,1280]{2,1,0:T(8,128)(2,1)S(1)}, u32[]{:S(2)}, u32[]{:S(2)}) collective-permute-start(bf16[1,48,1280]{2,1,0:T(8,128)(2,1)S(1)} %get-tuple-element.210.refs_2_), channel_id=1, source_target_pairs={{0,1},{1,0},{2,3},{3,2},{4,5},{5,4},{6,7},{7,6},{8,9},{9,8},{10,11... | collective-permute-start | bytes 368648 | tf_op jit(solution)/shard_map/ppermute | solution.py:526
  134.1 6.5 %collective-permute-start.34 = (bf16[1,48,1536]{2,1,0:T(8,128)(2,1)S(1)}, bf16[1,48,1536]{2,1,0:T(8,128)(2,1)S(1)}, u32[]{:S(2)}, u32[]{:S(2)}) collective-permute-start(bf16[1,48,1536]{2,1,0:T(8,128)(2,1)S(1)} %get-tuple-element.213), channel_id=1, source_target_pairs={{0,1},{1,0},{2,3},{3,2},{4,5},{5,4},{6,7},{7,6},{8,9},{9,8},{10,11... | collective-permute-start | bytes 442376 | tf_op jit(solution)/shard_map/ppermute | solution.py:526
  134.7 5.9 %collective-permute-start.35 = (bf16[1,48,1280]{2,1,0:T(8,128)(2,1)S(1)}, bf16[1,48,1280]{2,1,0:T(8,128)(2,1)S(1)}, u32[]{:S(2)}, u32[]{:S(2)}) collective-permute-start(bf16[1,48,1280]{2,1,0:T(8,128)(2,1)S(1)} %get-tuple-element.214), channel_id=1, source_target_pairs={{0,2},{1,3},{2,0},{3,1},{4,6},{5,7},{6,4},{7,5},{8,10},{9,11},{10,... | collective-permute-start | bytes 368648 | tf_op jit(solution)/shard_map/ppermute | solution.py:526
  (3 other events, 4.1 us)

commit v4 on v3

--- a/solution.py
+++ b/solution.py
@@ -12,7 +12,7 @@
 LANES = 128
 RANK, PLACE = 0, 1
 MICROSECONDS = dict(
-    project=4, summary=4, hidden_grad=2.5, mixer=8, ffn_first=6, ffn_rest=12, turn=7, chains=0.3, mixer_grads=0.3, adjoint=0.3, input_grads=0.3, tokens=0.3, ffn_sum4=8, out=3.5,
+    project=4, summary=4, hidden_grad=2.5, mixer=8, ffn_first=6, ffn_rest=12, turn=7, chains=0.3, mixer_grads=0.01, adjoint=3.74, input_grads=0.3, tokens=0.3, ffn_sum4=8, out=3.5,
     ffn_sum1=1.3, mixer_sum1=1.0, ffn_sum2=3, ffn_sum3=20,
 )
 COST = 1.15e9
@@ -66,6 +66,21 @@
 
 def at_step(t):
     return slice(CHUNKS * t, CHUNKS * (t + 1))
+
+
+def apart(v, perm_ref):
+    n = perm_ref.shape[0]
+    parts = [dot(v[:, c : c + n], perm_ref[...]).astype(BF) for c in range(0, v.shape[1], n)]
+    return jnp.concatenate([p[:, : n // 2] for p in parts] + [p[:, n // 2 :] for p in parts], axis=1)
+
+
+def together(re, im, perm_ref):
+    n = perm_ref.shape[0] // 2
+    parts = [
+        dot(jnp.concatenate([re[:, c : c + n], im[:, c : c + n]], axis=1), perm_ref[...], NT)
+        for c in range(0, re.shape[1], n)
+    ]
+    return jnp.concatenate(parts, axis=1)
 
 
 def reorder(order_ref, v, back=False):
@@ -99,7 +114,7 @@
     normed_ref[...] = normed
     put_halves(turned_ref, normed.T, 0, lo, bit_of(here_ref, PLACE, first))
     mixed = dot(normed, w_in_ref[...]).astype(BF)
-    pre_ref[:, :width] = dot(mixed, perm_ref[...]).astype(BF)
+    pre_ref[:, :width] = apart(mixed, perm_ref)
     pre_ref[:, width:] = (dot(normed, w_forget_ref[...]) + bias_ref[...][None]).astype(BF)
 
 
@@ -172,9 +187,9 @@
         hr, hi = hr + drv_re[at_step(t), :], hi + drv_im[at_step(t), :]
         st_re[at_step(t), :] = hr
         st_im[at_step(t), :] = hi
-    split = jnp.concatenate([st_re[...].astype(BF), st_im[...].astype(BF)], axis=1)
-    split_ref[...] = split
-    yf = dot(split, perm_ref[...], NT)
+    re, im = st_re[...].astype(BF), st_im[...].astype(BF)
+    split_ref[:, :ch], split_ref[:, ch:] = re, im
+    yf = together(re, im, perm_ref)
     y_ref[...] = yf.astype(BF)
     member = member_ref[...]
     inv = group_spread(lax.rsqrt(group_mean(yf * yf, member) + epsilon), member)
@@ -219,9 +234,9 @@
 
 
 def ffn_rest_kernel(
-    here_ref, n_ref, nt_ref, cot_ref, wg_ref, wu_ref, dh_ref, hid0_ref, dgv0_ref, duv0_ref,
-    gsend_ref, gkeep_ref, dsend_ref, dkeep_ref, hid_ref, dn_ref,
-    dgv_ref, duv_ref, ht_ref,
+    here_ref, n_ref, nt_ref, cot_ref, wg_ref, wu_ref, dh_ref, hid0_ref,
+    gsend_ref, gkeep_ref, dsend_ref, dkeep_ref, hid_ref, dgv_ref, duv_ref,
+    ht_ref,
     *, lo, rt, first,
 ):
     bit = bit_of(here_ref, PLACE, first)
@@ -240,13 +255,17 @@
         out = slice(j * half, (j + 1) * half)
         dsend_ref[out, :] = dot(ht_ref[j, :half, :], cot_ref[...]).astype(BF)
         dkeep_ref[out, :] = dot(ht_ref[j, half:, :], cot_ref[...]).astype(BF)
-    for rows in spans:
-        dn_ref[rows, :] = (
-            dot(dgv0_ref[rows, :], wg_ref[:, own], NT)
-            + dot(duv0_ref[rows, :], wu_ref[:, own], NT)
-            + dot(dgv_ref[rows, :], wg_ref[:, cut], NT)
-            + dot(duv_ref[rows, :], wu_ref[:, cut], NT)
-        )
+
+
+def ffn_back_kernel(dgv0_ref, duv0_ref, dgv_ref, duv_ref, wg_ref, wu_ref, dn_ref):
+    width = dn_ref.shape[1]
+    own, cut = slice(0, width), slice(width, 2 * width)
+    dn_ref[...] = (
+        dot(dgv0_ref[...], wg_ref[:, own], NT)
+        + dot(duv0_ref[...], wu_ref[:, own], NT)
+        + dot(dgv_ref[...], wg_ref[:, cut], NT)
+        + dot(duv_ref[...], wu_ref[:, cut], NT)
+    )
 
 
 def gate_kernel(normed_ref, w_ref, og_ref):
@@ -279,7 +298,7 @@
     dog_ref[...] = (dgated * gunit * gain * silu_slope(og, sig)).astype(BF)
     through = dgated * og * sig * gain
     dy = (ginv * (through - gunit * group_spread(group_mean(through * gunit, member), member))).astype(BF)
-    split_ref[...] = dot(dy, perm_ref[...]).astype(BF)
+    split_ref[...] = apart(dy, perm_ref)
 
 
 def chains_kernel(split_ref, lam_re, lam_im, chunk_ref, chain_ref, total_ref, dy_re, dy_im):
@@ -351,7 +370,7 @@
     dre = (keep * gr * silu_slope(pin_re, sig_re)).astype(BF)
     dim = (keep * gi * silu_slope(pin_im, sig_im)).astype(BF)
     dpz = (forget * keep * df).astype(BF)
-    dpre_ref[:, : 2 * ch] = dot(jnp.concatenate([dre, dim], axis=1), perm_ref[...], NT).astype(BF)
+    dpre_ref[:, : 2 * ch] = together(dre, dim, perm_ref).astype(BF)
     dpre_ref[:, 2 * ch :] = dpz
     sums = jnp.concatenate(
         [
@@ -681,14 +700,15 @@
     scan_scratch = [pltpu.VMEM((span, ch), F32)] * 2
 
     infos, here = call(
-        own_kernel, 1, [(whole(), phase), (whole(), init_state.transpose(0, 2, 1))],
+        own_kernel, 1, [(full(mine), phase), (full(segs, 2, mine), init_state.transpose(0, 2, 1))],
         [(whole(), (1 + segs, 2, ch), F32), (("smem",), (2,), jnp.int32)],
         [pltpu.VMEM((-(-(2 + 2 * segs) // 8) * 8, ch), F32)], [], "own",
     )
     infos = shift_all(infos, "seq", nseq)
 
     col = jnp.arange(width)
-    perm = (col[:, None] == 2 * (col % ch)[None, :] + (col // ch)[None, :]).astype(BF)
+    pair = jnp.arange(2 * LANES)
+    perm = (pair[:, None] == 2 * (pair % LANES)[None, :] + (pair // LANES)[None, :]).astype(BF)
     member = ((col[:, None] // (width // GROUPS)) == jnp.arange(LANES)[None, :]).astype(BF)
 
     place_of = jnp.arange(span)
@@ -699,7 +719,7 @@
         functools.partial(project_kernel, lo=lo, first=first), segs,
         [
             (rows(span, width), tokens.reshape(count, width)), (whole(width), norm_mix), (whole(width, width), w_in),
-            (whole(width, ch), w_forget), (whole(ch), forget_bias), (whole(width, width), perm), step_order,
+            (whole(width, ch), w_forget), (whole(ch), forget_bias), (whole(), perm), step_order,
         ],
         [
             (rows(span, width), (count, width), BF),
@@ -737,7 +757,7 @@
         + [(seg(2, ch, shift=1), i) for i in infos]
         + [
             (scan, lam_re), (scan, lam_im), (scan, drv_re), (scan, drv_im), (seg(4, CHUNKS, ch), chunk),
-            (whole(width, width), perm), (rows(span, width), x), (rows(span, width), og), (whole(width), norm_group),
+            (whole(), perm), (rows(span, width), x), (rows(span, width), og), (whole(width), norm_group),
             (whole(width, LANES), member), (whole(width, width), w_out),
         ],
         [
@@ -763,13 +783,12 @@
         [], [here], "ffn_first", (), 7,
     )
     pgot = swap(psend, "dp", ndp, first)
-    gsend, gkeep, dsend, dkeep, hid, dn = call(
+    gsend, gkeep, dsend, dkeep, hid, dgv1, duv1 = call(
         functools.partial(ffn_rest_kernel, lo=lo * tall, rt=span, first=first), 1,
-        [(whole(), a) for a in (normed_ffn, normed_ffn_t, cot, w_gate, w_up, dh, hid0, dgv0, duv0)],
-        [(whole(), (width // 2, 2 * width), BF)] * 2
-        + [(whole(), (hidden // 2, width), BF)] * 2
-        + [(whole(), wide, BF), (whole(), wide, F32)],
-        [pltpu.VMEM(wide, BF), pltpu.VMEM(wide, BF), pltpu.VMEM((tall, width, count), BF)], [here], "ffn_rest", (psend,), 7,
+        [(whole(), a) for a in (normed_ffn, normed_ffn_t, cot, w_gate, w_up, dh, hid0)],
+        [(whole(), (width // 2, 2 * width), BF)] * 2 + [(whole(), (hidden // 2, width), BF)] * 2
+        + [(whole(), wide, BF)] * 3,
+        [pltpu.VMEM((tall, width, count), BF)], [here], "ffn_rest", (psend,), 7,
     )
     ggot, dgot = swap(gsend, "dp", ndp, first), swap(dsend, "dp", ndp, first)
 
@@ -780,6 +799,13 @@
 
     def blocks(a, cols_n, tall_n=1):
         return a.reshape(nblk * tall_n, per, cols_n)
+
+    def ffn_back(*after):
+        return call(
+            ffn_back_kernel, segs,
+            [(rows(span, width), a) for a in (dgv0, duv0, dgv1, duv1)] + [(whole(), w_gate), (whole(), w_up)],
+            [(rows(span, width), wide, F32)], [], [], "ffn_back", after,
+        )[0]
 
     order = ()
     if fast:
@@ -788,21 +814,25 @@
             here, [(0, x_bit, [(p, 1, 0, 0, width)]), (1, y_bit, [(p, 1, 0, 1, width)])], "first_sum1", (gkeep,)
         )
         pa_got, pb_got = swap(pa_send, "dp", ndp, rest[0]), swap(pb_send, "dp", ndp, rest[1])
+        dn = ffn_back(pa_keep)
         g = [blocks(a, 2 * width) for a in (gkeep, ggot)]
         d = [blocks(a, width, tall) for a in (dkeep, dgot)]
         (fa_send, fa_keep), (fb_send, fb_keep) = combine(
             here, [(0, x_bit, [(g, 1, 0, 0, 2 * width)]), (1, y_bit, [(d, tall, i, 0, width) for i in range(tall)])],
-            "ffn_sum1", (pa_keep,),
+            "ffn_sum1", (dn,),
         )
         fa_got, fb_got = swap(fa_send, "dp", ndp, rest[0]), swap(fb_send, "dp", ndp, rest[1])
         order = (fa_keep,)
+
+    else:
+        dn = ffn_back()
 
     dmiddle, dbranch, dog, dy_split = call(
         turn_kernel, segs,
         [
             (rows(span, width), dn), (rows(span, width), middle), (rows(span, width), cot), (whole(width), norm_ffn),
             (whole(width, width), w_out), (rows(span, width), y), (rows(span, width), og), (whole(width), norm_group),
-            (whole(width, LANES), member), (whole(width, width), perm),
+            (whole(width, LANES), member), (whole(), perm),
         ],
         [
             (rows(span, width), (count, width), F32),
@@ -824,6 +854,25 @@
         scan_scratch, [], "chains", order,
     )
     adjs = shift_all(adj, "seq", nseq)
+    order = ()
+    if fast:
+        def one(keep, got):
+            return [([keep, got], 1, 0, 0, keep.shape[2])]
+
+        def rows_of(keep, got):
+            return one(*(a.reshape(2, per // 2, a.shape[2]) for a in (keep, got)))
+
+        (fa_send, fa_keep), (fb_send, fb_keep) = combine(
+            here,
+            [
+                (0, y_bit, [([pa], 1, 0, 0, width)] + one(fa_keep, fa_got)),
+                (0, x_bit, [([pb], 1, 0, 0, width)] + one(fb_keep, fb_got)),
+            ],
+            "ffn_sum2", (chain,),
+        )
+        fa_got, fb_got = swap(fa_send, "dp", ndp, rest[1]), swap(fb_send, "dp", ndp, rest[0])
+        order = (fa_keep,)
+
     ntile = width // 3
     osend, okeep = call(
         functools.partial(grads_kernel, pairs=2), width // ntile,
@@ -835,28 +884,10 @@
             (cols(width // 2, 2 * ntile), (width // 2, 2 * width), BF),
             (cols(width // 2, 2 * ntile), (width // 2, 2 * width), BF),
         ],
-        [], [], "mixer_grads", (chain,),
+        [], [], "mixer_grads", order,
     )
     late, *adjs = lax.optimization_barrier((osend, *adjs))
     ogot = swap(late, "dp", ndp, first)
-    order = ()
-    if fast:
-        def one(keep, got):
-            return [([keep, got], 1, 0, 0, keep.shape[2])]
-
-        def rows_of(keep, got):
-            return one(*(a.reshape(2, per // 2, a.shape[2]) for a in (keep, got)))
-
-        (fa_send, fa_keep), (fb_send, fb_keep) = combine(
-            here,
-            [
-                (0, y_bit, [([pa], 1, 0, 0, width)] + one(fa_keep, fa_got)),
-                (0, x_bit, [([pb], 1, 0, 0, width)] + one(fb_keep, fb_got)),
-            ],
-            "ffn_sum2", (osend, *adjs),
-        )
-        fa_got, fb_got = swap(fa_send, "dp", ndp, rest[1]), swap(fb_send, "dp", ndp, rest[0])
-        order = (fa_keep,)
 
     dpre, sums = call(
         functools.partial(adjoint_kernel, ranks=nseq), segs,
@@ -865,10 +896,10 @@
             (seg(span, 3 * ch), pre), (whole(2, ch), trig), (scan, lam_re), (scan, lam_im),
             (rows(span, width), dy_split),
             (rows(span, width), y_split), (seg(2, ch), start),
-            (seg(4, CHUNKS, ch), chunk), (seg(2, CHUNKS, ch), chain), (whole(width, width), perm),
+            (seg(4, CHUNKS, ch), chunk), (seg(2, CHUNKS, ch), chain), (whole(), perm),
         ],
         [(rows(span, 3 * ch), (count, 3 * ch), BF), (whole(2, ch), (2, ch), F32)],
-        scan_scratch, [here], "adjoint", order,
+        scan_scratch, [here], "adjoint", (osend,),
     )
     into = 3 * ch + LANES
     isend, ikeep = call(
@@ -932,6 +963,9 @@
         ra, rb = add_pairs([(ra_keep, ra_got), (rb_keep, rb_got)], "mixer_sum4", (fa,))
         ra_got, rb_got = over(ra, nseq, other), over(rb, nseq, lead)
 
+        ra, rb = add_pairs([(ra, ra_got), (rb, rb_got)], "mixer_sum5")
+        ra_got, rb_got = over(ra, nseq, lead), over(rb, nseq, other)
+
         def flat(*pairs):
             return [tuple(a.reshape(per // 2, a.shape[2]) for a in pair) for pair in pairs]
 
@@ -943,8 +977,6 @@
             [(full, (per, hidden)), (full, (per, hidden)), (full, (tall * per, width)), (full, (per,))],
             [(3, 2, [(0, 0), (1, 1)])], None, nseq, "ffn_out", (ra,),
         )
-        ra, rb = add_pairs([(ra, ra_got), (rb, rb_got)], "mixer_sum5", (ffn_done,))
-        ra_got, rb_got = over(ra, nseq, lead), over(rb, nseq, other)
         moves = [(0, n * ntile, ntile, n % 2, 0, (n // 2) * ntile) for n in range(2 * width // ntile)]
         moves += [(1, 0, width, 2, 0, 0), (1, width, ch, 3, 0, 0)]
         part_ogate, part_out, part_in, part_forget, part_mix, part_group, part_bias, part_phase, _ = finish(

time: 143 us -> 140 us (0.979)
  starting transfers between devices: 40.3 us -> 46.7 us
  waiting for transfers between devices: 28 us -> 22.4 us
  Pallas kernels: 70.8 us -> 68.1 us
    ppermute x9, waiting for transfers between devices: 4.07 us -> 0.02 us  [shift_all(): lax.ppermute(payload, axis, [(i, (i + k) % n) for i in range(n)])]
    ppermute x27, starting transfers between devices: 27.2 us -> 30.8 us  [swap(): return lax.ppermute(v, axis, [(i, i ^ bit) for i in range(n)])]
    ppermute x9, starting transfers between devices: 13.1 us -> 15.9 us  [shift_all(): lax.ppermute(payload, axis, [(i, (i + k) % n) for i in range(n)])]
    pallas_call x29 -> x30, Pallas kernels: 70.8 us -> 68.1 us  [call(): pl.pallas_call(body, grid_spec=pltpu.PrefetchScalarGridSpec(num_scalar_pr...]
    ppermute x27, waiting for transfers between devices: 24 us -> 22.4 us  [swap(): return lax.ppermute(v, axis, [(i, i ^ bit) for i in range(n)])]
  transfers between devices with their start and end apart: 36 -> 36, of which waited for: 15 -> 12; matrix products, arithmetic and copies ran while one was open for 0% -> 0% of each run, Pallas kernels for 38% -> 38%
where the time goes in v4:
time: 140 us
  Pallas kernels  68.1 us (49%)
  starting transfers between devices  46.7 us (33%)
  waiting for transfers between devices  22.4 us (16%)
  local copies, waits for them, and re-layouts  1.51 us (1%)
    pallas_call x30, Pallas kernels, call(): pl.pallas_call(body, grid_spec=pltpu.PrefetchScalarGridSpec(num_scalar_pr...  68.1 us
    ppermute x27, starting transfers between devices, swap(): return lax.ppermute(v, axis, [(i, i ^ bit) for i in range(n)])  30.8 us
    ppermute x27, waiting for transfers between devices, swap(): return lax.ppermute(v, axis, [(i, i ^ bit) for i in range(n)])  22.4 us
    ppermute x9, starting transfers between devices, shift_all(): lax.ppermute(payload, axis, [(i, (i + k) % n) for i in range(n)])  15.9 us
  transfers between devices with their start and end apart: 36, of which 12 were waited for; matrix products, arithmetic and copies ran while one was open for 0% of the time, Pallas kernels for 38%

profile of v4, /device:TPU:0, one launch (start us, length us, event | category | flops | bytes accessed | tf_op | source)
XLA Modules:
  0.0 140.1 jit_solution(3870657064345845893)
XLA Ops:
  2.6 3.1 %collective-permute-start = (f32[4,2,384]{2,1,0:T(2,128)S(1)}, f32[4,2,384]{2,1,0:T(2,128)S(1)}, u32[]{:S(2)}, u32[]{:S(2)}) collective-permute-start(f32[4,2,384]{2,1,0:T(2,128)S(1)} %get-tuple-element.123.refs_1_.refs_5_), channel_id=1, source_target_pairs={{0,1},{1,2},{2,3},{3,0},{4,5},{5,6},{6,7},{7,4},{8,9},{9,10},{10,1... | collective-permute-start | bytes 36872 | tf_op jit(solution)/shard_map/ppermute | solution.py:537
  5.7 2.6 %collective-permute-start.1 = (f32[4,2,384]{2,1,0:T(2,128)S(1)}, f32[4,2,384]{2,1,0:T(2,128)S(1)}, u32[]{:S(2)}, u32[]{:S(2)}) collective-permute-start(f32[4,2,384]{2,1,0:T(2,128)S(1)} %get-tuple-element.123.refs_1_.refs_5_), channel_id=1, source_target_pairs={{0,2},{1,3},{2,0},{3,1},{4,6},{5,7},{6,4},{7,5},{8,10},{9,11},{10,... | collective-permute-start | bytes 36872 | tf_op jit(solution)/shard_map/ppermute | solution.py:537
  8.3 1.3 collective-permute-start.2
  9.8 4.5 %project.1 = (bf16[768,768]{1,0:T(8,128)(2,1)S(1)}, bf16[768,768]{1,0:T(8,128)(2,1)S(1)}, bf16[768,768]{1,0:T(8,128)(2,1)S(1)}, bf16[3,256,1152]{2,1,0:T(8,128)(2,1)S(1)}) custom-call(s32[2]{0:T(128)S(1)} %get-tuple-element.121.refs_0_, bf16[768,768]{1,0:T(8,128)(2,1)S(1)} %bitcast.51, f32[768]{0:T(1024)S(1)} %copy-done.6, bf16[768,768]{1,0:T(8,128)(2,1)S(1)} %copy-done.3, ...), custom_call_target="tpu_custom_call" | custom-call | flops 4600000000 | bytes 1 | tf_op jit(solution)/shard_map/project/pallas_call | solution.py:520
  14.6 1.6 %summary.1 = (f32[2,384]{1,0:T(2,128)S(1)}, f32[3,4,8,384]{3,2,1,0:T(8,128)S(1)}, f32[3,4,384]{2,1,0:T(4,128)S(1)}, f32[768,384]{1,0:T(8,128)S(1)}, f32[768,384]...) custom-call(bf16[3,256,1152]{2,1,0:T(8,128)(2,1)S(1)} %get-tuple-element.122.refs_0_.refs_9_, ...), custom_call_target="tpu_custom_call" | custom-call | flops 4600000000 | bytes 1 | tf_op jit(solution)/shard_map/summary/pallas_call | solution.py:520
  17.4 2.7 %collective-permute-start.5 = (f32[3,4,384]{2,1,0:T(4,128)S(1)}, f32[3,4,384]{2,1,0:T(4,128)S(1)}, u32[]{:S(2)}, u32[]{:S(2)}) collective-permute-start(f32[3,4,384]{2,1,0:T(4,128)S(1)} %get-tuple-element.124.refs_1_), channel_id=1, source_target_pairs={{0,3},{1,0},{2,1},{3,2},{4,7},{5,4},{6,5},{7,6},{8,11},{9,8},{10,9... | collective-permute-start | bytes 55304 | tf_op jit(solution)/shard_map/ppermute | solution.py:537
  20.1 2.8 %hidden_grad.1 = (bf16[768,768]{1,0:T(8,128)(2,1)S(1)}, bf16[768,1536]{1,0:T(8,128)(2,1)S(1)}) custom-call(bf16[768,768]{1,0:T(8,128)(2,1)S(1)} %bitcast.52, bf16[1536,768]{1,0:T(8,128)(2,1)S(1)} %copy-done.9, bf16[256,256]{1,0:T(8,128)(2,1)S(1)} %get-tuple-element.228.refs_7_.refs_2_.refs_8_.refs_4_, ...), custom_call_target="tpu_custom_call" | custom-call | flops 2875000064 | bytes 1 | tf_op jit(solution)/shard_map/hidden_grad/pallas_call | solution.py:520
  22.9 1.1 gate.1.refs_16_.refs_6_
  24.2 5.3 %mixer.1 = (bf16[768,768]{1,0:T(8,128)(2,1)S(1)}, bf16[768,768]{1,0:T(8,128)(2,1)S(1)}, f32[3,2,384]{2,1,0:T(2,128)S(1)}, f32[3,2,96]{2,1,0:T(2,128)}, bf16[768,...) custom-call(s32[2]{0:T(128)S(1)} %get-tuple-element.121.refs_0_, f32[3,4,384]{2,1,0:T(4,128)S(1)} %get-tuple-element.124.refs_1_, ...), custom_call_target="tpu_custom_call" | custom-call | flops 9200000000 | bytes 1 | tf_op jit(solution)/shard_map/mixer/pallas_call | solution.py:520
  29.5 5.5 %ffn_first.1 = (bf16[384,1536]{1,0:T(8,128)(2,1)S(1)}, bf16[384,1536]{1,0:T(8,128)(2,1)S(1)}, bf16[768,768]{1,0:T(8,128)(2,1)S(1)}, bf16[768,768]{1,0:T(8,128)(2...) custom-call(s32[2]{0:T(128)S(1)} %get-tuple-element.121.refs_0_, ...), custom_call_target="tpu_custom_call" | custom-call | flops 6899999744 | bytes 1 | tf_op jit(solution)/shard_map/ffn_first/pallas_call | solution.py:520
  35.1 7.1 %ffn_rest.1 = (bf16[384,1536]{1,0:T(8,128)(2,1)S(1)}, bf16[384,1536]{1,0:T(8,128)(2,1)S(1)}, bf16[768,768]{1,0:T(8,128)(2,1)S(1)}, bf16[768,768]{1,0:T(8,128)(2,...) custom-call(s32[2]{0:T(128)S(1)} %get-tuple-element.121.refs_0_, ...), custom_call_target="tpu_custom_call" | custom-call | flops 13799999488 | bytes 1 | tf_op jit(solution)/shard_map/ffn_rest/pallas_call | solution.py:520
  42.8 0.8 first_sum1.1
  43.6 1.6 %collective-permute-start.10 = (bf16[2,96,768]{2,1,0:T(8,128)(2,1)S(1)}, bf16[2,96,768]{2,1,0:T(8,128)(2,1)S(1)}, u32[]{:S(2)}, u32[]{:S(2)}) collective-permute-start(bf16[2,96,768]{2,1,0:T(8,128)(2,1)S(1)} %get-tuple-element.158), channel_id=1, source_target_pairs={{0,16},{4,20},{8,24},{12,28},{16,0},{20,4},{24,8},{28,12},{1,17},{... | collective-permute-start | bytes 884744 | tf_op jit(solution)/shard_map/ppermute | solution.py:545
  45.2 1.5 %collective-permute-start.9 = (bf16[2,96,768]{2,1,0:T(8,128)(2,1)S(1)}, bf16[2,96,768]{2,1,0:T(8,128)(2,1)S(1)}, u32[]{:S(2)}, u32[]{:S(2)}) collective-permute-start(bf16[2,96,768]{2,1,0:T(8,128)(2,1)S(1)} %get-tuple-element.156), channel_id=1, source_target_pairs={{0,8},{4,12},{8,0},{12,4},{16,24},{20,28},{24,16},{28,20},{1,9},{5... | collective-permute-start | bytes 884744 | tf_op jit(solution)/shard_map/ppermute | solution.py:545
  46.7 4.3 %ffn_back.1.refs_5_.refs_0_ = f32[768,768]{1,0:T(8,128)S(1)} custom-call(bf16[768,768]{1,0:T(8,128)(2,1)S(1)} %get-tuple-element.141.refs_0_, bf16[768,768]{1,0:T(8,128)(2,1)S(1)} %get-tuple-element.142.refs_1_, bf16[768,768]{1,0:T(8,128)(2,1)S(1)} %get-tuple-element.143.refs_2_, bf16[768,768]{1,0:T(8,128)(2,1)S(1)} %get-tuple-element.144.refs_3_, ...), custom_call_target="tpu_custom_call" | custom-call | flops 920000000 | bytes 1 | tf_op jit(solution)/shard_map/ffn_back/pallas_call | solution.py:520
  51.0 1.1 ffn_sum1.1
  53.2 6.8 %turn.1 = (f32[768,768]{1,0:T(8,128)S(1)}, bf16[768,768]{1,0:T(8,128)(2,1)S(1)}, bf16[768,768]{1,0:T(8,128)(2,1)S(1)}, bf16[768,768]{1,0:T(8,128)(2,1)S(1)}) custom-call(f32[768,768]{1,0:T(8,128)S(1)} %ffn_back.1.refs_5_.refs_0_, f32[768,768]{1,0:T(8,128)S(1)} %get-tuple-element.132.refs_1_.refs_0_, bf16[768,768]{1,0:T(8,128)(2,1)S(1)} %get-tuple-element.137.refs_3_.refs_2_, ...), custom_call_target="tpu_custom_call" | custom-call | flops 8049999872 | bytes 1 | tf_op jit(solution)/shard_map/turn/pallas_call | solution.py:520
  61.6 1.5 %collective-permute-start.14 = (f32[3,2,384]{2,1,0:T(2,128)S(1)}, f32[3,2,384]{2,1,0:T(2,128)S(1)}, u32[]{:S(2)}, u32[]{:S(2)}) collective-permute-start(f32[3,2,384]{2,1,0:T(2,128)S(1)} %get-tuple-element.171.refs_5_), channel_id=1, source_target_pairs={{0,2},{1,3},{2,0},{3,1},{4,6},{5,7},{6,4},{7,5},{8,10},{9,11},{10,... | collective-permute-start | bytes 27656 | tf_op jit(solution)/shard_map/ppermute | solution.py:537
  63.1 2.8 %collective-permute-start.15 = (f32[3,2,384]{2,1,0:T(2,128)S(1)}, f32[3,2,384]{2,1,0:T(2,128)S(1)}, u32[]{:S(2)}, u32[]{:S(2)}) collective-permute-start(f32[3,2,384]{2,1,0:T(2,128)S(1)} %get-tuple-element.171.refs_5_), channel_id=1, source_target_pairs={{0,3},{1,0},{2,1},{3,2},{4,7},{5,4},{6,5},{7,6},{8,11},{9,8},{10,9... | collective-permute-start | bytes 27656 | tf_op jit(solution)/shard_map/ppermute | solution.py:537
  66.0 1.3 collective-permute-done.11.refs_3_
  67.6 0.8 ffn_sum2.1
  69.0 1.5 %collective-permute-start.19 = (bf16[1,96,2304]{2,1,0:T(8,128)(2,1)S(1)}, bf16[1,96,2304]{2,1,0:T(8,128)(2,1)S(1)}, u32[]{:S(2)}, u32[]{:S(2)}) collective-permute-start(bf16[1,96,2304]{2,1,0:T(8,128)(2,1)S(1)} %get-tuple-element.184), channel_id=1, source_target_pairs={{0,8},{4,12},{8,0},{12,4},{16,24},{20,28},{24,16},{28,20},{1,9},{5... | collective-permute-start | bytes 1327112 | tf_op jit(solution)/shard_map/ppermute | solution.py:545
  70.5 2.4 %mixer_grads.1 = (bf16[384,1536]{1,0:T(8,128)(2,1)S(1)}, bf16[384,1536]{1,0:T(8,128)(2,1)S(1)}) custom-call(bf16[768,768]{1,0:T(8,128)(2,1)S(1)} %get-tuple-element.140.refs_0_, bf16[768,768]{1,0:T(8,128)(2,1)S(1)} %get-tuple-element.153.refs_4_.refs_1_, bf16[768,768]{1,0:T(8,128)(2,1)S(1)} %get-tuple-element.154.refs_2_, ...), custom_call_target="tpu_custom_call" | custom-call | flops 11500000 | bytes 1 | tf_op jit(solution)/shard_map/mixer_grads/pallas_call | solution.py:520
  72.9 3.7 %adjoint.1 = (bf16[768,1152]{1,0:T(8,128)(2,1)S(1)}, f32[2,384]{1,0:T(2,128)S(1)}) custom-call(s32[2]{0:T(128)S(1)} %get-tuple-element.121.refs_0_, f32[3,4,384]{2,1,0:T(4,128)S(1)} %get-tuple-element.124.refs_1_, f32[3,4,384]{2,1,0:T(4,128)S(1)} %collective-permute-done.3.refs_2_, f32[3,4,384]{2,1,0:T(4,128)S(1)} %collective-permute-done.4.refs_3_, ...), custom_call_target="tpu_custom_call" | custom-call | flops 4301000192 | bytes 1 | tf_op jit(solution)/shard_map/adjoint/pallas_call | solution.py:520
  76.6 1.7 %input_grads.1 = (bf16[384,1280]{1,0:T(8,128)(2,1)S(1)}, bf16[384,1280]{1,0:T(8,128)(2,1)S(1)}) custom-call(bf16[768,768]{1,0:T(8,128)(2,1)S(1)} %get-tuple-element.140.refs_0_, bf16[768,1152]{1,0:T(8,128)(2,1)S(1)} %get-tuple-element.178.refs_1_.refs_0_, f32[2,384]{1,0:T(2,128)S(1)} %get-tuple-element.179.refs_2_), custom_call_target="tpu_custom_call" | custom-call | flops 345000000 | bytes 1 | tf_op jit(solution)/shard_map/input_grads/pallas_call | solution.py:520
  79.5 0.7 ffn_sum3.1
  80.9 1.5 %collective-permute-start.23 = (bf16[1,48,2304]{2,1,0:T(8,128)(2,1)S(1)}, bf16[1,48,2304]{2,1,0:T(8,128)(2,1)S(1)}, u32[]{:S(2)}, u32[]{:S(2)}) collective-permute-start(bf16[1,48,2304]{2,1,0:T(8,128)(2,1)S(1)} %get-tuple-element.192), channel_id=1, source_target_pairs={{0,2},{1,3},{2,0},{3,1},{4,6},{5,7},{6,4},{7,5},{8,10},{9,11},{10,... | collective-permute-start | bytes 663560 | tf_op jit(solution)/shard_map/ppermute | solution.py:545
  82.6 1.0 mixer_sum1.1
  83.7 1.6 %collective-permute-start.20 = (bf16[2,96,1536]{2,1,0:T(8,128)(2,1)S(1)}, bf16[2,96,1536]{2,1,0:T(8,128)(2,1)S(1)}, u32[]{:S(2)}, u32[]{:S(2)}) collective-permute-start(bf16[2,96,1536]{2,1,0:T(8,128)(2,1)S(1)} %get-tuple-element.187), channel_id=1, source_target_pairs={{0,8},{4,12},{8,0},{12,4},{16,24},{20,28},{24,16},{28,20},{1,9},{5... | collective-permute-start | bytes 1769480 | tf_op jit(solution)/shard_map/ppermute | solution.py:545
  85.3 1.5 %collective-permute-start.21 = (bf16[2,96,1280]{2,1,0:T(8,128)(2,1)S(1)}, bf16[2,96,1280]{2,1,0:T(8,128)(2,1)S(1)}, u32[]{:S(2)}, u32[]{:S(2)}) collective-permute-start(bf16[2,96,1280]{2,1,0:T(8,128)(2,1)S(1)} %get-tuple-element.189), channel_id=1, source_target_pairs={{0,16},{4,20},{8,24},{12,28},{16,0},{20,4},{24,8},{28,12},{1,17},{... | collective-permute-start | bytes 1474568 | tf_op jit(solution)/shard_map/ppermute | solution.py:545
  86.8 5.5 %tokens.1 = (bf16[768,768]{1,0:T(8,128)(2,1)}, f32[8,128]{1,0:T(8,128)S(1)}) custom-call(bf16[768,1152]{1,0:T(8,128)(2,1)S(1)} %get-tuple-element.178.refs_1_.refs_0_, bf16[768,768]{1,0:T(8,128)(2,1)S(1)} %get-tuple-element.153.refs_4_.refs_1_, bf16[768,768]{1,0:T(8,128)(2,1)S(1)} %copy-done.3, bf16[768,384]{1,0:T(8,128)(2,1)S(1)} %copy-done.4, ...), custom_call_target="tpu_custom_call" | custom-call | flops 345000000 | bytes 1 | tf_op jit(solution)/shard_map/tokens/pallas_call | solution.py:520
  92.4 1.5 %collective-permute-start.28 = (bf16[1,48,2304]{2,1,0:T(8,128)(2,1)S(1)}, bf16[1,48,2304]{2,1,0:T(8,128)(2,1)S(1)}, u32[]{:S(2)}, u32[]{:S(2)}) collective-permute-start(bf16[1,48,2304]{2,1,0:T(8,128)(2,1)S(1)} %get-tuple-element.195.refs_5_.refs_0_), channel_id=1, source_target_pairs={{0,2},{1,3},{2,0},{3,1},{4,6},{5,7},{6,4},{7,5},{8,10},{9,11},{10,... | collective-permute-start | bytes 663560 | tf_op jit(solution)/shard_map/ppermute | solution.py:545
  93.9 2.9 %collective-permute-start.29 = (bf16[1,48,2304]{2,1,0:T(8,128)(2,1)S(1)}, bf16[1,48,2304]{2,1,0:T(8,128)(2,1)S(1)}, u32[]{:S(2)}, u32[]{:S(2)}) collective-permute-start(bf16[1,48,2304]{2,1,0:T(8,128)(2,1)S(1)} %get-tuple-element.208.refs_2_), channel_id=1, source_target_pairs={{0,1},{1,0},{2,3},{3,2},{4,5},{5,4},{6,7},{7,6},{8,9},{9,8},{10,11... | collective-permute-start | bytes 663560 | tf_op jit(solution)/shard_map/ppermute | solution.py:545
  97.3 1.8 %collective-permute-done.20.refs_2_ = bf16[2,96,1536]{2,1,0:T(8,128)(2,1)S(1)} collective-permute-done((bf16[2,96,1536]{2,1,0:T(8,128)(2,1)S(1)}, bf16[2,96,1536]{2,1,0:T(8,128)(2,1)S(1)}, u32[]{:S(2)}, u32[]{:S(2)}) %collective-permute-start.20) | collective-permute-done | bytes 589856 | tf_op jit(solution)/shard_map/ppermute | solution.py:545
  99.1 0.8 mixer_sum2.1
  99.9 1.6 %collective-permute-start.24 = (bf16[1,96,1536]{2,1,0:T(8,128)(2,1)S(1)}, bf16[1,96,1536]{2,1,0:T(8,128)(2,1)S(1)}, u32[]{:S(2)}, u32[]{:S(2)}) collective-permute-start(bf16[1,96,1536]{2,1,0:T(8,128)(2,1)S(1)} %get-tuple-element.200), channel_id=1, source_target_pairs={{0,16},{4,20},{8,24},{12,28},{16,0},{20,4},{24,8},{28,12},{1,17},{... | collective-permute-start | bytes 884744 | tf_op jit(solution)/shard_map/ppermute | solution.py:545
  102.1 4.0 %out.1 = (bf16[768,768]{1,0:T(8,128)(2,1)}, f32[8,128]{1,0:T(8,128)S(1)}) custom-call(f32[768,768]{1,0:T(8,128)S(1)} %get-tuple-element.132.refs_1_.refs_0_, bf16[768,768]{1,0:T(8,128)(2,1)S(1)} %get-tuple-element.134.refs_7_.refs_1_, bf16[768,768]{1,0:T(8,128)(2,1)S(1)} %get-tuple-element.139.refs_2_, bf16[1536,768]{1,0:T(8,128)(2,1)S(1)} %copy-done.9, ...), custom_call_target="tpu_custom_call" | custom-call | flops 4024999936 | bytes 1 | tf_op jit(solution)/shard_map/out/pallas_call | solution.py:520
  106.1 2.3 %collective-permute-done.25 = bf16[1,96,1280]{2,1,0:T(8,128)(2,1)S(1)} collective-permute-done((bf16[1,96,1280]{2,1,0:T(8,128)(2,1)S(1)}, bf16[1,96,1280]{2,1,0:T(8,128)(2,1)S(1)}, u32[]{:S(2)}, u32[]{:S(2)}) %collective-permute-start.25) | collective-permute-done | bytes 245792 | tf_op jit(solution)/shard_map/ppermute | solution.py:545
  109.2 2.1 %collective-permute-start.27 = (bf16[1,48,1280]{2,1,0:T(8,128)(2,1)S(1)}, bf16[1,48,1280]{2,1,0:T(8,128)(2,1)S(1)}, u32[]{:S(2)}, u32[]{:S(2)}) collective-permute-start(bf16[1,48,1280]{2,1,0:T(8,128)(2,1)S(1)} %get-tuple-element.207), channel_id=1, source_target_pairs={{0,2},{1,3},{2,0},{3,1},{4,6},{5,7},{6,4},{7,5},{8,10},{9,11},{10,... | collective-permute-start | bytes 368648 | tf_op jit(solution)/shard_map/ppermute | solution.py:545
  111.4 4.3 %collective-permute-done.27.refs_3_ = bf16[1,48,1280]{2,1,0:T(8,128)(2,1)S(1)} collective-permute-done((bf16[1,48,1280]{2,1,0:T(8,128)(2,1)S(1)}, bf16[1,48,1280]{2,1,0:T(8,128)(2,1)S(1)}, u32[]{:S(2)}, u32[]{:S(2)}) %collective-permute-start.27) | collective-permute-done | bytes 122912 | tf_op jit(solution)/shard_map/ppermute | solution.py:545
  115.8 1.6 %collective-permute-start.30 = (bf16[1,48,1536]{2,1,0:T(8,128)(2,1)S(1)}, bf16[1,48,1536]{2,1,0:T(8,128)(2,1)S(1)}, u32[]{:S(2)}, u32[]{:S(2)}) collective-permute-start(bf16[1,48,1536]{2,1,0:T(8,128)(2,1)S(1)} %get-tuple-element.210.refs_0_), channel_id=1, source_target_pairs={{0,2},{1,3},{2,0},{3,1},{4,6},{5,7},{6,4},{7,5},{8,10},{9,11},{10,... | collective-permute-start | bytes 442376 | tf_op jit(solution)/shard_map/ppermute | solution.py:545
  117.4 2.7 %collective-permute-start.31 = (bf16[1,48,1280]{2,1,0:T(8,128)(2,1)S(1)}, bf16[1,48,1280]{2,1,0:T(8,128)(2,1)S(1)}, u32[]{:S(2)}, u32[]{:S(2)}) collective-permute-start(bf16[1,48,1280]{2,1,0:T(8,128)(2,1)S(1)} %get-tuple-element.211.refs_2_), channel_id=1, source_target_pairs={{0,1},{1,0},{2,3},{3,2},{4,5},{5,4},{6,7},{7,6},{8,9},{9,8},{10,11... | collective-permute-start | bytes 368648 | tf_op jit(solution)/shard_map/ppermute | solution.py:545
  120.1 0.8 collective-permute-start.35
  120.9 5.7 %collective-permute-done.31.refs_3_ = bf16[1,48,1280]{2,1,0:T(8,128)(2,1)S(1)} collective-permute-done((bf16[1,48,1280]{2,1,0:T(8,128)(2,1)S(1)}, bf16[1,48,1280]{2,1,0:T(8,128)(2,1)S(1)}, u32[]{:S(2)}, u32[]{:S(2)}) %collective-permute-start.31) | collective-permute-done | bytes 122912 | tf_op jit(solution)/shard_map/ppermute | solution.py:545
  127.0 4.0 %collective-permute-start.33 = (bf16[1,48,1280]{2,1,0:T(8,128)(2,1)S(1)}, bf16[1,48,1280]{2,1,0:T(8,128)(2,1)S(1)}, u32[]{:S(2)}, u32[]{:S(2)}) collective-permute-start(bf16[1,48,1280]{2,1,0:T(8,128)(2,1)S(1)} %get-tuple-element.213), channel_id=1, source_target_pairs={{0,2},{1,3},{2,0},{3,1},{4,6},{5,7},{6,4},{7,5},{8,10},{9,11},{10,... | collective-permute-start | bytes 368648 | tf_op jit(solution)/shard_map/ppermute | solution.py:545
  131.0 4.5 %collective-permute-done.34 = bf16[1,48,2304]{2,1,0:T(8,128)(2,1)S(1)} collective-permute-done((bf16[1,48,2304]{2,1,0:T(8,128)(2,1)S(1)}, bf16[1,48,2304]{2,1,0:T(8,128)(2,1)S(1)}, u32[]{:S(2)}, u32[]{:S(2)}) %collective-permute-start.34) | collective-permute-done | bytes 221216 | tf_op jit(solution)/shard_map/ppermute | solution.py:545
  135.5 2.1 %ffn_out.1 = (f32[96,1536]{1,0:T(8,128)}, f32[96,1536]{1,0:T(8,128)}, f32[192,768]{1,0:T(8,128)}, f32[96]{0:T(128)}, f32[8,128]{1,0:T(8,128)}) custom-call(s32[2]{0:T(128)S(1)} %get-tuple-element.121.refs_0_, bf16[48,2304]{1,0:T(8,128)(2,1)S(1)} %bitcast.44, bf16[48,2304]{1,0:T(8,128)(2,1)S(1)} %bitcast.46, bf16[48,2304]{1,0:T(8,128)(2,1)S(1)} %bitcast.45, ...), custom_call_target="tpu_custom_call" | custom-call | flops 920000000 | bytes 1 | tf_op jit(solution)/shard_map/ffn_out/pallas_call | solution.py:520
  138.3 1.8 %mixer_out.1 = (f32[96,768]{1,0:T(8,128)}, f32[96,768]{1,0:T(8,128)}, f32[96,768]{1,0:T(8,128)}, f32[96,384]{1,0:T(8,128)}, f32[96]{0:T(128)}, /*index=5*/f32[96...) custom-call(s32[2]{0:T(128)S(1)} %get-tuple-element.121.refs_0_, bf16[48,1536]{1,0:T(8,128)(2,1)S(1)} %bitcast.42, ...), custom_call_target="tpu_custom_call" | custom-call | flops 920000000 | bytes 1 | tf_op jit(solution)/shard_map/mixer_out/pallas_call | solution.py:520
  (89 shorter events, 13.0 us)
Async XLA Ops:
  2.0 7.8 %copy-start.3 = (bf16[768,768]{1,0:T(8,128)(2,1)S(1)}, bf16[768,768]{1,0:T(8,128)(2,1)}, u32[]{:S(2)}) copy-start(bf16[768,768]{1,0:T(8,128)(2,1)} %refs_7_.4) | copy-start | bytes 3538948
  2.0 7.8 %copy-start.4 = (bf16[768,384]{1,0:T(8,128)(2,1)S(1)}, bf16[768,384]{1,0:T(8,128)(2,1)}, u32[]{:S(2)}) copy-start(bf16[768,384]{1,0:T(8,128)(2,1)} %refs_8_.1) | copy-start | bytes 1769476
  2.0 7.8 %copy-start.6 = (f32[768]{0:T(1024)S(1)}, f32[768]{0:T(1024)}, u32[]{:S(2)}) copy-start(f32[768]{0:T(1024)} %refs_9_.1) | copy-start | bytes 9220
  2.0 7.8 %copy-start.10 = (bf16[3,256,768]{2,1,0:T(8,128)(2,1)S(1)}, bf16[3,256,768]{2,1,0:T(8,128)(2,1)}, u32[]{:S(2)}) copy-start(bf16[3,256,768]{2,1,0:T(8,128)(2,1)} %param.15) | copy-start | bytes 3538948
  2.0 7.8 %copy-start.13 = (f32[384]{0:T(512)S(1)}, f32[384]{0:T(512)}, u32[]{:S(2)}) copy-start(f32[384]{0:T(512)} %refs_5_.5) | copy-start | bytes 4612
  2.6 11.9 %collective-permute-start = (f32[4,2,384]{2,1,0:T(2,128)S(1)}, f32[4,2,384]{2,1,0:T(2,128)S(1)}, u32[]{:S(2)}, u32[]{:S(2)}) collective-permute-start(f32[4,2,384]{2,1,0:T(2,128)S(1)} %get-tuple-element.123.refs_1_.refs_5_), channel_id=1, source_target_pairs={{0,1},{1,2},{2,3},{3,0},{4,5},{5,6},{6,7},{7,4},{8,9},{9,10},{10,1... | collective-permute-start | bytes 36872 | tf_op jit(solution)/shard_map/ppermute | solution.py:537
  5.7 8.8 %collective-permute-start.1 = (f32[4,2,384]{2,1,0:T(2,128)S(1)}, f32[4,2,384]{2,1,0:T(2,128)S(1)}, u32[]{:S(2)}, u32[]{:S(2)}) collective-permute-start(f32[4,2,384]{2,1,0:T(2,128)S(1)} %get-tuple-element.123.refs_1_.refs_5_), channel_id=1, source_target_pairs={{0,2},{1,3},{2,0},{3,1},{4,6},{5,7},{6,4},{7,5},{8,10},{9,11},{10,... | collective-permute-start | bytes 36872 | tf_op jit(solution)/shard_map/ppermute | solution.py:537
  8.3 6.2 %collective-permute-start.2 = (f32[4,2,384]{2,1,0:T(2,128)S(1)}, f32[4,2,384]{2,1,0:T(2,128)S(1)}, u32[]{:S(2)}, u32[]{:S(2)}) collective-permute-start(f32[4,2,384]{2,1,0:T(2,128)S(1)} %get-tuple-element.123.refs_1_.refs_5_), channel_id=1, source_target_pairs={{0,3},{1,0},{2,1},{3,2},{4,7},{5,4},{6,5},{7,6},{8,11},{9,8},{10,9... | collective-permute-start | bytes 36872 | tf_op jit(solution)/shard_map/ppermute | solution.py:537
  14.5 5.5 %copy-start.9 = (bf16[1536,768]{1,0:T(8,128)(2,1)S(1)}, bf16[1536,768]{1,0:T(8,128)(2,1)}, u32[]{:S(2)}) copy-start(bf16[1536,768]{1,0:T(8,128)(2,1)} %refs_3_.9) | copy-start | bytes 7077892
  14.5 5.5 %copy-start.11 = (bf16[3,256,768]{2,1,0:T(8,128)(2,1)S(1)}, bf16[3,256,768]{2,1,0:T(8,128)(2,1)}, u32[]{:S(2)}) copy-start(bf16[3,256,768]{2,1,0:T(8,128)(2,1)} %param.29) | copy-start | bytes 3538948
  16.2 7.8 %collective-permute-start.3 = (f32[3,4,384]{2,1,0:T(4,128)S(1)}, f32[3,4,384]{2,1,0:T(4,128)S(1)}, u32[]{:S(2)}, u32[]{:S(2)}) collective-permute-start(f32[3,4,384]{2,1,0:T(4,128)S(1)} %get-tuple-element.124.refs_1_), channel_id=1, source_target_pairs={{0,1},{1,2},{2,3},{3,0},{4,5},{5,6},{6,7},{7,4},{8,9},{9,10},{10,1... | collective-permute-start | bytes 55304 | tf_op jit(solution)/shard_map/ppermute | solution.py:537
  16.9 7.1 %collective-permute-start.4 = (f32[3,4,384]{2,1,0:T(4,128)S(1)}, f32[3,4,384]{2,1,0:T(4,128)S(1)}, u32[]{:S(2)}, u32[]{:S(2)}) collective-permute-start(f32[3,4,384]{2,1,0:T(4,128)S(1)} %get-tuple-element.124.refs_1_), channel_id=1, source_target_pairs={{0,2},{1,3},{2,0},{3,1},{4,6},{5,7},{6,4},{7,5},{8,10},{9,11},{10,... | collective-permute-start | bytes 55304 | tf_op jit(solution)/shard_map/ppermute | solution.py:537
  17.4 6.6 %collective-permute-start.5 = (f32[3,4,384]{2,1,0:T(4,128)S(1)}, f32[3,4,384]{2,1,0:T(4,128)S(1)}, u32[]{:S(2)}, u32[]{:S(2)}) collective-permute-start(f32[3,4,384]{2,1,0:T(4,128)S(1)} %get-tuple-element.124.refs_1_), channel_id=1, source_target_pairs={{0,3},{1,0},{2,1},{3,2},{4,7},{5,4},{6,5},{7,6},{8,11},{9,8},{10,9... | collective-permute-start | bytes 55304 | tf_op jit(solution)/shard_map/ppermute | solution.py:537
  20.1 2.8 %copy-start = (bf16[768,768]{1,0:T(8,128)(2,1)S(1)}, bf16[768,768]{1,0:T(8,128)(2,1)}, u32[]{:S(2)}) copy-start(bf16[768,768]{1,0:T(8,128)(2,1)} %refs_5_.8) | copy-start | bytes 3538948
  22.9 1.3 copy-start.5
  24.2 5.3 %copy-start.1 = (bf16[768,1536]{1,0:T(8,128)(2,1)S(1)}, bf16[768,1536]{1,0:T(8,128)(2,1)}, u32[]{:S(2)}) copy-start(bf16[768,1536]{1,0:T(8,128)(2,1)} %refs_5_.9) | copy-start | bytes 7077892
  24.2 5.3 %copy-start.2 = (bf16[768,1536]{1,0:T(8,128)(2,1)S(1)}, bf16[768,1536]{1,0:T(8,128)(2,1)}, u32[]{:S(2)}) copy-start(bf16[768,1536]{1,0:T(8,128)(2,1)} %refs_6_.5) | copy-start | bytes 7077892
  24.2 5.3 %copy-start.7 = (f32[768]{0:T(1024)S(1)}, f32[768]{0:T(1024)}, u32[]{:S(2)}) copy-start(f32[768]{0:T(1024)} %refs_7_.5) | copy-start | bytes 9220
  35.0 7.8 %collective-permute-start.6 = (bf16[384,1536]{1,0:T(8,128)(2,1)S(1)}, bf16[384,1536]{1,0:T(8,128)(2,1)S(1)}, u32[]{:S(2)}, u32[]{:S(2)}) collective-permute-start(bf16[384,1536]{1,0:T(8,128)(2,1)S(1)} %get-tuple-element.138.refs_8_), channel_id=1, source_target_pairs={{0,4},{4,0},{8,12},{12,8},{16,20},{20,16},{24,28},{28,24},{1,5},{5... | collective-permute-start | bytes 3538952 | tf_op jit(solution)/shard_map/ppermute | solution.py:545
  42.2 8.8 %collective-permute-start.7 = (bf16[384,1536]{1,0:T(8,128)(2,1)S(1)}, bf16[384,1536]{1,0:T(8,128)(2,1)S(1)}, u32[]{:S(2)}, u32[]{:S(2)}) collective-permute-start(bf16[384,1536]{1,0:T(8,128)(2,1)S(1)} %get-tuple-element.149), channel_id=1, source_target_pairs={{0,4},{4,0},{8,12},{12,8},{16,20},{20,16},{24,28},{28,24},{1,5},{5... | collective-permute-start | bytes 3538952 | tf_op jit(solution)/shard_map/ppermute | solution.py:545
  42.7 8.3 %collective-permute-start.8 = (bf16[768,768]{1,0:T(8,128)(2,1)S(1)}, bf16[768,768]{1,0:T(8,128)(2,1)S(1)}, u32[]{:S(2)}, u32[]{:S(2)}) collective-permute-start(bf16[768,768]{1,0:T(8,128)(2,1)S(1)} %get-tuple-element.151), channel_id=1, source_target_pairs={{0,4},{4,0},{8,12},{12,8},{16,20},{20,16},{24,28},{28,24},{1,5},{5... | collective-permute-start | bytes 3538952 | tf_op jit(solution)/shard_map/ppermute | solution.py:545
  43.6 16.5 %collective-permute-start.10 = (bf16[2,96,768]{2,1,0:T(8,128)(2,1)S(1)}, bf16[2,96,768]{2,1,0:T(8,128)(2,1)S(1)}, u32[]{:S(2)}, u32[]{:S(2)}) collective-permute-start(bf16[2,96,768]{2,1,0:T(8,128)(2,1)S(1)} %get-tuple-element.158), channel_id=1, source_target_pairs={{0,16},{4,20},{8,24},{12,28},{16,0},{20,4},{24,8},{28,12},{1,17},{... | collective-permute-start | bytes 884744 | tf_op jit(solution)/shard_map/ppermute | solution.py:545
  45.2 14.9 %collective-permute-start.9 = (bf16[2,96,768]{2,1,0:T(8,128)(2,1)S(1)}, bf16[2,96,768]{2,1,0:T(8,128)(2,1)S(1)}, u32[]{:S(2)}, u32[]{:S(2)}) collective-permute-start(bf16[2,96,768]{2,1,0:T(8,128)(2,1)S(1)} %get-tuple-element.156), channel_id=1, source_target_pairs={{0,8},{4,12},{8,0},{12,4},{16,24},{20,28},{24,16},{28,20},{1,9},{5... | collective-permute-start | bytes 884744 | tf_op jit(solution)/shard_map/ppermute | solution.py:545
  52.1 15.2 %collective-permute-start.11 = (bf16[2,96,1536]{2,1,0:T(8,128)(2,1)S(1)}, bf16[2,96,1536]{2,1,0:T(8,128)(2,1)S(1)}, u32[]{:S(2)}, u32[]{:S(2)}) collective-permute-start(bf16[2,96,1536]{2,1,0:T(8,128)(2,1)S(1)} %get-tuple-element.160), channel_id=1, source_target_pairs={{0,8},{4,12},{8,0},{12,4},{16,24},{20,28},{24,16},{28,20},{1,9},{5... | collective-permute-start | bytes 1769480 | tf_op jit(solution)/shard_map/ppermute | solution.py:545
  52.7 14.8 %collective-permute-start.12 = (bf16[2,96,1536]{2,1,0:T(8,128)(2,1)S(1)}, bf16[2,96,1536]{2,1,0:T(8,128)(2,1)S(1)}, u32[]{:S(2)}, u32[]{:S(2)}) collective-permute-start(bf16[2,96,1536]{2,1,0:T(8,128)(2,1)S(1)} %get-tuple-element.163), channel_id=1, source_target_pairs={{0,16},{4,20},{8,24},{12,28},{16,0},{20,4},{24,8},{28,12},{1,17},{... | collective-permute-start | bytes 1769480 | tf_op jit(solution)/shard_map/ppermute | solution.py:545
  61.0 11.8 %collective-permute-start.13 = (f32[3,2,384]{2,1,0:T(2,128)S(1)}, f32[3,2,384]{2,1,0:T(2,128)S(1)}, u32[]{:S(2)}, u32[]{:S(2)}) collective-permute-start(f32[3,2,384]{2,1,0:T(2,128)S(1)} %get-tuple-element.171.refs_5_), channel_id=1, source_target_pairs={{0,1},{1,2},{2,3},{3,0},{4,5},{5,6},{6,7},{7,4},{8,9},{9,10},{10,1... | collective-permute-start | bytes 27656 | tf_op jit(solution)/shard_map/ppermute | solution.py:537
  61.6 11.2 %collective-permute-start.14 = (f32[3,2,384]{2,1,0:T(2,128)S(1)}, f32[3,2,384]{2,1,0:T(2,128)S(1)}, u32[]{:S(2)}, u32[]{:S(2)}) collective-permute-start(f32[3,2,384]{2,1,0:T(2,128)S(1)} %get-tuple-element.171.refs_5_), channel_id=1, source_target_pairs={{0,2},{1,3},{2,0},{3,1},{4,6},{5,7},{6,4},{7,5},{8,10},{9,11},{10,... | collective-permute-start | bytes 27656 | tf_op jit(solution)/shard_map/ppermute | solution.py:537
  63.1 9.7 %collective-permute-start.15 = (f32[3,2,384]{2,1,0:T(2,128)S(1)}, f32[3,2,384]{2,1,0:T(2,128)S(1)}, u32[]{:S(2)}, u32[]{:S(2)}) collective-permute-start(f32[3,2,384]{2,1,0:T(2,128)S(1)} %get-tuple-element.171.refs_5_), channel_id=1, source_target_pairs={{0,3},{1,0},{2,1},{3,2},{4,7},{5,4},{6,5},{7,6},{8,11},{9,8},{10,9... | collective-permute-start | bytes 27656 | tf_op jit(solution)/shard_map/ppermute | solution.py:537
  68.4 10.9 %collective-permute-start.18 = (bf16[1,96,2304]{2,1,0:T(8,128)(2,1)S(1)}, bf16[1,96,2304]{2,1,0:T(8,128)(2,1)S(1)}, u32[]{:S(2)}, u32[]{:S(2)}) collective-permute-start(bf16[1,96,2304]{2,1,0:T(8,128)(2,1)S(1)} %get-tuple-element.182), channel_id=1, source_target_pairs={{0,16},{4,20},{8,24},{12,28},{16,0},{20,4},{24,8},{28,12},{1,17},{... | collective-permute-start | bytes 1327112 | tf_op jit(solution)/shard_map/ppermute | solution.py:545
  69.0 10.5 %collective-permute-start.19 = (bf16[1,96,2304]{2,1,0:T(8,128)(2,1)S(1)}, bf16[1,96,2304]{2,1,0:T(8,128)(2,1)S(1)}, u32[]{:S(2)}, u32[]{:S(2)}) collective-permute-start(bf16[1,96,2304]{2,1,0:T(8,128)(2,1)S(1)} %get-tuple-element.184), channel_id=1, source_target_pairs={{0,8},{4,12},{8,0},{12,4},{16,24},{20,28},{24,16},{28,20},{1,9},{5... | collective-permute-start | bytes 1327112 | tf_op jit(solution)/shard_map/ppermute | solution.py:545
  78.3 4.2 %collective-permute-start.17 = (bf16[384,1280]{1,0:T(8,128)(2,1)S(1)}, bf16[384,1280]{1,0:T(8,128)(2,1)S(1)}, u32[]{:S(2)}, u32[]{:S(2)}) collective-permute-start(bf16[384,1280]{1,0:T(8,128)(2,1)S(1)} %get-tuple-element.181.refs_5_), channel_id=1, source_target_pairs={{0,4},{4,0},{8,12},{12,8},{16,20},{20,16},{24,28},{28,24},{1,5},{5... | collective-permute-start | bytes 2949128 | tf_op jit(solution)/shard_map/ppermute | solution.py:545
  78.4 4.2 %collective-permute-start.16 = (bf16[384,1536]{1,0:T(8,128)(2,1)S(1)}, bf16[384,1536]{1,0:T(8,128)(2,1)S(1)}, u32[]{:S(2)}, u32[]{:S(2)}) collective-permute-start(bf16[384,1536]{1,0:T(8,128)(2,1)S(1)} %get-tuple-element.170.refs_19_), channel_id=1, source_target_pairs={{0,4},{4,0},{8,12},{12,8},{16,20},{20,16},{24,28},{28,24},{1,5},{5... | collective-permute-start | bytes 3538952 | tf_op jit(solution)/shard_map/ppermute | solution.py:545
  80.3 12.0 %collective-permute-start.22 = (bf16[1,48,2304]{2,1,0:T(8,128)(2,1)S(1)}, bf16[1,48,2304]{2,1,0:T(8,128)(2,1)S(1)}, u32[]{:S(2)}, u32[]{:S(2)}) collective-permute-start(bf16[1,48,2304]{2,1,0:T(8,128)(2,1)S(1)} %get-tuple-element.190), channel_id=1, source_target_pairs={{0,1},{1,0},{2,3},{3,2},{4,5},{5,4},{6,7},{7,6},{8,9},{9,8},{10,11... | collective-permute-start | bytes 663560 | tf_op jit(solution)/shard_map/ppermute | solution.py:545
  80.9 11.4 %collective-permute-start.23 = (bf16[1,48,2304]{2,1,0:T(8,128)(2,1)S(1)}, bf16[1,48,2304]{2,1,0:T(8,128)(2,1)S(1)}, u32[]{:S(2)}, u32[]{:S(2)}) collective-permute-start(bf16[1,48,2304]{2,1,0:T(8,128)(2,1)S(1)} %get-tuple-element.192), channel_id=1, source_target_pairs={{0,2},{1,3},{2,0},{3,1},{4,6},{5,7},{6,4},{7,5},{8,10},{9,11},{10,... | collective-permute-start | bytes 663560 | tf_op jit(solution)/shard_map/ppermute | solution.py:545
  83.7 15.4 %collective-permute-start.20 = (bf16[2,96,1536]{2,1,0:T(8,128)(2,1)S(1)}, bf16[2,96,1536]{2,1,0:T(8,128)(2,1)S(1)}, u32[]{:S(2)}, u32[]{:S(2)}) collective-permute-start(bf16[2,96,1536]{2,1,0:T(8,128)(2,1)S(1)} %get-tuple-element.187), channel_id=1, source_target_pairs={{0,8},{4,12},{8,0},{12,4},{16,24},{20,28},{24,16},{28,20},{1,9},{5... | collective-permute-start | bytes 1769480 | tf_op jit(solution)/shard_map/ppermute | solution.py:545
  85.3 12.0 %collective-permute-start.21 = (bf16[2,96,1280]{2,1,0:T(8,128)(2,1)S(1)}, bf16[2,96,1280]{2,1,0:T(8,128)(2,1)S(1)}, u32[]{:S(2)}, u32[]{:S(2)}) collective-permute-start(bf16[2,96,1280]{2,1,0:T(8,128)(2,1)S(1)} %get-tuple-element.189), channel_id=1, source_target_pairs={{0,16},{4,20},{8,24},{12,28},{16,0},{20,4},{24,8},{28,12},{1,17},{... | collective-permute-start | bytes 1474568 | tf_op jit(solution)/shard_map/ppermute | solution.py:545
  92.4 18.9 %collective-permute-start.28 = (bf16[1,48,2304]{2,1,0:T(8,128)(2,1)S(1)}, bf16[1,48,2304]{2,1,0:T(8,128)(2,1)S(1)}, u32[]{:S(2)}, u32[]{:S(2)}) collective-permute-start(bf16[1,48,2304]{2,1,0:T(8,128)(2,1)S(1)} %get-tuple-element.195.refs_5_.refs_0_), channel_id=1, source_target_pairs={{0,2},{1,3},{2,0},{3,1},{4,6},{5,7},{6,4},{7,5},{8,10},{9,11},{10,... | collective-permute-start | bytes 663560 | tf_op jit(solution)/shard_map/ppermute | solution.py:545
  93.9 17.4 %collective-permute-start.29 = (bf16[1,48,2304]{2,1,0:T(8,128)(2,1)S(1)}, bf16[1,48,2304]{2,1,0:T(8,128)(2,1)S(1)}, u32[]{:S(2)}, u32[]{:S(2)}) collective-permute-start(bf16[1,48,2304]{2,1,0:T(8,128)(2,1)S(1)} %get-tuple-element.208.refs_2_), channel_id=1, source_target_pairs={{0,1},{1,0},{2,3},{3,2},{4,5},{5,4},{6,7},{7,6},{8,9},{9,8},{10,11... | collective-permute-start | bytes 663560 | tf_op jit(solution)/shard_map/ppermute | solution.py:545
  99.9 8.5 %collective-permute-start.24 = (bf16[1,96,1536]{2,1,0:T(8,128)(2,1)S(1)}, bf16[1,96,1536]{2,1,0:T(8,128)(2,1)S(1)}, u32[]{:S(2)}, u32[]{:S(2)}) collective-permute-start(bf16[1,96,1536]{2,1,0:T(8,128)(2,1)S(1)} %get-tuple-element.200), channel_id=1, source_target_pairs={{0,16},{4,20},{8,24},{12,28},{16,0},{20,4},{24,8},{28,12},{1,17},{... | collective-permute-start | bytes 884744 | tf_op jit(solution)/shard_map/ppermute | solution.py:545
  101.5 6.9 %collective-permute-start.25 = (bf16[1,96,1280]{2,1,0:T(8,128)(2,1)S(1)}, bf16[1,96,1280]{2,1,0:T(8,128)(2,1)S(1)}, u32[]{:S(2)}, u32[]{:S(2)}) collective-permute-start(bf16[1,96,1280]{2,1,0:T(8,128)(2,1)S(1)} %get-tuple-element.202), channel_id=1, source_target_pairs={{0,8},{4,12},{8,0},{12,4},{16,24},{20,28},{24,16},{28,20},{1,9},{5... | collective-permute-start | bytes 737288 | tf_op jit(solution)/shard_map/ppermute | solution.py:545
  109.1 6.7 %collective-permute-start.26 = (bf16[1,48,1536]{2,1,0:T(8,128)(2,1)S(1)}, bf16[1,48,1536]{2,1,0:T(8,128)(2,1)S(1)}, u32[]{:S(2)}, u32[]{:S(2)}) collective-permute-start(bf16[1,48,1536]{2,1,0:T(8,128)(2,1)S(1)} %get-tuple-element.205), channel_id=1, source_target_pairs={{0,1},{1,0},{2,3},{3,2},{4,5},{5,4},{6,7},{7,6},{8,9},{9,8},{10,11... | collective-permute-start | bytes 442376 | tf_op jit(solution)/shard_map/ppermute | solution.py:545
  109.2 6.6 %collective-permute-start.27 = (bf16[1,48,1280]{2,1,0:T(8,128)(2,1)S(1)}, bf16[1,48,1280]{2,1,0:T(8,128)(2,1)S(1)}, u32[]{:S(2)}, u32[]{:S(2)}) collective-permute-start(bf16[1,48,1280]{2,1,0:T(8,128)(2,1)S(1)} %get-tuple-element.207), channel_id=1, source_target_pairs={{0,2},{1,3},{2,0},{3,1},{4,6},{5,7},{6,4},{7,5},{8,10},{9,11},{10,... | collective-permute-start | bytes 368648 | tf_op jit(solution)/shard_map/ppermute | solution.py:545
  115.8 10.9 %collective-permute-start.30 = (bf16[1,48,1536]{2,1,0:T(8,128)(2,1)S(1)}, bf16[1,48,1536]{2,1,0:T(8,128)(2,1)S(1)}, u32[]{:S(2)}, u32[]{:S(2)}) collective-permute-start(bf16[1,48,1536]{2,1,0:T(8,128)(2,1)S(1)} %get-tuple-element.210.refs_0_), channel_id=1, source_target_pairs={{0,2},{1,3},{2,0},{3,1},{4,6},{5,7},{6,4},{7,5},{8,10},{9,11},{10,... | collective-permute-start | bytes 442376 | tf_op jit(solution)/shard_map/ppermute | solution.py:545
  117.4 9.3 %collective-permute-start.31 = (bf16[1,48,1280]{2,1,0:T(8,128)(2,1)S(1)}, bf16[1,48,1280]{2,1,0:T(8,128)(2,1)S(1)}, u32[]{:S(2)}, u32[]{:S(2)}) collective-permute-start(bf16[1,48,1280]{2,1,0:T(8,128)(2,1)S(1)} %get-tuple-element.211.refs_2_), channel_id=1, source_target_pairs={{0,1},{1,0},{2,3},{3,2},{4,5},{5,4},{6,7},{7,6},{8,9},{9,8},{10,11... | collective-permute-start | bytes 368648 | tf_op jit(solution)/shard_map/ppermute | solution.py:545
  120.1 15.4 %collective-permute-start.34 = (bf16[1,48,2304]{2,1,0:T(8,128)(2,1)S(1)}, bf16[1,48,2304]{2,1,0:T(8,128)(2,1)S(1)}, u32[]{:S(2)}, u32[]{:S(2)}) collective-permute-start(bf16[1,48,2304]{2,1,0:T(8,128)(2,1)S(1)} %get-tuple-element.209.refs_4_), channel_id=1, source_target_pairs={{0,1},{1,0},{2,3},{3,2},{4,5},{5,4},{6,7},{7,6},{8,9},{9,8},{10,11... | collective-permute-start | bytes 663560 | tf_op jit(solution)/shard_map/ppermute | solution.py:545
  120.1 15.3 %collective-permute-start.35 = (bf16[1,48,2304]{2,1,0:T(8,128)(2,1)S(1)}, bf16[1,48,2304]{2,1,0:T(8,128)(2,1)S(1)}, u32[]{:S(2)}, u32[]{:S(2)}) collective-permute-start(bf16[1,48,2304]{2,1,0:T(8,128)(2,1)S(1)} %get-tuple-element.222), channel_id=1, source_target_pairs={{0,2},{1,3},{2,0},{3,1},{4,6},{5,7},{6,4},{7,5},{8,10},{9,11},{10,... | collective-permute-start | bytes 663560 | tf_op jit(solution)/shard_map/ppermute | solution.py:545
  126.8 11.5 %collective-permute-start.32 = (bf16[1,48,1536]{2,1,0:T(8,128)(2,1)S(1)}, bf16[1,48,1536]{2,1,0:T(8,128)(2,1)S(1)}, u32[]{:S(2)}, u32[]{:S(2)}) collective-permute-start(bf16[1,48,1536]{2,1,0:T(8,128)(2,1)S(1)} %get-tuple-element.212.refs_8_), channel_id=1, source_target_pairs={{0,1},{1,0},{2,3},{3,2},{4,5},{5,4},{6,7},{7,6},{8,9},{9,8},{10,11... | collective-permute-start | bytes 442376 | tf_op jit(solution)/shard_map/ppermute | solution.py:545
  127.0 10.6 %collective-permute-start.33 = (bf16[1,48,1280]{2,1,0:T(8,128)(2,1)S(1)}, bf16[1,48,1280]{2,1,0:T(8,128)(2,1)S(1)}, u32[]{:S(2)}, u32[]{:S(2)}) collective-permute-start(bf16[1,48,1280]{2,1,0:T(8,128)(2,1)S(1)} %get-tuple-element.213), channel_id=1, source_target_pairs={{0,2},{1,3},{2,0},{3,1},{4,6},{5,7},{6,4},{7,5},{8,10},{9,11},{10,... | collective-permute-start | bytes 368648 | tf_op jit(solution)/shard_map/ppermute | solution.py:545
  (3 other events, 2.6 us)

commit v5 on v4

--- a/solution.py
+++ b/solution.py
@@ -153,7 +153,7 @@
     scalars, refs = refs[0], refs[1:]
     totals, inits, refs = refs[:ranks], refs[ranks : 2 * ranks], refs[2 * ranks :]
     lam_re, lam_im, drv_re, drv_im, chunk_ref, perm_ref, x_ref, og_ref, gain_ref, member_ref, w_out_ref = refs[:11]
-    y_ref, split_ref, start_ref, final_ref, turned_ref, middle_ref, st_re, st_im = refs[11:]
+    y_ref, split_ref, start_ref, final_ref, turned_ref, middle_ref, ginv_ref, st_re, st_im = refs[11:]
     span, ch = lam_re.shape
     rank, bit = scalars[RANK], bit_of(scalars, PLACE, first)
     init = inits[0][...]
@@ -192,7 +192,9 @@
     yf = together(re, im, perm_ref)
     y_ref[...] = yf.astype(BF)
     member = member_ref[...]
-    inv = group_spread(lax.rsqrt(group_mean(yf * yf, member) + epsilon), member)
+    inv = lax.rsqrt(group_mean(yf * yf, member) + epsilon)
+    ginv_ref[...] = inv
+    inv = group_spread(inv, member)
     gated = (yf * inv * gain_ref[...][None] * jax.nn.silu(og_ref[...].astype(F32))).astype(BF)
     put_halves(turned_ref, gated.T, 0, lo, bit)
     middle_ref[...] = x_ref[...].astype(F32) + dot(gated, w_out_ref[...])
@@ -257,15 +259,14 @@
         dkeep_ref[out, :] = dot(ht_ref[j, half:, :], cot_ref[...]).astype(BF)
 
 
-def ffn_back_kernel(dgv0_ref, duv0_ref, dgv_ref, duv_ref, wg_ref, wu_ref, dn_ref):
+def ffn_back_kernel(dgv_ref, duv_ref, wg_ref, wu_ref, *refs, tile):
+    before, dn_ref = refs[:-1], refs[-1]
     width = dn_ref.shape[1]
-    own, cut = slice(0, width), slice(width, 2 * width)
-    dn_ref[...] = (
-        dot(dgv0_ref[...], wg_ref[:, own], NT)
-        + dot(duv0_ref[...], wu_ref[:, own], NT)
-        + dot(dgv_ref[...], wg_ref[:, cut], NT)
-        + dot(duv_ref[...], wu_ref[:, cut], NT)
-    )
+    cut = slice(tile * width, (tile + 1) * width)
+    dn = dot(dgv_ref[...], wg_ref[:, cut], NT) + dot(duv_ref[...], wu_ref[:, cut], NT)
+    for ref in before:
+        dn = dn + ref[...]
+    dn_ref[...] = dn
 
 
 def gate_kernel(normed_ref, w_ref, og_ref):
@@ -279,7 +280,7 @@
 
 
 def turn_kernel(
-    dn_ref, middle_ref, cot_ref, ffn_gain_ref, w_out_ref, y_ref, og_ref, gain_ref, member_ref, perm_ref,
+    dn_ref, middle_ref, cot_ref, ffn_gain_ref, w_out_ref, y_ref, ginv_ref, og_ref, gain_ref, member_ref, perm_ref,
     dmiddle_ref, dbranch_ref, dog_ref, split_ref,
 ):
     v, up = middle_ref[...], dn_ref[...]
@@ -292,7 +293,7 @@
     dbranch_ref[...] = dbranch
     dgated = dot(dbranch, w_out_ref[...], NT)
     og, yf, member, gain = og_ref[...].astype(F32), y_ref[...].astype(F32), member_ref[...], gain_ref[...][None]
-    ginv = group_spread(lax.rsqrt(group_mean(yf * yf, member) + epsilon), member)
+    ginv = group_spread(ginv_ref[...], member)
     gunit = yf * ginv
     sig = jax.nn.sigmoid(og)
     dog_ref[...] = (dgated * gunit * gain * silu_slope(og, sig)).astype(BF)
@@ -751,7 +752,7 @@
         [(rows(span, width), (count, width), BF), (rows(span, hidden), (count, hidden), BF)], [], [], "hidden_grad",
         (lam_re,),
     )
-    y, y_split, start, final, gated_t, middle = call(
+    y, y_split, start, final, gated_t, middle, ginv = call(
         functools.partial(mixer_kernel, ranks=nseq, lo=lo, first=first), segs,
         [(seg(4, ch), t) for t in totals]
         + [(seg(2, ch, shift=1), i) for i in infos]
@@ -767,6 +768,7 @@
             (seg(2, mine), (segs, 2, mine), F32),
             (cols(width, span), (width, count), BF),
             (rows(span, width), (count, width), F32),
+            (rows(span, LANES), (count, LANES), F32),
         ],
         scan_scratch, [here], "mixer",
     )
@@ -800,10 +802,11 @@
     def blocks(a, cols_n, tall_n=1):
         return a.reshape(nblk * tall_n, per, cols_n)
 
-    def ffn_back(*after):
+    def ffn_back(tile, dgv, duv, before, *after):
         return call(
-            ffn_back_kernel, segs,
-            [(rows(span, width), a) for a in (dgv0, duv0, dgv1, duv1)] + [(whole(), w_gate), (whole(), w_up)],
+            functools.partial(ffn_back_kernel, tile=tile), segs,
+            [(rows(span, width), a) for a in (dgv, duv)] + [(whole(), w_gate), (whole(), w_up)]
+            + [(rows(span, width), a) for a in before],
             [(rows(span, width), wide, F32)], [], [], "ffn_back", after,
         )[0]
 
@@ -814,7 +817,7 @@
             here, [(0, x_bit, [(p, 1, 0, 0, width)]), (1, y_bit, [(p, 1, 0, 1, width)])], "first_sum1", (gkeep,)
         )
         pa_got, pb_got = swap(pa_send, "dp", ndp, rest[0]), swap(pb_send, "dp", ndp, rest[1])
-        dn = ffn_back(pa_keep)
+        dn = ffn_back(0, dgv0, duv0, (), pa_keep)
         g = [blocks(a, 2 * width) for a in (gkeep, ggot)]
         d = [blocks(a, width, tall) for a in (dkeep, dgot)]
         (fa_send, fa_keep), (fb_send, fb_keep) = combine(
@@ -823,15 +826,16 @@
         )
         fa_got, fb_got = swap(fa_send, "dp", ndp, rest[0]), swap(fb_send, "dp", ndp, rest[1])
         order = (fa_keep,)
-
     else:
-        dn = ffn_back()
+        dn = ffn_back(0, dgv0, duv0, ())
+    dn = ffn_back(1, dgv1, duv1, (dn,), *order)
 
     dmiddle, dbranch, dog, dy_split = call(
         turn_kernel, segs,
         [
             (rows(span, width), dn), (rows(span, width), middle), (rows(span, width), cot), (whole(width), norm_ffn),
-            (whole(width, width), w_out), (rows(span, width), y), (rows(span, width), og), (whole(width), norm_group),
+            (whole(width, width), w_out), (rows(span, width), y), (rows(span, LANES), ginv), (rows(span, width), og),
+            (whole(width), norm_group),
             (whole(width, LANES), member), (whole(), perm),
         ],
         [
@@ -923,7 +927,12 @@
         o = [blocks(a, 2 * width) for a in (okeep, ogot)]
         i = [blocks(a, into) for a in (ikeep, igot)]
         (ra_send, ra_keep), (rb_send, rb_keep) = combine(
-            here, [(0, x_bit, [(o, 1, 0, 0, 2 * width)]), (1, y_bit, [(i, 1, 0, 0, into)])], "mixer_sum1", (fa_keep,)
+            here,
+            [
+                (0, x_bit, [(o, 1, 0, 0, 2 * width - LANES)]),
+                (1, y_bit, [(i, 1, 0, 0, into), (o, 1, 0, 2 * width // LANES - 1, LANES)]),
+            ],
+            "mixer_sum1", (fa_keep,)
         )
         ra_got, rb_got = swap(ra_send, "dp", ndp, rest[0]), swap(rb_send, "dp", ndp, rest[1])
         order = (ra_keep,)
@@ -977,7 +986,8 @@
             [(full, (per, hidden)), (full, (per, hidden)), (full, (tall * per, width)), (full, (per,))],
             [(3, 2, [(0, 0), (1, 1)])], None, nseq, "ffn_out", (ra,),
         )
-        moves = [(0, n * ntile, ntile, n % 2, 0, (n // 2) * ntile) for n in range(2 * width // ntile)]
+        moves = [(0, n * ntile, ntile, n % 2, 0, (n // 2) * ntile) for n in range(2 * width // ntile - 1)]
+        moves += [(0, 2 * width - ntile, ntile - LANES, 1, 0, width - ntile), (1, into, LANES, 1, 0, width - LANES)]
         moves += [(1, 0, width, 2, 0, 0), (1, width, ch, 3, 0, 0)]
         part_ogate, part_out, part_in, part_forget, part_mix, part_group, part_bias, part_phase, _ = finish(
             here, flat((ra, ra_got), (rb, rb_got)), z_bits, moves,

time: 140 us -> 140 us (level)
  waiting for transfers between devices: 22.4 us -> 19.1 us
  starting transfers between devices: 46.7 us -> 49.2 us
    ppermute x27, waiting for transfers between devices: 22.4 us -> 19.1 us  [swap(): return lax.ppermute(v, axis, [(i, i ^ bit) for i in range(n)])]
    ppermute x27, starting transfers between devices: 30.8 us -> 33.3 us  [swap(): return lax.ppermute(v, axis, [(i, i ^ bit) for i in range(n)])]
    pallas_call x30 -> x31, Pallas kernels: 68.1 us -> 68.2 us  [call(): pl.pallas_call(body, grid_spec=pltpu.PrefetchScalarGridSpec(num_scalar_pr...]
  transfers between devices with their start and end apart: 36 -> 36, of which waited for: 12 -> 14; matrix products, arithmetic and copies ran while one was open for 0% -> 0% of each run, Pallas kernels for 38% -> 38%
where the time goes in v5:
time: 140 us; the launch traced here: 139 us
  Pallas kernels  68.2 us (49%)
  starting transfers between devices  49.2 us (35%)
  waiting for transfers between devices  19.1 us (14%)
  local copies, waits for them, and re-layouts  1.51 us (1%)
    pallas_call x31, Pallas kernels, call(): pl.pallas_call(body, grid_spec=pltpu.PrefetchScalarGridSpec(num_scalar_pr...  68.2 us
    ppermute x27, starting transfers between devices, swap(): return lax.ppermute(v, axis, [(i, i ^ bit) for i in range(n)])  33.3 us
    ppermute x27, waiting for transfers between devices, swap(): return lax.ppermute(v, axis, [(i, i ^ bit) for i in range(n)])  19.1 us
    ppermute x9, starting transfers between devices, shift_all(): lax.ppermute(payload, axis, [(i, (i + k) % n) for i in range(n)])  15.9 us
  transfers between devices with their start and end apart: 36, of which 14 were waited for; matrix products, arithmetic and copies ran while one was open for 0% of the time, Pallas kernels for 38%

profile of v5, /device:TPU:0, one launch (start us, length us, event | category | flops | bytes accessed | tf_op | source)
XLA Modules:
  0.0 139.3 jit_solution(13122343305268295659)
XLA Ops:
  2.6 3.1 %collective-permute-start = (f32[4,2,384]{2,1,0:T(2,128)S(1)}, f32[4,2,384]{2,1,0:T(2,128)S(1)}, u32[]{:S(2)}, u32[]{:S(2)}) collective-permute-start(f32[4,2,384]{2,1,0:T(2,128)S(1)} %get-tuple-element.124.refs_1_.refs_5_), channel_id=1, source_target_pairs={{0,1},{1,2},{2,3},{3,0},{4,5},{5,6},{6,7},{7,4},{8,9},{9,10},{10,1... | collective-permute-start | bytes 36872 | tf_op jit(solution)/shard_map/ppermute | solution.py:538
  5.7 2.6 %collective-permute-start.1 = (f32[4,2,384]{2,1,0:T(2,128)S(1)}, f32[4,2,384]{2,1,0:T(2,128)S(1)}, u32[]{:S(2)}, u32[]{:S(2)}) collective-permute-start(f32[4,2,384]{2,1,0:T(2,128)S(1)} %get-tuple-element.124.refs_1_.refs_5_), channel_id=1, source_target_pairs={{0,2},{1,3},{2,0},{3,1},{4,6},{5,7},{6,4},{7,5},{8,10},{9,11},{10,... | collective-permute-start | bytes 36872 | tf_op jit(solution)/shard_map/ppermute | solution.py:538
  8.3 1.3 collective-permute-start.2
  9.8 4.5 %project.1 = (bf16[768,768]{1,0:T(8,128)(2,1)S(1)}, bf16[768,768]{1,0:T(8,128)(2,1)S(1)}, bf16[768,768]{1,0:T(8,128)(2,1)S(1)}, bf16[3,256,1152]{2,1,0:T(8,128)(2,1)S(1)}) custom-call(s32[2]{0:T(128)S(1)} %get-tuple-element.122.refs_0_, bf16[768,768]{1,0:T(8,128)(2,1)S(1)} %bitcast.51, f32[768]{0:T(1024)S(1)} %copy-done.6, bf16[768,768]{1,0:T(8,128)(2,1)S(1)} %copy-done.3, ...), custom_call_target="tpu_custom_call" | custom-call | flops 4600000000 | bytes 1 | tf_op jit(solution)/shard_map/project/pallas_call | solution.py:521
  14.6 1.6 %summary.1 = (f32[2,384]{1,0:T(2,128)S(1)}, f32[3,4,8,384]{3,2,1,0:T(8,128)S(1)}, f32[3,4,384]{2,1,0:T(4,128)S(1)}, f32[768,384]{1,0:T(8,128)S(1)}, f32[768,384]...) custom-call(bf16[3,256,1152]{2,1,0:T(8,128)(2,1)S(1)} %get-tuple-element.123.refs_0_.refs_9_, ...), custom_call_target="tpu_custom_call" | custom-call | flops 4600000000 | bytes 1 | tf_op jit(solution)/shard_map/summary/pallas_call | solution.py:521
  17.4 2.7 %collective-permute-start.5 = (f32[3,4,384]{2,1,0:T(4,128)S(1)}, f32[3,4,384]{2,1,0:T(4,128)S(1)}, u32[]{:S(2)}, u32[]{:S(2)}) collective-permute-start(f32[3,4,384]{2,1,0:T(4,128)S(1)} %get-tuple-element.125.refs_1_), channel_id=1, source_target_pairs={{0,3},{1,0},{2,1},{3,2},{4,7},{5,4},{6,5},{7,6},{8,11},{9,8},{10,9... | collective-permute-start | bytes 55304 | tf_op jit(solution)/shard_map/ppermute | solution.py:538
  20.1 2.8 %hidden_grad.1 = (bf16[768,768]{1,0:T(8,128)(2,1)S(1)}, bf16[768,1536]{1,0:T(8,128)(2,1)S(1)}) custom-call(bf16[768,768]{1,0:T(8,128)(2,1)S(1)} %bitcast.52, bf16[1536,768]{1,0:T(8,128)(2,1)S(1)} %copy-done.9, bf16[256,256]{1,0:T(8,128)(2,1)S(1)} %get-tuple-element.230.refs_7_.refs_2_.refs_8_.refs_4_, ...), custom_call_target="tpu_custom_call" | custom-call | flops 2875000064 | bytes 1 | tf_op jit(solution)/shard_map/hidden_grad/pallas_call | solution.py:521
  22.9 1.1 gate.1.refs_16_.refs_7_
  24.2 5.3 %mixer.1 = (bf16[768,768]{1,0:T(8,128)(2,1)S(1)}, bf16[768,768]{1,0:T(8,128)(2,1)S(1)}, f32[3,2,384]{2,1,0:T(2,128)S(1)}, f32[3,2,96]{2,1,0:T(2,128)}, bf16[768,...) custom-call(s32[2]{0:T(128)S(1)} %get-tuple-element.122.refs_0_, ...), custom_call_target="tpu_custom_call" | custom-call | flops 9200000000 | bytes 1 | tf_op jit(solution)/shard_map/mixer/pallas_call | solution.py:521
  29.5 5.5 %ffn_first.1 = (bf16[384,1536]{1,0:T(8,128)(2,1)S(1)}, bf16[384,1536]{1,0:T(8,128)(2,1)S(1)}, bf16[768,768]{1,0:T(8,128)(2,1)S(1)}, bf16[768,768]{1,0:T(8,128)(2...) custom-call(s32[2]{0:T(128)S(1)} %get-tuple-element.122.refs_0_, ...), custom_call_target="tpu_custom_call" | custom-call | flops 6899999744 | bytes 1 | tf_op jit(solution)/shard_map/ffn_first/pallas_call | solution.py:521
  35.1 7.1 %ffn_rest.1 = (bf16[384,1536]{1,0:T(8,128)(2,1)S(1)}, bf16[384,1536]{1,0:T(8,128)(2,1)S(1)}, bf16[768,768]{1,0:T(8,128)(2,1)S(1)}, bf16[768,768]{1,0:T(8,128)(2,...) custom-call(s32[2]{0:T(128)S(1)} %get-tuple-element.122.refs_0_, ...), custom_call_target="tpu_custom_call" | custom-call | flops 13799999488 | bytes 1 | tf_op jit(solution)/shard_map/ffn_rest/pallas_call | solution.py:521
  43.7 1.6 %collective-permute-start.10 = (bf16[2,96,768]{2,1,0:T(8,128)(2,1)S(1)}, bf16[2,96,768]{2,1,0:T(8,128)(2,1)S(1)}, u32[]{:S(2)}, u32[]{:S(2)}) collective-permute-start(bf16[2,96,768]{2,1,0:T(8,128)(2,1)S(1)} %get-tuple-element.160), channel_id=1, source_target_pairs={{0,16},{4,20},{8,24},{12,28},{16,0},{20,4},{24,8},{28,12},{1,17},{... | collective-permute-start | bytes 884744 | tf_op jit(solution)/shard_map/ppermute | solution.py:546
  45.3 1.5 %collective-permute-start.9 = (bf16[2,96,768]{2,1,0:T(8,128)(2,1)S(1)}, bf16[2,96,768]{2,1,0:T(8,128)(2,1)S(1)}, u32[]{:S(2)}, u32[]{:S(2)}) collective-permute-start(bf16[2,96,768]{2,1,0:T(8,128)(2,1)S(1)} %get-tuple-element.158), channel_id=1, source_target_pairs={{0,8},{4,12},{8,0},{12,4},{16,24},{20,28},{24,16},{28,20},{1,9},{5... | collective-permute-start | bytes 884744 | tf_op jit(solution)/shard_map/ppermute | solution.py:546
  46.7 2.4 %ffn_back.2.refs_5_.refs_4_ = f32[768,768]{1,0:T(8,128)S(1)} custom-call(bf16[768,768]{1,0:T(8,128)(2,1)S(1)} %get-tuple-element.144.refs_0_, bf16[768,768]{1,0:T(8,128)(2,1)S(1)} %get-tuple-element.145.refs_1_, bf16[768,1536]{1,0:T(8,128)(2,1)S(1)} %copy-done, bf16[768,1536]{1,0:T(8,128)(2,1)S(1)} %copy-done.1, ...), custom_call_target="tpu_custom_call" | custom-call | flops 920000000 | bytes 1 | tf_op jit(solution)/shard_map/ffn_back/pallas_call | solution.py:521
  49.2 1.1 ffn_sum1.1
  51.4 2.5 %ffn_back.3.refs_0_ = f32[768,768]{1,0:T(8,128)S(1)} custom-call(bf16[768,768]{1,0:T(8,128)(2,1)S(1)} %get-tuple-element.142.refs_0_, bf16[768,768]{1,0:T(8,128)(2,1)S(1)} %get-tuple-element.143.refs_1_, bf16[768,1536]{1,0:T(8,128)(2,1)S(1)} %copy-done, bf16[768,1536]{1,0:T(8,128)(2,1)S(1)} %copy-done.1, f32[768,768]{1,0:T(8,128)S(1)} %ffn_back.2.refs_5_.refs_4_, ...), custom_call_target="tpu_custom_call" | custom-call | flops 920000000 | bytes 1 | tf_op jit(solution)/shard_map/ffn_back/pallas_call | solution.py:521
  53.9 6.4 %turn.1 = (f32[768,768]{1,0:T(8,128)S(1)}, bf16[768,768]{1,0:T(8,128)(2,1)S(1)}, bf16[768,768]{1,0:T(8,128)(2,1)S(1)}, bf16[768,768]{1,0:T(8,128)(2,1)S(1)}) custom-call(f32[768,768]{1,0:T(8,128)S(1)} %ffn_back.3.refs_0_, f32[768,768]{1,0:T(8,128)S(1)} %get-tuple-element.133.refs_1_.refs_0_, bf16[768,768]{1,0:T(8,128)(2,1)S(1)} %get-tuple-element.138.refs_3_.refs_2_, ...), custom_call_target="tpu_custom_call" | custom-call | flops 8049999872 | bytes 1 | tf_op jit(solution)/shard_map/turn/pallas_call | solution.py:521
  61.8 1.5 %collective-permute-start.14 = (f32[3,2,384]{2,1,0:T(2,128)S(1)}, f32[3,2,384]{2,1,0:T(2,128)S(1)}, u32[]{:S(2)}, u32[]{:S(2)}) collective-permute-start(f32[3,2,384]{2,1,0:T(2,128)S(1)} %get-tuple-element.173.refs_5_), channel_id=1, source_target_pairs={{0,2},{1,3},{2,0},{3,1},{4,6},{5,7},{6,4},{7,5},{8,10},{9,11},{10,... | collective-permute-start | bytes 27656 | tf_op jit(solution)/shard_map/ppermute | solution.py:538
  63.3 2.8 %collective-permute-start.15 = (f32[3,2,384]{2,1,0:T(2,128)S(1)}, f32[3,2,384]{2,1,0:T(2,128)S(1)}, u32[]{:S(2)}, u32[]{:S(2)}) collective-permute-start(f32[3,2,384]{2,1,0:T(2,128)S(1)} %get-tuple-element.173.refs_5_), channel_id=1, source_target_pairs={{0,3},{1,0},{2,1},{3,2},{4,7},{5,4},{6,5},{7,6},{8,11},{9,8},{10,9... | collective-permute-start | bytes 27656 | tf_op jit(solution)/shard_map/ppermute | solution.py:538
  66.1 0.8 collective-permute-done.11.refs_3_
  67.0 0.8 ffn_sum2.1
  68.6 1.5 %collective-permute-start.19 = (bf16[1,96,2304]{2,1,0:T(8,128)(2,1)S(1)}, bf16[1,96,2304]{2,1,0:T(8,128)(2,1)S(1)}, u32[]{:S(2)}, u32[]{:S(2)}) collective-permute-start(bf16[1,96,2304]{2,1,0:T(8,128)(2,1)S(1)} %get-tuple-element.186), channel_id=1, source_target_pairs={{0,8},{4,12},{8,0},{12,4},{16,24},{20,28},{24,16},{28,20},{1,9},{5... | collective-permute-start | bytes 1327112 | tf_op jit(solution)/shard_map/ppermute | solution.py:546
  70.0 2.4 %mixer_grads.1 = (bf16[384,1536]{1,0:T(8,128)(2,1)S(1)}, bf16[384,1536]{1,0:T(8,128)(2,1)S(1)}) custom-call(bf16[768,768]{1,0:T(8,128)(2,1)S(1)} %get-tuple-element.141.refs_0_, bf16[768,768]{1,0:T(8,128)(2,1)S(1)} %get-tuple-element.155.refs_4_.refs_1_, bf16[768,768]{1,0:T(8,128)(2,1)S(1)} %get-tuple-element.156.refs_2_, ...), custom_call_target="tpu_custom_call" | custom-call | flops 11500000 | bytes 1 | tf_op jit(solution)/shard_map/mixer_grads/pallas_call | solution.py:521
  72.4 3.7 %adjoint.1 = (bf16[768,1152]{1,0:T(8,128)(2,1)S(1)}, f32[2,384]{1,0:T(2,128)S(1)}) custom-call(s32[2]{0:T(128)S(1)} %get-tuple-element.122.refs_0_, f32[3,4,384]{2,1,0:T(4,128)S(1)} %get-tuple-element.125.refs_1_, f32[3,4,384]{2,1,0:T(4,128)S(1)} %collective-permute-done.3.refs_2_, f32[3,4,384]{2,1,0:T(4,128)S(1)} %collective-permute-done.4.refs_3_, ...), custom_call_target="tpu_custom_call" | custom-call | flops 4301000192 | bytes 1 | tf_op jit(solution)/shard_map/adjoint/pallas_call | solution.py:521
  76.1 1.7 %input_grads.1 = (bf16[384,1280]{1,0:T(8,128)(2,1)S(1)}, bf16[384,1280]{1,0:T(8,128)(2,1)S(1)}) custom-call(bf16[768,768]{1,0:T(8,128)(2,1)S(1)} %get-tuple-element.141.refs_0_, bf16[768,1152]{1,0:T(8,128)(2,1)S(1)} %get-tuple-element.180.refs_1_.refs_0_, f32[2,384]{1,0:T(2,128)S(1)} %get-tuple-element.181.refs_2_), custom_call_target="tpu_custom_call" | custom-call | flops 345000000 | bytes 1 | tf_op jit(solution)/shard_map/input_grads/pallas_call | solution.py:521
  81.0 1.5 %collective-permute-start.23 = (bf16[1,48,2304]{2,1,0:T(8,128)(2,1)S(1)}, bf16[1,48,2304]{2,1,0:T(8,128)(2,1)S(1)}, u32[]{:S(2)}, u32[]{:S(2)}) collective-permute-start(bf16[1,48,2304]{2,1,0:T(8,128)(2,1)S(1)} %get-tuple-element.194), channel_id=1, source_target_pairs={{0,2},{1,3},{2,0},{3,1},{4,6},{5,7},{6,4},{7,5},{8,10},{9,11},{10,... | collective-permute-start | bytes 663560 | tf_op jit(solution)/shard_map/ppermute | solution.py:546
  82.5 1.0 mixer_sum1.1
  83.6 1.6 %collective-permute-start.20 = (bf16[2,96,1408]{2,1,0:T(8,128)(2,1)S(1)}, bf16[2,96,1408]{2,1,0:T(8,128)(2,1)S(1)}, u32[]{:S(2)}, u32[]{:S(2)}) collective-permute-start(bf16[2,96,1408]{2,1,0:T(8,128)(2,1)S(1)} %get-tuple-element.189), channel_id=1, source_target_pairs={{0,8},{4,12},{8,0},{12,4},{16,24},{20,28},{24,16},{28,20},{1,9},{5... | collective-permute-start | bytes 1622024 | tf_op jit(solution)/shard_map/ppermute | solution.py:546
  85.1 1.4 %collective-permute-start.21 = (bf16[2,96,1408]{2,1,0:T(8,128)(2,1)S(1)}, bf16[2,96,1408]{2,1,0:T(8,128)(2,1)S(1)}, u32[]{:S(2)}, u32[]{:S(2)}) collective-permute-start(bf16[2,96,1408]{2,1,0:T(8,128)(2,1)S(1)} %get-tuple-element.191), channel_id=1, source_target_pairs={{0,16},{4,20},{8,24},{12,28},{16,0},{20,4},{24,8},{28,12},{1,17},{... | collective-permute-start | bytes 1622024 | tf_op jit(solution)/shard_map/ppermute | solution.py:546
  86.5 5.5 %tokens.1 = (bf16[768,768]{1,0:T(8,128)(2,1)}, f32[8,128]{1,0:T(8,128)S(1)}) custom-call(bf16[768,1152]{1,0:T(8,128)(2,1)S(1)} %get-tuple-element.180.refs_1_.refs_0_, bf16[768,768]{1,0:T(8,128)(2,1)S(1)} %get-tuple-element.155.refs_4_.refs_1_, bf16[768,768]{1,0:T(8,128)(2,1)S(1)} %copy-done.3, bf16[768,384]{1,0:T(8,128)(2,1)S(1)} %copy-done.4, ...), custom_call_target="tpu_custom_call" | custom-call | flops 345000000 | bytes 1 | tf_op jit(solution)/shard_map/tokens/pallas_call | solution.py:521
  92.2 1.5 %collective-permute-start.28 = (bf16[1,48,2304]{2,1,0:T(8,128)(2,1)S(1)}, bf16[1,48,2304]{2,1,0:T(8,128)(2,1)S(1)}, u32[]{:S(2)}, u32[]{:S(2)}) collective-permute-start(bf16[1,48,2304]{2,1,0:T(8,128)(2,1)S(1)} %get-tuple-element.197.refs_5_.refs_0_), channel_id=1, source_target_pairs={{0,2},{1,3},{2,0},{3,1},{4,6},{5,7},{6,4},{7,5},{8,10},{9,11},{10,... | collective-permute-start | bytes 663560 | tf_op jit(solution)/shard_map/ppermute | solution.py:546
  93.7 2.4 %collective-permute-start.29 = (bf16[1,48,2304]{2,1,0:T(8,128)(2,1)S(1)}, bf16[1,48,2304]{2,1,0:T(8,128)(2,1)S(1)}, u32[]{:S(2)}, u32[]{:S(2)}) collective-permute-start(bf16[1,48,2304]{2,1,0:T(8,128)(2,1)S(1)} %get-tuple-element.210.refs_2_), channel_id=1, source_target_pairs={{0,1},{1,0},{2,3},{3,2},{4,5},{5,4},{6,7},{7,6},{8,9},{9,8},{10,11... | collective-permute-start | bytes 663560 | tf_op jit(solution)/shard_map/ppermute | solution.py:546
  96.1 1.5 %collective-permute-done.20.refs_2_ = bf16[2,96,1408]{2,1,0:T(8,128)(2,1)S(1)} collective-permute-done((bf16[2,96,1408]{2,1,0:T(8,128)(2,1)S(1)}, bf16[2,96,1408]{2,1,0:T(8,128)(2,1)S(1)}, u32[]{:S(2)}, u32[]{:S(2)}) %collective-permute-start.20) | collective-permute-done | bytes 540704 | tf_op jit(solution)/shard_map/ppermute | solution.py:546
  98.7 1.4 %collective-permute-start.24 = (bf16[1,96,1408]{2,1,0:T(8,128)(2,1)S(1)}, bf16[1,96,1408]{2,1,0:T(8,128)(2,1)S(1)}, u32[]{:S(2)}, u32[]{:S(2)}) collective-permute-start(bf16[1,96,1408]{2,1,0:T(8,128)(2,1)S(1)} %get-tuple-element.202), channel_id=1, source_target_pairs={{0,16},{4,20},{8,24},{12,28},{16,0},{20,4},{24,8},{28,12},{1,17},{... | collective-permute-start | bytes 811016 | tf_op jit(solution)/shard_map/ppermute | solution.py:546
  100.1 1.5 %collective-permute-start.25 = (bf16[1,96,1408]{2,1,0:T(8,128)(2,1)S(1)}, bf16[1,96,1408]{2,1,0:T(8,128)(2,1)S(1)}, u32[]{:S(2)}, u32[]{:S(2)}) collective-permute-start(bf16[1,96,1408]{2,1,0:T(8,128)(2,1)S(1)} %get-tuple-element.204), channel_id=1, source_target_pairs={{0,8},{4,12},{8,0},{12,4},{16,24},{20,28},{24,16},{28,20},{1,9},{5... | collective-permute-start | bytes 811016 | tf_op jit(solution)/shard_map/ppermute | solution.py:546
  101.6 4.0 %out.1 = (bf16[768,768]{1,0:T(8,128)(2,1)}, f32[8,128]{1,0:T(8,128)S(1)}) custom-call(f32[768,768]{1,0:T(8,128)S(1)} %get-tuple-element.133.refs_1_.refs_0_, bf16[768,768]{1,0:T(8,128)(2,1)S(1)} %get-tuple-element.135.refs_7_.refs_1_, bf16[768,768]{1,0:T(8,128)(2,1)S(1)} %get-tuple-element.140.refs_2_, bf16[1536,768]{1,0:T(8,128)(2,1)S(1)} %copy-done.9, ...), custom_call_target="tpu_custom_call" | custom-call | flops 4024999936 | bytes 1 | tf_op jit(solution)/shard_map/out/pallas_call | solution.py:521
  105.9 0.9 collective-permute-done.25
  108.0 2.1 %collective-permute-start.27 = (bf16[1,48,1408]{2,1,0:T(8,128)(2,1)S(1)}, bf16[1,48,1408]{2,1,0:T(8,128)(2,1)S(1)}, u32[]{:S(2)}, u32[]{:S(2)}) collective-permute-start(bf16[1,48,1408]{2,1,0:T(8,128)(2,1)S(1)} %get-tuple-element.209), channel_id=1, source_target_pairs={{0,2},{1,3},{2,0},{3,1},{4,6},{5,7},{6,4},{7,5},{8,10},{9,11},{10,... | collective-permute-start | bytes 405512 | tf_op jit(solution)/shard_map/ppermute | solution.py:546
  110.2 2.3 %collective-permute-done.26.refs_1_ = bf16[1,48,1408]{2,1,0:T(8,128)(2,1)S(1)} collective-permute-done((bf16[1,48,1408]{2,1,0:T(8,128)(2,1)S(1)}, bf16[1,48,1408]{2,1,0:T(8,128)(2,1)S(1)}, u32[]{:S(2)}, u32[]{:S(2)}) %collective-permute-start.26) | collective-permute-done | bytes 135200 | tf_op jit(solution)/shard_map/ppermute | solution.py:546
  112.5 1.8 %collective-permute-done.27.refs_3_ = bf16[1,48,1408]{2,1,0:T(8,128)(2,1)S(1)} collective-permute-done((bf16[1,48,1408]{2,1,0:T(8,128)(2,1)S(1)}, bf16[1,48,1408]{2,1,0:T(8,128)(2,1)S(1)}, u32[]{:S(2)}, u32[]{:S(2)}) %collective-permute-start.27) | collective-permute-done | bytes 135200 | tf_op jit(solution)/shard_map/ppermute | solution.py:546
  114.4 1.8 %collective-permute-start.30 = (bf16[1,48,1408]{2,1,0:T(8,128)(2,1)S(1)}, bf16[1,48,1408]{2,1,0:T(8,128)(2,1)S(1)}, u32[]{:S(2)}, u32[]{:S(2)}) collective-permute-start(bf16[1,48,1408]{2,1,0:T(8,128)(2,1)S(1)} %get-tuple-element.212.refs_0_), channel_id=1, source_target_pairs={{0,2},{1,3},{2,0},{3,1},{4,6},{5,7},{6,4},{7,5},{8,10},{9,11},{10,... | collective-permute-start | bytes 405512 | tf_op jit(solution)/shard_map/ppermute | solution.py:546
  116.3 4.9 %collective-permute-start.31 = (bf16[1,48,1408]{2,1,0:T(8,128)(2,1)S(1)}, bf16[1,48,1408]{2,1,0:T(8,128)(2,1)S(1)}, u32[]{:S(2)}, u32[]{:S(2)}) collective-permute-start(bf16[1,48,1408]{2,1,0:T(8,128)(2,1)S(1)} %get-tuple-element.213.refs_2_), channel_id=1, source_target_pairs={{0,1},{1,0},{2,3},{3,2},{4,5},{5,4},{6,7},{7,6},{8,9},{9,8},{10,11... | collective-permute-start | bytes 405512 | tf_op jit(solution)/shard_map/ppermute | solution.py:546
  121.3 4.3 %collective-permute-done.30.refs_1_ = bf16[1,48,1408]{2,1,0:T(8,128)(2,1)S(1)} collective-permute-done((bf16[1,48,1408]{2,1,0:T(8,128)(2,1)S(1)}, bf16[1,48,1408]{2,1,0:T(8,128)(2,1)S(1)}, u32[]{:S(2)}, u32[]{:S(2)}) %collective-permute-start.30) | collective-permute-done | bytes 135200 | tf_op jit(solution)/shard_map/ppermute | solution.py:546
  125.7 3.2 %collective-permute-done.31.refs_3_ = bf16[1,48,1408]{2,1,0:T(8,128)(2,1)S(1)} collective-permute-done((bf16[1,48,1408]{2,1,0:T(8,128)(2,1)S(1)}, bf16[1,48,1408]{2,1,0:T(8,128)(2,1)S(1)}, u32[]{:S(2)}, u32[]{:S(2)}) %collective-permute-start.31) | collective-permute-done | bytes 135200 | tf_op jit(solution)/shard_map/ppermute | solution.py:546
  129.0 4.0 %collective-permute-start.33 = (bf16[1,48,1408]{2,1,0:T(8,128)(2,1)S(1)}, bf16[1,48,1408]{2,1,0:T(8,128)(2,1)S(1)}, u32[]{:S(2)}, u32[]{:S(2)}) collective-permute-start(bf16[1,48,1408]{2,1,0:T(8,128)(2,1)S(1)} %get-tuple-element.215), channel_id=1, source_target_pairs={{0,2},{1,3},{2,0},{3,1},{4,6},{5,7},{6,4},{7,5},{8,10},{9,11},{10,... | collective-permute-start | bytes 405512 | tf_op jit(solution)/shard_map/ppermute | solution.py:546
  133.1 0.9 collective-permute-done.34
  134.0 2.1 %ffn_out.1 = (f32[96,1536]{1,0:T(8,128)}, f32[96,1536]{1,0:T(8,128)}, f32[192,768]{1,0:T(8,128)}, f32[96]{0:T(128)}, f32[8,128]{1,0:T(8,128)}) custom-call(s32[2]{0:T(128)S(1)} %get-tuple-element.122.refs_0_, bf16[48,2304]{1,0:T(8,128)(2,1)S(1)} %bitcast.44, bf16[48,2304]{1,0:T(8,128)(2,1)S(1)} %bitcast.46, bf16[48,2304]{1,0:T(8,128)(2,1)S(1)} %bitcast.45, ...), custom_call_target="tpu_custom_call" | custom-call | flops 920000000 | bytes 1 | tf_op jit(solution)/shard_map/ffn_out/pallas_call | solution.py:521
  137.6 1.8 %mixer_out.1 = (f32[96,768]{1,0:T(8,128)}, f32[96,768]{1,0:T(8,128)}, f32[96,768]{1,0:T(8,128)}, f32[96,384]{1,0:T(8,128)}, f32[96]{0:T(128)}, /*index=5*/f32[96...) custom-call(s32[2]{0:T(128)S(1)} %get-tuple-element.122.refs_0_, bf16[48,1408]{1,0:T(8,128)(2,1)S(1)} %bitcast.42, ...), custom_call_target="tpu_custom_call" | custom-call | flops 920000000 | bytes 1 | tf_op jit(solution)/shard_map/mixer_out/pallas_call | solution.py:521
  (90 shorter events, 16.3 us)
Async XLA Ops:
  2.0 7.8 %copy-start.3 = (bf16[768,768]{1,0:T(8,128)(2,1)S(1)}, bf16[768,768]{1,0:T(8,128)(2,1)}, u32[]{:S(2)}) copy-start(bf16[768,768]{1,0:T(8,128)(2,1)} %refs_7_.2) | copy-start | bytes 3538948
  2.0 7.8 %copy-start.4 = (bf16[768,384]{1,0:T(8,128)(2,1)S(1)}, bf16[768,384]{1,0:T(8,128)(2,1)}, u32[]{:S(2)}) copy-start(bf16[768,384]{1,0:T(8,128)(2,1)} %refs_8_.3) | copy-start | bytes 1769476
  2.0 7.8 %copy-start.6 = (f32[768]{0:T(1024)S(1)}, f32[768]{0:T(1024)}, u32[]{:S(2)}) copy-start(f32[768]{0:T(1024)} %refs_9_.1) | copy-start | bytes 9220
  2.0 7.8 %copy-start.10 = (bf16[3,256,768]{2,1,0:T(8,128)(2,1)S(1)}, bf16[3,256,768]{2,1,0:T(8,128)(2,1)}, u32[]{:S(2)}) copy-start(bf16[3,256,768]{2,1,0:T(8,128)(2,1)} %param.15) | copy-start | bytes 3538948
  2.0 7.8 %copy-start.13 = (f32[384]{0:T(512)S(1)}, f32[384]{0:T(512)}, u32[]{:S(2)}) copy-start(f32[384]{0:T(512)} %refs_5_.4) | copy-start | bytes 4612
  2.6 11.9 %collective-permute-start = (f32[4,2,384]{2,1,0:T(2,128)S(1)}, f32[4,2,384]{2,1,0:T(2,128)S(1)}, u32[]{:S(2)}, u32[]{:S(2)}) collective-permute-start(f32[4,2,384]{2,1,0:T(2,128)S(1)} %get-tuple-element.124.refs_1_.refs_5_), channel_id=1, source_target_pairs={{0,1},{1,2},{2,3},{3,0},{4,5},{5,6},{6,7},{7,4},{8,9},{9,10},{10,1... | collective-permute-start | bytes 36872 | tf_op jit(solution)/shard_map/ppermute | solution.py:538
  5.7 8.8 %collective-permute-start.1 = (f32[4,2,384]{2,1,0:T(2,128)S(1)}, f32[4,2,384]{2,1,0:T(2,128)S(1)}, u32[]{:S(2)}, u32[]{:S(2)}) collective-permute-start(f32[4,2,384]{2,1,0:T(2,128)S(1)} %get-tuple-element.124.refs_1_.refs_5_), channel_id=1, source_target_pairs={{0,2},{1,3},{2,0},{3,1},{4,6},{5,7},{6,4},{7,5},{8,10},{9,11},{10,... | collective-permute-start | bytes 36872 | tf_op jit(solution)/shard_map/ppermute | solution.py:538
  8.3 6.2 %collective-permute-start.2 = (f32[4,2,384]{2,1,0:T(2,128)S(1)}, f32[4,2,384]{2,1,0:T(2,128)S(1)}, u32[]{:S(2)}, u32[]{:S(2)}) collective-permute-start(f32[4,2,384]{2,1,0:T(2,128)S(1)} %get-tuple-element.124.refs_1_.refs_5_), channel_id=1, source_target_pairs={{0,3},{1,0},{2,1},{3,2},{4,7},{5,4},{6,5},{7,6},{8,11},{9,8},{10,9... | collective-permute-start | bytes 36872 | tf_op jit(solution)/shard_map/ppermute | solution.py:538
  14.5 5.5 %copy-start.9 = (bf16[1536,768]{1,0:T(8,128)(2,1)S(1)}, bf16[1536,768]{1,0:T(8,128)(2,1)}, u32[]{:S(2)}) copy-start(bf16[1536,768]{1,0:T(8,128)(2,1)} %refs_3_.13) | copy-start | bytes 7077892
  14.5 5.5 %copy-start.11 = (bf16[3,256,768]{2,1,0:T(8,128)(2,1)S(1)}, bf16[3,256,768]{2,1,0:T(8,128)(2,1)}, u32[]{:S(2)}) copy-start(bf16[3,256,768]{2,1,0:T(8,128)(2,1)} %param.29) | copy-start | bytes 3538948
  16.2 7.8 %collective-permute-start.3 = (f32[3,4,384]{2,1,0:T(4,128)S(1)}, f32[3,4,384]{2,1,0:T(4,128)S(1)}, u32[]{:S(2)}, u32[]{:S(2)}) collective-permute-start(f32[3,4,384]{2,1,0:T(4,128)S(1)} %get-tuple-element.125.refs_1_), channel_id=1, source_target_pairs={{0,1},{1,2},{2,3},{3,0},{4,5},{5,6},{6,7},{7,4},{8,9},{9,10},{10,1... | collective-permute-start | bytes 55304 | tf_op jit(solution)/shard_map/ppermute | solution.py:538
  16.9 7.1 %collective-permute-start.4 = (f32[3,4,384]{2,1,0:T(4,128)S(1)}, f32[3,4,384]{2,1,0:T(4,128)S(1)}, u32[]{:S(2)}, u32[]{:S(2)}) collective-permute-start(f32[3,4,384]{2,1,0:T(4,128)S(1)} %get-tuple-element.125.refs_1_), channel_id=1, source_target_pairs={{0,2},{1,3},{2,0},{3,1},{4,6},{5,7},{6,4},{7,5},{8,10},{9,11},{10,... | collective-permute-start | bytes 55304 | tf_op jit(solution)/shard_map/ppermute | solution.py:538
  17.4 6.6 %collective-permute-start.5 = (f32[3,4,384]{2,1,0:T(4,128)S(1)}, f32[3,4,384]{2,1,0:T(4,128)S(1)}, u32[]{:S(2)}, u32[]{:S(2)}) collective-permute-start(f32[3,4,384]{2,1,0:T(4,128)S(1)} %get-tuple-element.125.refs_1_), channel_id=1, source_target_pairs={{0,3},{1,0},{2,1},{3,2},{4,7},{5,4},{6,5},{7,6},{8,11},{9,8},{10,9... | collective-permute-start | bytes 55304 | tf_op jit(solution)/shard_map/ppermute | solution.py:538
  20.1 2.8 %copy-start.2 = (bf16[768,768]{1,0:T(8,128)(2,1)S(1)}, bf16[768,768]{1,0:T(8,128)(2,1)}, u32[]{:S(2)}) copy-start(bf16[768,768]{1,0:T(8,128)(2,1)} %refs_5_.6) | copy-start | bytes 3538948
  22.9 1.3 copy-start.5
  24.2 5.4 %copy-start = (bf16[768,1536]{1,0:T(8,128)(2,1)S(1)}, bf16[768,1536]{1,0:T(8,128)(2,1)}, u32[]{:S(2)}) copy-start(bf16[768,1536]{1,0:T(8,128)(2,1)} %refs_5_.7) | copy-start | bytes 7077892
  24.2 5.4 %copy-start.1 = (bf16[768,1536]{1,0:T(8,128)(2,1)S(1)}, bf16[768,1536]{1,0:T(8,128)(2,1)}, u32[]{:S(2)}) copy-start(bf16[768,1536]{1,0:T(8,128)(2,1)} %refs_6_.5) | copy-start | bytes 7077892
  24.2 5.4 %copy-start.8 = (f32[768]{0:T(1024)S(1)}, f32[768]{0:T(1024)}, u32[]{:S(2)}) copy-start(f32[768]{0:T(1024)} %refs_7_.3) | copy-start | bytes 9220
  35.0 7.8 %collective-permute-start.6 = (bf16[384,1536]{1,0:T(8,128)(2,1)S(1)}, bf16[384,1536]{1,0:T(8,128)(2,1)S(1)}, u32[]{:S(2)}, u32[]{:S(2)}) collective-permute-start(bf16[384,1536]{1,0:T(8,128)(2,1)S(1)} %get-tuple-element.139.refs_8_), channel_id=1, source_target_pairs={{0,4},{4,0},{8,12},{12,8},{16,20},{20,16},{24,28},{28,24},{1,5},{5... | collective-permute-start | bytes 3538952 | tf_op jit(solution)/shard_map/ppermute | solution.py:546
  42.2 7.0 %collective-permute-start.7 = (bf16[384,1536]{1,0:T(8,128)(2,1)S(1)}, bf16[384,1536]{1,0:T(8,128)(2,1)S(1)}, u32[]{:S(2)}, u32[]{:S(2)}) collective-permute-start(bf16[384,1536]{1,0:T(8,128)(2,1)S(1)} %get-tuple-element.149), channel_id=1, source_target_pairs={{0,4},{4,0},{8,12},{12,8},{16,20},{20,16},{24,28},{28,24},{1,5},{5... | collective-permute-start | bytes 3538952 | tf_op jit(solution)/shard_map/ppermute | solution.py:546
  42.7 6.4 %collective-permute-start.8 = (bf16[768,768]{1,0:T(8,128)(2,1)S(1)}, bf16[768,768]{1,0:T(8,128)(2,1)S(1)}, u32[]{:S(2)}, u32[]{:S(2)}) collective-permute-start(bf16[768,768]{1,0:T(8,128)(2,1)S(1)} %get-tuple-element.151), channel_id=1, source_target_pairs={{0,4},{4,0},{8,12},{12,8},{16,20},{20,16},{24,28},{28,24},{1,5},{5... | collective-permute-start | bytes 3538952 | tf_op jit(solution)/shard_map/ppermute | solution.py:546
  43.7 16.6 %collective-permute-start.10 = (bf16[2,96,768]{2,1,0:T(8,128)(2,1)S(1)}, bf16[2,96,768]{2,1,0:T(8,128)(2,1)S(1)}, u32[]{:S(2)}, u32[]{:S(2)}) collective-permute-start(bf16[2,96,768]{2,1,0:T(8,128)(2,1)S(1)} %get-tuple-element.160), channel_id=1, source_target_pairs={{0,16},{4,20},{8,24},{12,28},{16,0},{20,4},{24,8},{28,12},{1,17},{... | collective-permute-start | bytes 884744 | tf_op jit(solution)/shard_map/ppermute | solution.py:546
  45.3 15.0 %collective-permute-start.9 = (bf16[2,96,768]{2,1,0:T(8,128)(2,1)S(1)}, bf16[2,96,768]{2,1,0:T(8,128)(2,1)S(1)}, u32[]{:S(2)}, u32[]{:S(2)}) collective-permute-start(bf16[2,96,768]{2,1,0:T(8,128)(2,1)S(1)} %get-tuple-element.158), channel_id=1, source_target_pairs={{0,8},{4,12},{8,0},{12,4},{16,24},{20,28},{24,16},{28,20},{1,9},{5... | collective-permute-start | bytes 884744 | tf_op jit(solution)/shard_map/ppermute | solution.py:546
  50.3 16.7 %collective-permute-start.11 = (bf16[2,96,1536]{2,1,0:T(8,128)(2,1)S(1)}, bf16[2,96,1536]{2,1,0:T(8,128)(2,1)S(1)}, u32[]{:S(2)}, u32[]{:S(2)}) collective-permute-start(bf16[2,96,1536]{2,1,0:T(8,128)(2,1)S(1)} %get-tuple-element.162), channel_id=1, source_target_pairs={{0,8},{4,12},{8,0},{12,4},{16,24},{20,28},{24,16},{28,20},{1,9},{5... | collective-permute-start | bytes 1769480 | tf_op jit(solution)/shard_map/ppermute | solution.py:546
  50.9 16.1 %collective-permute-start.12 = (bf16[2,96,1536]{2,1,0:T(8,128)(2,1)S(1)}, bf16[2,96,1536]{2,1,0:T(8,128)(2,1)S(1)}, u32[]{:S(2)}, u32[]{:S(2)}) collective-permute-start(bf16[2,96,1536]{2,1,0:T(8,128)(2,1)S(1)} %get-tuple-element.165), channel_id=1, source_target_pairs={{0,16},{4,20},{8,24},{12,28},{16,0},{20,4},{24,8},{28,12},{1,17},{... | collective-permute-start | bytes 1769480 | tf_op jit(solution)/shard_map/ppermute | solution.py:546
  61.1 11.3 %collective-permute-start.13 = (f32[3,2,384]{2,1,0:T(2,128)S(1)}, f32[3,2,384]{2,1,0:T(2,128)S(1)}, u32[]{:S(2)}, u32[]{:S(2)}) collective-permute-start(f32[3,2,384]{2,1,0:T(2,128)S(1)} %get-tuple-element.173.refs_5_), channel_id=1, source_target_pairs={{0,1},{1,2},{2,3},{3,0},{4,5},{5,6},{6,7},{7,4},{8,9},{9,10},{10,1... | collective-permute-start | bytes 27656 | tf_op jit(solution)/shard_map/ppermute | solution.py:538
  61.8 10.6 %collective-permute-start.14 = (f32[3,2,384]{2,1,0:T(2,128)S(1)}, f32[3,2,384]{2,1,0:T(2,128)S(1)}, u32[]{:S(2)}, u32[]{:S(2)}) collective-permute-start(f32[3,2,384]{2,1,0:T(2,128)S(1)} %get-tuple-element.173.refs_5_), channel_id=1, source_target_pairs={{0,2},{1,3},{2,0},{3,1},{4,6},{5,7},{6,4},{7,5},{8,10},{9,11},{10,... | collective-permute-start | bytes 27656 | tf_op jit(solution)/shard_map/ppermute | solution.py:538
  63.3 9.2 %collective-permute-start.15 = (f32[3,2,384]{2,1,0:T(2,128)S(1)}, f32[3,2,384]{2,1,0:T(2,128)S(1)}, u32[]{:S(2)}, u32[]{:S(2)}) collective-permute-start(f32[3,2,384]{2,1,0:T(2,128)S(1)} %get-tuple-element.173.refs_5_), channel_id=1, source_target_pairs={{0,3},{1,0},{2,1},{3,2},{4,7},{5,4},{6,5},{7,6},{8,11},{9,8},{10,9... | collective-permute-start | bytes 27656 | tf_op jit(solution)/shard_map/ppermute | solution.py:538
  67.8 11.5 %collective-permute-start.18 = (bf16[1,96,2304]{2,1,0:T(8,128)(2,1)S(1)}, bf16[1,96,2304]{2,1,0:T(8,128)(2,1)S(1)}, u32[]{:S(2)}, u32[]{:S(2)}) collective-permute-start(bf16[1,96,2304]{2,1,0:T(8,128)(2,1)S(1)} %get-tuple-element.184), channel_id=1, source_target_pairs={{0,16},{4,20},{8,24},{12,28},{16,0},{20,4},{24,8},{28,12},{1,17},{... | collective-permute-start | bytes 1327112 | tf_op jit(solution)/shard_map/ppermute | solution.py:546
  68.6 11.0 %collective-permute-start.19 = (bf16[1,96,2304]{2,1,0:T(8,128)(2,1)S(1)}, bf16[1,96,2304]{2,1,0:T(8,128)(2,1)S(1)}, u32[]{:S(2)}, u32[]{:S(2)}) collective-permute-start(bf16[1,96,2304]{2,1,0:T(8,128)(2,1)S(1)} %get-tuple-element.186), channel_id=1, source_target_pairs={{0,8},{4,12},{8,0},{12,4},{16,24},{20,28},{24,16},{28,20},{1,9},{5... | collective-permute-start | bytes 1327112 | tf_op jit(solution)/shard_map/ppermute | solution.py:546
  77.9 4.6 %collective-permute-start.17 = (bf16[384,1280]{1,0:T(8,128)(2,1)S(1)}, bf16[384,1280]{1,0:T(8,128)(2,1)S(1)}, u32[]{:S(2)}, u32[]{:S(2)}) collective-permute-start(bf16[384,1280]{1,0:T(8,128)(2,1)S(1)} %get-tuple-element.183.refs_5_), channel_id=1, source_target_pairs={{0,4},{4,0},{8,12},{12,8},{16,20},{20,16},{24,28},{28,24},{1,5},{5... | collective-permute-start | bytes 2949128 | tf_op jit(solution)/shard_map/ppermute | solution.py:546
  78.0 4.5 %collective-permute-start.16 = (bf16[384,1536]{1,0:T(8,128)(2,1)S(1)}, bf16[384,1536]{1,0:T(8,128)(2,1)S(1)}, u32[]{:S(2)}, u32[]{:S(2)}) collective-permute-start(bf16[384,1536]{1,0:T(8,128)(2,1)S(1)} %get-tuple-element.172.refs_19_), channel_id=1, source_target_pairs={{0,4},{4,0},{8,12},{12,8},{16,20},{20,16},{24,28},{28,24},{1,5},{5... | collective-permute-start | bytes 3538952 | tf_op jit(solution)/shard_map/ppermute | solution.py:546
  80.4 11.7 %collective-permute-start.22 = (bf16[1,48,2304]{2,1,0:T(8,128)(2,1)S(1)}, bf16[1,48,2304]{2,1,0:T(8,128)(2,1)S(1)}, u32[]{:S(2)}, u32[]{:S(2)}) collective-permute-start(bf16[1,48,2304]{2,1,0:T(8,128)(2,1)S(1)} %get-tuple-element.192), channel_id=1, source_target_pairs={{0,1},{1,0},{2,3},{3,2},{4,5},{5,4},{6,7},{7,6},{8,9},{9,8},{10,11... | collective-permute-start | bytes 663560 | tf_op jit(solution)/shard_map/ppermute | solution.py:546
  81.0 11.1 %collective-permute-start.23 = (bf16[1,48,2304]{2,1,0:T(8,128)(2,1)S(1)}, bf16[1,48,2304]{2,1,0:T(8,128)(2,1)S(1)}, u32[]{:S(2)}, u32[]{:S(2)}) collective-permute-start(bf16[1,48,2304]{2,1,0:T(8,128)(2,1)S(1)} %get-tuple-element.194), channel_id=1, source_target_pairs={{0,2},{1,3},{2,0},{3,1},{4,6},{5,7},{6,4},{7,5},{8,10},{9,11},{10,... | collective-permute-start | bytes 663560 | tf_op jit(solution)/shard_map/ppermute | solution.py:546
  83.6 14.1 %collective-permute-start.20 = (bf16[2,96,1408]{2,1,0:T(8,128)(2,1)S(1)}, bf16[2,96,1408]{2,1,0:T(8,128)(2,1)S(1)}, u32[]{:S(2)}, u32[]{:S(2)}) collective-permute-start(bf16[2,96,1408]{2,1,0:T(8,128)(2,1)S(1)} %get-tuple-element.189), channel_id=1, source_target_pairs={{0,8},{4,12},{8,0},{12,4},{16,24},{20,28},{24,16},{28,20},{1,9},{5... | collective-permute-start | bytes 1622024 | tf_op jit(solution)/shard_map/ppermute | solution.py:546
  85.1 12.8 %collective-permute-start.21 = (bf16[2,96,1408]{2,1,0:T(8,128)(2,1)S(1)}, bf16[2,96,1408]{2,1,0:T(8,128)(2,1)S(1)}, u32[]{:S(2)}, u32[]{:S(2)}) collective-permute-start(bf16[2,96,1408]{2,1,0:T(8,128)(2,1)S(1)} %get-tuple-element.191), channel_id=1, source_target_pairs={{0,16},{4,20},{8,24},{12,28},{16,0},{20,4},{24,8},{28,12},{1,17},{... | collective-permute-start | bytes 1622024 | tf_op jit(solution)/shard_map/ppermute | solution.py:546
  92.2 17.9 %collective-permute-start.28 = (bf16[1,48,2304]{2,1,0:T(8,128)(2,1)S(1)}, bf16[1,48,2304]{2,1,0:T(8,128)(2,1)S(1)}, u32[]{:S(2)}, u32[]{:S(2)}) collective-permute-start(bf16[1,48,2304]{2,1,0:T(8,128)(2,1)S(1)} %get-tuple-element.197.refs_5_.refs_0_), channel_id=1, source_target_pairs={{0,2},{1,3},{2,0},{3,1},{4,6},{5,7},{6,4},{7,5},{8,10},{9,11},{10,... | collective-permute-start | bytes 663560 | tf_op jit(solution)/shard_map/ppermute | solution.py:546
  93.7 16.4 %collective-permute-start.29 = (bf16[1,48,2304]{2,1,0:T(8,128)(2,1)S(1)}, bf16[1,48,2304]{2,1,0:T(8,128)(2,1)S(1)}, u32[]{:S(2)}, u32[]{:S(2)}) collective-permute-start(bf16[1,48,2304]{2,1,0:T(8,128)(2,1)S(1)} %get-tuple-element.210.refs_2_), channel_id=1, source_target_pairs={{0,1},{1,0},{2,3},{3,2},{4,5},{5,4},{6,7},{7,6},{8,9},{9,8},{10,11... | collective-permute-start | bytes 663560 | tf_op jit(solution)/shard_map/ppermute | solution.py:546
  98.7 7.2 %collective-permute-start.24 = (bf16[1,96,1408]{2,1,0:T(8,128)(2,1)S(1)}, bf16[1,96,1408]{2,1,0:T(8,128)(2,1)S(1)}, u32[]{:S(2)}, u32[]{:S(2)}) collective-permute-start(bf16[1,96,1408]{2,1,0:T(8,128)(2,1)S(1)} %get-tuple-element.202), channel_id=1, source_target_pairs={{0,16},{4,20},{8,24},{12,28},{16,0},{20,4},{24,8},{28,12},{1,17},{... | collective-permute-start | bytes 811016 | tf_op jit(solution)/shard_map/ppermute | solution.py:546
  100.1 6.7 %collective-permute-start.25 = (bf16[1,96,1408]{2,1,0:T(8,128)(2,1)S(1)}, bf16[1,96,1408]{2,1,0:T(8,128)(2,1)S(1)}, u32[]{:S(2)}, u32[]{:S(2)}) collective-permute-start(bf16[1,96,1408]{2,1,0:T(8,128)(2,1)S(1)} %get-tuple-element.204), channel_id=1, source_target_pairs={{0,8},{4,12},{8,0},{12,4},{16,24},{20,28},{24,16},{28,20},{1,9},{5... | collective-permute-start | bytes 811016 | tf_op jit(solution)/shard_map/ppermute | solution.py:546
  107.5 5.1 %collective-permute-start.26 = (bf16[1,48,1408]{2,1,0:T(8,128)(2,1)S(1)}, bf16[1,48,1408]{2,1,0:T(8,128)(2,1)S(1)}, u32[]{:S(2)}, u32[]{:S(2)}) collective-permute-start(bf16[1,48,1408]{2,1,0:T(8,128)(2,1)S(1)} %get-tuple-element.207), channel_id=1, source_target_pairs={{0,1},{1,0},{2,3},{3,2},{4,5},{5,4},{6,7},{7,6},{8,9},{9,8},{10,11... | collective-permute-start | bytes 405512 | tf_op jit(solution)/shard_map/ppermute | solution.py:546
  108.0 6.3 %collective-permute-start.27 = (bf16[1,48,1408]{2,1,0:T(8,128)(2,1)S(1)}, bf16[1,48,1408]{2,1,0:T(8,128)(2,1)S(1)}, u32[]{:S(2)}, u32[]{:S(2)}) collective-permute-start(bf16[1,48,1408]{2,1,0:T(8,128)(2,1)S(1)} %get-tuple-element.209), channel_id=1, source_target_pairs={{0,2},{1,3},{2,0},{3,1},{4,6},{5,7},{6,4},{7,5},{8,10},{9,11},{10,... | collective-permute-start | bytes 405512 | tf_op jit(solution)/shard_map/ppermute | solution.py:546
  114.4 11.2 %collective-permute-start.30 = (bf16[1,48,1408]{2,1,0:T(8,128)(2,1)S(1)}, bf16[1,48,1408]{2,1,0:T(8,128)(2,1)S(1)}, u32[]{:S(2)}, u32[]{:S(2)}) collective-permute-start(bf16[1,48,1408]{2,1,0:T(8,128)(2,1)S(1)} %get-tuple-element.212.refs_0_), channel_id=1, source_target_pairs={{0,2},{1,3},{2,0},{3,1},{4,6},{5,7},{6,4},{7,5},{8,10},{9,11},{10,... | collective-permute-start | bytes 405512 | tf_op jit(solution)/shard_map/ppermute | solution.py:546
  116.3 12.6 %collective-permute-start.31 = (bf16[1,48,1408]{2,1,0:T(8,128)(2,1)S(1)}, bf16[1,48,1408]{2,1,0:T(8,128)(2,1)S(1)}, u32[]{:S(2)}, u32[]{:S(2)}) collective-permute-start(bf16[1,48,1408]{2,1,0:T(8,128)(2,1)S(1)} %get-tuple-element.213.refs_2_), channel_id=1, source_target_pairs={{0,1},{1,0},{2,3},{3,2},{4,5},{5,4},{6,7},{7,6},{8,9},{9,8},{10,11... | collective-permute-start | bytes 405512 | tf_op jit(solution)/shard_map/ppermute | solution.py:546
  121.2 12.8 %collective-permute-start.34 = (bf16[1,48,2304]{2,1,0:T(8,128)(2,1)S(1)}, bf16[1,48,2304]{2,1,0:T(8,128)(2,1)S(1)}, u32[]{:S(2)}, u32[]{:S(2)}) collective-permute-start(bf16[1,48,2304]{2,1,0:T(8,128)(2,1)S(1)} %get-tuple-element.211.refs_4_), channel_id=1, source_target_pairs={{0,1},{1,0},{2,3},{3,2},{4,5},{5,4},{6,7},{7,6},{8,9},{9,8},{10,11... | collective-permute-start | bytes 663560 | tf_op jit(solution)/shard_map/ppermute | solution.py:546
  121.2 12.8 %collective-permute-start.35 = (bf16[1,48,2304]{2,1,0:T(8,128)(2,1)S(1)}, bf16[1,48,2304]{2,1,0:T(8,128)(2,1)S(1)}, u32[]{:S(2)}, u32[]{:S(2)}) collective-permute-start(bf16[1,48,2304]{2,1,0:T(8,128)(2,1)S(1)} %get-tuple-element.224), channel_id=1, source_target_pairs={{0,2},{1,3},{2,0},{3,1},{4,6},{5,7},{6,4},{7,5},{8,10},{9,11},{10,... | collective-permute-start | bytes 663560 | tf_op jit(solution)/shard_map/ppermute | solution.py:546
  129.0 7.9 %collective-permute-start.32 = (bf16[1,48,1408]{2,1,0:T(8,128)(2,1)S(1)}, bf16[1,48,1408]{2,1,0:T(8,128)(2,1)S(1)}, u32[]{:S(2)}, u32[]{:S(2)}) collective-permute-start(bf16[1,48,1408]{2,1,0:T(8,128)(2,1)S(1)} %get-tuple-element.214.refs_8_), channel_id=1, source_target_pairs={{0,1},{1,0},{2,3},{3,2},{4,5},{5,4},{6,7},{7,6},{8,9},{9,8},{10,11... | collective-permute-start | bytes 405512 | tf_op jit(solution)/shard_map/ppermute | solution.py:546
  129.0 8.5 %collective-permute-start.33 = (bf16[1,48,1408]{2,1,0:T(8,128)(2,1)S(1)}, bf16[1,48,1408]{2,1,0:T(8,128)(2,1)S(1)}, u32[]{:S(2)}, u32[]{:S(2)}) collective-permute-start(bf16[1,48,1408]{2,1,0:T(8,128)(2,1)S(1)} %get-tuple-element.215), channel_id=1, source_target_pairs={{0,2},{1,3},{2,0},{3,1},{4,6},{5,7},{6,4},{7,5},{8,10},{9,11},{10,... | collective-permute-start | bytes 405512 | tf_op jit(solution)/shard_map/ppermute | solution.py:546
  (3 other events, 2.6 us)
